TPU v7x, 32 devices: a whole 2x2x4 slice. The times are simulated.
32 devices in a mesh: groups: 2 (over y), seq: 8 (over z, x), head: 2 (over core).
Axes of the slice: x: 2, y: 2, z: 4, core: 2. Of those that a mesh axis runs over, the one named last changes fastest.
Arguments:
- queries: bfloat16 [8192, 2560], P(('groups', 'seq'), 'head'), parts along dimension 0, may hold values from -52 to 52
- keys: bfloat16 [8192, 512], P(('groups', 'seq'), 'head'), parts along dimension 0, may hold values from -4 to 4
- values: bfloat16 [8192, 512], P(('groups', 'seq'), 'head'), parts along dimension 0, may hold values from -4 to 4
- dest_shard: int32 [8192], P(('groups', 'seq')), parts along dimension 0, may hold values from 0 to 7, as said below
- dest_slot: int32 [8192], P(('groups', 'seq')), parts along dimension 0, may hold values from 0 to 511, as said below
- ancestors: int32 [64, 4], P(('groups', 'seq')), parts along dimension 0, may hold values from 0 to 31, as said below
Outputs:
- attended: bfloat16 [8192, 2560], P(('groups', 'seq'), 'head'), parts along dimension 0
There are 2 independent parts, one for each index of `groups`. A program takes and returns all parts, laid end to end along the dimension named above; each array names one. Nothing has to cross between parts.
Inputs may be any that keep to these rules, and one draw needn't show every extreme that they name: `dest_shard`: each shard sends 0, 64 or 128 of its rows to each shard, 128 to some, and every shard receives 512 rows in all. `dest_slot`: with dest_shard, a one-to-one map of the rows of a slab onto the balanced rows. `ancestors`: each entry of block b's list is a block from max(0, b - 4) to b; the first is its parent in its rollout tree, each further one the parent of the one before; b itself marks an unused entry; repeats may occur.
All inputs are finite; a program needn't handle non-finite values.
Results may differ from a plain program's by a relative error of at most 0.0048.
Values may be sent and summed in bfloat16 or wider, within the bound.
No kernel may reach another device: no remote copies, remote signals or barrier semaphores. Data moves between devices by JAX's collectives and lax.ppermute only.
A program may use at most 64 MiB of HBM per device.

v0:
```python
import math

import jax
import jax.numpy as jnp
from jax import lax
from jax.sharding import PartitionSpec as P

HEAD_SIZE = 128


def from_behind(block, axis, distance):
    devices = range(lax.axis_size(axis))
    route = [(i - distance, i) for i in devices if i - distance in devices]
    return lax.ppermute(block, axis, route)


def bucket_index(dest_shard, shards, capacity):
    onehot = (dest_shard[:, None] == jnp.arange(shards, dtype=jnp.int32)[None, :]).astype(jnp.int32)
    before = jnp.cumsum(onehot, axis=0) - onehot
    position = jnp.sum(before * onehot, axis=1)
    return dest_shard * capacity + position


def pack_rows(source, index, total):
    buffer = jnp.zeros((total, source.shape[1]), source.dtype)
    return buffer.at[index].set(source, mode="drop")


def place_rows(received, slots, count):
    target = jnp.zeros((count, received.shape[1]), received.dtype)
    return target.at[slots].set(received, mode="drop")


def mask_bias(anc_rows, shard, block_size):
    block_count = anc_rows.shape[0]
    query_blocks = shard * block_count + jnp.arange(block_count, dtype=jnp.int32)
    key_blocks = shard * block_count - block_count + jnp.arange(2 * block_count, dtype=jnp.int32)
    listed = jnp.any(anc_rows[:, :, None] == key_blocks[None, None, :], axis=1)
    earlier = (listed & (key_blocks[None, :] < query_blocks[:, None])).astype(jnp.bfloat16)
    itself = (key_blocks[None, :] == query_blocks[:, None]).astype(jnp.bfloat16)
    count = block_count * block_size
    query_pos = jnp.arange(count, dtype=jnp.int32)
    key_pos = jnp.arange(2 * count, dtype=jnp.int32)
    row_onehot = (
        query_pos[:, None] // block_size == jnp.arange(block_count, dtype=jnp.int32)[None, :]
    ).astype(jnp.bfloat16)
    col_onehot = (
        jnp.arange(2 * block_count, dtype=jnp.int32)[:, None] == key_pos[None, :] // block_size
    ).astype(jnp.bfloat16)
    earlier_rows = jnp.dot(
        jnp.dot(row_onehot, earlier, preferred_element_type=jnp.float32).astype(jnp.bfloat16),
        col_onehot,
        preferred_element_type=jnp.float32,
    )
    itself_rows = jnp.dot(
        jnp.dot(row_onehot, itself, preferred_element_type=jnp.float32).astype(jnp.bfloat16),
        col_onehot,
        preferred_element_type=jnp.float32,
    )
    causal = key_pos[None, :] - count <= query_pos[:, None]
    seen = (earlier_rows > 0.5) | (itself_rows > 0.5) & causal
    return jnp.where(seen, 0.0, -1e30).astype(jnp.float32)


def attend(query_rows, key_rows, value_rows, bias):
    q_heads = query_rows.shape[1] // HEAD_SIZE
    ratio = q_heads // (key_rows.shape[1] // HEAD_SIZE)
    scale = 1.0 / math.sqrt(HEAD_SIZE)

    def one_head(head, result):
        group = head // ratio
        query_part = lax.dynamic_slice_in_dim(query_rows, head * HEAD_SIZE, HEAD_SIZE, 1)
        key_part = lax.dynamic_slice_in_dim(key_rows, group * HEAD_SIZE, HEAD_SIZE, 1)
        value_part = lax.dynamic_slice_in_dim(value_rows, group * HEAD_SIZE, HEAD_SIZE, 1)
        scores = (
            lax.dot_general(
                query_part, key_part, (((1,), (1,)), ((), ())), preferred_element_type=jnp.float32
            )
            * scale
            + bias
        )
        peak = jnp.max(scores, axis=1, keepdims=True)
        expo = jnp.exp(scores - peak)
        weights = (expo / jnp.sum(expo, axis=1, keepdims=True)).astype(jnp.bfloat16)
        output = jnp.dot(weights, value_part, preferred_element_type=jnp.float32).astype(
            jnp.bfloat16
        )
        return lax.dynamic_update_slice_in_dim(result, output, head * HEAD_SIZE, 1)

    return lax.fori_loop(0, q_heads, one_head, jnp.zeros(query_rows.shape, jnp.bfloat16))


def local(queries, keys, values, dest_shard, dest_slot, ancestors):
    count = queries.shape[0]
    shards = lax.axis_size("seq")
    capacity = 2 * count // shards
    total = shards * capacity
    index = bucket_index(dest_shard, shards, capacity)
    empty_slots = jnp.full((total,), count, jnp.int32)
    slot_buffer = empty_slots.at[index].set(dest_slot)
    query_pack = pack_rows(queries, index, total)
    key_pack = pack_rows(keys, index, total)
    value_pack = pack_rows(values, index, total)
    moved = (
        lax.all_to_all(query_pack, "seq", split_axis=0, concat_axis=0, tiled=True),
        lax.all_to_all(key_pack, "seq", split_axis=0, concat_axis=0, tiled=True),
        lax.all_to_all(value_pack, "seq", split_axis=0, concat_axis=0, tiled=True),
    )
    got_slots = lax.all_to_all(slot_buffer, "seq", split_axis=0, concat_axis=0, tiled=True)
    own_q = place_rows(moved[0], got_slots, count)
    own_k = place_rows(moved[1], got_slots, count)
    own_v = place_rows(moved[2], got_slots, count)
    prior_k, prior_v = from_behind((own_k, own_v), "seq", 1)
    bias = mask_bias(ancestors, lax.axis_index("seq"), count // ancestors.shape[0])
    keys_all = jnp.concatenate([prior_k, own_k], axis=0)
    values_all = jnp.concatenate([prior_v, own_v], axis=0)
    return attend(own_q, keys_all, values_all, bias)


def solution(mesh):
    return jax.shard_map(
        local,
        mesh=mesh,
        in_specs=(
            P(("groups", "seq"), "head"),
            P(("groups", "seq"), "head"),
            P(("groups", "seq"), "head"),
            P(("groups", "seq")),
            P(("groups", "seq")),
            P(("groups", "seq"), None),
        ),
        out_specs=P(("groups", "seq"), "head"),
        check_vma=False,
    )
```

profile of v0, /device:TPU:16, one launch (start us, length us, event | category | flops | bytes accessed | tf_op | source)
XLA Modules:
  0.0 168.0 jit_solution(8725337372464127351)
XLA Ops:
  0.0 0.7 fusion.31
  0.7 1.1 reduce-window.6
  2.1 0.8 fusion.28
  2.8 0.7 compare_select_fusion.1
  3.5 3.2 %scatter_custom_fusion = s32[1024]{0:T(1024)} fusion(s32[512]{0:T(512)S(1)} %compare_select_fusion.1, s32[512]{0:T(512)} %param.12, s32[]{:T(128)} %constant.149.clone.1), kind=kCustom, calls=%fused_computation.69 | custom fusion | bytes 4608 | tf_op jit(solution)/shard_map/scatter | solution.py:100
  6.7 6.1 %all-to-all-start = ((s32[8,128,1]{1,2,0:T(1,128)}), s32[8,128,1]{1,2,0:T(1,128)S(1)}, u32[]{:S(2)}, u32[]{:S(2)}) async-start(s32[8,128,1]{1,2,0:T(1,128)} %bitcast.4), calls=%async_computation | async-start | bytes 8192 | tf_op jit(solution)/shard_map/all_to_all | solution.py:109
  12.8 3.5 %scatter_custom_fusion.3 = bf16[1024,256]{1,0:T(8,128)(2,1)} fusion(s32[512]{0:T(512)S(1)} %compare_select_fusion.1, bf16[512,256]{1,0:T(8,128)(2,1)} %param.9, bf16[]{:T(256)} %constant.148.clone.1), kind=kCustom, calls=%fused_computation.34 | custom fusion | bytes 524800 | tf_op jit(solution)/shard_map/scatter | solution.py:26
  16.4 0.6 all-to-all-done
  16.9 5.8 %all-to-all-start.2 = ((bf16[8,128,256]{2,1,0:T(8,128)(2,1)}), bf16[8,128,256]{2,1,0:T(8,128)(2,1)S(1)}, u32[]{:S(2)}, u32[]{:S(2)}) async-start(bf16[8,128,256]{2,1,0:T(8,128)(2,1)} %bitcast.9), calls=%async_computation.2 | async-start | bytes 1048576 | tf_op jit(solution)/shard_map/all_to_all | solution.py:106
  22.7 3.5 %scatter_custom_fusion.5 = bf16[1024,256]{1,0:T(8,128)(2,1)} fusion(s32[512]{0:T(512)S(1)} %compare_select_fusion.1, bf16[512,256]{1,0:T(8,128)(2,1)} %param.10, bf16[]{:T(256)} %constant.148.clone.1), kind=kCustom, calls=%fused_computation.32 | custom fusion | bytes 524800 | tf_op jit(solution)/shard_map/scatter | solution.py:26
  26.2 7.9 %all-to-all-done.2 = bf16[8,128,256]{2,1,0:T(8,128)(2,1)S(1)} async-done(((bf16[8,128,256]{2,1,0:T(8,128)(2,1)}), bf16[8,128,256]{2,1,0:T(8,128)(2,1)S(1)}, u32[]{:S(2)}, u32[]{:S(2)}) %all-to-all-start.2) | async-done | bytes 524320 | tf_op jit(solution)/shard_map/all_to_all | solution.py:106
  34.2 5.8 %all-to-all-start.3 = ((bf16[8,128,256]{2,1,0:T(8,128)(2,1)}), bf16[8,128,256]{2,1,0:T(8,128)(2,1)S(1)}, u32[]{:S(2)}, u32[]{:S(2)}) async-start(bf16[8,128,256]{2,1,0:T(8,128)(2,1)} %bitcast.11), calls=%async_computation.3 | async-start | bytes 1048576 | tf_op jit(solution)/shard_map/all_to_all | solution.py:107
  40.0 5.4 %scatter_custom_fusion.1 = bf16[1024,1280]{1,0:T(8,128)(2,1)} fusion(s32[512]{0:T(512)S(1)} %compare_select_fusion.1, bf16[512,1280]{1,0:T(8,128)(2,1)} %param.8, bf16[]{:T(256)} %constant.148.clone.1), kind=kCustom, calls=%fused_computation.22 | custom fusion | bytes 2621952 | tf_op jit(solution)/shard_map/scatter | solution.py:26
  45.4 6.2 %all-to-all-done.3 = bf16[8,128,256]{2,1,0:T(8,128)(2,1)S(1)} async-done(((bf16[8,128,256]{2,1,0:T(8,128)(2,1)}), bf16[8,128,256]{2,1,0:T(8,128)(2,1)S(1)}, u32[]{:S(2)}, u32[]{:S(2)}) %all-to-all-start.3) | async-done | bytes 524320 | tf_op jit(solution)/shard_map/all_to_all | solution.py:107
  51.6 6.6 %all-to-all-start.1 = ((bf16[8,128,1280]{2,1,0:T(8,128)(2,1)}), bf16[8,128,1280]{2,1,0:T(8,128)(2,1)}, u32[]{:S(2)}, u32[]{:S(2)}) async-start(bf16[8,128,1280]{2,1,0:T(8,128)(2,1)} %bitcast.7), calls=%async_computation.1 | async-start | bytes 5242880 | tf_op jit(solution)/shard_map/all_to_all | solution.py:105
  58.3 2.1 %fusion.12 = f32[512,1024]{1,0:T(8,128)} fusion(s32[512]{0:T(512)S(1)} %add_select_fusion.1, s32[1024]{0:T(1024)S(1)} %get-tuple-element.175, pred[4,8]{1,0:T(4,128)(4,1)S(1)} %compare_reduce_fusion, s32[8]{0:T(128)S(1)} %iota_add_fusion.2, s32[4]{0:T(128)S(1)} %iota_add_fusion.1), kind=kOutput, calls=%fused_computation.26 | convolution fusion | flops 8435776 | bytes 2103376 | tf_op jit(solution)/shard_map/dot_general | solution.py:50
  60.4 5.0 %scatter_custom_fusion.4 = bf16[512,256]{1,0:T(8,128)(2,1)S(1)} fusion(s32[1024]{0:T(1024)S(1)} %bitcast.24, bf16[1024,256]{1,0:T(8,128)(2,1)S(1)} %bitcast.21, bf16[]{:T(256)} %constant.148.clone.1), kind=kCustom, calls=%fused_computation.40 | custom fusion | bytes 262146 | tf_op jit(solution)/shard_map/scatter | solution.py:31
  65.4 3.4 %collective-permute-start = (bf16[512,256]{1,0:T(8,128)(2,1)S(1)}, bf16[512,256]{1,0:T(8,128)(2,1)S(1)}, u32[]{:S(2)}, u32[]{:S(2)}) collective-permute-start(bf16[512,256]{1,0:T(8,128)(2,1)S(1)} %scatter_custom_fusion.4), channel_id=1, source_target_pairs={{0,2},{2,4},{4,6},{6,8},{8,10},{10,12},{12,14},{1,3},{3,5},{5,7},{... | collective-permute-start | bytes 786440 | tf_op jit(solution)/shard_map/ppermute | solution.py:14
  68.8 5.0 %scatter_custom_fusion.6 = bf16[512,256]{1,0:T(8,128)(2,1)S(1)} fusion(s32[1024]{0:T(1024)S(1)} %bitcast.25, bf16[1024,256]{1,0:T(8,128)(2,1)S(1)} %bitcast.22, bf16[]{:T(256)} %constant.148.clone.1), kind=kCustom, calls=%fused_computation.38 | custom fusion | bytes 262146 | tf_op jit(solution)/shard_map/scatter | solution.py:31
  73.7 3.4 %collective-permute-start.1 = (bf16[512,256]{1,0:T(8,128)(2,1)S(1)}, bf16[512,256]{1,0:T(8,128)(2,1)}, u32[]{:S(2)}, u32[]{:S(2)}) collective-permute-start(bf16[512,256]{1,0:T(8,128)(2,1)S(1)} %scatter_custom_fusion.6), channel_id=1, source_target_pairs={{0,2},{2,4},{4,6},{6,8},{8,10},{10,12},{12,14},{1,3},{3,5},{5,7},{... | collective-permute-start | bytes 786440 | tf_op jit(solution)/shard_map/ppermute | solution.py:14
  77.1 2.6 %fusion.9 = f32[512,1024]{1,0:T(8,128)S(1)} fusion(f32[512,1024]{1,0:T(8,128)} %fusion.12, s32[1024]{0:T(1024)S(1)} %get-tuple-element.176, s32[512]{0:T(512)S(1)} %add_select_fusion.1, s32[1024]{0:T(1024)S(1)} %get-tuple-element.175, s32[8]{0:T(128)S(1)} %iota_add_fusion.2, s32[4]{0:T(128)S(1)} %iota_add_fusion.1), kind=kOutput, calls=%fused_computation.21 | convolution fusion | flops 11581472 | bytes 4204592 | tf_op jit(solution)/shard_map/dot_general | solution.py:55
  79.7 41.0 %collective-permute-done = bf16[512,256]{1,0:T(8,128)(2,1)S(1)} collective-permute-done((bf16[512,256]{1,0:T(8,128)(2,1)S(1)}, bf16[512,256]{1,0:T(8,128)(2,1)S(1)}, u32[]{:S(2)}, u32[]{:S(2)}) %collective-permute-start) | collective-permute-done | bytes 262176 | tf_op jit(solution)/shard_map/ppermute | solution.py:14
  120.7 5.6 %collective-permute-done.1 = bf16[512,256]{1,0:T(8,128)(2,1)} collective-permute-done((bf16[512,256]{1,0:T(8,128)(2,1)S(1)}, bf16[512,256]{1,0:T(8,128)(2,1)}, u32[]{:S(2)}, u32[]{:S(2)}) %collective-permute-start.1) | collective-permute-done | bytes 262176 | tf_op jit(solution)/shard_map/ppermute | solution.py:14
  126.3 1.8 %pad_maximum_fusion.1 = bf16[1024,256]{1,0:T(8,128)(2,1)} fusion(bf16[512,256]{1,0:T(8,128)(2,1)S(1)} %scatter_custom_fusion.6, bf16[512,256]{1,0:T(8,128)(2,1)} %collective-permute-done.1), kind=kLoop, calls=%fused_computation.30 | loop fusion | flops 1048576 | bytes 1048576 | tf_op jit(solution)/shard_map/concatenate | solution.py:116
  128.1 7.2 %scatter_custom_fusion.2 = bf16[512,1280]{1,0:T(8,128)(2,1)} fusion(s32[1024]{0:T(1024)S(1)} %bitcast.26, bf16[1024,1280]{1,0:T(8,128)(2,1)} %bitcast.8, bf16[]{:T(256)} %constant.148.clone.1), kind=kCustom, calls=%fused_computation.27 | custom fusion | bytes 1311232 | tf_op jit(solution)/shard_map/scatter | solution.py:31
  135.3 1.1 broadcast.160
  136.5 31.5 %while.15 = (s32[]{:T(128)}, bf16[512,1280]{1,0:T(8,128)(2,1)}, bf16[512,1280]{1,0:T(8,128)(2,1)}, bf16[1024,256]{1,0:T(8,128)(2,1)S(1)}, f32[512,1024]{1,0:T(8,...) while((s32[]{:T(128)}, bf16[512,1280]{1,0:T(8,128)(2,1)}, ...), condition=%wide.region_14.15_spmd, body=%wide.region_11.14_spmd.sunk | while | flops 272694272 | bytes 9185591 | solution.py:90
  136.5 1.4 fusion.60
  137.9 0.5 fusion.61
  138.4 1.2 fusion.62
  139.6 1.4 fusion.60
  141.6 1.2 fusion.62
  142.8 1.4 fusion.60
  144.7 1.2 fusion.62
  145.9 1.4 fusion.60
  147.9 1.2 fusion.62
  149.1 1.4 fusion.60
  151.0 1.2 fusion.62
  152.2 1.4 fusion.60
  154.2 1.2 fusion.62
  155.4 1.4 fusion.60
  157.3 1.2 fusion.62
  158.5 1.4 fusion.60
  160.5 1.2 fusion.62
  161.7 1.4 fusion.60
  163.6 1.2 fusion.62
  164.9 1.4 fusion.60
  166.8 1.2 fusion.62
  (24 shorter events, 5.0 us)
Async XLA Ops:
  6.7 10.2 %all-to-all-start = ((s32[8,128,1]{1,2,0:T(1,128)}), s32[8,128,1]{1,2,0:T(1,128)S(1)}, u32[]{:S(2)}, u32[]{:S(2)}) async-start(s32[8,128,1]{1,2,0:T(1,128)} %bitcast.4), calls=%async_computation | async-start | bytes 8192 | tf_op jit(solution)/shard_map/all_to_all | solution.py:109
  16.9 17.2 %all-to-all-start.2 = ((bf16[8,128,256]{2,1,0:T(8,128)(2,1)}), bf16[8,128,256]{2,1,0:T(8,128)(2,1)S(1)}, u32[]{:S(2)}, u32[]{:S(2)}) async-start(bf16[8,128,256]{2,1,0:T(8,128)(2,1)} %bitcast.9), calls=%async_computation.2 | async-start | bytes 1048576 | tf_op jit(solution)/shard_map/all_to_all | solution.py:106
  34.2 17.4 %all-to-all-start.3 = ((bf16[8,128,256]{2,1,0:T(8,128)(2,1)}), bf16[8,128,256]{2,1,0:T(8,128)(2,1)S(1)}, u32[]{:S(2)}, u32[]{:S(2)}) async-start(bf16[8,128,256]{2,1,0:T(8,128)(2,1)} %bitcast.11), calls=%async_computation.3 | async-start | bytes 1048576 | tf_op jit(solution)/shard_map/all_to_all | solution.py:107
  51.6 6.6 %copy-start.1 = (s32[4,4]{1,0:T(4,128)S(1)}, s32[4,4]{1,0:T(4,128)}, u32[]{:S(2)}) copy-start(s32[4,4]{1,0:T(4,128)} %param.13) | copy-start | bytes 196
  51.6 76.5 %all-to-all-start.1 = ((bf16[8,128,1280]{2,1,0:T(8,128)(2,1)}), bf16[8,128,1280]{2,1,0:T(8,128)(2,1)}, u32[]{:S(2)}, u32[]{:S(2)}) async-start(bf16[8,128,1280]{2,1,0:T(8,128)(2,1)} %bitcast.7), calls=%async_computation.1 | async-start | bytes 5242880 | tf_op jit(solution)/shard_map/all_to_all | solution.py:105
  65.4 55.3 %collective-permute-start = (bf16[512,256]{1,0:T(8,128)(2,1)S(1)}, bf16[512,256]{1,0:T(8,128)(2,1)S(1)}, u32[]{:S(2)}, u32[]{:S(2)}) collective-permute-start(bf16[512,256]{1,0:T(8,128)(2,1)S(1)} %scatter_custom_fusion.4), channel_id=1, source_target_pairs={{0,2},{2,4},{4,6},{6,8},{8,10},{10,12},{12,14},{1,3},{3,5},{5,7},{... | collective-permute-start | bytes 786440 | tf_op jit(solution)/shard_map/ppermute | solution.py:14
  73.7 52.6 %collective-permute-start.1 = (bf16[512,256]{1,0:T(8,128)(2,1)S(1)}, bf16[512,256]{1,0:T(8,128)(2,1)}, u32[]{:S(2)}, u32[]{:S(2)}) collective-permute-start(bf16[512,256]{1,0:T(8,128)(2,1)S(1)} %scatter_custom_fusion.6), channel_id=1, source_target_pairs={{0,2},{2,4},{4,6},{6,8},{8,10},{10,12},{12,14},{1,3},{3,5},{5,7},{... | collective-permute-start | bytes 786440 | tf_op jit(solution)/shard_map/ppermute | solution.py:14
  128.1 8.4 %copy-start = (bf16[1024,256]{1,0:T(8,128)(2,1)S(1)}, bf16[1024,256]{1,0:T(8,128)(2,1)}, u32[]{:S(2)}) copy-start(bf16[1024,256]{1,0:T(8,128)(2,1)} %pad_maximum_fusion.1) | copy-start | bytes 1572868
where the time goes:
time: 169 us; the launch traced here: 168 us
  waiting for transfers between devices  61.2 us (36%)
  local copies, waits for them, and re-layouts  34.2 us (20%)
  starting transfers between devices  31.1 us (18%)
  matrix products  31.1 us (18%)
  other arithmetic  10.4 us (6%)
    ppermute x2, waiting for transfers between devices, from_behind(): return lax.ppermute(block, axis, route)  46.6 us
    scatter x3, local copies, waits for them, and re-layouts, place_rows(): return target.at[slots].set(received, mode='drop')  17.1 us
    dot_general x10, matrix products, one_head(): lax.dot_general(query_part, key_part, (((1,), (1,)), ((), ())), preferred...  14.2 us
    scatter x3, local copies, waits for them, and re-layouts, pack_rows(): return buffer.at[index].set(source, mode='drop')  12.5 us
    dot_general x10, matrix products, one_head(): jnp.dot(weights, value_part, preferred_element_type=jnp.float32)  12.1 us
    all_to_all x1, waiting for transfers between devices, local(): lax.all_to_all(key_pack, 'seq', split_axis=0, concat_axis=0, tiled=True)  7.93 us
    ppermute x2, starting transfers between devices, from_behind(): return lax.ppermute(block, axis, route)  6.76 us
    all_to_all x1, starting transfers between devices, local(): lax.all_to_all(query_pack, 'seq', split_axis=0, concat_axis=0, tiled=True)  6.57 us
  transfers between devices with their start and end apart: 6, of which 5 were waited for; matrix products, arithmetic and copies ran while one was open for 17% of the time, Pallas kernels for 0%

commit v1 on v0

v1 whole, which is shorter than its diff:
```python
import functools
import math

import jax
import jax.numpy as jnp
from jax import lax
from jax.experimental import pallas as pl
from jax.experimental.pallas import tpu as pltpu
from jax.sharding import PartitionSpec as P

HEAD_SIZE = 128
META = 8
RADIX = 32
NO_DEST = 255.0
NEG = -1e30
VMEM_LIMIT = 56 * 1024 * 1024

VM = pl.BlockSpec(memory_space=pltpu.VMEM)
SM = pl.BlockSpec(memory_space=pltpu.SMEM)
HB = pl.BlockSpec(memory_space=pl.ANY)


def params():
    return pltpu.CompilerParams(vmem_limit_bytes=VMEM_LIMIT)


def iota(shape, axis):
    return lax.broadcasted_iota(jnp.int32, shape, axis)


def matmul(a, b):
    return jnp.dot(a, b, preferred_element_type=jnp.float32)


def matmul_nt(a, b):
    return lax.dot_general(a, b, (((1,), (1,)), ((), ())), preferred_element_type=jnp.float32)


def select_rows(index, start, rows, dtype=jnp.bfloat16):
    return (iota((rows, index.shape[1]), 0) + start == index).astype(dtype)


def pack_kv_kernel(shards, unit, me_ref, dest_ref, slot_ref, k_ref, v_ref, q_ref, *outs):
    blocks, over, index_ref = outs[:shards], outs[shards], outs[shards + 1]
    count = k_ref.shape[0]
    kv = k_ref.shape[1]
    me = me_ref[0]
    dest = dest_ref[...].reshape(1, count)
    code = slot_ref[...].reshape(1, count) + 1
    onehot = (iota((shards, count), 0) == dest).astype(jnp.bfloat16)
    earlier = (iota((count, count), 0) < iota((count, count), 1)).astype(jnp.bfloat16)
    before = matmul(onehot, earlier)
    position = jnp.sum(before * onehot.astype(jnp.float32), axis=0, keepdims=True).astype(jnp.int32)
    base = position < unit
    index = jnp.where(base, (dest ^ me) * unit + position, -1)
    index_ref[...] = index
    over_index = jnp.where(base, -1, position - unit)
    totals = matmul_nt(jnp.ones((META, count), jnp.bfloat16), onehot)
    flags = (totals > unit + 0.5).astype(jnp.float32)
    over_dest = jnp.max(jnp.where(base, -1, dest))
    over_value = jnp.where(over_dest < 0, NO_DEST, over_dest.astype(jnp.float32))

    row = iota((META, count), 0)
    codes = jnp.where(row == 0, code // RADIX, jnp.where(row == 1, code % RADIX, 0))
    codes = codes.astype(jnp.float32).astype(jnp.bfloat16)

    def meta(picked, tail, width):
        sent = matmul_nt(codes, picked)
        sent = jnp.concatenate([sent, tail, jnp.zeros((META, width - unit - tail.shape[1]), jnp.float32)], axis=1)
        return sent

    flag_rows = jnp.where(iota((META, shards), 0) == 2, flags, 0.0)
    for r in range(shards):
        picked = select_rows(index, r * unit, unit)
        blocks[r][0:unit, 0:kv] = matmul(picked, k_ref[...]).astype(jnp.bfloat16)
        blocks[r][0:unit, kv : 2 * kv] = matmul(picked, v_ref[...]).astype(jnp.bfloat16)
        blocks[r][unit : unit + META, :] = meta(picked, flag_rows, 2 * kv).astype(jnp.bfloat16)
    picked = select_rows(over_index, 0, unit)
    width = q_ref.shape[1]
    over[0:unit, 0:width] = matmul(picked, q_ref[...]).astype(jnp.bfloat16)
    over[0:unit, width : width + kv] = matmul(picked, k_ref[...]).astype(jnp.bfloat16)
    over[0:unit, width + kv : width + 2 * kv] = matmul(picked, v_ref[...]).astype(jnp.bfloat16)
    full = width + 2 * kv
    tail = meta(picked, jnp.zeros((META, 0 + unit), jnp.float32), full)
    tail = jnp.where(iota((META, full), 0) == 2, over_value, tail)
    over[unit : unit + META, :] = tail.astype(jnp.bfloat16)


def pack_kv(me, dest, slot, keys, values, queries, shards, unit):
    width = 2 * keys.shape[1]
    full = width + queries.shape[1]
    shapes = [jax.ShapeDtypeStruct((unit + META, width), jnp.bfloat16)] * shards
    shapes += [jax.ShapeDtypeStruct((unit + META, full), jnp.bfloat16)]
    shapes += [jax.ShapeDtypeStruct((1, keys.shape[0]), jnp.int32)]
    outs = pl.pallas_call(
        functools.partial(pack_kv_kernel, shards, unit),
        out_shape=shapes,
        in_specs=[SM, VM, VM, VM, VM, VM],
        out_specs=[VM] * len(shapes),
        compiler_params=params(),
        name="pack_kv",
    )(me, dest, slot, keys, values, queries)
    return outs[:shards], outs[shards], outs[shards + 1]


def pack_q_kernel(shards, unit, index_ref, q_ref, *blocks):
    index = index_ref[...]
    for r in range(shards):
        picked = select_rows(index, r * unit, unit)
        blocks[r][...] = matmul(picked, q_ref[...]).astype(jnp.bfloat16)


def pack_q(index, queries, shards, unit):
    return pl.pallas_call(
        functools.partial(pack_q_kernel, shards, unit),
        out_shape=[jax.ShapeDtypeStruct((unit, queries.shape[1]), jnp.bfloat16)] * shards,
        in_specs=[VM, VM],
        out_specs=[VM] * shards,
        compiler_params=params(),
        name="pack_q",
    )(index, queries)


def pick_over_kernel(unit, me_ref, a_ref, b_ref, c_ref, d_ref, keep_ref, send_ref):
    me = me_ref[0].astype(jnp.float32)
    other = (me_ref[0] ^ 1).astype(jnp.float32)
    keep = jnp.zeros(keep_ref.shape, jnp.float32)
    send = jnp.zeros(keep_ref.shape, jnp.float32)
    for ref in (a_ref, b_ref, c_ref, d_ref):
        block = ref[...].astype(jnp.float32)
        target = block[unit + 2 : unit + 3, :]
        keep = jnp.where(target == me, block, keep)
        send = jnp.where(target == other, block, send)
    keep_ref[...] = keep.astype(jnp.bfloat16)
    send_ref[...] = send.astype(jnp.bfloat16)


def pick_over(me, held, unit):
    return pl.pallas_call(
        functools.partial(pick_over_kernel, unit),
        out_shape=[jax.ShapeDtypeStruct(held[0].shape, jnp.bfloat16)] * 2,
        in_specs=[SM] + [VM] * 4,
        out_specs=[VM, VM],
        compiler_params=params(),
        name="pick_over",
    )(me, *held)


def crowded_kernel(shards, unit, *refs):
    blocks, out_ref = refs[:shards], refs[shards]
    by_dest = jnp.zeros((1, shards), jnp.float32)
    most = jnp.zeros((1, 1), jnp.float32)
    for ref in blocks:
        flags = ref[2:3, unit : unit + shards].astype(jnp.float32)
        by_dest += flags
        most = jnp.maximum(most, jnp.sum(flags, axis=1, keepdims=True))
    most = jnp.maximum(most, jnp.max(by_dest, axis=1, keepdims=True))
    out_ref[...] = jnp.broadcast_to((most > 1.5).astype(jnp.int32), out_ref.shape)


def crowded(blocks, shards, unit):
    width = blocks[0].shape[1]
    spec = pl.BlockSpec((META, width), lambda i: (unit // META, 0))
    return pl.pallas_call(
        functools.partial(crowded_kernel, shards, unit),
        out_shape=jax.ShapeDtypeStruct((8, 128), jnp.int32),
        grid=(1,),
        in_specs=[spec] * shards,
        out_specs=pl.BlockSpec((8, 128), lambda i: (0, 0)),
        compiler_params=params(),
        name="crowded",
    )(*blocks)


def place_kv_kernel(pieces, unit, count, has_extra, *refs):
    it = iter(refs)
    flag_ref = next(it) if has_extra else None
    base = [next(it) for _ in range(pieces)]
    over = [next(it) for _ in range(2)]
    if has_extra:
        extra_ref, extra_code = next(it), next(it)
    placed_ref, codes_ref = next(it), next(it)
    width = placed_ref.shape[1]
    rows, codes = [], []

    def decode(meta):
        return (meta[0:1, 0:unit] * RADIX + meta[1:2, 0:unit]).astype(jnp.int32)

    for ref in base:
        rows.append(ref[0:unit, :])
        codes.append(decode(ref[unit : unit + META, :].astype(jnp.float32)))
    left = over[0].shape[1] - width
    for ref in over:
        rows.append(ref[0:unit, left:])
        codes.append(decode(ref[unit : unit + META, 0:128].astype(jnp.float32)))
    code = jnp.concatenate(codes, axis=1)
    if has_extra:
        is_over = iota(code.shape, 1) >= pieces * unit
        code = jnp.where(is_over & (flag_ref[0] > 0), 0, code)
    codes_ref[...] = code
    onehot = select_rows(code, 1, count)
    placed = matmul(onehot, jnp.concatenate(rows, axis=0))
    placed_ref[...] = placed.astype(jnp.bfloat16)
    if has_extra:

        @pl.when(flag_ref[0] > 0)
        def _():
            more = matmul(select_rows(extra_code[...], 1, count), extra_ref[...])
            placed_ref[...] += more.astype(jnp.bfloat16)


def place_kv(flag, base, over, extra, extra_code, unit, count):
    width = base[0].shape[1]
    raw = (len(base) + 2) * unit
    return pl.pallas_call(
        functools.partial(place_kv_kernel, len(base), unit, count, True),
        out_shape=[
            jax.ShapeDtypeStruct((count, width), jnp.bfloat16),
            jax.ShapeDtypeStruct((1, raw), jnp.int32),
        ],
        in_specs=[SM] + [VM] * (len(base) + 4),
        out_specs=[VM, VM],
        compiler_params=params(),
        name="place_kv",
    )(flag, *base, *over, extra, extra_code)


def attend_core(shard, anc_ref, q_pl, kv_all, out_ref):
    count, width = out_ref.shape
    block_count = anc_ref.shape[0]
    size = count // block_count
    kv_width = kv_all.shape[1] // 2
    groups = kv_width // HEAD_SIZE
    ratio = width // kv_width
    window = (block_count + 1) * size
    scale = math.log2(math.e) / math.sqrt(HEAD_SIZE)
    lane = iota((size, window), 1)
    for b in range(block_count):
        first = (shard - 1) * block_count + b
        key_block = lane // size + first
        seen = lane < 0
        for a in range(anc_ref.shape[1]):
            seen = seen | (key_block == anc_ref[b, a])
        own = lane >= block_count * size
        causal = lane - block_count * size <= iota((size, window), 0)
        seen = (seen & (lane < block_count * size)) | (own & causal)
        bias = jnp.where(seen, 0.0, NEG)
        for g in range(groups):
            columns = [(g * ratio + h) * HEAD_SIZE for h in range(ratio)]
            q = jnp.concatenate(
                [q_pl[b * size : (b + 1) * size, c : c + HEAD_SIZE] for c in columns], axis=0
            )
            k = kv_all[b * size : b * size + window, g * HEAD_SIZE : (g + 1) * HEAD_SIZE]
            v = kv_all[
                b * size : b * size + window,
                kv_width + g * HEAD_SIZE : kv_width + (g + 1) * HEAD_SIZE,
            ]
            scores = (matmul_nt(q, k) * scale).reshape(ratio, size, window) + bias[None]
            scores = scores.reshape(ratio * size, window)
            peak = jnp.max(scores, axis=1, keepdims=True)
            expo = jnp.exp2(scores - peak)
            total = jnp.sum(expo, axis=1, keepdims=True)
            weights = (expo * (1.0 / total)).astype(jnp.bfloat16)
            output = matmul(weights, v).astype(jnp.bfloat16)
            for h, c in enumerate(columns):
                out_ref[b * size : (b + 1) * size, c : c + HEAD_SIZE] = output[h * size : (h + 1) * size]


def attend_kernel(pieces, unit, me_ref, flag_ref, anc_ref, code_ref, *refs):
    it = iter(refs)
    base = [next(it) for _ in range(pieces)]
    over = [next(it) for _ in range(2)]
    own_kv, prior_kv, extra_ref, extra_code = next(it), next(it), next(it), next(it)
    out_ref = next(it)
    raw, q_pl, kv_all, extra_vm, sems, extra_sem = (next(it) for _ in range(6))
    count, width = out_ref.shape
    copies = [
        pltpu.make_async_copy(ref, raw.at[pl.ds(i * unit, unit), :], sems.at[i]) for i, ref in enumerate(base)
    ]
    for j, ref in enumerate(over):
        i = pieces + j
        copies.append(
            pltpu.make_async_copy(
                ref.at[pl.ds(0, unit), pl.ds(0, width)], raw.at[pl.ds(i * unit, unit), :], sems.at[i]
            )
        )
    copies.append(pltpu.make_async_copy(prior_kv, kv_all.at[pl.ds(0, count), :], sems.at[pieces + 2]))
    copies.append(pltpu.make_async_copy(own_kv, kv_all.at[pl.ds(count, count), :], sems.at[pieces + 3]))
    for c in copies:
        c.start()
    onehot = select_rows(code_ref[...], 1, count)
    for c in copies:
        c.wait()
    q_pl[...] = matmul(onehot, raw[...]).astype(jnp.bfloat16)

    @pl.when(flag_ref[0] > 0)
    def _():
        copy = pltpu.make_async_copy(extra_ref, extra_vm, extra_sem)
        copy.start()
        copy.wait()
        q_pl[...] += matmul(select_rows(extra_code[...], 1, count), extra_vm[...]).astype(jnp.bfloat16)

    attend_core(me_ref[0], anc_ref, q_pl, kv_all, out_ref)


def attend(me, flag, ancestors, codes, base, over, own_kv, prior_kv, extra, extra_code, unit):
    count = own_kv.shape[0]
    width = base[0].shape[1]
    pieces = len(base)
    raw = (pieces + 2) * unit
    return pl.pallas_call(
        functools.partial(attend_kernel, pieces, unit),
        out_shape=jax.ShapeDtypeStruct((count, width), jnp.bfloat16),
        in_specs=[SM, SM, SM, VM] + [HB] * (pieces + 5) + [VM],
        out_specs=VM,
        scratch_shapes=[
            pltpu.VMEM((raw, width), jnp.bfloat16),
            pltpu.VMEM((count, width), jnp.bfloat16),
            pltpu.VMEM((2 * count, own_kv.shape[1]), jnp.bfloat16),
            pltpu.VMEM(extra.shape, jnp.bfloat16),
            pltpu.SemaphoreType.DMA((pieces + 4,)),
            pltpu.SemaphoreType.DMA,
        ],
        compiler_params=params(),
        name="attend",
    )(me, flag, ancestors, codes, *base, *over, own_kv, prior_kv, extra, extra_code)


def attend_padded_kernel(me_ref, anc_ref, code_ref, raw_ref, own_kv, prior_kv, out_ref, q_pl, kv_all):
    count = out_ref.shape[0]
    kv_all[0:count, :] = prior_kv[...]
    kv_all[count : 2 * count, :] = own_kv[...]
    q_pl[...] = matmul(select_rows(code_ref[...], 1, count), raw_ref[...]).astype(jnp.bfloat16)
    attend_core(me_ref[0], anc_ref, q_pl, kv_all, out_ref)


def attend_padded(me, ancestors, codes, raw, own_kv, prior_kv):
    count, width = own_kv.shape[0], raw.shape[1]
    return pl.pallas_call(
        attend_padded_kernel,
        out_shape=jax.ShapeDtypeStruct((count, width), jnp.bfloat16),
        in_specs=[SM, SM] + [VM] * 4,
        out_specs=VM,
        scratch_shapes=[
            pltpu.VMEM((count, width), jnp.bfloat16),
            pltpu.VMEM((2 * count, own_kv.shape[1]), jnp.bfloat16),
        ],
        compiler_params=params(),
        name="attend_padded",
    )(me, ancestors, codes, raw, own_kv, prior_kv)


def positions(dest_shard, shards):
    onehot = (dest_shard[:, None] == jnp.arange(shards, dtype=jnp.int32)[None, :]).astype(jnp.int32)
    before = jnp.cumsum(onehot, axis=0) - onehot
    return jnp.sum(before * onehot, axis=1)


def exchange(source, index, total):
    buffer = jnp.zeros((total,) + source.shape[1:], source.dtype).at[index].set(source, mode="drop")
    return lax.all_to_all(buffer, "seq", split_axis=0, concat_axis=0, tiled=True)


def from_behind(block):
    n = lax.axis_size("seq")
    return lax.ppermute(block, "seq", [(i, i + 1) for i in range(n - 1)])


def swap(block, r):
    n = lax.axis_size("seq")
    return lax.ppermute(block, "seq", [(i, i ^ r) for i in range(n)])


def padded_plan(me, queries, keys, values, dest_shard, dest_slot, ancestors):
    count = queries.shape[0]
    shards = lax.axis_size("seq")
    capacity = 2 * count // shards
    total = shards * capacity
    index = dest_shard * capacity + positions(dest_shard, shards)
    kv = exchange(jnp.concatenate([keys, values], axis=1), index, total)
    raw = exchange(queries, index, total)
    code = exchange(dest_slot + 1, index, total)
    slots = jnp.where(code > 0, code - 1, count)
    own_kv = jnp.zeros((count, kv.shape[1]), kv.dtype).at[slots].set(kv, mode="drop")
    prior_kv = from_behind(own_kv)
    return attend_padded(me, ancestors, code.reshape(1, total), raw, own_kv, prior_kv)


def swap_plan(me, queries, keys, values, dest_shard, dest_slot, ancestors):
    count = queries.shape[0]
    shards = lax.axis_size("seq")
    unit = count // shards
    kv_blocks, over, index = pack_kv(me, dest_shard, dest_slot, keys, values, queries, shards, unit)
    first = swap(over, 4)
    got_kv = [kv_blocks[0]] + [swap(kv_blocks[r], r) for r in range(1, shards)]
    q_blocks = pack_q(index, queries, shards, unit)
    got_q = [q_blocks[0]] + [swap(q_blocks[r], r) for r in range(1, shards)]
    second = [swap(over, 2), swap(first, 2)]
    keep, send = pick_over(me, [over, first, *second], unit)
    over_rows = [keep, swap(send, 1)]
    flag = crowded(got_kv, shards, unit)[0, :1]
    width = queries.shape[1]

    def more():
        place = positions(dest_shard, shards) - unit
        at = jnp.where(place >= 0, dest_shard * unit + place, count)
        rows = exchange(jnp.concatenate([queries, keys, values], axis=1), at, count)
        return rows[:, :width], rows[:, width:], exchange(dest_slot + 1, at, count).reshape(1, count)

    def nothing():
        return (
            jnp.zeros(queries.shape, jnp.bfloat16),
            jnp.zeros((count, 2 * keys.shape[1]), jnp.bfloat16),
            jnp.zeros((1, count), jnp.int32),
        )

    extra_q, extra_kv, extra_code = lax.cond(flag[0] > 0, more, nothing)
    own_kv, codes = place_kv(flag, got_kv, over_rows, extra_kv, extra_code, unit, count)
    prior_kv = from_behind(own_kv)
    return attend(me, flag, ancestors, codes, got_q, over_rows, own_kv, prior_kv, extra_q, extra_code, unit)


def local(queries, keys, values, dest_shard, dest_slot, ancestors):
    shards = lax.axis_size("seq")
    me = lax.axis_index("seq").astype(jnp.int32).reshape(1)
    plan = swap_plan if shards == 8 and queries.shape[0] % (16 * shards) == 0 else padded_plan
    return plan(me, queries, keys, values, dest_shard, dest_slot, ancestors)


def solution(mesh):
    rows = P(("groups", "seq"))
    heads = P(("groups", "seq"), "head")
    return jax.shard_map(
        local,
        mesh=mesh,
        in_specs=(heads, heads, heads, rows, rows, P(("groups", "seq"), None)),
        out_specs=heads,
        check_vma=False,
    )
```

time: 169 us -> 122 us (0.72)
  matrix products: 31.1 us -> 0 us
  local copies, waits for them, and re-layouts: 34.2 us -> 5.46 us
  Pallas kernels: 0 us -> 27.5 us
  other arithmetic: 10.4 us -> 0 us
  starting transfers between devices: 31.1 us -> 27.4 us
    scatter x7 -> x0, local copies, waits for them, and re-layouts: 32.8 us -> none  [the longest x3 17.1 us: place_rows(): return target.at[slots].set(received, mode='drop')]
    dot_general x22 -> x0, matrix products: 31.1 us -> none  [the longest x10 14.2 us: one_head(): lax.dot_general(query_part, key_part, (((1,), (1,)), ((), ())), preferred...]
    pallas_call x0 -> x6, Pallas kernels: none -> 27.5 us  [the longest x1 12.6 us: attend(): pl.pallas_call(functools.partial(attend_kernel, pieces, unit), out_shape=...]
    all_to_all x4 -> x0, starting transfers between devices: 24.3 us -> none  [the longest x1 6.57 us: local(): lax.all_to_all(query_pack, 'seq', split_axis=0, concat_axis=0, tiled=True)]
    ppermute x2 -> x19, starting transfers between devices: 6.76 us -> 27.4 us  [the longest x18 23.1 us: swap(): return lax.ppermute(block, 'seq', [(i, i ^ r) for i in range(n)])]
    all_to_all x4 -> x0, waiting for transfers between devices: 14.7 us -> none  [the longest x1 7.93 us: local(): lax.all_to_all(key_pack, 'seq', split_axis=0, concat_axis=0, tiled=True)]
    ppermute x2 -> x19, waiting for transfers between devices: 46.6 us -> 60.7 us  [the longest x18 60.7 us: swap(): return lax.ppermute(block, 'seq', [(i, i ^ r) for i in range(n)])]
    reduce_sum x11 -> x0, other arithmetic: 5.91 us -> none  [the longest x10 5.13 us: one_head(): weights = (expo / jnp.sum(expo, axis=1, keepdims=True)).astype(jnp.bfloat16)]
  transfers between devices with their start and end apart: 6 -> 19, of which waited for: 5 -> 9; matrix products, arithmetic and copies ran while one was open for 17% -> 3% of each run, Pallas kernels for 0% -> 4%
where the time goes in v1:
time: 122 us
  waiting for transfers between devices  60.7 us (50%)
  Pallas kernels  27.5 us (23%)
  starting transfers between devices  27.4 us (22%)
  local copies, waits for them, and re-layouts  5.46 us (4%)
    ppermute x18, waiting for transfers between devices, swap(): return lax.ppermute(block, 'seq', [(i, i ^ r) for i in range(n)])  60.7 us
    ppermute x18, starting transfers between devices, swap(): return lax.ppermute(block, 'seq', [(i, i ^ r) for i in range(n)])  23.1 us
    pallas_call x1, Pallas kernels, attend(): pl.pallas_call(functools.partial(attend_kernel, pieces, unit), out_shape=...  12.6 us
    ppermute x1, starting transfers between devices, from_behind(): return lax.ppermute(block, 'seq', [(i, i + 1) for i in range(n - 1)])  4.3 us
    pallas_call x1, Pallas kernels, pack_kv(): pl.pallas_call(functools.partial(pack_kv_kernel, shards, unit), out_shape...  3.89 us
    pallas_call x1, Pallas kernels, place_kv(): pl.pallas_call(functools.partial(place_kv_kernel, len(base), unit, count,...  3.56 us
    pallas_call x1, Pallas kernels, pack_q(): pl.pallas_call(functools.partial(pack_q_kernel, shards, unit), out_shape=...  3.28 us
    pallas_call x1, Pallas kernels, pick_over(): pl.pallas_call(functools.partial(pick_over_kernel, unit), out_shape=[jax....  2.5 us
  transfers between devices with their start and end apart: 19, of which 9 were waited for; matrix products, arithmetic and copies ran while one was open for 3% of the time, Pallas kernels for 4%

profile of v1, /device:TPU:16, one launch (start us, length us, event | category | flops | bytes accessed | tf_op | source)
XLA Modules:
  0.0 122.1 jit_solution(11943374284863891558)
XLA Ops:
  0.0 3.9 %pack_kv.1 = (bf16[72,512]{1,0:T(8,128)(2,1)}, bf16[72,512]{1,0:T(8,128)(2,1)}, bf16[72,512]{1,0:T(8,128)(2,1)}, bf16[72,512]{1,0:T(8,128)(2,1)}, bf16[72,512]{1...) custom-call(s32[1]{0:T(128)} %bitcast.6.me_ref, ...), custom_call_target="tpu_custom_call" | custom-call | tf_op jit(solution)/shard_map/pack_kv/pallas_call | solution.py:95
  3.9 0.0 collective-permute-start.7
  3.9 1.9 %collective-permute-start.8 = (bf16[72,1792]{1,0:T(8,128)(2,1)}, bf16[72,1792]{1,0:T(8,128)(2,1)S(1)}, u32[]{:S(2)}, u32[]{:S(2)}) collective-permute-start(bf16[72,1792]{1,0:T(8,128)(2,1)} %get-tuple-element.53.a_ref), channel_id=1, source_target_pairs={{0,4},{2,6},{4,0},{6,2},{8,12},{10,14},{12,8},{14,10},{1,5},{3,7},... | collective-permute-start | bytes 774152 | tf_op jit(solution)/shard_map/ppermute | solution.py:371
  5.8 9.7 %collective-permute-done.7.b_ref = bf16[72,1792]{1,0:T(8,128)(2,1)S(1)} collective-permute-done((bf16[72,1792]{1,0:T(8,128)(2,1)}, bf16[72,1792]{1,0:T(8,128)(2,1)S(1)}, u32[]{:S(2)}, u32[]{:S(2)}) %collective-permute-start.7) | collective-permute-done | bytes 258080 | tf_op jit(solution)/shard_map/ppermute | solution.py:371
  15.6 4.4 %collective-permute-start.9 = (bf16[72,1792]{1,0:T(8,128)(2,1)S(1)}, bf16[72,1792]{1,0:T(8,128)(2,1)S(1)}, u32[]{:S(2)}, u32[]{:S(2)}) collective-permute-start(bf16[72,1792]{1,0:T(8,128)(2,1)S(1)} %collective-permute-done.7.b_ref), channel_id=1, source_target_pairs={{0,4},{2,6},{4,0},{6,2},{8,12},{10,14},{12,8},{14,10},{1,5},{3,7},... | collective-permute-start | bytes 774152 | tf_op jit(solution)/shard_map/ppermute | solution.py:371
  20.0 0.0 collective-permute-done.8.c_ref
  20.0 6.4 %collective-permute-done.9.d_ref = bf16[72,1792]{1,0:T(8,128)(2,1)S(1)} collective-permute-done((bf16[72,1792]{1,0:T(8,128)(2,1)S(1)}, bf16[72,1792]{1,0:T(8,128)(2,1)S(1)}, u32[]{:S(2)}, u32[]{:S(2)}) %collective-permute-start.9) | collective-permute-done | bytes 258080 | tf_op jit(solution)/shard_map/ppermute | solution.py:371
  26.4 0.7 copy-done.13
  27.1 2.5 %pick_over.1 = (bf16[72,1792]{1,0:T(8,128)(2,1)}, bf16[72,1792]{1,0:T(8,128)(2,1)}) custom-call(s32[1]{0:T(128)} %bitcast.6.me_ref, bf16[72,1792]{1,0:T(8,128)(2,1)} %get-tuple-element.53.a_ref, bf16[72,1792]{1,0:T(8,128)(2,1)} %copy-done.11, bf16[72,1792]{1,0:T(8,128)(2,1)} %copy-done.12, bf16[72,1792]{1,0:T(8,128)(2,1)} %copy-done.13), custom_call_target="tpu_custom_call" | custom-call | tf_op jit(solution)/shard_map/pick_over/pallas_call | solution.py:139
  29.6 1.5 %collective-permute-start.10 = (bf16[72,1792]{1,0:T(8,128)(2,1)}, bf16[72,1792]{1,0:T(8,128)(2,1)}, u32[]{:S(2)}, u32[]{:S(2)}) collective-permute-start(bf16[72,1792]{1,0:T(8,128)(2,1)} %get-tuple-element.55), channel_id=1, source_target_pairs={{0,2},{2,0},{4,6},{6,4},{8,10},{10,8},{12,14},{14,12},{1,3},{3,1},... | collective-permute-start | bytes 774152 | tf_op jit(solution)/shard_map/ppermute | solution.py:371
  31.1 0.5 collective-permute-start
  31.6 1.8 %collective-permute-start.1 = (bf16[72,512]{1,0:T(8,128)(2,1)}, bf16[72,512]{1,0:T(8,128)(2,1)S(1)}, u32[]{:S(2)}, u32[]{:S(2)}) collective-permute-start(bf16[72,512]{1,0:T(8,128)(2,1)} %get-tuple-element.47), channel_id=1, source_target_pairs={{0,4},{2,6},{4,0},{6,2},{8,12},{10,14},{12,8},{14,10},{1,5},{3,7},... | collective-permute-start | bytes 221192 | tf_op jit(solution)/shard_map/ppermute | solution.py:371
  33.4 1.2 collective-permute-start.2
  34.6 0.0 collective-permute-start.3
  34.6 6.0 %collective-permute-done.refs_1_.refs_2_ = bf16[72,512]{1,0:T(8,128)(2,1)S(1)} collective-permute-done((bf16[72,512]{1,0:T(8,128)(2,1)}, bf16[72,512]{1,0:T(8,128)(2,1)S(1)}, u32[]{:S(2)}, u32[]{:S(2)}) %collective-permute-start) | collective-permute-done | bytes 73760 | tf_op jit(solution)/shard_map/ppermute | solution.py:371
  40.6 0.0 collective-permute-start.4
  40.6 0.0 collective-permute-done.1.refs_2_.refs_3_
  40.6 3.8 %collective-permute-start.5 = (bf16[72,512]{1,0:T(8,128)(2,1)}, bf16[72,512]{1,0:T(8,128)(2,1)S(1)}, u32[]{:S(2)}, u32[]{:S(2)}) collective-permute-start(bf16[72,512]{1,0:T(8,128)(2,1)} %get-tuple-element.51), channel_id=1, source_target_pairs={{0,12},{2,14},{4,8},{6,10},{8,4},{10,6},{12,0},{14,2},{1,13},{3,15... | collective-permute-start | bytes 221192 | tf_op jit(solution)/shard_map/ppermute | solution.py:371
  44.4 0.1 collective-permute-start.6
  44.5 2.6 %collective-permute-done.4.refs_5_.refs_6_ = bf16[72,512]{1,0:T(8,128)(2,1)S(1)} collective-permute-done((bf16[72,512]{1,0:T(8,128)(2,1)}, bf16[72,512]{1,0:T(8,128)(2,1)S(1)}, u32[]{:S(2)}, u32[]{:S(2)}) %collective-permute-start.4) | collective-permute-done | bytes 73760 | tf_op jit(solution)/shard_map/ppermute | solution.py:371
  47.1 5.2 %collective-permute-done.5.refs_6_.refs_7_ = bf16[72,512]{1,0:T(8,128)(2,1)S(1)} collective-permute-done((bf16[72,512]{1,0:T(8,128)(2,1)}, bf16[72,512]{1,0:T(8,128)(2,1)S(1)}, u32[]{:S(2)}, u32[]{:S(2)}) %collective-permute-start.5) | collective-permute-done | bytes 73760 | tf_op jit(solution)/shard_map/ppermute | solution.py:371
  52.2 0.0 collective-permute-done.6.refs_7_.refs_8_
  52.3 0.6 copy-done.9
  52.9 0.0 copy-done.10
  52.9 1.6 %crowded.1 = s32[8,128]{1,0:T(8,128)} custom-call(bf16[72,512]{1,0:T(8,128)(2,1)} %get-tuple-element.45.refs_0_.refs_1_, bf16[72,512]{1,0:T(8,128)(2,1)} %copy-done.4, bf16[72,512]{1,0:T(8,128)(2,1)} %copy-done.5, bf16[72,512]{1,0:T(8,128)(2,1)} %copy-done.6, bf16[72,512]{1,0:T(8,128)(2,1)} %copy-done.7, bf16[72,512]{1,0:T(8,128)(2,1)} %copy-done.8, ...), custom_call_target="tpu_custom_call" | custom-call | tf_op jit(solution)/shard_map/crowded/pallas_call | solution.py:164
  54.5 1.2 %slice.15 = s32[1,1]{1,0:T(1,128)} slice(s32[8,128]{1,0:T(8,128)} %crowded.1), slice={[0:1], [0:1]} | slice | bytes 8 | tf_op jit(solution)/shard_map/slice | solution.py:401
  56.5 2.0 %conditional.1 = (bf16[512,1280]{1,0:T(8,128)(2,1)}, bf16[512,512]{1,0:T(8,128)(2,1)}, s32[1,512]{1,0:T(1,128)S(1)}) conditional(s32[]{:T(128)} %bitcast.8, () %tuple.13, (s32[512]{0:T(512)S(1)}, bf16[512,1280]{1,0:T(8,128)(2,1)S(1)}, bf16[512,256]{1,0:T(8,128)(2,1)S(1)}, bf16[512,256]{1,0:T(8,128)(2,1)S(1)}, s32[512]{0:T(512)S(1)}) %tuple.21), branch_computations={%region_0.0_spmd, %region_1.7_spmd} | conditional | flops 6062200 | bytes 12952596 | solution.py:417
  56.5 1.2 broadcast.30
  57.6 0.8 broadcast.31
  58.5 3.6 %place_kv.1 = (bf16[512,512]{1,0:T(8,128)(2,1)}, s32[1,640]{1,0:T(1,128)}) custom-call(s32[1]{0:T(128)} %bitcast.7.refs_0_.flag_ref, bf16[72,512]{1,0:T(8,128)(2,1)} %get-tuple-element.45.refs_0_.refs_1_, bf16[72,512]{1,0:T(8,128)(2,1)} %copy-done.4, bf16[72,512]{1,0:T(8,128)(2,1)} %copy-done.5, bf16[72,512]{1,0:T(8,128)(2,1)} %copy-done.6, ...), custom_call_target="tpu_custom_call" | custom-call | tf_op jit(solution)/shard_map/place_kv/pallas_call | solution.py:215
  62.0 4.3 %collective-permute-start.18 = (bf16[512,512]{1,0:T(8,128)(2,1)}, bf16[512,512]{1,0:T(8,128)(2,1)S(1)}, u32[]{:S(2)}, u32[]{:S(2)}) collective-permute-start(bf16[512,512]{1,0:T(8,128)(2,1)} %get-tuple-element.68.refs_10_), channel_id=1, source_target_pairs={{0,2},{2,4},{4,6},{6,8},{8,10},{10,12},{12,14},{1,3},{3,5},{5,7},{... | collective-permute-start | bytes 1572872 | tf_op jit(solution)/shard_map/ppermute | solution.py:366
  66.3 3.3 %pack_q.1 = (bf16[64,1280]{1,0:T(8,128)(2,1)}, bf16[64,1280]{1,0:T(8,128)(2,1)}, bf16[64,1280]{1,0:T(8,128)(2,1)}, bf16[64,1280]{1,0:T(8,128)(2,1)}, bf16[64,128...) custom-call(s32[1,512]{1,0:T(1,128)} %get-tuple-element.59.index_ref, ...), custom_call_target="tpu_custom_call" | custom-call | tf_op jit(solution)/shard_map/pack_q/pallas_call | solution.py:114
  69.6 0.3 collective-permute-start.11
  69.9 0.0 collective-permute-start.12
  69.9 3.2 %collective-permute-start.13 = (bf16[64,1280]{1,0:T(8,128)(2,1)}, bf16[64,1280]{1,0:T(8,128)(2,1)S(1)}, u32[]{:S(2)}, u32[]{:S(2)}) collective-permute-start(bf16[64,1280]{1,0:T(8,128)(2,1)} %get-tuple-element.63), channel_id=1, source_target_pairs={{0,6},{2,4},{4,2},{6,0},{8,14},{10,12},{12,10},{14,8},{1,7},{3,5},... | collective-permute-start | bytes 491528 | tf_op jit(solution)/shard_map/ppermute | solution.py:371
  73.1 0.0 collective-permute-start.14
  73.1 10.6 %collective-permute-done.11.refs_1_ = bf16[64,1280]{1,0:T(8,128)(2,1)S(1)} collective-permute-done((bf16[64,1280]{1,0:T(8,128)(2,1)}, bf16[64,1280]{1,0:T(8,128)(2,1)S(1)}, u32[]{:S(2)}, u32[]{:S(2)}) %collective-permute-start.11) | collective-permute-done | bytes 163872 | tf_op jit(solution)/shard_map/ppermute | solution.py:371
  83.7 0.0 collective-permute-done.12.refs_2_
  83.7 1.3 %collective-permute-start.16 = (bf16[64,1280]{1,0:T(8,128)(2,1)}, bf16[64,1280]{1,0:T(8,128)(2,1)S(1)}, u32[]{:S(2)}, u32[]{:S(2)}) collective-permute-start(bf16[64,1280]{1,0:T(8,128)(2,1)} %get-tuple-element.66), channel_id=1, source_target_pairs={{0,12},{2,14},{4,8},{6,10},{8,4},{10,6},{12,0},{14,2},{1,13},{3,15... | collective-permute-start | bytes 491528 | tf_op jit(solution)/shard_map/ppermute | solution.py:371
  85.0 3.1 %collective-permute-start.17 = (bf16[64,1280]{1,0:T(8,128)(2,1)}, bf16[64,1280]{1,0:T(8,128)(2,1)S(1)}, u32[]{:S(2)}, u32[]{:S(2)}) collective-permute-start(bf16[64,1280]{1,0:T(8,128)(2,1)} %get-tuple-element.67), channel_id=1, source_target_pairs={{0,14},{2,12},{4,10},{6,8},{8,6},{10,4},{12,2},{14,0},{1,15},{3,13... | collective-permute-start | bytes 491528 | tf_op jit(solution)/shard_map/ppermute | solution.py:371
  88.2 0.0 collective-permute-done.14.refs_4_
  88.2 10.9 %collective-permute-done.15.refs_5_ = bf16[64,1280]{1,0:T(8,128)(2,1)S(1)} collective-permute-done((bf16[64,1280]{1,0:T(8,128)(2,1)}, bf16[64,1280]{1,0:T(8,128)(2,1)S(1)}, u32[]{:S(2)}, u32[]{:S(2)}) %collective-permute-start.15) | collective-permute-done | bytes 163872 | tf_op jit(solution)/shard_map/ppermute | solution.py:371
  99.1 5.1 %collective-permute-done.16.refs_6_ = bf16[64,1280]{1,0:T(8,128)(2,1)S(1)} collective-permute-done((bf16[64,1280]{1,0:T(8,128)(2,1)}, bf16[64,1280]{1,0:T(8,128)(2,1)S(1)}, u32[]{:S(2)}, u32[]{:S(2)}) %collective-permute-start.16) | collective-permute-done | bytes 163872 | tf_op jit(solution)/shard_map/ppermute | solution.py:371
  104.2 4.2 %collective-permute-done.17.refs_7_ = bf16[64,1280]{1,0:T(8,128)(2,1)S(1)} collective-permute-done((bf16[64,1280]{1,0:T(8,128)(2,1)}, bf16[64,1280]{1,0:T(8,128)(2,1)S(1)}, u32[]{:S(2)}, u32[]{:S(2)}) %collective-permute-start.17) | collective-permute-done | bytes 163872 | tf_op jit(solution)/shard_map/ppermute | solution.py:371
  108.4 0.0 collective-permute-done.18.refs_11_
  108.5 0.6 copy-done.20
  109.1 0.2 copy-done.3
  109.3 12.6 %attend.1 = bf16[512,1280]{1,0:T(8,128)(2,1)} custom-call(s32[1]{0:T(128)} %bitcast.6.me_ref, s32[1]{0:T(128)} %bitcast.7.refs_0_.flag_ref, s32[4,4]{1,0:T(4,128)} %anc_ref.1, s32[1,640]{1,0:T(1,128)} %get-tuple-element.58.code_ref, bf16[64,1280]{1,0:T(8,128)(2,1)} %get-tuple-element.60.refs_0_, bf16[64,1280]{1,0:T(8,128)(2,1)} %copy-done.14, ...), custom_call_target="tpu_custom_call" | custom-call | tf_op jit(solution)/shard_map/attend/pallas_call | solution.py:311
  (47 shorter events, 0.1 us)
Async XLA Ops:
  0.0 56.4 %copy-start.2 = (bf16[512,256]{1,0:T(8,128)(2,1)S(1)}, bf16[512,256]{1,0:T(8,128)(2,1)}, u32[]{:S(2)}) copy-start(bf16[512,256]{1,0:T(8,128)(2,1)} %v_ref.1) | copy-start | bytes 786436
  0.0 56.4 %copy-start.21 = (s32[512]{0:T(512)S(1)}, s32[512]{0:T(512)}, u32[]{:S(2)}) copy-start(s32[512]{0:T(512)} %dest_ref.1) | copy-start | bytes 6148
  0.0 56.4 %copy-start.22 = (s32[512]{0:T(512)S(1)}, s32[512]{0:T(512)}, u32[]{:S(2)}) copy-start(s32[512]{0:T(512)} %slot_ref.1) | copy-start | bytes 6148
  0.0 56.4 %copy-start = (bf16[512,1280]{1,0:T(8,128)(2,1)S(1)}, bf16[512,1280]{1,0:T(8,128)(2,1)}, u32[]{:S(2)}) copy-start(bf16[512,1280]{1,0:T(8,128)(2,1)} %q_ref.3) | copy-start | bytes 3932164
  0.0 56.4 %copy-start.1 = (bf16[512,256]{1,0:T(8,128)(2,1)S(1)}, bf16[512,256]{1,0:T(8,128)(2,1)}, u32[]{:S(2)}) copy-start(bf16[512,256]{1,0:T(8,128)(2,1)} %k_ref.1) | copy-start | bytes 786436
  3.9 11.7 %collective-permute-start.7 = (bf16[72,1792]{1,0:T(8,128)(2,1)}, bf16[72,1792]{1,0:T(8,128)(2,1)S(1)}, u32[]{:S(2)}, u32[]{:S(2)}) collective-permute-start(bf16[72,1792]{1,0:T(8,128)(2,1)} %get-tuple-element.53.a_ref), channel_id=1, source_target_pairs={{0,8},{2,10},{4,12},{6,14},{8,0},{10,2},{12,4},{14,6},{1,9},{3,11}... | collective-permute-start | bytes 774152 | tf_op jit(solution)/shard_map/ppermute | solution.py:371
  3.9 16.1 %collective-permute-start.8 = (bf16[72,1792]{1,0:T(8,128)(2,1)}, bf16[72,1792]{1,0:T(8,128)(2,1)S(1)}, u32[]{:S(2)}, u32[]{:S(2)}) collective-permute-start(bf16[72,1792]{1,0:T(8,128)(2,1)} %get-tuple-element.53.a_ref), channel_id=1, source_target_pairs={{0,4},{2,6},{4,0},{6,2},{8,12},{10,14},{12,8},{14,10},{1,5},{3,7},... | collective-permute-start | bytes 774152 | tf_op jit(solution)/shard_map/ppermute | solution.py:371
  15.6 10.8 %copy-start.11 = (bf16[72,1792]{1,0:T(8,128)(2,1)}, bf16[72,1792]{1,0:T(8,128)(2,1)S(1)}, u32[]{:S(2)}) copy-start(bf16[72,1792]{1,0:T(8,128)(2,1)S(1)} %collective-permute-done.7.b_ref) | copy-start | bytes 774148
  15.6 10.8 %collective-permute-start.9 = (bf16[72,1792]{1,0:T(8,128)(2,1)S(1)}, bf16[72,1792]{1,0:T(8,128)(2,1)S(1)}, u32[]{:S(2)}, u32[]{:S(2)}) collective-permute-start(bf16[72,1792]{1,0:T(8,128)(2,1)S(1)} %collective-permute-done.7.b_ref), channel_id=1, source_target_pairs={{0,4},{2,6},{4,0},{6,2},{8,12},{10,14},{12,8},{14,10},{1,5},{3,7},... | collective-permute-start | bytes 774152 | tf_op jit(solution)/shard_map/ppermute | solution.py:371
  20.0 6.4 %copy-start.12 = (bf16[72,1792]{1,0:T(8,128)(2,1)}, bf16[72,1792]{1,0:T(8,128)(2,1)S(1)}, u32[]{:S(2)}) copy-start(bf16[72,1792]{1,0:T(8,128)(2,1)S(1)} %collective-permute-done.8.c_ref) | copy-start | bytes 774148
  26.4 0.7 copy-start.13
  29.6 28.9 %collective-permute-start.10 = (bf16[72,1792]{1,0:T(8,128)(2,1)}, bf16[72,1792]{1,0:T(8,128)(2,1)}, u32[]{:S(2)}, u32[]{:S(2)}) collective-permute-start(bf16[72,1792]{1,0:T(8,128)(2,1)} %get-tuple-element.55), channel_id=1, source_target_pairs={{0,2},{2,0},{4,6},{6,4},{8,10},{10,8},{12,14},{14,12},{1,3},{3,1},... | collective-permute-start | bytes 774152 | tf_op jit(solution)/shard_map/ppermute | solution.py:371
  31.1 9.5 %collective-permute-start = (bf16[72,512]{1,0:T(8,128)(2,1)}, bf16[72,512]{1,0:T(8,128)(2,1)S(1)}, u32[]{:S(2)}, u32[]{:S(2)}) collective-permute-start(bf16[72,512]{1,0:T(8,128)(2,1)} %get-tuple-element.46), channel_id=1, source_target_pairs={{0,2},{2,0},{4,6},{6,4},{8,10},{10,8},{12,14},{14,12},{1,3},{3,1},... | collective-permute-start | bytes 221192 | tf_op jit(solution)/shard_map/ppermute | solution.py:371
  31.6 9.0 %collective-permute-start.1 = (bf16[72,512]{1,0:T(8,128)(2,1)}, bf16[72,512]{1,0:T(8,128)(2,1)S(1)}, u32[]{:S(2)}, u32[]{:S(2)}) collective-permute-start(bf16[72,512]{1,0:T(8,128)(2,1)} %get-tuple-element.47), channel_id=1, source_target_pairs={{0,4},{2,6},{4,0},{6,2},{8,12},{10,14},{12,8},{14,10},{1,5},{3,7},... | collective-permute-start | bytes 221192 | tf_op jit(solution)/shard_map/ppermute | solution.py:371
  33.4 11.0 %collective-permute-start.2 = (bf16[72,512]{1,0:T(8,128)(2,1)}, bf16[72,512]{1,0:T(8,128)(2,1)S(1)}, u32[]{:S(2)}, u32[]{:S(2)}) collective-permute-start(bf16[72,512]{1,0:T(8,128)(2,1)} %get-tuple-element.48), channel_id=1, source_target_pairs={{0,6},{2,4},{4,2},{6,0},{8,14},{10,12},{12,10},{14,8},{1,7},{3,5},... | collective-permute-start | bytes 221192 | tf_op jit(solution)/shard_map/ppermute | solution.py:371
  34.6 9.9 %collective-permute-start.3 = (bf16[72,512]{1,0:T(8,128)(2,1)}, bf16[72,512]{1,0:T(8,128)(2,1)S(1)}, u32[]{:S(2)}, u32[]{:S(2)}) collective-permute-start(bf16[72,512]{1,0:T(8,128)(2,1)} %get-tuple-element.49), channel_id=1, source_target_pairs={{0,8},{2,10},{4,12},{6,14},{8,0},{10,2},{12,4},{14,6},{1,9},{3,11}... | collective-permute-start | bytes 221192 | tf_op jit(solution)/shard_map/ppermute | solution.py:371
  40.6 11.6 %copy-start.4 = (bf16[72,512]{1,0:T(8,128)(2,1)}, bf16[72,512]{1,0:T(8,128)(2,1)S(1)}, u32[]{:S(2)}) copy-start(bf16[72,512]{1,0:T(8,128)(2,1)S(1)} %collective-permute-done.refs_1_.refs_2_) | copy-start | bytes 221188
  40.6 6.5 %collective-permute-start.4 = (bf16[72,512]{1,0:T(8,128)(2,1)}, bf16[72,512]{1,0:T(8,128)(2,1)S(1)}, u32[]{:S(2)}, u32[]{:S(2)}) collective-permute-start(bf16[72,512]{1,0:T(8,128)(2,1)} %get-tuple-element.50), channel_id=1, source_target_pairs={{0,10},{2,8},{4,14},{6,12},{8,2},{10,0},{12,6},{14,4},{1,11},{3,9}... | collective-permute-start | bytes 221192 | tf_op jit(solution)/shard_map/ppermute | solution.py:371
  40.6 11.6 %copy-start.5 = (bf16[72,512]{1,0:T(8,128)(2,1)}, bf16[72,512]{1,0:T(8,128)(2,1)S(1)}, u32[]{:S(2)}) copy-start(bf16[72,512]{1,0:T(8,128)(2,1)S(1)} %collective-permute-done.1.refs_2_.refs_3_) | copy-start | bytes 221188
  40.6 11.6 %collective-permute-start.5 = (bf16[72,512]{1,0:T(8,128)(2,1)}, bf16[72,512]{1,0:T(8,128)(2,1)S(1)}, u32[]{:S(2)}, u32[]{:S(2)}) collective-permute-start(bf16[72,512]{1,0:T(8,128)(2,1)} %get-tuple-element.51), channel_id=1, source_target_pairs={{0,12},{2,14},{4,8},{6,10},{8,4},{10,6},{12,0},{14,2},{1,13},{3,15... | collective-permute-start | bytes 221192 | tf_op jit(solution)/shard_map/ppermute | solution.py:371
  44.4 7.8 %copy-start.6 = (bf16[72,512]{1,0:T(8,128)(2,1)}, bf16[72,512]{1,0:T(8,128)(2,1)S(1)}, u32[]{:S(2)}) copy-start(bf16[72,512]{1,0:T(8,128)(2,1)S(1)} %collective-permute-done.2.refs_3_.refs_4_) | copy-start | bytes 221188
  44.4 7.8 %collective-permute-start.6 = (bf16[72,512]{1,0:T(8,128)(2,1)}, bf16[72,512]{1,0:T(8,128)(2,1)S(1)}, u32[]{:S(2)}, u32[]{:S(2)}) collective-permute-start(bf16[72,512]{1,0:T(8,128)(2,1)} %get-tuple-element.52), channel_id=1, source_target_pairs={{0,14},{2,12},{4,10},{6,8},{8,6},{10,4},{12,2},{14,0},{1,15},{3,13... | collective-permute-start | bytes 221192 | tf_op jit(solution)/shard_map/ppermute | solution.py:371
  44.5 7.8 %copy-start.7 = (bf16[72,512]{1,0:T(8,128)(2,1)}, bf16[72,512]{1,0:T(8,128)(2,1)S(1)}, u32[]{:S(2)}) copy-start(bf16[72,512]{1,0:T(8,128)(2,1)S(1)} %collective-permute-done.3.refs_4_.refs_5_) | copy-start | bytes 221188
  47.0 5.2 %copy-start.8 = (bf16[72,512]{1,0:T(8,128)(2,1)}, bf16[72,512]{1,0:T(8,128)(2,1)S(1)}, u32[]{:S(2)}) copy-start(bf16[72,512]{1,0:T(8,128)(2,1)S(1)} %collective-permute-done.4.refs_5_.refs_6_) | copy-start | bytes 221188
  52.2 0.6 copy-start.9
  52.2 0.7 copy-start.10
  62.0 46.4 %collective-permute-start.18 = (bf16[512,512]{1,0:T(8,128)(2,1)}, bf16[512,512]{1,0:T(8,128)(2,1)S(1)}, u32[]{:S(2)}, u32[]{:S(2)}) collective-permute-start(bf16[512,512]{1,0:T(8,128)(2,1)} %get-tuple-element.68.refs_10_), channel_id=1, source_target_pairs={{0,2},{2,4},{4,6},{6,8},{8,10},{10,12},{12,14},{1,3},{3,5},{5,7},{... | collective-permute-start | bytes 1572872 | tf_op jit(solution)/shard_map/ppermute | solution.py:366
  69.6 14.1 %collective-permute-start.11 = (bf16[64,1280]{1,0:T(8,128)(2,1)}, bf16[64,1280]{1,0:T(8,128)(2,1)S(1)}, u32[]{:S(2)}, u32[]{:S(2)}) collective-permute-start(bf16[64,1280]{1,0:T(8,128)(2,1)} %get-tuple-element.61), channel_id=1, source_target_pairs={{0,2},{2,0},{4,6},{6,4},{8,10},{10,8},{12,14},{14,12},{1,3},{3,1},... | collective-permute-start | bytes 491528 | tf_op jit(solution)/shard_map/ppermute | solution.py:371
  69.9 13.8 %collective-permute-start.12 = (bf16[64,1280]{1,0:T(8,128)(2,1)}, bf16[64,1280]{1,0:T(8,128)(2,1)S(1)}, u32[]{:S(2)}, u32[]{:S(2)}) collective-permute-start(bf16[64,1280]{1,0:T(8,128)(2,1)} %get-tuple-element.62), channel_id=1, source_target_pairs={{0,4},{2,6},{4,0},{6,2},{8,12},{10,14},{12,8},{14,10},{1,5},{3,7},... | collective-permute-start | bytes 491528 | tf_op jit(solution)/shard_map/ppermute | solution.py:371
  69.9 15.1 %collective-permute-start.13 = (bf16[64,1280]{1,0:T(8,128)(2,1)}, bf16[64,1280]{1,0:T(8,128)(2,1)S(1)}, u32[]{:S(2)}, u32[]{:S(2)}) collective-permute-start(bf16[64,1280]{1,0:T(8,128)(2,1)} %get-tuple-element.63), channel_id=1, source_target_pairs={{0,6},{2,4},{4,2},{6,0},{8,14},{10,12},{12,10},{14,8},{1,7},{3,5},... | collective-permute-start | bytes 491528 | tf_op jit(solution)/shard_map/ppermute | solution.py:371
  73.1 15.1 %collective-permute-start.14 = (bf16[64,1280]{1,0:T(8,128)(2,1)}, bf16[64,1280]{1,0:T(8,128)(2,1)S(1)}, u32[]{:S(2)}, u32[]{:S(2)}) collective-permute-start(bf16[64,1280]{1,0:T(8,128)(2,1)} %get-tuple-element.64), channel_id=1, source_target_pairs={{0,8},{2,10},{4,12},{6,14},{8,0},{10,2},{12,4},{14,6},{1,9},{3,11}... | collective-permute-start | bytes 491528 | tf_op jit(solution)/shard_map/ppermute | solution.py:371
  83.7 24.7 %copy-start.14 = (bf16[64,1280]{1,0:T(8,128)(2,1)}, bf16[64,1280]{1,0:T(8,128)(2,1)S(1)}, u32[]{:S(2)}) copy-start(bf16[64,1280]{1,0:T(8,128)(2,1)S(1)} %collective-permute-done.11.refs_1_) | copy-start | bytes 491524
  83.7 15.4 %collective-permute-start.15 = (bf16[64,1280]{1,0:T(8,128)(2,1)}, bf16[64,1280]{1,0:T(8,128)(2,1)S(1)}, u32[]{:S(2)}, u32[]{:S(2)}) collective-permute-start(bf16[64,1280]{1,0:T(8,128)(2,1)} %get-tuple-element.65), channel_id=1, source_target_pairs={{0,10},{2,8},{4,14},{6,12},{8,2},{10,0},{12,6},{14,4},{1,11},{3,9}... | collective-permute-start | bytes 491528 | tf_op jit(solution)/shard_map/ppermute | solution.py:371
  83.7 24.7 %copy-start.15 = (bf16[64,1280]{1,0:T(8,128)(2,1)}, bf16[64,1280]{1,0:T(8,128)(2,1)S(1)}, u32[]{:S(2)}) copy-start(bf16[64,1280]{1,0:T(8,128)(2,1)S(1)} %collective-permute-done.12.refs_2_) | copy-start | bytes 491524
  83.7 20.4 %collective-permute-start.16 = (bf16[64,1280]{1,0:T(8,128)(2,1)}, bf16[64,1280]{1,0:T(8,128)(2,1)S(1)}, u32[]{:S(2)}, u32[]{:S(2)}) collective-permute-start(bf16[64,1280]{1,0:T(8,128)(2,1)} %get-tuple-element.66), channel_id=1, source_target_pairs={{0,12},{2,14},{4,8},{6,10},{8,4},{10,6},{12,0},{14,2},{1,13},{3,15... | collective-permute-start | bytes 491528 | tf_op jit(solution)/shard_map/ppermute | solution.py:371
  85.0 23.4 %copy-start.16 = (bf16[64,1280]{1,0:T(8,128)(2,1)}, bf16[64,1280]{1,0:T(8,128)(2,1)S(1)}, u32[]{:S(2)}) copy-start(bf16[64,1280]{1,0:T(8,128)(2,1)S(1)} %collective-permute-done.13.refs_3_) | copy-start | bytes 491524
  85.0 23.4 %collective-permute-start.17 = (bf16[64,1280]{1,0:T(8,128)(2,1)}, bf16[64,1280]{1,0:T(8,128)(2,1)S(1)}, u32[]{:S(2)}, u32[]{:S(2)}) collective-permute-start(bf16[64,1280]{1,0:T(8,128)(2,1)} %get-tuple-element.67), channel_id=1, source_target_pairs={{0,14},{2,12},{4,10},{6,8},{8,6},{10,4},{12,2},{14,0},{1,15},{3,13... | collective-permute-start | bytes 491528 | tf_op jit(solution)/shard_map/ppermute | solution.py:371
  88.2 20.3 %copy-start.17 = (bf16[64,1280]{1,0:T(8,128)(2,1)}, bf16[64,1280]{1,0:T(8,128)(2,1)S(1)}, u32[]{:S(2)}) copy-start(bf16[64,1280]{1,0:T(8,128)(2,1)S(1)} %collective-permute-done.14.refs_4_) | copy-start | bytes 491524
  99.1 9.4 %copy-start.18 = (bf16[64,1280]{1,0:T(8,128)(2,1)}, bf16[64,1280]{1,0:T(8,128)(2,1)S(1)}, u32[]{:S(2)}) copy-start(bf16[64,1280]{1,0:T(8,128)(2,1)S(1)} %collective-permute-done.15.refs_5_) | copy-start | bytes 491524
  104.2 4.3 %copy-start.19 = (bf16[64,1280]{1,0:T(8,128)(2,1)}, bf16[64,1280]{1,0:T(8,128)(2,1)S(1)}, u32[]{:S(2)}) copy-start(bf16[64,1280]{1,0:T(8,128)(2,1)S(1)} %collective-permute-done.16.refs_6_) | copy-start | bytes 491524
  108.4 0.7 copy-start.20
  108.4 0.9 copy-start.3

commit v2 on v1

--- a/solution.py
+++ b/solution.py
@@ -13,15 +13,18 @@
 RADIX = 32
 NO_DEST = 255.0
 NEG = -1e30
-VMEM_LIMIT = 56 * 1024 * 1024
 
 VM = pl.BlockSpec(memory_space=pltpu.VMEM)
 SM = pl.BlockSpec(memory_space=pltpu.SMEM)
 HB = pl.BlockSpec(memory_space=pl.ANY)
 
 
-def params():
-    return pltpu.CompilerParams(vmem_limit_bytes=VMEM_LIMIT)
+def light():
+    return pl.CostEstimate(flops=0, bytes_accessed=0, transcendentals=0)
+
+
+def params(mebibytes=56):
+    return pltpu.CompilerParams(vmem_limit_bytes=mebibytes * 1024 * 1024)
 
 
 def iota(shape, axis):
@@ -53,7 +56,7 @@
     position = jnp.sum(before * onehot.astype(jnp.float32), axis=0, keepdims=True).astype(jnp.int32)
     base = position < unit
     index = jnp.where(base, (dest ^ me) * unit + position, -1)
-    index_ref[...] = index
+    index_ref[...] = jnp.where(base, dest * unit + position, -1)
     over_index = jnp.where(base, -1, position - unit)
     totals = matmul_nt(jnp.ones((META, count), jnp.bfloat16), onehot)
     flags = (totals > unit + 0.5).astype(jnp.float32)
@@ -97,26 +100,26 @@
         out_shape=shapes,
         in_specs=[SM, VM, VM, VM, VM, VM],
         out_specs=[VM] * len(shapes),
-        compiler_params=params(),
+        compiler_params=params(16),
+        cost_estimate=light(),
         name="pack_kv",
     )(me, dest, slot, keys, values, queries)
     return outs[:shards], outs[shards], outs[shards + 1]
 
 
-def pack_q_kernel(shards, unit, index_ref, q_ref, *blocks):
-    index = index_ref[...]
-    for r in range(shards):
-        picked = select_rows(index, r * unit, unit)
-        blocks[r][...] = matmul(picked, q_ref[...]).astype(jnp.bfloat16)
-
-
-def pack_q(index, queries, shards, unit):
-    return pl.pallas_call(
-        functools.partial(pack_q_kernel, shards, unit),
-        out_shape=[jax.ShapeDtypeStruct((unit, queries.shape[1]), jnp.bfloat16)] * shards,
+def pack_q_kernel(index_ref, q_ref, out_ref):
+    picked = select_rows(index_ref[...], 0, out_ref.shape[0])
+    out_ref[...] = matmul(picked, q_ref[...]).astype(jnp.bfloat16)
+
+
+def pack_q(index, queries):
+    return pl.pallas_call(
+        pack_q_kernel,
+        out_shape=jax.ShapeDtypeStruct(queries.shape, jnp.bfloat16),
         in_specs=[VM, VM],
-        out_specs=[VM] * shards,
-        compiler_params=params(),
+        out_specs=VM,
+        compiler_params=params(12),
+        cost_estimate=light(),
         name="pack_q",
     )(index, queries)
 
@@ -141,7 +144,8 @@
         out_shape=[jax.ShapeDtypeStruct(held[0].shape, jnp.bfloat16)] * 2,
         in_specs=[SM] + [VM] * 4,
         out_specs=[VM, VM],
-        compiler_params=params(),
+        compiler_params=params(8),
+        cost_estimate=light(),
         name="pick_over",
     )(me, *held)
 
@@ -167,19 +171,15 @@
         grid=(1,),
         in_specs=[spec] * shards,
         out_specs=pl.BlockSpec((8, 128), lambda i: (0, 0)),
-        compiler_params=params(),
+        compiler_params=params(4),
+        cost_estimate=light(),
         name="crowded",
     )(*blocks)
 
 
-def place_kv_kernel(pieces, unit, count, has_extra, *refs):
-    it = iter(refs)
-    flag_ref = next(it) if has_extra else None
-    base = [next(it) for _ in range(pieces)]
-    over = [next(it) for _ in range(2)]
-    if has_extra:
-        extra_ref, extra_code = next(it), next(it)
-    placed_ref, codes_ref = next(it), next(it)
+def place_kv_kernel(pieces, unit, count, *refs):
+    base, over = refs[:pieces], refs[pieces : pieces + 2]
+    placed_ref, codes_ref = refs[pieces + 2 :]
     width = placed_ref.shape[1]
     rows, codes = [], []
 
@@ -194,35 +194,26 @@
         rows.append(ref[0:unit, left:])
         codes.append(decode(ref[unit : unit + META, 0:128].astype(jnp.float32)))
     code = jnp.concatenate(codes, axis=1)
-    if has_extra:
-        is_over = iota(code.shape, 1) >= pieces * unit
-        code = jnp.where(is_over & (flag_ref[0] > 0), 0, code)
     codes_ref[...] = code
-    onehot = select_rows(code, 1, count)
-    placed = matmul(onehot, jnp.concatenate(rows, axis=0))
+    placed = matmul(select_rows(code, 1, count), jnp.concatenate(rows, axis=0))
     placed_ref[...] = placed.astype(jnp.bfloat16)
-    if has_extra:
-
-        @pl.when(flag_ref[0] > 0)
-        def _():
-            more = matmul(select_rows(extra_code[...], 1, count), extra_ref[...])
-            placed_ref[...] += more.astype(jnp.bfloat16)
-
-
-def place_kv(flag, base, over, extra, extra_code, unit, count):
+
+
+def place_kv(base, over, unit, count):
     width = base[0].shape[1]
     raw = (len(base) + 2) * unit
     return pl.pallas_call(
-        functools.partial(place_kv_kernel, len(base), unit, count, True),
+        functools.partial(place_kv_kernel, len(base), unit, count),
         out_shape=[
             jax.ShapeDtypeStruct((count, width), jnp.bfloat16),
             jax.ShapeDtypeStruct((1, raw), jnp.int32),
         ],
-        in_specs=[SM] + [VM] * (len(base) + 4),
+        in_specs=[VM] * (len(base) + 2),
         out_specs=[VM, VM],
-        compiler_params=params(),
+        compiler_params=params(10),
+        cost_estimate=light(),
         name="place_kv",
-    )(flag, *base, *over, extra, extra_code)
+    )(*base, *over)
 
 
 def attend_core(shard, anc_ref, q_pl, kv_all, out_ref):
@@ -266,17 +257,18 @@
                 out_ref[b * size : (b + 1) * size, c : c + HEAD_SIZE] = output[h * size : (h + 1) * size]
 
 
-def attend_kernel(pieces, unit, me_ref, flag_ref, anc_ref, code_ref, *refs):
-    it = iter(refs)
-    base = [next(it) for _ in range(pieces)]
-    over = [next(it) for _ in range(2)]
-    own_kv, prior_kv, extra_ref, extra_code = next(it), next(it), next(it), next(it)
-    out_ref = next(it)
-    raw, q_pl, kv_all, extra_vm, sems, extra_sem = (next(it) for _ in range(6))
+def attend_kernel(pieces, unit, me_ref, anc_ref, code_ref, *refs):
+    base, over = refs[0], refs[1:3]
+    own_kv, prior_kv, out_ref, raw, q_pl, kv_all, sems = refs[3:]
     count, width = out_ref.shape
-    copies = [
-        pltpu.make_async_copy(ref, raw.at[pl.ds(i * unit, unit), :], sems.at[i]) for i, ref in enumerate(base)
-    ]
+    copies = []
+    for r in range(pieces):
+        start = pl.multiple_of((me_ref[0] ^ r) * unit, unit)
+        copies.append(
+            pltpu.make_async_copy(
+                base.at[pl.ds(start, unit), :], raw.at[pl.ds(r * unit, unit), :], sems.at[r]
+            )
+        )
     for j, ref in enumerate(over):
         i = pieces + j
         copies.append(
@@ -292,38 +284,28 @@
     for c in copies:
         c.wait()
     q_pl[...] = matmul(onehot, raw[...]).astype(jnp.bfloat16)
-
-    @pl.when(flag_ref[0] > 0)
-    def _():
-        copy = pltpu.make_async_copy(extra_ref, extra_vm, extra_sem)
-        copy.start()
-        copy.wait()
-        q_pl[...] += matmul(select_rows(extra_code[...], 1, count), extra_vm[...]).astype(jnp.bfloat16)
-
     attend_core(me_ref[0], anc_ref, q_pl, kv_all, out_ref)
 
 
-def attend(me, flag, ancestors, codes, base, over, own_kv, prior_kv, extra, extra_code, unit):
-    count = own_kv.shape[0]
-    width = base[0].shape[1]
-    pieces = len(base)
+def attend(me, ancestors, codes, base, over, own_kv, prior_kv, unit):
+    count, width = base.shape
+    pieces = count // unit
     raw = (pieces + 2) * unit
     return pl.pallas_call(
         functools.partial(attend_kernel, pieces, unit),
         out_shape=jax.ShapeDtypeStruct((count, width), jnp.bfloat16),
-        in_specs=[SM, SM, SM, VM] + [HB] * (pieces + 5) + [VM],
+        in_specs=[SM, SM, VM] + [HB] * 5,
         out_specs=VM,
         scratch_shapes=[
             pltpu.VMEM((raw, width), jnp.bfloat16),
             pltpu.VMEM((count, width), jnp.bfloat16),
             pltpu.VMEM((2 * count, own_kv.shape[1]), jnp.bfloat16),
-            pltpu.VMEM(extra.shape, jnp.bfloat16),
             pltpu.SemaphoreType.DMA((pieces + 4,)),
-            pltpu.SemaphoreType.DMA,
         ],
-        compiler_params=params(),
+        compiler_params=params(28),
+        cost_estimate=light(),
         name="attend",
-    )(me, flag, ancestors, codes, *base, *over, own_kv, prior_kv, extra, extra_code)
+    )(me, ancestors, codes, base, *over, own_kv, prior_kv)
 
 
 def attend_padded_kernel(me_ref, anc_ref, code_ref, raw_ref, own_kv, prior_kv, out_ref, q_pl, kv_all):
@@ -391,33 +373,18 @@
     shards = lax.axis_size("seq")
     unit = count // shards
     kv_blocks, over, index = pack_kv(me, dest_shard, dest_slot, keys, values, queries, shards, unit)
+    got_q = lax.all_to_all(pack_q(index, queries), "seq", split_axis=0, concat_axis=0, tiled=True)
     first = swap(over, 4)
     got_kv = [kv_blocks[0]] + [swap(kv_blocks[r], r) for r in range(1, shards)]
-    q_blocks = pack_q(index, queries, shards, unit)
-    got_q = [q_blocks[0]] + [swap(q_blocks[r], r) for r in range(1, shards)]
     second = [swap(over, 2), swap(first, 2)]
     keep, send = pick_over(me, [over, first, *second], unit)
     over_rows = [keep, swap(send, 1)]
-    flag = crowded(got_kv, shards, unit)[0, :1]
-    width = queries.shape[1]
-
-    def more():
-        place = positions(dest_shard, shards) - unit
-        at = jnp.where(place >= 0, dest_shard * unit + place, count)
-        rows = exchange(jnp.concatenate([queries, keys, values], axis=1), at, count)
-        return rows[:, :width], rows[:, width:], exchange(dest_slot + 1, at, count).reshape(1, count)
-
-    def nothing():
-        return (
-            jnp.zeros(queries.shape, jnp.bfloat16),
-            jnp.zeros((count, 2 * keys.shape[1]), jnp.bfloat16),
-            jnp.zeros((1, count), jnp.int32),
-        )
-
-    extra_q, extra_kv, extra_code = lax.cond(flag[0] > 0, more, nothing)
-    own_kv, codes = place_kv(flag, got_kv, over_rows, extra_kv, extra_code, unit, count)
+    own_kv, codes = place_kv(got_kv, over_rows, unit, count)
     prior_kv = from_behind(own_kv)
-    return attend(me, flag, ancestors, codes, got_q, over_rows, own_kv, prior_kv, extra_q, extra_code, unit)
+    result = attend(me, ancestors, codes, got_q, over_rows, own_kv, prior_kv, unit)
+    flag = crowded(got_kv, shards, unit)[0, 0]
+    args = (queries, keys, values, dest_shard, dest_slot, ancestors)
+    return lax.cond(flag > 0, lambda: padded_plan(me, *args), lambda: result)
 
 
 def local(queries, keys, values, dest_shard, dest_slot, ancestors):

time: 122 us -> 110 us (0.902)
  Pallas kernels: 27.5 us -> 17.9 us
  local copies, waits for them, and re-layouts: 5.46 us -> 0.59 us
  waiting for transfers between devices: 60.7 us -> 64.4 us
  starting transfers between devices: 27.4 us -> 25 us
    ppermute x1, waiting for transfers between devices: 0.01 us -> 8.98 us  [from_behind(): return lax.ppermute(block, 'seq', [(i, i + 1) for i in range(n - 1)])]
    ppermute x18 -> x11, starting transfers between devices: 23.1 us -> 15 us  [swap(): return lax.ppermute(block, 'seq', [(i, i ^ r) for i in range(n)])]
    all_to_all x0 -> x1, starting transfers between devices: none -> 6.14 us  [swap_plan(): lax.all_to_all(pack_q(index, queries), 'seq', split_axis=0, concat_axis=0...]
    ppermute x18 -> x11, waiting for transfers between devices: 60.7 us -> 55.4 us  [swap(): return lax.ppermute(block, 'seq', [(i, i ^ r) for i in range(n)])]
    pallas_call x2, Pallas kernels: 6.84 us -> 2.52 us  [the longest x1 1.91 us: pack_q(): pl.pallas_call(pack_q_kernel, out_shape=jax.ShapeDtypeStruct(queries.shap...]
    unnamed x46 -> x12, local copies, waits for them, and re-layouts: 2.22 us -> 0.03 us
    pallas_call x1, Pallas kernels: 2.5 us -> 0.46 us  [pick_over(): pl.pallas_call(functools.partial(pick_over_kernel, unit), out_shape=[jax....]
    another operation x3 -> x0, local copies, waits for them, and re-layouts: 1.99 us -> none
  transfers between devices with their start and end apart: 19 -> 13, of which waited for: 9 -> 7; matrix products, arithmetic and copies ran while one was open for 3% -> 1% of each run, Pallas kernels for 4% -> 1%
where the time goes in v2:
time: 110 us; the launch traced here: 109 us
  waiting for transfers between devices  64.4 us (59%)
  starting transfers between devices  25 us (23%)
  Pallas kernels  17.9 us (16%)
    ppermute x11, waiting for transfers between devices, swap(): return lax.ppermute(block, 'seq', [(i, i ^ r) for i in range(n)])  55.4 us
    ppermute x11, starting transfers between devices, swap(): return lax.ppermute(block, 'seq', [(i, i ^ r) for i in range(n)])  15 us
    pallas_call x1, Pallas kernels, attend(): pl.pallas_call(functools.partial(attend_kernel, pieces, unit), out_shape=...  11.6 us
    ppermute x1, waiting for transfers between devices, from_behind(): return lax.ppermute(block, 'seq', [(i, i + 1) for i in range(n - 1)])  8.98 us
    all_to_all x1, starting transfers between devices, swap_plan(): lax.all_to_all(pack_q(index, queries), 'seq', split_axis=0, concat_axis=0...  6.14 us
    ppermute x1, starting transfers between devices, from_behind(): return lax.ppermute(block, 'seq', [(i, i + 1) for i in range(n - 1)])  3.83 us
    pallas_call x1, Pallas kernels, pack_kv(): pl.pallas_call(functools.partial(pack_kv_kernel, shards, unit), out_shape...  3.1 us
  transfers between devices with their start and end apart: 13, of which 7 were waited for; matrix products, arithmetic and copies ran while one was open for 1% of the time, Pallas kernels for 1%

profile of v2, /device:TPU:16, one launch (start us, length us, event | category | flops | bytes accessed | tf_op | source)
XLA Modules:
  0.0 109.0 jit_solution(4982750099806127261)
XLA Ops:
  0.0 0.0 copy-start.1
  0.0 3.1 %pack_kv.1 = (bf16[72,512]{1,0:T(8,128)(2,1)S(1)}, bf16[72,512]{1,0:T(8,128)(2,1)S(1)}, bf16[72,512]{1,0:T(8,128)(2,1)S(1)}, bf16[72,512]{1,0:T(8,128)(2,1)S(1)}...) custom-call(s32[1]{0:T(128)} %bitcast.12.me_ref, ...), custom_call_target="tpu_custom_call" | custom-call | tf_op jit(solution)/shard_map/pack_kv/pallas_call | solution.py:98
  3.1 0.0 copy-done.1
  3.1 1.9 %pack_q.1 = bf16[512,1280]{1,0:T(8,128)(2,1)} custom-call(s32[1,512]{1,0:T(1,128)S(1)} %get-tuple-element.56.index_ref, bf16[512,1280]{1,0:T(8,128)(2,1)S(1)} %copy-done.1), custom_call_target="tpu_custom_call" | custom-call | tf_op jit(solution)/shard_map/pack_q/pallas_call | solution.py:116
  5.0 6.1 %all-to-all-start.3 = ((bf16[8,64,1280]{2,1,0:T(8,128)(2,1)}), bf16[8,64,1280]{2,1,0:T(8,128)(2,1)S(1)}, u32[]{:S(2)}, u32[]{:S(2)}) async-start(bf16[8,64,1280]{2,1,0:T(8,128)(2,1)} %bitcast.14), calls=%async_computation.3 | async-start | bytes 2621440 | tf_op jit(solution)/shard_map/all_to_all | solution.py:376
  11.2 0.0 copy-start.8
  11.2 0.1 collective-permute-start.8
  11.2 2.0 %collective-permute-start.9 = (bf16[72,1792]{1,0:T(8,128)(2,1)S(1)}, bf16[72,1792]{1,0:T(8,128)(2,1)S(1)}, u32[]{:S(2)}, u32[]{:S(2)}) collective-permute-start(bf16[72,1792]{1,0:T(8,128)(2,1)S(1)} %get-tuple-element.52.a_ref), channel_id=1, source_target_pairs={{0,4},{2,6},{4,0},{6,2},{8,12},{10,14},{12,8},{14,10},{1,5},{3,7},... | collective-permute-start | bytes 774152 | tf_op jit(solution)/shard_map/ppermute | solution.py:353
  13.2 37.0 %collective-permute-done.8.b_ref = bf16[72,1792]{1,0:T(8,128)(2,1)S(1)} collective-permute-done((bf16[72,1792]{1,0:T(8,128)(2,1)S(1)}, bf16[72,1792]{1,0:T(8,128)(2,1)S(1)}, u32[]{:S(2)}, u32[]{:S(2)}) %collective-permute-start.8) | collective-permute-done | bytes 258080 | tf_op jit(solution)/shard_map/ppermute | solution.py:353
  50.2 2.6 %collective-permute-start.10 = (bf16[72,1792]{1,0:T(8,128)(2,1)S(1)}, bf16[72,1792]{1,0:T(8,128)(2,1)S(1)}, u32[]{:S(2)}, u32[]{:S(2)}) collective-permute-start(bf16[72,1792]{1,0:T(8,128)(2,1)S(1)} %collective-permute-done.8.b_ref), channel_id=1, source_target_pairs={{0,4},{2,6},{4,0},{6,2},{8,12},{10,14},{12,8},{14,10},{1,5},{3,7},... | collective-permute-start | bytes 774152 | tf_op jit(solution)/shard_map/ppermute | solution.py:353
  52.9 0.0 collective-permute-done.9.c_ref
  52.9 6.4 %collective-permute-done.10.d_ref = bf16[72,1792]{1,0:T(8,128)(2,1)S(1)} collective-permute-done((bf16[72,1792]{1,0:T(8,128)(2,1)S(1)}, bf16[72,1792]{1,0:T(8,128)(2,1)S(1)}, u32[]{:S(2)}, u32[]{:S(2)}) %collective-permute-start.10) | collective-permute-done | bytes 258080 | tf_op jit(solution)/shard_map/ppermute | solution.py:353
  59.3 0.5 pick_over.1
  59.7 1.4 %collective-permute-start.11 = (bf16[72,1792]{1,0:T(8,128)(2,1)S(1)}, bf16[72,1792]{1,0:T(8,128)(2,1)S(1)}, u32[]{:S(2)}, u32[]{:S(2)}) collective-permute-start(bf16[72,1792]{1,0:T(8,128)(2,1)S(1)} %get-tuple-element.54), channel_id=1, source_target_pairs={{0,2},{2,0},{4,6},{6,4},{8,10},{10,8},{12,14},{14,12},{1,3},{3,1},... | collective-permute-start | bytes 774152 | tf_op jit(solution)/shard_map/ppermute | solution.py:353
  61.1 0.7 collective-permute-start.1
  61.8 1.7 %collective-permute-start.2 = (bf16[72,512]{1,0:T(8,128)(2,1)S(1)}, bf16[72,512]{1,0:T(8,128)(2,1)S(1)}, u32[]{:S(2)}, u32[]{:S(2)}) collective-permute-start(bf16[72,512]{1,0:T(8,128)(2,1)S(1)} %get-tuple-element.46), channel_id=1, source_target_pairs={{0,4},{2,6},{4,0},{6,2},{8,12},{10,14},{12,8},{14,10},{1,5},{3,7},... | collective-permute-start | bytes 221192 | tf_op jit(solution)/shard_map/ppermute | solution.py:353
  63.6 1.0 collective-permute-start.3
  64.6 1.6 %collective-permute-start.4 = (bf16[72,512]{1,0:T(8,128)(2,1)S(1)}, bf16[72,512]{1,0:T(8,128)(2,1)S(1)}, u32[]{:S(2)}, u32[]{:S(2)}) collective-permute-start(bf16[72,512]{1,0:T(8,128)(2,1)S(1)} %get-tuple-element.48), channel_id=1, source_target_pairs={{0,8},{2,10},{4,12},{6,14},{8,0},{10,2},{12,4},{14,6},{1,9},{3,11}... | collective-permute-start | bytes 221192 | tf_op jit(solution)/shard_map/ppermute | solution.py:353
  66.2 4.3 %collective-permute-done.1.refs_1_ = bf16[72,512]{1,0:T(8,128)(2,1)S(1)} collective-permute-done((bf16[72,512]{1,0:T(8,128)(2,1)S(1)}, bf16[72,512]{1,0:T(8,128)(2,1)S(1)}, u32[]{:S(2)}, u32[]{:S(2)}) %collective-permute-start.1) | collective-permute-done | bytes 73760 | tf_op jit(solution)/shard_map/ppermute | solution.py:353
  70.6 1.0 collective-permute-start.5
  71.6 0.0 collective-permute-done.2.refs_2_
  71.6 2.6 %collective-permute-start.6 = (bf16[72,512]{1,0:T(8,128)(2,1)S(1)}, bf16[72,512]{1,0:T(8,128)(2,1)S(1)}, u32[]{:S(2)}, u32[]{:S(2)}) collective-permute-start(bf16[72,512]{1,0:T(8,128)(2,1)S(1)} %get-tuple-element.50), channel_id=1, source_target_pairs={{0,12},{2,14},{4,8},{6,10},{8,4},{10,6},{12,0},{14,2},{1,13},{3,15... | collective-permute-start | bytes 221192 | tf_op jit(solution)/shard_map/ppermute | solution.py:353
  74.2 0.0 collective-permute-done.3.refs_3_
  74.2 0.2 collective-permute-start.7
  74.4 0.0 collective-permute-done.4.refs_4_
  74.4 2.4 %collective-permute-done.5.refs_5_ = bf16[72,512]{1,0:T(8,128)(2,1)S(1)} collective-permute-done((bf16[72,512]{1,0:T(8,128)(2,1)S(1)}, bf16[72,512]{1,0:T(8,128)(2,1)S(1)}, u32[]{:S(2)}, u32[]{:S(2)}) %collective-permute-start.5) | collective-permute-done | bytes 73760 | tf_op jit(solution)/shard_map/ppermute | solution.py:353
  76.8 4.9 %collective-permute-done.6.refs_6_ = bf16[72,512]{1,0:T(8,128)(2,1)S(1)} collective-permute-done((bf16[72,512]{1,0:T(8,128)(2,1)S(1)}, bf16[72,512]{1,0:T(8,128)(2,1)S(1)}, u32[]{:S(2)}, u32[]{:S(2)}) %collective-permute-start.6) | collective-permute-done | bytes 73760 | tf_op jit(solution)/shard_map/ppermute | solution.py:353
  81.7 0.3 collective-permute-done.7.refs_7_
  82.0 0.0 collective-permute-done.11.refs_9_.refs_2_
  82.1 0.6 place_kv.1
  82.7 3.8 %collective-permute-start.12 = (bf16[512,512]{1,0:T(8,128)(2,1)S(1)}, bf16[512,512]{1,0:T(8,128)(2,1)S(1)}, u32[]{:S(2)}, u32[]{:S(2)}) collective-permute-start(bf16[512,512]{1,0:T(8,128)(2,1)S(1)} %get-tuple-element.57.refs_3_), channel_id=1, source_target_pairs={{0,2},{2,4},{4,6},{6,8},{8,10},{10,12},{12,14},{1,3},{3,5},{5,7},{... | collective-permute-start | bytes 1572872 | tf_op jit(solution)/shard_map/ppermute | solution.py:348
  86.5 0.2 crowded.1
  86.7 0.6 slice.9
  87.9 9.0 %collective-permute-done.12.refs_4_ = bf16[512,512]{1,0:T(8,128)(2,1)S(1)} collective-permute-done((bf16[512,512]{1,0:T(8,128)(2,1)S(1)}, bf16[512,512]{1,0:T(8,128)(2,1)S(1)}, u32[]{:S(2)}, u32[]{:S(2)}) %collective-permute-start.12) | collective-permute-done | bytes 524320 | tf_op jit(solution)/shard_map/ppermute | solution.py:348
  96.9 0.0 all-to-all-done.3
  96.9 0.0 copy-done.8
  96.9 0.0 copy-start.4
  96.9 0.0 copy-start.5
  96.9 0.0 copy-start.7
  96.9 0.0 copy-start.9
  97.0 11.6 %attend.1 = bf16[512,1280]{1,0:T(8,128)(2,1)} custom-call(s32[1]{0:T(128)} %bitcast.12.me_ref, s32[4,4]{1,0:T(4,128)S(1)} %copy-done.8, s32[1,640]{1,0:T(1,128)S(1)} %get-tuple-element.55.code_ref, bf16[512,1280]{1,0:T(8,128)(2,1)S(1)} %bitcast.24, bf16[72,1792]{1,0:T(8,128)(2,1)S(1)} %get-tuple-element.53.refs_8_.refs_1_, ...), custom_call_target="tpu_custom_call" | custom-call | tf_op jit(solution)/shard_map/attend/pallas_call | solution.py:294
  108.5 0.0 copy-done.4
  108.5 0.0 copy-done.5
  108.5 0.0 copy-done.7
  108.6 0.0 copy-done.9
  108.6 0.2 conditional.1
Async XLA Ops:
  0.0 3.1 %copy-start.1 = (bf16[512,1280]{1,0:T(8,128)(2,1)S(1)}, bf16[512,1280]{1,0:T(8,128)(2,1)}, u32[]{:S(2)}) copy-start(bf16[512,1280]{1,0:T(8,128)(2,1)} %q_ref.3) | copy-start | bytes 3932164
  5.0 91.9 %all-to-all-start.3 = ((bf16[8,64,1280]{2,1,0:T(8,128)(2,1)}), bf16[8,64,1280]{2,1,0:T(8,128)(2,1)S(1)}, u32[]{:S(2)}, u32[]{:S(2)}) async-start(bf16[8,64,1280]{2,1,0:T(8,128)(2,1)} %bitcast.14), calls=%async_computation.3 | async-start | bytes 2621440 | tf_op jit(solution)/shard_map/all_to_all | solution.py:376
  11.2 85.7 %copy-start.8 = (s32[4,4]{1,0:T(4,128)S(1)}, s32[4,4]{1,0:T(4,128)}, u32[]{:S(2)}) copy-start(s32[4,4]{1,0:T(4,128)} %anc_ref.1) | copy-start | bytes 196
  11.2 39.1 %collective-permute-start.8 = (bf16[72,1792]{1,0:T(8,128)(2,1)S(1)}, bf16[72,1792]{1,0:T(8,128)(2,1)S(1)}, u32[]{:S(2)}, u32[]{:S(2)}) collective-permute-start(bf16[72,1792]{1,0:T(8,128)(2,1)S(1)} %get-tuple-element.52.a_ref), channel_id=1, source_target_pairs={{0,8},{2,10},{4,12},{6,14},{8,0},{10,2},{12,4},{14,6},{1,9},{3,11}... | collective-permute-start | bytes 774152 | tf_op jit(solution)/shard_map/ppermute | solution.py:353
  11.2 41.6 %collective-permute-start.9 = (bf16[72,1792]{1,0:T(8,128)(2,1)S(1)}, bf16[72,1792]{1,0:T(8,128)(2,1)S(1)}, u32[]{:S(2)}, u32[]{:S(2)}) collective-permute-start(bf16[72,1792]{1,0:T(8,128)(2,1)S(1)} %get-tuple-element.52.a_ref), channel_id=1, source_target_pairs={{0,4},{2,6},{4,0},{6,2},{8,12},{10,14},{12,8},{14,10},{1,5},{3,7},... | collective-permute-start | bytes 774152 | tf_op jit(solution)/shard_map/ppermute | solution.py:353
  50.2 9.0 %collective-permute-start.10 = (bf16[72,1792]{1,0:T(8,128)(2,1)S(1)}, bf16[72,1792]{1,0:T(8,128)(2,1)S(1)}, u32[]{:S(2)}, u32[]{:S(2)}) collective-permute-start(bf16[72,1792]{1,0:T(8,128)(2,1)S(1)} %collective-permute-done.8.b_ref), channel_id=1, source_target_pairs={{0,4},{2,6},{4,0},{6,2},{8,12},{10,14},{12,8},{14,10},{1,5},{3,7},... | collective-permute-start | bytes 774152 | tf_op jit(solution)/shard_map/ppermute | solution.py:353
  59.7 22.3 %collective-permute-start.11 = (bf16[72,1792]{1,0:T(8,128)(2,1)S(1)}, bf16[72,1792]{1,0:T(8,128)(2,1)S(1)}, u32[]{:S(2)}, u32[]{:S(2)}) collective-permute-start(bf16[72,1792]{1,0:T(8,128)(2,1)S(1)} %get-tuple-element.54), channel_id=1, source_target_pairs={{0,2},{2,0},{4,6},{6,4},{8,10},{10,8},{12,14},{14,12},{1,3},{3,1},... | collective-permute-start | bytes 774152 | tf_op jit(solution)/shard_map/ppermute | solution.py:353
  61.1 9.5 %collective-permute-start.1 = (bf16[72,512]{1,0:T(8,128)(2,1)S(1)}, bf16[72,512]{1,0:T(8,128)(2,1)S(1)}, u32[]{:S(2)}, u32[]{:S(2)}) collective-permute-start(bf16[72,512]{1,0:T(8,128)(2,1)S(1)} %get-tuple-element.45), channel_id=1, source_target_pairs={{0,2},{2,0},{4,6},{6,4},{8,10},{10,8},{12,14},{14,12},{1,3},{3,1},... | collective-permute-start | bytes 221192 | tf_op jit(solution)/shard_map/ppermute | solution.py:353
  61.8 9.8 %collective-permute-start.2 = (bf16[72,512]{1,0:T(8,128)(2,1)S(1)}, bf16[72,512]{1,0:T(8,128)(2,1)S(1)}, u32[]{:S(2)}, u32[]{:S(2)}) collective-permute-start(bf16[72,512]{1,0:T(8,128)(2,1)S(1)} %get-tuple-element.46), channel_id=1, source_target_pairs={{0,4},{2,6},{4,0},{6,2},{8,12},{10,14},{12,8},{14,10},{1,5},{3,7},... | collective-permute-start | bytes 221192 | tf_op jit(solution)/shard_map/ppermute | solution.py:353
  63.6 10.6 %collective-permute-start.3 = (bf16[72,512]{1,0:T(8,128)(2,1)S(1)}, bf16[72,512]{1,0:T(8,128)(2,1)S(1)}, u32[]{:S(2)}, u32[]{:S(2)}) collective-permute-start(bf16[72,512]{1,0:T(8,128)(2,1)S(1)} %get-tuple-element.47), channel_id=1, source_target_pairs={{0,6},{2,4},{4,2},{6,0},{8,14},{10,12},{12,10},{14,8},{1,7},{3,5},... | collective-permute-start | bytes 221192 | tf_op jit(solution)/shard_map/ppermute | solution.py:353
  64.6 9.9 %collective-permute-start.4 = (bf16[72,512]{1,0:T(8,128)(2,1)S(1)}, bf16[72,512]{1,0:T(8,128)(2,1)S(1)}, u32[]{:S(2)}, u32[]{:S(2)}) collective-permute-start(bf16[72,512]{1,0:T(8,128)(2,1)S(1)} %get-tuple-element.48), channel_id=1, source_target_pairs={{0,8},{2,10},{4,12},{6,14},{8,0},{10,2},{12,4},{14,6},{1,9},{3,11}... | collective-permute-start | bytes 221192 | tf_op jit(solution)/shard_map/ppermute | solution.py:353
  70.6 6.3 %collective-permute-start.5 = (bf16[72,512]{1,0:T(8,128)(2,1)S(1)}, bf16[72,512]{1,0:T(8,128)(2,1)S(1)}, u32[]{:S(2)}, u32[]{:S(2)}) collective-permute-start(bf16[72,512]{1,0:T(8,128)(2,1)S(1)} %get-tuple-element.49), channel_id=1, source_target_pairs={{0,10},{2,8},{4,14},{6,12},{8,2},{10,0},{12,6},{14,4},{1,11},{3,9}... | collective-permute-start | bytes 221192 | tf_op jit(solution)/shard_map/ppermute | solution.py:353
  71.6 10.1 %collective-permute-start.6 = (bf16[72,512]{1,0:T(8,128)(2,1)S(1)}, bf16[72,512]{1,0:T(8,128)(2,1)S(1)}, u32[]{:S(2)}, u32[]{:S(2)}) collective-permute-start(bf16[72,512]{1,0:T(8,128)(2,1)S(1)} %get-tuple-element.50), channel_id=1, source_target_pairs={{0,12},{2,14},{4,8},{6,10},{8,4},{10,6},{12,0},{14,2},{1,13},{3,15... | collective-permute-start | bytes 221192 | tf_op jit(solution)/shard_map/ppermute | solution.py:353
  74.2 7.8 %collective-permute-start.7 = (bf16[72,512]{1,0:T(8,128)(2,1)S(1)}, bf16[72,512]{1,0:T(8,128)(2,1)S(1)}, u32[]{:S(2)}, u32[]{:S(2)}) collective-permute-start(bf16[72,512]{1,0:T(8,128)(2,1)S(1)} %get-tuple-element.51), channel_id=1, source_target_pairs={{0,14},{2,12},{4,10},{6,8},{8,6},{10,4},{12,2},{14,0},{1,15},{3,13... | collective-permute-start | bytes 221192 | tf_op jit(solution)/shard_map/ppermute | solution.py:353
  82.7 14.2 %collective-permute-start.12 = (bf16[512,512]{1,0:T(8,128)(2,1)S(1)}, bf16[512,512]{1,0:T(8,128)(2,1)S(1)}, u32[]{:S(2)}, u32[]{:S(2)}) collective-permute-start(bf16[512,512]{1,0:T(8,128)(2,1)S(1)} %get-tuple-element.57.refs_3_), channel_id=1, source_target_pairs={{0,2},{2,4},{4,6},{6,8},{8,10},{10,12},{12,14},{1,3},{3,5},{5,7},{... | collective-permute-start | bytes 1572872 | tf_op jit(solution)/shard_map/ppermute | solution.py:348
  96.9 11.6 %copy-start.4 = (bf16[512,256]{1,0:T(8,128)(2,1)S(1)}, bf16[512,256]{1,0:T(8,128)(2,1)}, u32[]{:S(2)}) copy-start(bf16[512,256]{1,0:T(8,128)(2,1)} %k_ref.1) | copy-start | bytes 786436
  96.9 11.6 %copy-start.5 = (bf16[512,256]{1,0:T(8,128)(2,1)S(1)}, bf16[512,256]{1,0:T(8,128)(2,1)}, u32[]{:S(2)}) copy-start(bf16[512,256]{1,0:T(8,128)(2,1)} %v_ref.1) | copy-start | bytes 786436
  96.9 11.6 %copy-start.7 = (s32[512]{0:T(512)S(1)}, s32[512]{0:T(512)}, u32[]{:S(2)}) copy-start(s32[512]{0:T(512)} %dest_ref.1) | copy-start | bytes 6148
  96.9 11.6 %copy-start.9 = (s32[512]{0:T(512)S(1)}, s32[512]{0:T(512)}, u32[]{:S(2)}) copy-start(s32[512]{0:T(512)} %slot_ref.1) | copy-start | bytes 6148

commit v3 on v2

--- a/solution.py
+++ b/solution.py
@@ -56,7 +56,7 @@
     position = jnp.sum(before * onehot.astype(jnp.float32), axis=0, keepdims=True).astype(jnp.int32)
     base = position < unit
     index = jnp.where(base, (dest ^ me) * unit + position, -1)
-    index_ref[...] = jnp.where(base, dest * unit + position, -1)
+    index_ref[...] = index
     over_index = jnp.where(base, -1, position - unit)
     totals = matmul_nt(jnp.ones((META, count), jnp.bfloat16), onehot)
     flags = (totals > unit + 0.5).astype(jnp.float32)
@@ -107,21 +107,32 @@
     return outs[:shards], outs[shards], outs[shards + 1]
 
 
-def pack_q_kernel(index_ref, q_ref, out_ref):
-    picked = select_rows(index_ref[...], 0, out_ref.shape[0])
-    out_ref[...] = matmul(picked, q_ref[...]).astype(jnp.bfloat16)
-
-
-def pack_q(index, queries):
-    return pl.pallas_call(
-        pack_q_kernel,
-        out_shape=jax.ShapeDtypeStruct(queries.shape, jnp.bfloat16),
-        in_specs=[VM, VM],
-        out_specs=VM,
-        compiler_params=params(12),
-        cost_estimate=light(),
-        name="pack_q",
-    )(index, queries)
+def pack_q_kernel(unit, cuts, index_ref, q_ref, *outs):
+    index = index_ref[...]
+    outs = iter(outs)
+    for r, parts in enumerate(cuts):
+        picked = select_rows(index, r * unit, unit)
+        width = q_ref.shape[1] // parts
+        for i in range(parts):
+            rows = matmul(picked, q_ref[:, i * width : (i + 1) * width])
+            next(outs)[...] = rows.astype(jnp.bfloat16)
+
+
+def pack_q(index, queries, unit, cuts):
+    width = queries.shape[1]
+    shapes = [jax.ShapeDtypeStruct((unit, width // n), jnp.bfloat16) for n in cuts for _ in range(n)]
+    outs = iter(
+        pl.pallas_call(
+            functools.partial(pack_q_kernel, unit, cuts),
+            out_shape=shapes,
+            in_specs=[VM, VM],
+            out_specs=[VM] * len(shapes),
+            compiler_params=params(12),
+            cost_estimate=light(),
+            name="pack_q",
+        )(index, queries)
+    )
+    return [[next(outs) for _ in range(n)] for n in cuts]
 
 
 def pick_over_kernel(unit, me_ref, a_ref, b_ref, c_ref, d_ref, keep_ref, send_ref):
@@ -177,52 +188,64 @@
     )(*blocks)
 
 
+def decode(meta, unit):
+    meta = meta.astype(jnp.float32)
+    return (meta[0:1, 0:unit] * RADIX + meta[1:2, 0:unit]).astype(jnp.int32)
+
+
 def place_kv_kernel(pieces, unit, count, *refs):
-    base, over = refs[:pieces], refs[pieces : pieces + 2]
-    placed_ref, codes_ref = refs[pieces + 2 :]
-    width = placed_ref.shape[1]
-    rows, codes = [], []
-
-    def decode(meta):
-        return (meta[0:1, 0:unit] * RADIX + meta[1:2, 0:unit]).astype(jnp.int32)
-
-    for ref in base:
-        rows.append(ref[0:unit, :])
-        codes.append(decode(ref[unit : unit + META, :].astype(jnp.float32)))
-    left = over[0].shape[1] - width
-    for ref in over:
-        rows.append(ref[0:unit, left:])
-        codes.append(decode(ref[unit : unit + META, 0:128].astype(jnp.float32)))
-    code = jnp.concatenate(codes, axis=1)
+    base, (placed_ref, codes_ref) = refs[:pieces], refs[pieces:]
+    code = jnp.concatenate([decode(ref[unit : unit + META, :], unit) for ref in base], axis=1)
     codes_ref[...] = code
-    placed = matmul(select_rows(code, 1, count), jnp.concatenate(rows, axis=0))
-    placed_ref[...] = placed.astype(jnp.bfloat16)
-
-
-def place_kv(base, over, unit, count):
+    rows = jnp.concatenate([ref[0:unit, :] for ref in base], axis=0)
+    placed_ref[...] = matmul(select_rows(code, 1, count), rows).astype(jnp.bfloat16)
+
+
+def place_kv(base, unit, count):
     width = base[0].shape[1]
-    raw = (len(base) + 2) * unit
+    raw = len(base) * unit
     return pl.pallas_call(
         functools.partial(place_kv_kernel, len(base), unit, count),
         out_shape=[
             jax.ShapeDtypeStruct((count, width), jnp.bfloat16),
             jax.ShapeDtypeStruct((1, raw), jnp.int32),
         ],
-        in_specs=[VM] * (len(base) + 2),
+        in_specs=[VM] * len(base),
         out_specs=[VM, VM],
         compiler_params=params(10),
         cost_estimate=light(),
         name="place_kv",
-    )(*base, *over)
-
-
-def attend_core(shard, anc_ref, q_pl, kv_all, out_ref):
+    )(*base)
+
+
+def merge_over_kernel(a_ref, b_ref, q_ref, kv_ref):
+    rows, width = q_ref.shape
+    q_ref[...] = a_ref[0:rows, 0:width] + b_ref[0:rows, 0:width]
+    kv_ref[...] = a_ref[:, width:] + b_ref[:, width:]
+    kv_ref[rows:, 0:HEAD_SIZE] = a_ref[rows:, 0:HEAD_SIZE] + b_ref[rows:, 0:HEAD_SIZE]
+
+
+def merge_over(kept, got, unit, kv_width):
+    width = kept.shape[1] - kv_width
+    return pl.pallas_call(
+        merge_over_kernel,
+        out_shape=[
+            jax.ShapeDtypeStruct((unit, width), jnp.bfloat16),
+            jax.ShapeDtypeStruct((unit + META, kv_width), jnp.bfloat16),
+        ],
+        in_specs=[VM, VM],
+        out_specs=[VM, VM],
+        compiler_params=params(4),
+        cost_estimate=light(),
+        name="merge_over",
+    )(kept, got)
+
+
+def attend_core(shard, anc_ref, q_pl, kv_all, out_ref, groups):
     count, width = out_ref.shape
     block_count = anc_ref.shape[0]
     size = count // block_count
-    kv_width = kv_all.shape[1] // 2
-    groups = kv_width // HEAD_SIZE
-    ratio = width // kv_width
+    ratio = width // groups // HEAD_SIZE
     window = (block_count + 1) * size
     scale = math.log2(math.e) / math.sqrt(HEAD_SIZE)
     lane = iota((size, window), 1)
@@ -244,7 +267,7 @@
             k = kv_all[b * size : b * size + window, g * HEAD_SIZE : (g + 1) * HEAD_SIZE]
             v = kv_all[
                 b * size : b * size + window,
-                kv_width + g * HEAD_SIZE : kv_width + (g + 1) * HEAD_SIZE,
+                (groups + g) * HEAD_SIZE : (groups + g + 1) * HEAD_SIZE,
             ]
             scores = (matmul_nt(q, k) * scale).reshape(ratio, size, window) + bias[None]
             scores = scores.reshape(ratio * size, window)
@@ -257,55 +280,73 @@
                 out_ref[b * size : (b + 1) * size, c : c + HEAD_SIZE] = output[h * size : (h + 1) * size]
 
 
-def attend_kernel(pieces, unit, me_ref, anc_ref, code_ref, *refs):
-    base, over = refs[0], refs[1:3]
-    own_kv, prior_kv, out_ref, raw, q_pl, kv_all, sems = refs[3:]
-    count, width = out_ref.shape
+def attend_kernel(pieces, unit, group, me_ref, anc_ref, code_ref, over_ref, behind_ref, *refs):
+    base, over_q, own_kv, prior_kv = refs[:pieces], *refs[pieces : pieces + 3]
+    out_ref, raw, q_pl, kv_all, sems = refs[-5:]
+    count, width = q_pl.shape
+    kv_width = own_kv.shape[1] // 2
     copies = []
-    for r in range(pieces):
-        start = pl.multiple_of((me_ref[0] ^ r) * unit, unit)
-        copies.append(
-            pltpu.make_async_copy(
-                base.at[pl.ds(start, unit), :], raw.at[pl.ds(r * unit, unit), :], sems.at[r]
+
+    def fetch(source, target):
+        copies.append(pltpu.make_async_copy(source, target, sems.at[len(copies)]))
+
+    for r, ref in enumerate(base):
+        start = group * width if ref.shape[1] > width else 0
+        fetch(ref.at[:, pl.ds(start, width)], raw.at[pl.ds(r * unit, unit), :])
+    fetch(over_q.at[:, pl.ds(group * width, width)], raw.at[pl.ds(pieces * unit, unit), :])
+    for j, ref in enumerate((prior_kv, own_kv)):
+        for h in range(2):
+            fetch(
+                ref.at[:, pl.ds(h * kv_width + group * HEAD_SIZE, HEAD_SIZE)],
+                kv_all.at[pl.ds(j * count, count), pl.ds(h * HEAD_SIZE, HEAD_SIZE)],
             )
-        )
-    for j, ref in enumerate(over):
-        i = pieces + j
-        copies.append(
-            pltpu.make_async_copy(
-                ref.at[pl.ds(0, unit), pl.ds(0, width)], raw.at[pl.ds(i * unit, unit), :], sems.at[i]
-            )
-        )
-    copies.append(pltpu.make_async_copy(prior_kv, kv_all.at[pl.ds(0, count), :], sems.at[pieces + 2]))
-    copies.append(pltpu.make_async_copy(own_kv, kv_all.at[pl.ds(count, count), :], sems.at[pieces + 3]))
     for c in copies:
         c.start()
-    onehot = select_rows(code_ref[...], 1, count)
+    own_over = decode(over_ref[unit : unit + META, :], unit)
+    behind_over = decode(behind_ref[unit : unit + META, :], unit)
+    onehot = select_rows(jnp.concatenate([code_ref[...], own_over], axis=1), 1, count)
     for c in copies:
         c.wait()
     q_pl[...] = matmul(onehot, raw[...]).astype(jnp.bfloat16)
-    attend_core(me_ref[0], anc_ref, q_pl, kv_all, out_ref)
-
-
-def attend(me, ancestors, codes, base, over, own_kv, prior_kv, unit):
-    count, width = base.shape
-    pieces = count // unit
-    raw = (pieces + 2) * unit
+    for j, (code, ref) in enumerate(((behind_over, behind_ref), (own_over, over_ref))):
+        picked = select_rows(code, 1, count)
+        for h in range(2):
+            c = h * kv_width + group * HEAD_SIZE
+            rows = matmul(picked, ref[0:unit, c : c + HEAD_SIZE]).astype(jnp.bfloat16)
+            kv_all[j * count : (j + 1) * count, h * HEAD_SIZE : (h + 1) * HEAD_SIZE] += rows
+    attend_core(me_ref[0], anc_ref, q_pl, kv_all, out_ref, 1)
+
+
+def attend(me, ancestors, codes, over_kv, behind_kv, base, over_q, own_kv, prior_kv, unit, group, groups, sofar):
+    count = own_kv.shape[0]
+    width = over_q.shape[1] // groups
+    pieces = len(base)
+    args = [me, ancestors, codes, over_kv, behind_kv, *base, over_q, own_kv, prior_kv]
+    aliases = {}
+    if sofar is not None:
+        aliases = {len(args): 0}
+        args.append(sofar)
+
+    def whole(x):
+        return pl.BlockSpec(x.shape, lambda i: (0, 0))
+
     return pl.pallas_call(
-        functools.partial(attend_kernel, pieces, unit),
-        out_shape=jax.ShapeDtypeStruct((count, width), jnp.bfloat16),
-        in_specs=[SM, SM, VM] + [HB] * 5,
-        out_specs=VM,
+        functools.partial(attend_kernel, pieces, unit, group),
+        out_shape=jax.ShapeDtypeStruct((count, width * groups), jnp.bfloat16),
+        grid=(1,),
+        in_specs=[SM, SM, whole(codes), whole(over_kv), whole(behind_kv)] + [HB] * (len(args) - 5),
+        out_specs=pl.BlockSpec((count, width), lambda i: (0, group)),
         scratch_shapes=[
-            pltpu.VMEM((raw, width), jnp.bfloat16),
+            pltpu.VMEM(((pieces + 1) * unit, width), jnp.bfloat16),
             pltpu.VMEM((count, width), jnp.bfloat16),
-            pltpu.VMEM((2 * count, own_kv.shape[1]), jnp.bfloat16),
-            pltpu.SemaphoreType.DMA((pieces + 4,)),
+            pltpu.VMEM((2 * count, 2 * HEAD_SIZE), jnp.bfloat16),
+            pltpu.SemaphoreType.DMA((pieces + 5,)),
         ],
-        compiler_params=params(28),
+        input_output_aliases=aliases,
+        compiler_params=params(24),
         cost_estimate=light(),
         name="attend",
-    )(me, ancestors, codes, base, *over, own_kv, prior_kv)
+    )(*args)
 
 
 def attend_padded_kernel(me_ref, anc_ref, code_ref, raw_ref, own_kv, prior_kv, out_ref, q_pl, kv_all):
@@ -313,7 +354,7 @@
     kv_all[0:count, :] = prior_kv[...]
     kv_all[count : 2 * count, :] = own_kv[...]
     q_pl[...] = matmul(select_rows(code_ref[...], 1, count), raw_ref[...]).astype(jnp.bfloat16)
-    attend_core(me_ref[0], anc_ref, q_pl, kv_all, out_ref)
+    attend_core(me_ref[0], anc_ref, q_pl, kv_all, out_ref, kv_all.shape[1] // (2 * HEAD_SIZE))
 
 
 def attend_padded(me, ancestors, codes, raw, own_kv, prior_kv):
@@ -368,20 +409,84 @@
     return attend_padded(me, ancestors, code.reshape(1, total), raw, own_kv, prior_kv)
 
 
+def after(block, *done):
+    return lax.optimization_barrier((block, *done))[0]
+
+
+class Line:
+    def __init__(self, depth):
+        self.depth, self.done = depth, []
+
+    def send(self, move, block, *also):
+        wait = self.done[-self.depth : len(self.done) - self.depth + 1]
+        self.done.append(move(after(block, *wait, *also)))
+        return self.done[-1]
+
+    def swap(self, block, r, *also):
+        return self.send(lambda x: swap(x, r), block, *also)
+
+
 def swap_plan(me, queries, keys, values, dest_shard, dest_slot, ancestors):
     count = queries.shape[0]
     shards = lax.axis_size("seq")
     unit = count // shards
+    groups = keys.shape[1] // HEAD_SIZE
     kv_blocks, over, index = pack_kv(me, dest_shard, dest_slot, keys, values, queries, shards, unit)
-    got_q = lax.all_to_all(pack_q(index, queries), "seq", split_axis=0, concat_axis=0, tiled=True)
-    first = swap(over, 4)
-    got_kv = [kv_blocks[0]] + [swap(kv_blocks[r], r) for r in range(1, shards)]
-    second = [swap(over, 2), swap(first, 2)]
+    cuts = [1] * 4 + [groups] * 4
+    q_blocks = pack_q(index, queries, unit, cuts)
+    line = Line(5)
+    got_kv = [kv_blocks[0]] + [None] * 7
+    got_q = [q_blocks[0] * groups] + [[None] * groups for _ in range(7)]
+
+    def kv(r, *also):
+        got_kv[r] = line.swap(kv_blocks[r], r, *also)
+
+    def q(r, g=None):
+        if g is None:
+            got_q[r] = [line.swap(q_blocks[r][0], r)] * groups
+        else:
+            got_q[r][g] = line.swap(q_blocks[r][g], r)
+
+    first = line.swap(over, 4)
+    for r in (4, 5, 6, 7):
+        kv(r)
+    kv(1, q_blocks[0][0])
+    kv(2)
+    q(4, 0)
+    kv(3)
+    q(5, 0)
+    second = [line.swap(over, 2), line.swap(first, 2)]
+    q(6, 0)
+    own_kv, codes = place_kv(got_kv, unit, count)
+    prior_kv = line.send(from_behind, own_kv)
+    q(7, 0)
     keep, send = pick_over(me, [over, first, *second], unit)
-    over_rows = [keep, swap(send, 1)]
-    own_kv, codes = place_kv(got_kv, over_rows, unit, count)
-    prior_kv = from_behind(own_kv)
-    result = attend(me, ancestors, codes, got_q, over_rows, own_kv, prior_kv, unit)
+    last = line.swap(send, 1)
+    over_q, over_kv = merge_over(keep, last, unit, own_kv.shape[1])
+    for r in (1, 2, 3):
+        q(r)
+    q(4, 1)
+    behind_kv = line.send(from_behind, over_kv)
+    q(5, 1)
+    q(6, 1)
+    q(7, 1)
+    result = None
+    for g in range(groups):
+        result = attend(
+            me,
+            ancestors,
+            codes,
+            over_kv,
+            behind_kv,
+            [pieces[g] for pieces in got_q],
+            over_q,
+            own_kv,
+            prior_kv,
+            unit,
+            g,
+            groups,
+            result,
+        )
     flag = crowded(got_kv, shards, unit)[0, 0]
     args = (queries, keys, values, dest_shard, dest_slot, ancestors)
     return lax.cond(flag > 0, lambda: padded_plan(me, *args), lambda: result)

time: 110 us -> 112 us (1.018)
  starting transfers between devices: 25 us -> 52.2 us
  waiting for transfers between devices: 64.4 us -> 37.6 us
  Pallas kernels: 17.9 us -> 19.3 us
    ppermute x11 -> x22, starting transfers between devices: 15 us -> 44.7 us  [swap(): return lax.ppermute(block, 'seq', [(i, i ^ r) for i in range(n)])]
    ppermute x11 -> x22, waiting for transfers between devices: 55.4 us -> 33.5 us  [swap(): return lax.ppermute(block, 'seq', [(i, i ^ r) for i in range(n)])]
    all_to_all x1 -> x0, starting transfers between devices: 6.14 us -> none  [swap_plan(): lax.all_to_all(pack_q(index, queries), 'seq', split_axis=0, concat_axis=0...]
    ppermute x1 -> x2, waiting for transfers between devices: 8.98 us -> 4.08 us  [from_behind(): return lax.ppermute(block, 'seq', [(i, i + 1) for i in range(n - 1)])]
    ppermute x1 -> x2, starting transfers between devices: 3.83 us -> 7.48 us  [from_behind(): return lax.ppermute(block, 'seq', [(i, i + 1) for i in range(n - 1)])]
    pallas_call x2 -> x4, Pallas kernels: 13.5 us -> 15.1 us  [the longest x2 13.1 us: attend(): pl.pallas_call(functools.partial(attend_kernel, pieces, unit, group), out...]
  transfers between devices with their start and end apart: 13 -> 24, of which waited for: 7 -> 8; matrix products, arithmetic and copies ran while one was open for 1% -> 0% of each run, Pallas kernels for 1% -> 8%
where the time goes in v3:
time: 112 us; the launch traced here: 111 us
  starting transfers between devices  52.2 us (47%)
  waiting for transfers between devices  37.6 us (34%)
  Pallas kernels  19.3 us (17%)
    ppermute x22, starting transfers between devices, swap(): return lax.ppermute(block, 'seq', [(i, i ^ r) for i in range(n)])  44.7 us
    ppermute x22, waiting for transfers between devices, swap(): return lax.ppermute(block, 'seq', [(i, i ^ r) for i in range(n)])  33.5 us
    pallas_call x2, Pallas kernels, attend(): pl.pallas_call(functools.partial(attend_kernel, pieces, unit, group), out...  13.1 us
    ppermute x2, starting transfers between devices, from_behind(): return lax.ppermute(block, 'seq', [(i, i + 1) for i in range(n - 1)])  7.48 us
    ppermute x2, waiting for transfers between devices, from_behind(): return lax.ppermute(block, 'seq', [(i, i + 1) for i in range(n - 1)])  4.08 us
    pallas_call x1, Pallas kernels, pack_kv(): pl.pallas_call(functools.partial(pack_kv_kernel, shards, unit), out_shape...  3.1 us
  transfers between devices with their start and end apart: 24, of which 8 were waited for; matrix products, arithmetic and copies ran while one was open for 0% of the time, Pallas kernels for 8%

profile of v3, /device:TPU:16, one launch (start us, length us, event | category | flops | bytes accessed | tf_op | source)
XLA Modules:
  0.0 111.1 jit_solution(16997183266465210017)
XLA Ops:
  0.0 3.1 %pack_kv.1 = (bf16[72,512]{1,0:T(8,128)(2,1)S(1)}, bf16[72,512]{1,0:T(8,128)(2,1)S(1)}, bf16[72,512]{1,0:T(8,128)(2,1)S(1)}, bf16[72,512]{1,0:T(8,128)(2,1)S(1)}...) custom-call(s32[1]{0:T(128)} %bitcast.12.me_ref, ...), custom_call_target="tpu_custom_call" | custom-call | tf_op jit(solution)/shard_map/pack_kv/pallas_call | solution.py:98
  3.1 0.1 collective-permute-start.1
  3.2 2.9 %collective-permute-start.3 = (bf16[72,512]{1,0:T(8,128)(2,1)S(1)}, bf16[72,512]{1,0:T(8,128)(2,1)S(1)}, u32[]{:S(2)}, u32[]{:S(2)}) collective-permute-start(bf16[72,512]{1,0:T(8,128)(2,1)S(1)} %get-tuple-element.85), channel_id=1, source_target_pairs={{0,8},{2,10},{4,12},{6,14},{8,0},{10,2},{12,4},{14,6},{1,9},{3,11}... | collective-permute-start | bytes 221192 | tf_op jit(solution)/shard_map/ppermute | solution.py:394
  6.1 11.5 %collective-permute-done.3.refs_4_ = bf16[72,512]{1,0:T(8,128)(2,1)S(1)} collective-permute-done((bf16[72,512]{1,0:T(8,128)(2,1)S(1)}, bf16[72,512]{1,0:T(8,128)(2,1)S(1)}, u32[]{:S(2)}, u32[]{:S(2)}) %collective-permute-start.3) | collective-permute-done | bytes 73760 | tf_op jit(solution)/shard_map/ppermute | solution.py:394
  17.6 2.6 %collective-permute-start.5 = (bf16[72,512]{1,0:T(8,128)(2,1)S(1)}, bf16[72,512]{1,0:T(8,128)(2,1)S(1)}, u32[]{:S(2)}, u32[]{:S(2)}) collective-permute-start(bf16[72,512]{1,0:T(8,128)(2,1)S(1)} %get-tuple-element.89), channel_id=1, source_target_pairs={{0,12},{2,14},{4,8},{6,10},{8,4},{10,6},{12,0},{14,2},{1,13},{3,15... | collective-permute-start | bytes 221192 | tf_op jit(solution)/shard_map/ppermute | solution.py:394
  20.3 5.2 %collective-permute-start.7 = (bf16[72,512]{1,0:T(8,128)(2,1)S(1)}, bf16[72,512]{1,0:T(8,128)(2,1)S(1)}, u32[]{:S(2)}, u32[]{:S(2)}) collective-permute-start(bf16[72,512]{1,0:T(8,128)(2,1)S(1)} %get-tuple-element.91), channel_id=1, source_target_pairs={{0,10},{2,8},{4,14},{6,12},{8,2},{10,0},{12,6},{14,4},{1,11},{3,9}... | collective-permute-start | bytes 221192 | tf_op jit(solution)/shard_map/ppermute | solution.py:394
  25.5 1.9 %pack_q.1 = (bf16[64,1280]{1,0:T(8,128)(2,1)S(1)}, bf16[64,1280]{1,0:T(8,128)(2,1)S(1)}, bf16[64,1280]{1,0:T(8,128)(2,1)S(1)}, bf16[64,1280]{1,0:T(8,128)(2,1)S(...) custom-call(s32[1,512]{1,0:T(1,128)S(1)} %get-tuple-element.81.index, ...), custom_call_target="tpu_custom_call" | custom-call | tf_op jit(solution)/shard_map/pack_q/pallas_call | solution.py:125
  27.4 1.5 %collective-permute-start.4 = (bf16[72,512]{1,0:T(8,128)(2,1)S(1)}, bf16[72,512]{1,0:T(8,128)(2,1)S(1)}, u32[]{:S(2)}, u32[]{:S(2)}) collective-permute-start(bf16[72,512]{1,0:T(8,128)(2,1)S(1)} %get-tuple-element.86), channel_id=1, source_target_pairs={{0,4},{2,6},{4,0},{6,2},{8,12},{10,14},{12,8},{14,10},{1,5},{3,7},... | collective-permute-start | bytes 221192 | tf_op jit(solution)/shard_map/ppermute | solution.py:394
  29.0 0.5 collective-permute-start.2
  29.5 1.5 %collective-permute-start.6 = (bf16[72,512]{1,0:T(8,128)(2,1)S(1)}, bf16[72,512]{1,0:T(8,128)(2,1)S(1)}, u32[]{:S(2)}, u32[]{:S(2)}) collective-permute-start(bf16[72,512]{1,0:T(8,128)(2,1)S(1)} %get-tuple-element.90), channel_id=1, source_target_pairs={{0,6},{2,4},{4,2},{6,0},{8,14},{10,12},{12,10},{14,8},{1,7},{3,5},... | collective-permute-start | bytes 221192 | tf_op jit(solution)/shard_map/ppermute | solution.py:394
  31.0 2.9 %collective-permute-done.8.refs_7_ = bf16[72,512]{1,0:T(8,128)(2,1)S(1)} collective-permute-done((bf16[72,512]{1,0:T(8,128)(2,1)S(1)}, bf16[72,512]{1,0:T(8,128)(2,1)S(1)}, u32[]{:S(2)}, u32[]{:S(2)}) %collective-permute-start.8) | collective-permute-done | bytes 73760 | tf_op jit(solution)/shard_map/ppermute | solution.py:394
  33.9 1.6 %collective-permute-done.2.refs_1_ = bf16[72,512]{1,0:T(8,128)(2,1)S(1)} collective-permute-done((bf16[72,512]{1,0:T(8,128)(2,1)S(1)}, bf16[72,512]{1,0:T(8,128)(2,1)S(1)}, u32[]{:S(2)}, u32[]{:S(2)}) %collective-permute-start.2) | collective-permute-done | bytes 73760 | tf_op jit(solution)/shard_map/ppermute | solution.py:394
  35.5 0.5 place_kv.1
  36.0 3.3 %collective-permute-start.17 = (bf16[512,512]{1,0:T(8,128)(2,1)S(1)}, bf16[512,512]{1,0:T(8,128)(2,1)S(1)}, u32[]{:S(2)}, u32[]{:S(2)}) collective-permute-start(bf16[512,512]{1,0:T(8,128)(2,1)S(1)} %get-tuple-element.111.refs_9_), channel_id=1, source_target_pairs={{0,2},{2,4},{4,6},{6,8},{8,10},{10,12},{12,14},{1,3},{3,5},{5,7},{... | collective-permute-start | bytes 1572872 | tf_op jit(solution)/shard_map/ppermute | solution.py:389
  39.3 0.7 collective-permute-start.10
  40.0 1.4 %collective-permute-start.9 = (bf16[72,1792]{1,0:T(8,128)(2,1)S(1)}, bf16[72,1792]{1,0:T(8,128)(2,1)S(1)}, u32[]{:S(2)}, u32[]{:S(2)}) collective-permute-start(bf16[72,1792]{1,0:T(8,128)(2,1)S(1)} %get-tuple-element.94.a_ref), channel_id=1, source_target_pairs={{0,4},{2,6},{4,0},{6,2},{8,12},{10,14},{12,8},{14,10},{1,5},{3,7},... | collective-permute-start | bytes 774152 | tf_op jit(solution)/shard_map/ppermute | solution.py:394
  41.4 1.4 %collective-permute-start.14 = (bf16[64,640]{1,0:T(8,128)(2,1)S(1)}, bf16[64,640]{1,0:T(8,128)(2,1)S(1)}, u32[]{:S(2)}, u32[]{:S(2)}) collective-permute-start(bf16[64,640]{1,0:T(8,128)(2,1)S(1)} %get-tuple-element.106), channel_id=1, source_target_pairs={{0,8},{2,10},{4,12},{6,14},{8,0},{10,2},{12,4},{14,6},{1,9},{3,11}... | collective-permute-start | bytes 245768 | tf_op jit(solution)/shard_map/ppermute | solution.py:394
  42.8 5.8 %collective-permute-done.10.d_ref = bf16[72,1792]{1,0:T(8,128)(2,1)S(1)} collective-permute-done((bf16[72,1792]{1,0:T(8,128)(2,1)S(1)}, bf16[72,1792]{1,0:T(8,128)(2,1)S(1)}, u32[]{:S(2)}, u32[]{:S(2)}) %collective-permute-start.10) | collective-permute-done | bytes 258080 | tf_op jit(solution)/shard_map/ppermute | solution.py:394
  48.5 4.1 %collective-permute-done.9.c_ref = bf16[72,1792]{1,0:T(8,128)(2,1)S(1)} collective-permute-done((bf16[72,1792]{1,0:T(8,128)(2,1)S(1)}, bf16[72,1792]{1,0:T(8,128)(2,1)S(1)}, u32[]{:S(2)}, u32[]{:S(2)}) %collective-permute-start.9) | collective-permute-done | bytes 258080 | tf_op jit(solution)/shard_map/ppermute | solution.py:394
  52.7 0.5 pick_over.1
  53.1 10.7 %collective-permute-start.11 = (bf16[72,1792]{1,0:T(8,128)(2,1)S(1)}, bf16[72,1792]{1,0:T(8,128)(2,1)S(1)}, u32[]{:S(2)}, u32[]{:S(2)}) collective-permute-start(bf16[72,1792]{1,0:T(8,128)(2,1)S(1)} %get-tuple-element.98), channel_id=1, source_target_pairs={{0,2},{2,0},{4,6},{6,4},{8,10},{10,8},{12,14},{14,12},{1,3},{3,1},... | collective-permute-start | bytes 774152 | tf_op jit(solution)/shard_map/ppermute | solution.py:394
  63.8 1.1 collective-permute-start.15
  64.9 3.3 %collective-permute-start.19 = (bf16[64,640]{1,0:T(8,128)(2,1)S(1)}, bf16[64,640]{1,0:T(8,128)(2,1)S(1)}, u32[]{:S(2)}, u32[]{:S(2)}) collective-permute-start(bf16[64,640]{1,0:T(8,128)(2,1)S(1)} %get-tuple-element.116), channel_id=1, source_target_pairs={{0,10},{2,8},{4,14},{6,12},{8,2},{10,0},{12,6},{14,4},{1,11},{3,9}... | collective-permute-start | bytes 245768 | tf_op jit(solution)/shard_map/ppermute | solution.py:394
  68.2 1.7 %collective-permute-done.15.refs_6_ = bf16[64,640]{1,0:T(8,128)(2,1)S(1)} collective-permute-done((bf16[64,640]{1,0:T(8,128)(2,1)S(1)}, bf16[64,640]{1,0:T(8,128)(2,1)S(1)}, u32[]{:S(2)}, u32[]{:S(2)}) %collective-permute-start.15) | collective-permute-done | bytes 81952 | tf_op jit(solution)/shard_map/ppermute | solution.py:394
  69.9 3.3 %collective-permute-start.16 = (bf16[64,1280]{1,0:T(8,128)(2,1)S(1)}, bf16[64,1280]{1,0:T(8,128)(2,1)S(1)}, u32[]{:S(2)}, u32[]{:S(2)}) collective-permute-start(bf16[64,1280]{1,0:T(8,128)(2,1)S(1)} %get-tuple-element.108), channel_id=1, source_target_pairs={{0,4},{2,6},{4,0},{6,2},{8,12},{10,14},{12,8},{14,10},{1,5},{3,7},... | collective-permute-start | bytes 491528 | tf_op jit(solution)/shard_map/ppermute | solution.py:394
  73.2 0.2 collective-permute-start.13
  73.5 0.0 collective-permute-done.17.refs_10_
  73.5 1.2 %collective-permute-start.18 = (bf16[64,1280]{1,0:T(8,128)(2,1)S(1)}, bf16[64,1280]{1,0:T(8,128)(2,1)S(1)}, u32[]{:S(2)}, u32[]{:S(2)}) collective-permute-start(bf16[64,1280]{1,0:T(8,128)(2,1)S(1)} %get-tuple-element.112), channel_id=1, source_target_pairs={{0,6},{2,4},{4,2},{6,0},{8,14},{10,12},{12,10},{14,8},{1,7},{3,5},... | collective-permute-start | bytes 491528 | tf_op jit(solution)/shard_map/ppermute | solution.py:394
  74.7 0.0 collective-permute-done.19.refs_5_
  74.7 0.1 collective-permute-start.20
  74.8 5.9 %collective-permute-done.20.refs_7_ = bf16[64,640]{1,0:T(8,128)(2,1)S(1)} collective-permute-done((bf16[64,640]{1,0:T(8,128)(2,1)S(1)}, bf16[64,640]{1,0:T(8,128)(2,1)S(1)}, u32[]{:S(2)}, u32[]{:S(2)}) %collective-permute-start.20) | collective-permute-done | bytes 81952 | tf_op jit(solution)/shard_map/ppermute | solution.py:394
  80.7 3.2 %collective-permute-start.21 = (bf16[64,640]{1,0:T(8,128)(2,1)S(1)}, bf16[64,640]{1,0:T(8,128)(2,1)S(1)}, u32[]{:S(2)}, u32[]{:S(2)}) collective-permute-start(bf16[64,640]{1,0:T(8,128)(2,1)S(1)} %get-tuple-element.118), channel_id=1, source_target_pairs={{0,8},{2,10},{4,12},{6,14},{8,0},{10,2},{12,4},{14,6},{1,9},{3,11}... | collective-permute-start | bytes 245768 | tf_op jit(solution)/shard_map/ppermute | solution.py:394
  83.8 0.0 collective-permute-done.16.refs_2_
  83.8 2.1 %collective-permute-start.23 = (bf16[64,640]{1,0:T(8,128)(2,1)S(1)}, bf16[64,640]{1,0:T(8,128)(2,1)S(1)}, u32[]{:S(2)}, u32[]{:S(2)}) collective-permute-start(bf16[64,640]{1,0:T(8,128)(2,1)S(1)} %get-tuple-element.122), channel_id=1, source_target_pairs={{0,12},{2,14},{4,8},{6,10},{8,4},{10,6},{12,0},{14,2},{1,13},{3,15... | collective-permute-start | bytes 245768 | tf_op jit(solution)/shard_map/ppermute | solution.py:394
  86.0 0.0 collective-permute-done.13.refs_1_
  86.0 0.6 collective-permute-start.22
  86.6 1.1 %collective-permute-start.24 = (bf16[64,640]{1,0:T(8,128)(2,1)S(1)}, bf16[64,640]{1,0:T(8,128)(2,1)S(1)}, u32[]{:S(2)}, u32[]{:S(2)}) collective-permute-start(bf16[64,640]{1,0:T(8,128)(2,1)S(1)} %get-tuple-element.124), channel_id=1, source_target_pairs={{0,14},{2,12},{4,10},{6,8},{8,6},{10,4},{12,2},{14,0},{1,15},{3,13... | collective-permute-start | bytes 245768 | tf_op jit(solution)/shard_map/ppermute | solution.py:394
  87.7 4.1 %collective-permute-start.12 = (bf16[72,512]{1,0:T(8,128)(2,1)S(1)}, bf16[72,512]{1,0:T(8,128)(2,1)S(1)}, u32[]{:S(2)}, u32[]{:S(2)}) collective-permute-start(bf16[72,512]{1,0:T(8,128)(2,1)S(1)} %get-tuple-element.100.over_ref), channel_id=1, source_target_pairs={{0,2},{2,4},{4,6},{6,8},{8,10},{10,12},{12,14},{1,3},{3,5},{5,7},{... | collective-permute-start | bytes 221192 | tf_op jit(solution)/shard_map/ppermute | solution.py:389
  91.9 0.2 crowded.1
  92.1 0.5 slice.9
  93.3 4.1 %collective-permute-done.12.behind_ref = bf16[72,512]{1,0:T(8,128)(2,1)S(1)} collective-permute-done((bf16[72,512]{1,0:T(8,128)(2,1)S(1)}, bf16[72,512]{1,0:T(8,128)(2,1)S(1)}, u32[]{:S(2)}, u32[]{:S(2)}) %collective-permute-start.12) | collective-permute-done | bytes 73760 | tf_op jit(solution)/shard_map/ppermute | solution.py:389
  97.3 6.5 %attend.2.refs_11_ = bf16[512,1280]{1,0:T(8,128)(2,1)} custom-call(s32[1]{0:T(128)} %bitcast.12.me_ref, s32[4,4]{1,0:T(4,128)S(1)} %copy-done.7, s32[1,512]{1,0:T(1,128)S(1)} %get-tuple-element.93.code_ref, bf16[72,512]{1,0:T(8,128)(2,1)S(1)} %get-tuple-element.100.over_ref, bf16[72,512]{1,0:T(8,128)(2,1)S(1)} %collective-permute-done.12.behind_ref, ...), custom_call_target="tpu_custom_call" | custom-call | tf_op jit(solution)/shard_map/attend/pallas_call | solution.py:333
  103.9 0.0 copy-start.3
  103.9 0.0 copy-start.4
  103.9 0.0 copy-start.6
  103.9 0.0 copy-start.8
  104.0 6.6 %attend.3 = bf16[512,1280]{1,0:T(8,128)(2,1)} custom-call(s32[1]{0:T(128)} %bitcast.12.me_ref, s32[4,4]{1,0:T(4,128)S(1)} %copy-done.7, s32[1,512]{1,0:T(1,128)S(1)} %get-tuple-element.93.code_ref, bf16[72,512]{1,0:T(8,128)(2,1)S(1)} %get-tuple-element.100.over_ref, ...), custom_call_target="tpu_custom_call", output_to_operand_aliasing={{}: (16, {})} | custom-call | tf_op jit(solution)/shard_map/attend/pallas_call | solution.py:333
  110.6 0.3 conditional.1
  (22 shorter events, 0.1 us)
Async XLA Ops:
  0.0 25.5 %copy-start.1 = (bf16[512,1280]{1,0:T(8,128)(2,1)S(1)}, bf16[512,1280]{1,0:T(8,128)(2,1)}, u32[]{:S(2)}) copy-start(bf16[512,1280]{1,0:T(8,128)(2,1)} %q_ref.3) | copy-start | bytes 3932164
  3.1 14.5 %collective-permute-start.1 = (bf16[72,1792]{1,0:T(8,128)(2,1)S(1)}, bf16[72,1792]{1,0:T(8,128)(2,1)S(1)}, u32[]{:S(2)}, u32[]{:S(2)}) collective-permute-start(bf16[72,1792]{1,0:T(8,128)(2,1)S(1)} %get-tuple-element.94.a_ref), channel_id=1, source_target_pairs={{0,8},{2,10},{4,12},{6,14},{8,0},{10,2},{12,4},{14,6},{1,9},{3,11}... | collective-permute-start | bytes 774152 | tf_op jit(solution)/shard_map/ppermute | solution.py:394
  3.2 14.4 %collective-permute-start.3 = (bf16[72,512]{1,0:T(8,128)(2,1)S(1)}, bf16[72,512]{1,0:T(8,128)(2,1)S(1)}, u32[]{:S(2)}, u32[]{:S(2)}) collective-permute-start(bf16[72,512]{1,0:T(8,128)(2,1)S(1)} %get-tuple-element.85), channel_id=1, source_target_pairs={{0,8},{2,10},{4,12},{6,14},{8,0},{10,2},{12,4},{14,6},{1,9},{3,11}... | collective-permute-start | bytes 221192 | tf_op jit(solution)/shard_map/ppermute | solution.py:394
  17.6 11.9 %collective-permute-start.5 = (bf16[72,512]{1,0:T(8,128)(2,1)S(1)}, bf16[72,512]{1,0:T(8,128)(2,1)S(1)}, u32[]{:S(2)}, u32[]{:S(2)}) collective-permute-start(bf16[72,512]{1,0:T(8,128)(2,1)S(1)} %get-tuple-element.89), channel_id=1, source_target_pairs={{0,12},{2,14},{4,8},{6,10},{8,4},{10,6},{12,0},{14,2},{1,13},{3,15... | collective-permute-start | bytes 221192 | tf_op jit(solution)/shard_map/ppermute | solution.py:394
  20.3 10.7 %collective-permute-start.7 = (bf16[72,512]{1,0:T(8,128)(2,1)S(1)}, bf16[72,512]{1,0:T(8,128)(2,1)S(1)}, u32[]{:S(2)}, u32[]{:S(2)}) collective-permute-start(bf16[72,512]{1,0:T(8,128)(2,1)S(1)} %get-tuple-element.91), channel_id=1, source_target_pairs={{0,10},{2,8},{4,14},{6,12},{8,2},{10,0},{12,6},{14,4},{1,11},{3,9}... | collective-permute-start | bytes 221192 | tf_op jit(solution)/shard_map/ppermute | solution.py:394
  25.5 8.4 %collective-permute-start.8 = (bf16[72,512]{1,0:T(8,128)(2,1)S(1)}, bf16[72,512]{1,0:T(8,128)(2,1)S(1)}, u32[]{:S(2)}, u32[]{:S(2)}) collective-permute-start(bf16[72,512]{1,0:T(8,128)(2,1)S(1)} %get-tuple-element.92), channel_id=1, source_target_pairs={{0,14},{2,12},{4,10},{6,8},{8,6},{10,4},{12,2},{14,0},{1,15},{3,13... | collective-permute-start | bytes 221192 | tf_op jit(solution)/shard_map/ppermute | solution.py:394
  27.4 6.4 %collective-permute-start.4 = (bf16[72,512]{1,0:T(8,128)(2,1)S(1)}, bf16[72,512]{1,0:T(8,128)(2,1)S(1)}, u32[]{:S(2)}, u32[]{:S(2)}) collective-permute-start(bf16[72,512]{1,0:T(8,128)(2,1)S(1)} %get-tuple-element.86), channel_id=1, source_target_pairs={{0,4},{2,6},{4,0},{6,2},{8,12},{10,14},{12,8},{14,10},{1,5},{3,7},... | collective-permute-start | bytes 221192 | tf_op jit(solution)/shard_map/ppermute | solution.py:394
  29.0 6.5 %collective-permute-start.2 = (bf16[72,512]{1,0:T(8,128)(2,1)S(1)}, bf16[72,512]{1,0:T(8,128)(2,1)S(1)}, u32[]{:S(2)}, u32[]{:S(2)}) collective-permute-start(bf16[72,512]{1,0:T(8,128)(2,1)S(1)} %get-tuple-element.83), channel_id=1, source_target_pairs={{0,2},{2,0},{4,6},{6,4},{8,10},{10,8},{12,14},{14,12},{1,3},{3,1},... | collective-permute-start | bytes 221192 | tf_op jit(solution)/shard_map/ppermute | solution.py:394
  29.5 6.0 %collective-permute-start.6 = (bf16[72,512]{1,0:T(8,128)(2,1)S(1)}, bf16[72,512]{1,0:T(8,128)(2,1)S(1)}, u32[]{:S(2)}, u32[]{:S(2)}) collective-permute-start(bf16[72,512]{1,0:T(8,128)(2,1)S(1)} %get-tuple-element.90), channel_id=1, source_target_pairs={{0,6},{2,4},{4,2},{6,0},{8,14},{10,12},{12,10},{14,8},{1,7},{3,5},... | collective-permute-start | bytes 221192 | tf_op jit(solution)/shard_map/ppermute | solution.py:394
  35.5 61.9 %copy-start.7 = (s32[4,4]{1,0:T(4,128)S(1)}, s32[4,4]{1,0:T(4,128)}, u32[]{:S(2)}) copy-start(s32[4,4]{1,0:T(4,128)} %anc_ref.3) | copy-start | bytes 196
  36.0 37.5 %collective-permute-start.17 = (bf16[512,512]{1,0:T(8,128)(2,1)S(1)}, bf16[512,512]{1,0:T(8,128)(2,1)S(1)}, u32[]{:S(2)}, u32[]{:S(2)}) collective-permute-start(bf16[512,512]{1,0:T(8,128)(2,1)S(1)} %get-tuple-element.111.refs_9_), channel_id=1, source_target_pairs={{0,2},{2,4},{4,6},{6,8},{8,10},{10,12},{12,14},{1,3},{3,5},{5,7},{... | collective-permute-start | bytes 1572872 | tf_op jit(solution)/shard_map/ppermute | solution.py:389
  39.3 9.2 %collective-permute-start.10 = (bf16[72,1792]{1,0:T(8,128)(2,1)S(1)}, bf16[72,1792]{1,0:T(8,128)(2,1)S(1)}, u32[]{:S(2)}, u32[]{:S(2)}) collective-permute-start(bf16[72,1792]{1,0:T(8,128)(2,1)S(1)} %collective-permute-done.1.b_ref), channel_id=1, source_target_pairs={{0,4},{2,6},{4,0},{6,2},{8,12},{10,14},{12,8},{14,10},{1,5},{3,7},... | collective-permute-start | bytes 774152 | tf_op jit(solution)/shard_map/ppermute | solution.py:394
  40.0 12.7 %collective-permute-start.9 = (bf16[72,1792]{1,0:T(8,128)(2,1)S(1)}, bf16[72,1792]{1,0:T(8,128)(2,1)S(1)}, u32[]{:S(2)}, u32[]{:S(2)}) collective-permute-start(bf16[72,1792]{1,0:T(8,128)(2,1)S(1)} %get-tuple-element.94.a_ref), channel_id=1, source_target_pairs={{0,4},{2,6},{4,0},{6,2},{8,12},{10,14},{12,8},{14,10},{1,5},{3,7},... | collective-permute-start | bytes 774152 | tf_op jit(solution)/shard_map/ppermute | solution.py:394
  41.4 22.4 %collective-permute-start.14 = (bf16[64,640]{1,0:T(8,128)(2,1)S(1)}, bf16[64,640]{1,0:T(8,128)(2,1)S(1)}, u32[]{:S(2)}, u32[]{:S(2)}) collective-permute-start(bf16[64,640]{1,0:T(8,128)(2,1)S(1)} %get-tuple-element.106), channel_id=1, source_target_pairs={{0,8},{2,10},{4,12},{6,14},{8,0},{10,2},{12,4},{14,6},{1,9},{3,11}... | collective-permute-start | bytes 245768 | tf_op jit(solution)/shard_map/ppermute | solution.py:394
  53.1 34.5 %collective-permute-start.11 = (bf16[72,1792]{1,0:T(8,128)(2,1)S(1)}, bf16[72,1792]{1,0:T(8,128)(2,1)S(1)}, u32[]{:S(2)}, u32[]{:S(2)}) collective-permute-start(bf16[72,1792]{1,0:T(8,128)(2,1)S(1)} %get-tuple-element.98), channel_id=1, source_target_pairs={{0,2},{2,0},{4,6},{6,4},{8,10},{10,8},{12,14},{14,12},{1,3},{3,1},... | collective-permute-start | bytes 774152 | tf_op jit(solution)/shard_map/ppermute | solution.py:394
  63.8 6.1 %collective-permute-start.15 = (bf16[64,640]{1,0:T(8,128)(2,1)S(1)}, bf16[64,640]{1,0:T(8,128)(2,1)S(1)}, u32[]{:S(2)}, u32[]{:S(2)}) collective-permute-start(bf16[64,640]{1,0:T(8,128)(2,1)S(1)} %get-tuple-element.107), channel_id=1, source_target_pairs={{0,12},{2,14},{4,8},{6,10},{8,4},{10,6},{12,0},{14,2},{1,13},{3,15... | collective-permute-start | bytes 245768 | tf_op jit(solution)/shard_map/ppermute | solution.py:394
  64.9 9.8 %collective-permute-start.19 = (bf16[64,640]{1,0:T(8,128)(2,1)S(1)}, bf16[64,640]{1,0:T(8,128)(2,1)S(1)}, u32[]{:S(2)}, u32[]{:S(2)}) collective-permute-start(bf16[64,640]{1,0:T(8,128)(2,1)S(1)} %get-tuple-element.116), channel_id=1, source_target_pairs={{0,10},{2,8},{4,14},{6,12},{8,2},{10,0},{12,6},{14,4},{1,11},{3,9}... | collective-permute-start | bytes 245768 | tf_op jit(solution)/shard_map/ppermute | solution.py:394
  69.9 14.0 %collective-permute-start.16 = (bf16[64,1280]{1,0:T(8,128)(2,1)S(1)}, bf16[64,1280]{1,0:T(8,128)(2,1)S(1)}, u32[]{:S(2)}, u32[]{:S(2)}) collective-permute-start(bf16[64,1280]{1,0:T(8,128)(2,1)S(1)} %get-tuple-element.108), channel_id=1, source_target_pairs={{0,4},{2,6},{4,0},{6,2},{8,12},{10,14},{12,8},{14,10},{1,5},{3,7},... | collective-permute-start | bytes 491528 | tf_op jit(solution)/shard_map/ppermute | solution.py:394
  73.2 12.8 %collective-permute-start.13 = (bf16[64,1280]{1,0:T(8,128)(2,1)S(1)}, bf16[64,1280]{1,0:T(8,128)(2,1)S(1)}, u32[]{:S(2)}, u32[]{:S(2)}) collective-permute-start(bf16[64,1280]{1,0:T(8,128)(2,1)S(1)} %get-tuple-element.102), channel_id=1, source_target_pairs={{0,2},{2,0},{4,6},{6,4},{8,10},{10,8},{12,14},{14,12},{1,3},{3,1},... | collective-permute-start | bytes 491528 | tf_op jit(solution)/shard_map/ppermute | solution.py:394
  73.5 13.1 %collective-permute-start.18 = (bf16[64,1280]{1,0:T(8,128)(2,1)S(1)}, bf16[64,1280]{1,0:T(8,128)(2,1)S(1)}, u32[]{:S(2)}, u32[]{:S(2)}) collective-permute-start(bf16[64,1280]{1,0:T(8,128)(2,1)S(1)} %get-tuple-element.112), channel_id=1, source_target_pairs={{0,6},{2,4},{4,2},{6,0},{8,14},{10,12},{12,10},{14,8},{1,7},{3,5},... | collective-permute-start | bytes 491528 | tf_op jit(solution)/shard_map/ppermute | solution.py:394
  74.7 6.0 %collective-permute-start.20 = (bf16[64,640]{1,0:T(8,128)(2,1)S(1)}, bf16[64,640]{1,0:T(8,128)(2,1)S(1)}, u32[]{:S(2)}, u32[]{:S(2)}) collective-permute-start(bf16[64,640]{1,0:T(8,128)(2,1)S(1)} %get-tuple-element.117), channel_id=1, source_target_pairs={{0,14},{2,12},{4,10},{6,8},{8,6},{10,4},{12,2},{14,0},{1,15},{3,13... | collective-permute-start | bytes 245768 | tf_op jit(solution)/shard_map/ppermute | solution.py:394
  80.7 23.3 %collective-permute-start.21 = (bf16[64,640]{1,0:T(8,128)(2,1)S(1)}, bf16[64,640]{1,0:T(8,128)(2,1)S(1)}, u32[]{:S(2)}, u32[]{:S(2)}) collective-permute-start(bf16[64,640]{1,0:T(8,128)(2,1)S(1)} %get-tuple-element.118), channel_id=1, source_target_pairs={{0,8},{2,10},{4,12},{6,14},{8,0},{10,2},{12,4},{14,6},{1,9},{3,11}... | collective-permute-start | bytes 245768 | tf_op jit(solution)/shard_map/ppermute | solution.py:394
  83.8 20.1 %collective-permute-start.23 = (bf16[64,640]{1,0:T(8,128)(2,1)S(1)}, bf16[64,640]{1,0:T(8,128)(2,1)S(1)}, u32[]{:S(2)}, u32[]{:S(2)}) collective-permute-start(bf16[64,640]{1,0:T(8,128)(2,1)S(1)} %get-tuple-element.122), channel_id=1, source_target_pairs={{0,12},{2,14},{4,8},{6,10},{8,4},{10,6},{12,0},{14,2},{1,13},{3,15... | collective-permute-start | bytes 245768 | tf_op jit(solution)/shard_map/ppermute | solution.py:394
  86.0 18.0 %collective-permute-start.22 = (bf16[64,640]{1,0:T(8,128)(2,1)S(1)}, bf16[64,640]{1,0:T(8,128)(2,1)S(1)}, u32[]{:S(2)}, u32[]{:S(2)}) collective-permute-start(bf16[64,640]{1,0:T(8,128)(2,1)S(1)} %get-tuple-element.120), channel_id=1, source_target_pairs={{0,10},{2,8},{4,14},{6,12},{8,2},{10,0},{12,6},{14,4},{1,11},{3,9}... | collective-permute-start | bytes 245768 | tf_op jit(solution)/shard_map/ppermute | solution.py:394
  86.6 17.4 %collective-permute-start.24 = (bf16[64,640]{1,0:T(8,128)(2,1)S(1)}, bf16[64,640]{1,0:T(8,128)(2,1)S(1)}, u32[]{:S(2)}, u32[]{:S(2)}) collective-permute-start(bf16[64,640]{1,0:T(8,128)(2,1)S(1)} %get-tuple-element.124), channel_id=1, source_target_pairs={{0,14},{2,12},{4,10},{6,8},{8,6},{10,4},{12,2},{14,0},{1,15},{3,13... | collective-permute-start | bytes 245768 | tf_op jit(solution)/shard_map/ppermute | solution.py:394
  87.7 9.6 %collective-permute-start.12 = (bf16[72,512]{1,0:T(8,128)(2,1)S(1)}, bf16[72,512]{1,0:T(8,128)(2,1)S(1)}, u32[]{:S(2)}, u32[]{:S(2)}) collective-permute-start(bf16[72,512]{1,0:T(8,128)(2,1)S(1)} %get-tuple-element.100.over_ref), channel_id=1, source_target_pairs={{0,2},{2,4},{4,6},{6,8},{8,10},{10,12},{12,14},{1,3},{3,5},{5,7},{... | collective-permute-start | bytes 221192 | tf_op jit(solution)/shard_map/ppermute | solution.py:389
  103.9 6.7 %copy-start.3 = (bf16[512,256]{1,0:T(8,128)(2,1)S(1)}, bf16[512,256]{1,0:T(8,128)(2,1)}, u32[]{:S(2)}) copy-start(bf16[512,256]{1,0:T(8,128)(2,1)} %k_ref.1) | copy-start | bytes 786436
  103.9 6.7 %copy-start.4 = (bf16[512,256]{1,0:T(8,128)(2,1)S(1)}, bf16[512,256]{1,0:T(8,128)(2,1)}, u32[]{:S(2)}) copy-start(bf16[512,256]{1,0:T(8,128)(2,1)} %v_ref.1) | copy-start | bytes 786436
  103.9 6.7 %copy-start.6 = (s32[512]{0:T(512)S(1)}, s32[512]{0:T(512)}, u32[]{:S(2)}) copy-start(s32[512]{0:T(512)} %dest_ref.1) | copy-start | bytes 6148
  103.9 6.7 %copy-start.8 = (s32[512]{0:T(512)S(1)}, s32[512]{0:T(512)}, u32[]{:S(2)}) copy-start(s32[512]{0:T(512)} %slot_ref.1) | copy-start | bytes 6148

commit v4 on v2

v4 whole, which is shorter than its diff:
```python
import functools
import math

import jax
import jax.numpy as jnp
from jax import lax
from jax.experimental import pallas as pl
from jax.experimental.pallas import tpu as pltpu
from jax.sharding import PartitionSpec as P

HEAD_SIZE = 128
META = 8
RADIX = 32
NO_DEST = 255.0
NEG = -1e30

VM = pl.BlockSpec(memory_space=pltpu.VMEM)
SM = pl.BlockSpec(memory_space=pltpu.SMEM)
HB = pl.BlockSpec(memory_space=pl.ANY)


def light():
    return pl.CostEstimate(flops=0, bytes_accessed=0, transcendentals=0)


def params(mebibytes=56):
    return pltpu.CompilerParams(vmem_limit_bytes=mebibytes * 1024 * 1024)


def iota(shape, axis):
    return lax.broadcasted_iota(jnp.int32, shape, axis)


def matmul(a, b):
    return jnp.dot(a, b, preferred_element_type=jnp.float32)


def matmul_nt(a, b):
    return lax.dot_general(a, b, (((1,), (1,)), ((), ())), preferred_element_type=jnp.float32)


def select_rows(index, start, rows, dtype=jnp.bfloat16):
    return (iota((rows, index.shape[1]), 0) + start == index).astype(dtype)


def pack_kv_kernel(shards, unit, dest_ref, slot_ref, k_ref, v_ref, q_ref, blocks, over, index_ref):
    count, kv = k_ref.shape
    dest = dest_ref[...].reshape(1, count)
    code = slot_ref[...].reshape(1, count) + 1
    onehot = (iota((shards, count), 0) == dest).astype(jnp.bfloat16)
    earlier = (iota((count, count), 0) < iota((count, count), 1)).astype(jnp.bfloat16)
    before = matmul(onehot, earlier)
    position = jnp.sum(before * onehot.astype(jnp.float32), axis=0, keepdims=True).astype(jnp.int32)
    base = position < unit
    index = jnp.where(base, dest * unit + position, -1)
    index_ref[...] = index
    over_index = jnp.where(base, -1, position - unit)
    totals = matmul_nt(jnp.ones((META, count), jnp.bfloat16), onehot)
    flags = jnp.where(iota((META, shards), 0) == 2, (totals > unit + 0.5).astype(jnp.float32), 0.0)
    over_dest = jnp.max(jnp.where(base, -1, dest))
    over_value = jnp.where(over_dest < 0, NO_DEST, over_dest.astype(jnp.float32))

    row = iota((META, count), 0)
    codes = jnp.where(row == 0, code // RADIX, jnp.where(row == 1, code % RADIX, 0))
    codes = codes.astype(jnp.float32).astype(jnp.bfloat16)

    picked = select_rows(index, 0, count)
    k_rows = matmul(picked, k_ref[...]).astype(jnp.bfloat16)
    v_rows = matmul(picked, v_ref[...]).astype(jnp.bfloat16)
    sent = matmul_nt(codes, picked)
    step = unit + META
    for d in range(shards):
        rows = slice(d * unit, (d + 1) * unit)
        blocks[d * step : d * step + unit, 0:kv] = k_rows[rows]
        blocks[d * step : d * step + unit, kv : 2 * kv] = v_rows[rows]
        meta = jnp.concatenate(
            [sent[:, rows], flags, jnp.zeros((META, 2 * kv - unit - shards), jnp.float32)], axis=1
        )
        blocks[d * step + unit : (d + 1) * step, :] = meta.astype(jnp.bfloat16)
    picked = select_rows(over_index, 0, unit)
    width = q_ref.shape[1]
    over[0:unit, 0:width] = matmul(picked, q_ref[...]).astype(jnp.bfloat16)
    over[0:unit, width : width + kv] = matmul(picked, k_ref[...]).astype(jnp.bfloat16)
    over[0:unit, width + kv : width + 2 * kv] = matmul(picked, v_ref[...]).astype(jnp.bfloat16)
    full = width + 2 * kv
    sent = matmul_nt(codes, picked)
    meta = jnp.concatenate([sent, jnp.zeros((META, full - unit), jnp.float32)], axis=1)
    meta = jnp.where(iota((META, full), 0) == 2, over_value, meta)
    over[unit : unit + META, :] = meta.astype(jnp.bfloat16)


def pack_kv(dest, slot, keys, values, queries, shards, unit):
    width = 2 * keys.shape[1]
    full = width + queries.shape[1]
    shapes = [
        jax.ShapeDtypeStruct((shards * (unit + META), width), jnp.bfloat16),
        jax.ShapeDtypeStruct((unit + META, full), jnp.bfloat16),
        jax.ShapeDtypeStruct((1, keys.shape[0]), jnp.int32),
    ]
    return pl.pallas_call(
        functools.partial(pack_kv_kernel, shards, unit),
        out_shape=shapes,
        in_specs=[VM] * 5,
        out_specs=[VM] * 3,
        compiler_params=params(16),
        cost_estimate=light(),
        name="pack_kv",
    )(dest, slot, keys, values, queries)


def pack_q_kernel(index_ref, q_ref, out_ref):
    picked = select_rows(index_ref[...], 0, q_ref.shape[0])
    out_ref[...] = matmul(picked, q_ref[...]).astype(jnp.bfloat16)


def pack_q(index, queries):
    return pl.pallas_call(
        pack_q_kernel,
        out_shape=jax.ShapeDtypeStruct(queries.shape, jnp.bfloat16),
        in_specs=[VM, VM],
        out_specs=VM,
        compiler_params=params(12),
        cost_estimate=light(),
        name="pack_q",
    )(index, queries)


def pick_over_kernel(unit, me_ref, a_ref, b_ref, c_ref, d_ref, keep_ref, send_ref):
    me = me_ref[0].astype(jnp.float32)
    other = (me_ref[0] ^ 1).astype(jnp.float32)
    keep = jnp.zeros(keep_ref.shape, jnp.float32)
    send = jnp.zeros(keep_ref.shape, jnp.float32)
    for ref in (a_ref, b_ref, c_ref, d_ref):
        block = ref[...].astype(jnp.float32)
        target = block[unit + 2 : unit + 3, :]
        keep = jnp.where(target == me, block, keep)
        send = jnp.where(target == other, block, send)
    keep_ref[...] = keep.astype(jnp.bfloat16)
    send_ref[...] = send.astype(jnp.bfloat16)


def pick_over(me, held, unit):
    return pl.pallas_call(
        functools.partial(pick_over_kernel, unit),
        out_shape=[jax.ShapeDtypeStruct(held[0].shape, jnp.bfloat16)] * 2,
        in_specs=[SM] + [VM] * 4,
        out_specs=[VM, VM],
        compiler_params=params(8),
        cost_estimate=light(),
        name="pick_over",
    )(me, *held)


def decode(meta, unit):
    meta = meta.astype(jnp.float32)
    return (meta[0:1, 0:unit] * RADIX + meta[1:2, 0:unit]).astype(jnp.int32)


def place_kv_kernel(shards, unit, got_ref, placed_ref, codes_ref, crowd_ref):
    step = unit + META
    count = placed_ref.shape[0]
    metas = [got_ref[s * step + unit : (s + 1) * step, 0:HEAD_SIZE] for s in range(shards)]
    code = jnp.concatenate([decode(meta, unit) for meta in metas], axis=1)
    codes_ref[...] = code
    rows = jnp.concatenate([got_ref[s * step : s * step + unit, :] for s in range(shards)], axis=0)
    placed_ref[...] = matmul(select_rows(code, 1, count), rows).astype(jnp.bfloat16)
    by_dest = jnp.zeros((1, shards), jnp.float32)
    most = jnp.zeros((1, 1), jnp.float32)
    for meta in metas:
        flags = meta[2:3, unit : unit + shards].astype(jnp.float32)
        by_dest += flags
        most = jnp.maximum(most, jnp.sum(flags, axis=1, keepdims=True))
    most = jnp.maximum(most, jnp.max(by_dest, axis=1, keepdims=True))
    crowd_ref[...] = jnp.broadcast_to((most > 1.5).astype(jnp.int32), crowd_ref.shape)


def place_kv(got, shards, unit):
    count = shards * unit
    return pl.pallas_call(
        functools.partial(place_kv_kernel, shards, unit),
        out_shape=[
            jax.ShapeDtypeStruct((count, got.shape[1]), jnp.bfloat16),
            jax.ShapeDtypeStruct((1, count), jnp.int32),
            jax.ShapeDtypeStruct((8, 128), jnp.int32),
        ],
        in_specs=[VM],
        out_specs=[VM, VM, VM],
        compiler_params=params(10),
        cost_estimate=light(),
        name="place_kv",
    )(got)


def merge_over_kernel(a_ref, b_ref, q_ref, kv_ref):
    rows, width = q_ref.shape
    q_ref[...] = a_ref[0:rows, 0:width] + b_ref[0:rows, 0:width]
    kv_ref[...] = a_ref[:, width:] + b_ref[:, width:]
    kv_ref[rows:, 0:HEAD_SIZE] = a_ref[rows:, 0:HEAD_SIZE] + b_ref[rows:, 0:HEAD_SIZE]


def merge_over(kept, got, unit, kv_width):
    width = kept.shape[1] - kv_width
    return pl.pallas_call(
        merge_over_kernel,
        out_shape=[
            jax.ShapeDtypeStruct((unit, width), jnp.bfloat16),
            jax.ShapeDtypeStruct((unit + META, kv_width), jnp.bfloat16),
        ],
        in_specs=[VM, VM],
        out_specs=[VM, VM],
        compiler_params=params(4),
        cost_estimate=light(),
        name="merge_over",
    )(kept, got)


def attend_core(shard, anc_ref, q_pl, kv_all, out_ref, groups):
    count, width = out_ref.shape
    block_count = anc_ref.shape[0]
    size = count // block_count
    ratio = width // groups // HEAD_SIZE
    window = (block_count + 1) * size
    scale = math.log2(math.e) / math.sqrt(HEAD_SIZE)
    lane = iota((size, window), 1)
    for b in range(block_count):
        first = (shard - 1) * block_count + b
        key_block = lane // size + first
        seen = lane < 0
        for a in range(anc_ref.shape[1]):
            seen = seen | (key_block == anc_ref[b, a])
        own = lane >= block_count * size
        causal = lane - block_count * size <= iota((size, window), 0)
        seen = (seen & (lane < block_count * size)) | (own & causal)
        bias = jnp.where(seen, 0.0, NEG)
        for g in range(groups):
            columns = [(g * ratio + h) * HEAD_SIZE for h in range(ratio)]
            q = jnp.concatenate(
                [q_pl[b * size : (b + 1) * size, c : c + HEAD_SIZE] for c in columns], axis=0
            )
            k = kv_all[b * size : b * size + window, g * HEAD_SIZE : (g + 1) * HEAD_SIZE]
            v = kv_all[
                b * size : b * size + window,
                (groups + g) * HEAD_SIZE : (groups + g + 1) * HEAD_SIZE,
            ]
            scores = (matmul_nt(q, k) * scale).reshape(ratio, size, window) + bias[None]
            scores = scores.reshape(ratio * size, window)
            peak = jnp.max(scores, axis=1, keepdims=True)
            expo = jnp.exp2(scores - peak)
            total = jnp.sum(expo, axis=1, keepdims=True)
            weights = (expo * (1.0 / total)).astype(jnp.bfloat16)
            output = matmul(weights, v).astype(jnp.bfloat16)
            for h, c in enumerate(columns):
                out_ref[b * size : (b + 1) * size, c : c + HEAD_SIZE] = output[h * size : (h + 1) * size]


def attend_kernel(unit, groups, me_ref, anc_ref, code_ref, over_ref, behind_ref, *refs):
    base, over_q, own_kv, prior_kv, out_ref, raw, q_pl, kv_all, sems = refs
    count, width = out_ref.shape
    copies = [
        pltpu.make_async_copy(base, raw.at[pl.ds(0, count), :], sems.at[0]),
        pltpu.make_async_copy(over_q, raw.at[pl.ds(count, unit), :], sems.at[1]),
        pltpu.make_async_copy(prior_kv, kv_all.at[pl.ds(0, count), :], sems.at[2]),
        pltpu.make_async_copy(own_kv, kv_all.at[pl.ds(count, count), :], sems.at[3]),
    ]
    for c in copies:
        c.start()
    own_over = decode(over_ref[unit : unit + META, :], unit)
    behind_over = decode(behind_ref[unit : unit + META, :], unit)
    onehot = select_rows(jnp.concatenate([code_ref[...], own_over], axis=1), 1, count)
    for c in copies:
        c.wait()
    q_pl[...] = matmul(onehot, raw[...]).astype(jnp.bfloat16)
    for j, (code, ref) in enumerate(((behind_over, behind_ref), (own_over, over_ref))):
        rows = matmul(select_rows(code, 1, count), ref[0:unit, :]).astype(jnp.bfloat16)
        kv_all[j * count : (j + 1) * count, :] += rows
    attend_core(me_ref[0], anc_ref, q_pl, kv_all, out_ref, groups)


def attend(me, ancestors, codes, over_kv, behind_kv, base, over_q, own_kv, prior_kv, unit):
    count, width = base.shape
    groups = own_kv.shape[1] // (2 * HEAD_SIZE)
    return pl.pallas_call(
        functools.partial(attend_kernel, unit, groups),
        out_shape=jax.ShapeDtypeStruct((count, width), jnp.bfloat16),
        in_specs=[SM, SM, VM, VM, VM] + [HB] * 4,
        out_specs=VM,
        scratch_shapes=[
            pltpu.VMEM((count + unit, width), jnp.bfloat16),
            pltpu.VMEM((count, width), jnp.bfloat16),
            pltpu.VMEM((2 * count, own_kv.shape[1]), jnp.bfloat16),
            pltpu.SemaphoreType.DMA((4,)),
        ],
        compiler_params=params(28),
        cost_estimate=light(),
        name="attend",
    )(me, ancestors, codes, over_kv, behind_kv, base, over_q, own_kv, prior_kv)


def attend_padded_kernel(me_ref, anc_ref, code_ref, raw_ref, own_kv, prior_kv, out_ref, q_pl, kv_all):
    count = out_ref.shape[0]
    kv_all[0:count, :] = prior_kv[...]
    kv_all[count : 2 * count, :] = own_kv[...]
    q_pl[...] = matmul(select_rows(code_ref[...], 1, count), raw_ref[...]).astype(jnp.bfloat16)
    attend_core(me_ref[0], anc_ref, q_pl, kv_all, out_ref, kv_all.shape[1] // (2 * HEAD_SIZE))


def attend_padded(me, ancestors, codes, raw, own_kv, prior_kv):
    count, width = own_kv.shape[0], raw.shape[1]
    return pl.pallas_call(
        attend_padded_kernel,
        out_shape=jax.ShapeDtypeStruct((count, width), jnp.bfloat16),
        in_specs=[SM, SM] + [VM] * 4,
        out_specs=VM,
        scratch_shapes=[
            pltpu.VMEM((count, width), jnp.bfloat16),
            pltpu.VMEM((2 * count, own_kv.shape[1]), jnp.bfloat16),
        ],
        compiler_params=params(),
        name="attend_padded",
    )(me, ancestors, codes, raw, own_kv, prior_kv)


def positions(dest_shard, shards):
    onehot = (dest_shard[:, None] == jnp.arange(shards, dtype=jnp.int32)[None, :]).astype(jnp.int32)
    before = jnp.cumsum(onehot, axis=0) - onehot
    return jnp.sum(before * onehot, axis=1)


def exchange(source, index, total):
    buffer = jnp.zeros((total,) + source.shape[1:], source.dtype).at[index].set(source, mode="drop")
    return lax.all_to_all(buffer, "seq", split_axis=0, concat_axis=0, tiled=True)


def from_behind(block):
    n = lax.axis_size("seq")
    return lax.ppermute(block, "seq", [(i, i + 1) for i in range(n - 1)])


def swap(block, r):
    n = lax.axis_size("seq")
    return lax.ppermute(block, "seq", [(i, i ^ r) for i in range(n)])


def padded_plan(me, queries, keys, values, dest_shard, dest_slot, ancestors):
    count = queries.shape[0]
    shards = lax.axis_size("seq")
    capacity = 2 * count // shards
    total = shards * capacity
    index = dest_shard * capacity + positions(dest_shard, shards)
    kv = exchange(jnp.concatenate([keys, values], axis=1), index, total)
    raw = exchange(queries, index, total)
    code = exchange(dest_slot + 1, index, total)
    slots = jnp.where(code > 0, code - 1, count)
    own_kv = jnp.zeros((count, kv.shape[1]), kv.dtype).at[slots].set(kv, mode="drop")
    prior_kv = from_behind(own_kv)
    return attend_padded(me, ancestors, code.reshape(1, total), raw, own_kv, prior_kv)


def after(block, *done):
    return lax.optimization_barrier((block, *done))[0]


def all_to_all(blocks):
    return lax.all_to_all(blocks, "seq", split_axis=0, concat_axis=0, tiled=True)


def swap_plan(me, queries, keys, values, dest_shard, dest_slot, ancestors):
    count = queries.shape[0]
    shards = lax.axis_size("seq")
    unit = count // shards
    kv_blocks, over, index = pack_kv(dest_shard, dest_slot, keys, values, queries, shards, unit)
    got_kv = all_to_all(kv_blocks)
    first = swap(over, 4)
    own_kv, codes, crowd = place_kv(got_kv, shards, unit)
    prior_kv = from_behind(own_kv)
    got_q = all_to_all(after(pack_q(index, queries), own_kv, first))
    second = [swap(over, 2), swap(first, 2)]
    keep, send = pick_over(me, [over, first, *second], unit)
    over_q, over_kv = merge_over(keep, swap(send, 1), unit, own_kv.shape[1])
    behind_kv = from_behind(over_kv)
    result = attend(me, ancestors, codes, over_kv, behind_kv, got_q, over_q, own_kv, prior_kv, unit)
    args = (queries, keys, values, dest_shard, dest_slot, ancestors)
    return lax.cond(crowd[0, 0] > 0, lambda: padded_plan(me, *args), lambda: result)


def local(queries, keys, values, dest_shard, dest_slot, ancestors):
    shards = lax.axis_size("seq")
    me = lax.axis_index("seq").astype(jnp.int32).reshape(1)
    plan = swap_plan if shards == 8 and queries.shape[0] % (16 * shards) == 0 else padded_plan
    return plan(me, queries, keys, values, dest_shard, dest_slot, ancestors)


def solution(mesh):
    rows = P(("groups", "seq"))
    heads = P(("groups", "seq"), "head")
    return jax.shard_map(
        local,
        mesh=mesh,
        in_specs=(heads, heads, heads, rows, rows, P(("groups", "seq"), None)),
        out_specs=heads,
        check_vma=False,
    )
```

time: 110 us -> 109 us (level)
  the two profiles are of different devices: /device:TPU:16 before, /device:TPU:8 now
where the time goes in v4:
time: 109 us
  waiting for transfers between devices  64 us (59%)
  starting transfers between devices  25.6 us (23%)
  Pallas kernels  17.6 us (16%)
    ppermute x4, waiting for transfers between devices, swap(): return lax.ppermute(block, 'seq', [(i, i ^ r) for i in range(n)])  45.2 us
    all_to_all x2, waiting for transfers between devices, all_to_all(): lax.all_to_all(blocks, 'seq', split_axis=0, concat_axis=0, tiled=True)  14.7 us
    all_to_all x2, starting transfers between devices, all_to_all(): lax.all_to_all(blocks, 'seq', split_axis=0, concat_axis=0, tiled=True)  13.5 us
    pallas_call x1, Pallas kernels, attend(): pl.pallas_call(functools.partial(attend_kernel, unit, groups), out_shape=...  10.2 us
    ppermute x4, starting transfers between devices, swap(): return lax.ppermute(block, 'seq', [(i, i ^ r) for i in range(n)])  6.81 us
    ppermute x2, starting transfers between devices, from_behind(): return lax.ppermute(block, 'seq', [(i, i + 1) for i in range(n - 1)])  5.28 us
    ppermute x2, waiting for transfers between devices, from_behind(): return lax.ppermute(block, 'seq', [(i, i + 1) for i in range(n - 1)])  4.04 us
    pallas_call x1, Pallas kernels, pack_kv(): pl.pallas_call(functools.partial(pack_kv_kernel, shards, unit), out_shape...  3.26 us
  transfers between devices with their start and end apart: 8, of which 6 were waited for; matrix products, arithmetic and copies ran while one was open for 0% of the time, Pallas kernels for 4%

profile of v4, /device:TPU:8, one launch (start us, length us, event | category | flops | bytes accessed | tf_op | source)
XLA Modules:
  0.0 109.0 jit_solution(8587770337479917749)
XLA Ops:
  0.0 3.3 %pack_kv.1 = (bf16[576,512]{1,0:T(8,128)(2,1)}, bf16[72,1792]{1,0:T(8,128)(2,1)S(1)}, s32[1,512]{1,0:T(1,128)S(1)}) custom-call(s32[512]{0:T(512)} %dest_ref.1, s32[512]{0:T(512)} %slot_ref.1, bf16[512,256]{1,0:T(8,128)(2,1)} %k_ref.1, bf16[512,256]{1,0:T(8,128)(2,1)} %v_ref.1, bf16[512,1280]{1,0:T(8,128)(2,1)} %q_ref.3), custom_call_target="tpu_custom_call" | custom-call | tf_op jit(solution)/shard_map/pack_kv/pallas_call | solution.py:100
  3.3 6.3 %all-to-all-start.3 = ((bf16[8,72,512]{2,1,0:T(8,128)(2,1)}), bf16[8,72,512]{2,1,0:T(8,128)(2,1)S(1)}, u32[]{:S(2)}, u32[]{:S(2)}) async-start(bf16[8,72,512]{2,1,0:T(8,128)(2,1)} %bitcast.12), calls=%async_computation.3 | async-start | bytes 1179648 | tf_op jit(solution)/shard_map/all_to_all | solution.py:364
  9.5 2.4 %collective-permute-start.1 = (bf16[72,1792]{1,0:T(8,128)(2,1)S(1)}, bf16[72,1792]{1,0:T(8,128)(2,1)S(1)}, u32[]{:S(2)}, u32[]{:S(2)}) collective-permute-start(bf16[72,1792]{1,0:T(8,128)(2,1)S(1)} %get-tuple-element.44.a_ref), channel_id=1, source_target_pairs={{0,8},{2,10},{4,12},{6,14},{8,0},{10,2},{12,4},{14,6},{1,9},{3,11}... | collective-permute-start | bytes 774152 | tf_op jit(solution)/shard_map/ppermute | solution.py:341
  11.9 3.2 %pack_q.1 = bf16[512,1280]{1,0:T(8,128)(2,1)} custom-call(s32[1,512]{1,0:T(1,128)S(1)} %get-tuple-element.48.index_ref, bf16[512,1280]{1,0:T(8,128)(2,1)} %q_ref.3), custom_call_target="tpu_custom_call" | custom-call | tf_op jit(solution)/shard_map/pack_q/pallas_call | solution.py:117
  15.1 14.7 %all-to-all-done.3 = bf16[8,72,512]{2,1,0:T(8,128)(2,1)S(1)} async-done(((bf16[8,72,512]{2,1,0:T(8,128)(2,1)}), bf16[8,72,512]{2,1,0:T(8,128)(2,1)S(1)}, u32[]{:S(2)}, u32[]{:S(2)}) %all-to-all-start.3) | async-done | bytes 589856 | tf_op jit(solution)/shard_map/all_to_all | solution.py:364
  29.8 0.5 place_kv.1
  30.3 2.5 %collective-permute-done.1.b_ref = bf16[72,1792]{1,0:T(8,128)(2,1)S(1)} collective-permute-done((bf16[72,1792]{1,0:T(8,128)(2,1)S(1)}, bf16[72,1792]{1,0:T(8,128)(2,1)S(1)}, u32[]{:S(2)}, u32[]{:S(2)}) %collective-permute-start.1) | collective-permute-done | bytes 258080 | tf_op jit(solution)/shard_map/ppermute | solution.py:341
  32.8 7.3 %all-to-all-start.4 = ((bf16[8,64,1280]{2,1,0:T(8,128)(2,1)}), bf16[8,64,1280]{2,1,0:T(8,128)(2,1)S(1)}, u32[]{:S(2)}, u32[]{:S(2)}) async-start(bf16[8,64,1280]{2,1,0:T(8,128)(2,1)} %bitcast.16), calls=%async_computation.4 | async-start | bytes 2621440 | tf_op jit(solution)/shard_map/all_to_all | solution.py:364
  40.1 0.0 copy-start.7
  40.1 0.1 collective-permute-start.2
  40.2 2.0 %collective-permute-start.3 = (bf16[72,1792]{1,0:T(8,128)(2,1)S(1)}, bf16[72,1792]{1,0:T(8,128)(2,1)S(1)}, u32[]{:S(2)}, u32[]{:S(2)}) collective-permute-start(bf16[72,1792]{1,0:T(8,128)(2,1)S(1)} %collective-permute-done.1.b_ref), channel_id=1, source_target_pairs={{0,4},{2,6},{4,0},{6,2},{8,12},{10,14},{12,8},{14,10},{1,5},{3,7},... | collective-permute-start | bytes 774152 | tf_op jit(solution)/shard_map/ppermute | solution.py:341
  42.1 3.4 %collective-permute-start.6 = (bf16[512,512]{1,0:T(8,128)(2,1)S(1)}, bf16[512,512]{1,0:T(8,128)(2,1)S(1)}, u32[]{:S(2)}, u32[]{:S(2)}) collective-permute-start(bf16[512,512]{1,0:T(8,128)(2,1)S(1)} %get-tuple-element.49.refs_2_), channel_id=1, source_target_pairs={{0,2},{2,4},{4,6},{6,8},{8,10},{10,12},{12,14},{1,3},{3,5},{5,7},{... | collective-permute-start | bytes 1572872 | tf_op jit(solution)/shard_map/ppermute | solution.py:336
  45.5 23.7 %collective-permute-done.2.c_ref = bf16[72,1792]{1,0:T(8,128)(2,1)S(1)} collective-permute-done((bf16[72,1792]{1,0:T(8,128)(2,1)S(1)}, bf16[72,1792]{1,0:T(8,128)(2,1)S(1)}, u32[]{:S(2)}, u32[]{:S(2)}) %collective-permute-start.2) | collective-permute-done | bytes 258080 | tf_op jit(solution)/shard_map/ppermute | solution.py:341
  69.2 4.6 %collective-permute-done.3.d_ref = bf16[72,1792]{1,0:T(8,128)(2,1)S(1)} collective-permute-done((bf16[72,1792]{1,0:T(8,128)(2,1)S(1)}, bf16[72,1792]{1,0:T(8,128)(2,1)S(1)}, u32[]{:S(2)}, u32[]{:S(2)}) %collective-permute-start.3) | collective-permute-done | bytes 258080 | tf_op jit(solution)/shard_map/ppermute | solution.py:341
  73.8 0.5 pick_over.1
  74.3 2.4 %collective-permute-start.4 = (bf16[72,1792]{1,0:T(8,128)(2,1)S(1)}, bf16[72,1792]{1,0:T(8,128)(2,1)S(1)}, u32[]{:S(2)}, u32[]{:S(2)}) collective-permute-start(bf16[72,1792]{1,0:T(8,128)(2,1)S(1)} %get-tuple-element.46), channel_id=1, source_target_pairs={{0,2},{2,0},{4,6},{6,4},{8,10},{10,8},{12,14},{14,12},{1,3},{3,1},... | collective-permute-start | bytes 774152 | tf_op jit(solution)/shard_map/ppermute | solution.py:341
  76.7 14.4 %collective-permute-done.4.b_ref = bf16[72,1792]{1,0:T(8,128)(2,1)S(1)} collective-permute-done((bf16[72,1792]{1,0:T(8,128)(2,1)S(1)}, bf16[72,1792]{1,0:T(8,128)(2,1)S(1)}, u32[]{:S(2)}, u32[]{:S(2)}) %collective-permute-start.4) | collective-permute-done | bytes 258080 | tf_op jit(solution)/shard_map/ppermute | solution.py:341
  91.1 1.9 %collective-permute-start.5 = (bf16[72,512]{1,0:T(8,128)(2,1)S(1)}, bf16[72,512]{1,0:T(8,128)(2,1)S(1)}, u32[]{:S(2)}, u32[]{:S(2)}) collective-permute-start(bf16[72,512]{1,0:T(8,128)(2,1)S(1)} %get-tuple-element.47.over_ref), channel_id=1, source_target_pairs={{0,2},{2,4},{4,6},{6,8},{8,10},{10,12},{12,14},{1,3},{3,5},{5,7},{... | collective-permute-start | bytes 221192 | tf_op jit(solution)/shard_map/ppermute | solution.py:336
  93.1 0.5 slice.9
  94.2 4.0 %collective-permute-done.5.behind_ref = bf16[72,512]{1,0:T(8,128)(2,1)S(1)} collective-permute-done((bf16[72,512]{1,0:T(8,128)(2,1)S(1)}, bf16[72,512]{1,0:T(8,128)(2,1)S(1)}, u32[]{:S(2)}, u32[]{:S(2)}) %collective-permute-start.5) | collective-permute-done | bytes 73760 | tf_op jit(solution)/shard_map/ppermute | solution.py:336
  98.3 0.0 collective-permute-done.6.refs_3_
  98.3 0.0 all-to-all-done.4
  98.3 0.0 copy-done.7
  98.3 0.0 copy-start.3
  98.3 0.0 copy-start.4
  98.3 0.0 copy-start.6
  98.3 0.0 copy-start.8
  98.3 10.2 %attend.1 = bf16[512,1280]{1,0:T(8,128)(2,1)} custom-call(s32[1]{0:T(128)} %bitcast.15.me_ref, s32[4,4]{1,0:T(4,128)S(1)} %copy-done.7, s32[1,512]{1,0:T(1,128)S(1)} %get-tuple-element.43.code_ref, bf16[72,512]{1,0:T(8,128)(2,1)S(1)} %get-tuple-element.47.over_ref, bf16[72,512]{1,0:T(8,128)(2,1)S(1)} %collective-permute-done.5.behind_ref, ...), custom_call_target="tpu_custom_call" | custom-call | tf_op jit(solution)/shard_map/attend/pallas_call | solution.py:282
  108.5 0.0 copy-done.3
  108.5 0.0 copy-done.4
  108.5 0.0 copy-done.6
  108.5 0.0 copy-done.8
  108.5 0.2 conditional.1
  (1 shorter events, 0.0 us)
Async XLA Ops:
  3.3 26.6 %all-to-all-start.3 = ((bf16[8,72,512]{2,1,0:T(8,128)(2,1)}), bf16[8,72,512]{2,1,0:T(8,128)(2,1)S(1)}, u32[]{:S(2)}, u32[]{:S(2)}) async-start(bf16[8,72,512]{2,1,0:T(8,128)(2,1)} %bitcast.12), calls=%async_computation.3 | async-start | bytes 1179648 | tf_op jit(solution)/shard_map/all_to_all | solution.py:364
  9.5 23.3 %collective-permute-start.1 = (bf16[72,1792]{1,0:T(8,128)(2,1)S(1)}, bf16[72,1792]{1,0:T(8,128)(2,1)S(1)}, u32[]{:S(2)}, u32[]{:S(2)}) collective-permute-start(bf16[72,1792]{1,0:T(8,128)(2,1)S(1)} %get-tuple-element.44.a_ref), channel_id=1, source_target_pairs={{0,8},{2,10},{4,12},{6,14},{8,0},{10,2},{12,4},{14,6},{1,9},{3,11}... | collective-permute-start | bytes 774152 | tf_op jit(solution)/shard_map/ppermute | solution.py:341
  32.8 65.5 %all-to-all-start.4 = ((bf16[8,64,1280]{2,1,0:T(8,128)(2,1)}), bf16[8,64,1280]{2,1,0:T(8,128)(2,1)S(1)}, u32[]{:S(2)}, u32[]{:S(2)}) async-start(bf16[8,64,1280]{2,1,0:T(8,128)(2,1)} %bitcast.16), calls=%async_computation.4 | async-start | bytes 2621440 | tf_op jit(solution)/shard_map/all_to_all | solution.py:364
  40.1 58.2 %copy-start.7 = (s32[4,4]{1,0:T(4,128)S(1)}, s32[4,4]{1,0:T(4,128)}, u32[]{:S(2)}) copy-start(s32[4,4]{1,0:T(4,128)} %anc_ref.1) | copy-start | bytes 196
  40.1 29.1 %collective-permute-start.2 = (bf16[72,1792]{1,0:T(8,128)(2,1)S(1)}, bf16[72,1792]{1,0:T(8,128)(2,1)S(1)}, u32[]{:S(2)}, u32[]{:S(2)}) collective-permute-start(bf16[72,1792]{1,0:T(8,128)(2,1)S(1)} %get-tuple-element.44.a_ref), channel_id=1, source_target_pairs={{0,4},{2,6},{4,0},{6,2},{8,12},{10,14},{12,8},{14,10},{1,5},{3,7},... | collective-permute-start | bytes 774152 | tf_op jit(solution)/shard_map/ppermute | solution.py:341
  40.2 33.6 %collective-permute-start.3 = (bf16[72,1792]{1,0:T(8,128)(2,1)S(1)}, bf16[72,1792]{1,0:T(8,128)(2,1)S(1)}, u32[]{:S(2)}, u32[]{:S(2)}) collective-permute-start(bf16[72,1792]{1,0:T(8,128)(2,1)S(1)} %collective-permute-done.1.b_ref), channel_id=1, source_target_pairs={{0,4},{2,6},{4,0},{6,2},{8,12},{10,14},{12,8},{14,10},{1,5},{3,7},... | collective-permute-start | bytes 774152 | tf_op jit(solution)/shard_map/ppermute | solution.py:341
  42.1 56.1 %collective-permute-start.6 = (bf16[512,512]{1,0:T(8,128)(2,1)S(1)}, bf16[512,512]{1,0:T(8,128)(2,1)S(1)}, u32[]{:S(2)}, u32[]{:S(2)}) collective-permute-start(bf16[512,512]{1,0:T(8,128)(2,1)S(1)} %get-tuple-element.49.refs_2_), channel_id=1, source_target_pairs={{0,2},{2,4},{4,6},{6,8},{8,10},{10,12},{12,14},{1,3},{3,5},{5,7},{... | collective-permute-start | bytes 1572872 | tf_op jit(solution)/shard_map/ppermute | solution.py:336
  74.3 16.8 %collective-permute-start.4 = (bf16[72,1792]{1,0:T(8,128)(2,1)S(1)}, bf16[72,1792]{1,0:T(8,128)(2,1)S(1)}, u32[]{:S(2)}, u32[]{:S(2)}) collective-permute-start(bf16[72,1792]{1,0:T(8,128)(2,1)S(1)} %get-tuple-element.46), channel_id=1, source_target_pairs={{0,2},{2,0},{4,6},{6,4},{8,10},{10,8},{12,14},{14,12},{1,3},{3,1},... | collective-permute-start | bytes 774152 | tf_op jit(solution)/shard_map/ppermute | solution.py:341
  91.1 7.1 %collective-permute-start.5 = (bf16[72,512]{1,0:T(8,128)(2,1)S(1)}, bf16[72,512]{1,0:T(8,128)(2,1)S(1)}, u32[]{:S(2)}, u32[]{:S(2)}) collective-permute-start(bf16[72,512]{1,0:T(8,128)(2,1)S(1)} %get-tuple-element.47.over_ref), channel_id=1, source_target_pairs={{0,2},{2,4},{4,6},{6,8},{8,10},{10,12},{12,14},{1,3},{3,5},{5,7},{... | collective-permute-start | bytes 221192 | tf_op jit(solution)/shard_map/ppermute | solution.py:336
  98.3 10.2 %copy-start.3 = (bf16[512,256]{1,0:T(8,128)(2,1)S(1)}, bf16[512,256]{1,0:T(8,128)(2,1)}, u32[]{:S(2)}) copy-start(bf16[512,256]{1,0:T(8,128)(2,1)} %k_ref.1) | copy-start | bytes 786436
  98.3 10.2 %copy-start.4 = (bf16[512,256]{1,0:T(8,128)(2,1)S(1)}, bf16[512,256]{1,0:T(8,128)(2,1)}, u32[]{:S(2)}) copy-start(bf16[512,256]{1,0:T(8,128)(2,1)} %v_ref.1) | copy-start | bytes 786436
  98.3 10.2 %copy-start.6 = (s32[512]{0:T(512)S(1)}, s32[512]{0:T(512)}, u32[]{:S(2)}) copy-start(s32[512]{0:T(512)} %dest_ref.1) | copy-start | bytes 6148
  98.3 10.2 %copy-start.8 = (s32[512]{0:T(512)S(1)}, s32[512]{0:T(512)}, u32[]{:S(2)}) copy-start(s32[512]{0:T(512)} %slot_ref.1) | copy-start | bytes 6148

commit v5 on v4

v5 whole, which is shorter than its diff:
```python
import functools
import math

import jax
import jax.numpy as jnp
from jax import lax
from jax.experimental import pallas as pl
from jax.experimental.pallas import tpu as pltpu
from jax.sharding import PartitionSpec as P

HEAD_SIZE = 128
PIECE = 8
RADIX = 32
NO_DEST = 255.0
NEG = -1e30

VM = pl.BlockSpec(memory_space=pltpu.VMEM)
SM = pl.BlockSpec(memory_space=pltpu.SMEM)
HB = pl.BlockSpec(memory_space=pl.ANY)


def light():
    return pl.CostEstimate(flops=0, bytes_accessed=0, transcendentals=0)


def params(mebibytes=56):
    return pltpu.CompilerParams(vmem_limit_bytes=mebibytes * 1024 * 1024)


def iota(shape, axis):
    return lax.broadcasted_iota(jnp.int32, shape, axis)


def matmul(a, b):
    return jnp.dot(a, b, preferred_element_type=jnp.float32)


def matmul_nt(a, b):
    return lax.dot_general(a, b, (((1,), (1,)), ((), ())), preferred_element_type=jnp.float32)


def select_rows(index, start, rows, dtype=jnp.bfloat16):
    return (iota((rows, index.shape[1]), 0) + start == index).astype(dtype)


def strips(width, kv_width):
    return [(c, min(c + kv_width, width)) for c in range(0, width, kv_width)]


def pack_kv_kernel(shards, unit, me_ref, dest_ref, slot_ref, k_ref, v_ref, q_ref, *outs):
    blocks, index_ref = outs[:shards], outs[shards]
    count, kv = k_ref.shape
    dest = dest_ref[...].reshape(1, count)
    code = slot_ref[...].reshape(1, count) + 1
    onehot = (iota((shards, count), 0) == dest).astype(jnp.bfloat16)
    earlier = (iota((count, count), 0) < iota((count, count), 1)).astype(jnp.bfloat16)
    before = matmul(onehot, earlier)
    position = jnp.sum(before * onehot.astype(jnp.float32), axis=0, keepdims=True).astype(jnp.int32)
    base = position < unit
    index = jnp.where(base, ((dest - me_ref[0]) & (shards - 1)) * unit + position, -1)
    index_ref[...] = index
    over_index = jnp.where(base, -1, position - unit)
    totals = matmul_nt(jnp.ones((PIECE, count), jnp.bfloat16), onehot)
    flags = jnp.where(iota((PIECE, shards), 0) == 2, (totals > unit + 0.5).astype(jnp.float32), 0.0)
    flags = jnp.concatenate([flags, jnp.zeros((PIECE, unit - shards), jnp.float32)], axis=1)
    over_dest = jnp.max(jnp.where(base, -1, dest))
    over_value = jnp.where(over_dest < 0, NO_DEST, over_dest.astype(jnp.float32))

    row = iota((PIECE, count), 0)
    codes = jnp.where(row == 0, code // RADIX, jnp.where(row == 1, code % RADIX, 0))
    codes = codes.astype(jnp.float32).astype(jnp.bfloat16)

    picked = select_rows(index, 0, count)
    k_rows = matmul(picked, k_ref[...]).astype(jnp.bfloat16)
    v_rows = matmul(picked, v_ref[...]).astype(jnp.bfloat16)
    sent = matmul_nt(codes, picked)
    picked = select_rows(over_index, 0, unit)
    over_k = matmul(picked, k_ref[...])
    over_v = matmul(picked, v_ref[...])
    over_q = matmul(picked, q_ref[...])
    over_sent = matmul_nt(codes, picked)
    over_sent = jnp.where(iota((PIECE, unit), 0) == 2, over_value, over_sent)
    empty = jnp.zeros((PIECE, unit), jnp.float32)
    for r in range(shards):
        rows = slice(r * unit, (r + 1) * unit)
        blocks[r][0:unit, 0:kv] = k_rows[rows]
        blocks[r][0:unit, kv : 2 * kv] = v_rows[rows]
        piece = slice(r * PIECE, (r + 1) * PIECE)
        meta = jnp.concatenate([sent[:, rows], flags, over_sent, empty], axis=1)
        tail = [jnp.concatenate([over_k[piece], over_v[piece]], axis=1)]
        for start, stop in strips(over_q.shape[1], 2 * kv):
            tail.append(over_q[piece, start:stop])
        tail[-1] = jnp.concatenate([tail[-1], meta], axis=1)
        blocks[r][unit:, :] = jnp.concatenate(tail, axis=0).astype(jnp.bfloat16)


def pack_kv(me, dest, slot, keys, values, queries, shards, unit):
    kv_width = 2 * keys.shape[1]
    rows = unit + PIECE * (1 + len(strips(queries.shape[1], kv_width)))
    shapes = [jax.ShapeDtypeStruct((rows, kv_width), jnp.bfloat16)] * shards
    shapes += [jax.ShapeDtypeStruct((1, keys.shape[0]), jnp.int32)]
    outs = pl.pallas_call(
        functools.partial(pack_kv_kernel, shards, unit),
        out_shape=shapes,
        in_specs=[SM] + [VM] * 5,
        out_specs=[VM] * len(shapes),
        compiler_params=params(16),
        cost_estimate=light(),
        name="pack_kv",
    )(me, dest, slot, keys, values, queries)
    return outs[:shards], outs[shards]


def pack_q_kernel(unit, index_ref, q_ref, *blocks):
    for r, block in enumerate(blocks):
        picked = select_rows(index_ref[...], r * unit, unit)
        block[0:unit, :] = matmul(picked, q_ref[...]).astype(jnp.bfloat16)


def pack_q(index, queries, shards, unit):
    return pl.pallas_call(
        functools.partial(pack_q_kernel, unit),
        out_shape=[jax.ShapeDtypeStruct((unit + 2 * PIECE, queries.shape[1]), jnp.bfloat16)] * shards,
        in_specs=[VM, VM],
        out_specs=[VM] * shards,
        compiler_params=params(12),
        cost_estimate=light(),
        name="pack_q",
    )(index, queries)


def by_lane(parts, row):
    lane = iota((1, parts[0].shape[1]), 1) // PIECE
    total = jnp.zeros(lane.shape, jnp.float32)
    for r, part in enumerate(parts):
        total += jnp.where(lane == r, part[row : row + 1, :], 0.0)
    return total


def decode(high, low):
    return (high * RADIX + low).astype(jnp.int32)


def relay_kernel(shards, unit, me_ref, *refs):
    got = refs[:shards]
    placed_ref, codes_ref, crowd_ref = refs[2 * shards : 2 * shards + 3]
    blocks = refs[2 * shards + 3 : 3 * shards + 3]
    tails, sems = refs[3 * shards + 3 :]
    count, kv_width = placed_ref.shape
    width = tails.shape[2]
    cuts = strips(width, kv_width)
    meta_at = cuts[-1][1] - cuts[-1][0]
    ends = [ref[unit:, :].astype(jnp.float32) for ref in got]
    metas = [end[-PIECE:, meta_at:] for end in ends]

    over = [meta[:, 2 * unit : 3 * unit] for meta in metas]
    dest = by_lane(over, 2).astype(jnp.int32)
    part = iota(dest.shape, 1) % PIECE
    to = jnp.where(dest < shards, ((dest - me_ref[0]) & (shards - 1)) * PIECE + part, -1)
    behind = jnp.where(dest < shards - 1, ((dest + 1 - me_ref[0]) & (shards - 1)) * PIECE + part, -1)
    to, behind = select_rows(to, 0, shards * PIECE), select_rows(behind, 0, shards * PIECE)
    over_kv = jnp.concatenate([end[0:PIECE] for end in ends], axis=0).astype(jnp.bfloat16)
    row = iota((PIECE, unit), 0)
    codes = jnp.where(row == 0, by_lane(over, 0), jnp.where(row == 1, by_lane(over, 1), 0.0)).astype(jnp.bfloat16)
    meta = jnp.concatenate([matmul_nt(codes, to), matmul_nt(codes, behind)], axis=1)
    meta = jnp.concatenate([meta, jnp.zeros((PIECE, width - 2 * kv_width - 2 * unit), jnp.float32)], axis=1)
    to_kv, behind_kv = matmul(to, over_kv), matmul(behind, over_kv)
    to_q = []
    for i, (start, stop) in enumerate(cuts):
        strip = [end[(i + 1) * PIECE : (i + 2) * PIECE, 0 : stop - start] for end in ends]
        to_q.append(matmul(to, jnp.concatenate(strip, axis=0).astype(jnp.bfloat16)))
    to_q = jnp.concatenate(to_q, axis=1)
    copies = []
    for r in range(shards):
        piece = slice(r * PIECE, (r + 1) * PIECE)
        lower = jnp.concatenate([to_kv[piece], behind_kv[piece], meta], axis=1)
        tails[r] = jnp.concatenate([to_q[piece], lower], axis=0).astype(jnp.bfloat16)
        copies.append(pltpu.make_async_copy(tails.at[r], blocks[r].at[pl.ds(unit, 2 * PIECE), :], sems.at[r]))
        copies[-1].start()

    code = jnp.concatenate([decode(meta[0:1, 0:unit], meta[1:2, 0:unit]) for meta in metas], axis=1)
    codes_ref[...] = code
    rows = jnp.concatenate([ref[0:unit, :] for ref in got], axis=0)
    placed_ref[...] = matmul(select_rows(code, 1, count), rows).astype(jnp.bfloat16)
    by_dest = jnp.zeros((1, unit), jnp.float32)
    most = jnp.zeros((1, 1), jnp.float32)
    for meta in metas:
        flags = meta[2:3, unit : 2 * unit]
        by_dest += flags
        most = jnp.maximum(most, jnp.sum(flags, axis=1, keepdims=True))
    most = jnp.maximum(most, jnp.max(by_dest, axis=1, keepdims=True))
    crowd_ref[...] = jnp.broadcast_to((most > 1.5).astype(jnp.int32), crowd_ref.shape)
    for c in copies:
        c.wait()


def relay(me, got, q_blocks, unit):
    shards = len(got)
    count = shards * unit
    shape = q_blocks[0].shape
    outs = pl.pallas_call(
        functools.partial(relay_kernel, shards, unit),
        out_shape=[
            jax.ShapeDtypeStruct((count, got[0].shape[1]), jnp.bfloat16),
            jax.ShapeDtypeStruct((1, count), jnp.int32),
            jax.ShapeDtypeStruct((8, 128), jnp.int32),
        ]
        + [jax.ShapeDtypeStruct(shape, jnp.bfloat16)] * shards,
        in_specs=[SM] + [VM] * shards + [HB] * shards,
        out_specs=[VM] * 3 + [HB] * shards,
        scratch_shapes=[
            pltpu.VMEM((shards, 2 * PIECE, shape[1]), jnp.bfloat16),
            pltpu.SemaphoreType.DMA((shards,)),
        ],
        input_output_aliases={1 + shards + r: 3 + r for r in range(shards)},
        compiler_params=params(10),
        cost_estimate=light(),
        name="relay",
    )(me, *got, *q_blocks)
    return outs[0], outs[1], outs[2], outs[3:]


def attend_core(shard, anc_ref, q_pl, kv_all, out_ref, groups):
    count, width = out_ref.shape
    block_count = anc_ref.shape[0]
    size = count // block_count
    ratio = width // groups // HEAD_SIZE
    window = (block_count + 1) * size
    scale = math.log2(math.e) / math.sqrt(HEAD_SIZE)
    lane = iota((size, window), 1)
    for b in range(block_count):
        first = (shard - 1) * block_count + b
        key_block = lane // size + first
        seen = lane < 0
        for a in range(anc_ref.shape[1]):
            seen = seen | (key_block == anc_ref[b, a])
        own = lane >= block_count * size
        causal = lane - block_count * size <= iota((size, window), 0)
        seen = (seen & (lane < block_count * size)) | (own & causal)
        bias = jnp.where(seen, 0.0, NEG)
        for g in range(groups):
            columns = [(g * ratio + h) * HEAD_SIZE for h in range(ratio)]
            q = jnp.concatenate(
                [q_pl[b * size : (b + 1) * size, c : c + HEAD_SIZE] for c in columns], axis=0
            )
            k = kv_all[b * size : b * size + window, g * HEAD_SIZE : (g + 1) * HEAD_SIZE]
            v = kv_all[
                b * size : b * size + window,
                (groups + g) * HEAD_SIZE : (groups + g + 1) * HEAD_SIZE,
            ]
            scores = (matmul_nt(q, k) * scale).reshape(ratio, size, window) + bias[None]
            scores = scores.reshape(ratio * size, window)
            peak = jnp.max(scores, axis=1, keepdims=True)
            expo = jnp.exp2(scores - peak)
            total = jnp.sum(expo, axis=1, keepdims=True)
            weights = (expo * (1.0 / total)).astype(jnp.bfloat16)
            output = matmul(weights, v).astype(jnp.bfloat16)
            for h, c in enumerate(columns):
                out_ref[b * size : (b + 1) * size, c : c + HEAD_SIZE] = output[h * size : (h + 1) * size]


def attend_kernel(shards, unit, groups, me_ref, anc_ref, code_ref, *refs):
    got, own_kv, prior_kv = refs[:shards], *refs[shards : shards + 2]
    out_ref, raw, tails, q_pl, kv_all, sems = refs[shards + 2 :]
    count, width = out_ref.shape
    kv_width = own_kv.shape[1]
    copies = []

    def fetch(source, target):
        copies.append(pltpu.make_async_copy(source, target, sems.at[len(copies)]))
        copies[-1].start()

    for r, ref in enumerate(got):
        fetch(ref.at[pl.ds(unit, 2 * PIECE), :], tails.at[r])
        fetch(ref.at[pl.ds(0, unit), :], raw.at[pl.ds(r * unit, unit), :])
    fetch(prior_kv, kv_all.at[pl.ds(0, count), :])
    fetch(own_kv, kv_all.at[pl.ds(count, count), :])
    for c in copies:
        c.wait()
    ends = [tails[r].astype(jnp.float32) for r in range(shards)]
    metas = [end[PIECE:, 2 * kv_width :] for end in ends]
    own = [meta[:, 0:unit] for meta in metas]
    behind = [meta[:, unit : 2 * unit] for meta in metas]
    own = decode(by_lane(own, 0), by_lane(own, 1))
    behind = decode(by_lane(behind, 0), by_lane(behind, 1))
    raw[count:, :] = jnp.concatenate([end[0:PIECE] for end in ends], axis=0).astype(jnp.bfloat16)
    onehot = select_rows(jnp.concatenate([code_ref[...], own], axis=1), 1, count)
    q_pl[...] = matmul(onehot, raw[...]).astype(jnp.bfloat16)
    for j, (code, start) in enumerate(((behind, kv_width), (own, 0))):
        rows = jnp.concatenate([end[PIECE:, start : start + kv_width] for end in ends], axis=0)
        rows = matmul(select_rows(code, 1, count), rows.astype(jnp.bfloat16))
        kv_all[j * count : (j + 1) * count, :] += rows.astype(jnp.bfloat16)
    attend_core(me_ref[0], anc_ref, q_pl, kv_all, out_ref, groups)


def attend(me, ancestors, codes, got, own_kv, prior_kv, unit):
    shards = len(got)
    count, width = shards * unit, got[0].shape[1]
    groups = own_kv.shape[1] // (2 * HEAD_SIZE)
    return pl.pallas_call(
        functools.partial(attend_kernel, shards, unit, groups),
        out_shape=jax.ShapeDtypeStruct((count, width), jnp.bfloat16),
        in_specs=[SM, SM, VM] + [HB] * (shards + 2),
        out_specs=VM,
        scratch_shapes=[
            pltpu.VMEM((count + shards * PIECE, width), jnp.bfloat16),
            pltpu.VMEM((shards, 2 * PIECE, width), jnp.bfloat16),
            pltpu.VMEM((count, width), jnp.bfloat16),
            pltpu.VMEM((2 * count, own_kv.shape[1]), jnp.bfloat16),
            pltpu.SemaphoreType.DMA((2 * shards + 2,)),
        ],
        compiler_params=params(28),
        cost_estimate=light(),
        name="attend",
    )(me, ancestors, codes, *got, own_kv, prior_kv)


def attend_padded_kernel(me_ref, anc_ref, code_ref, raw_ref, own_kv, prior_kv, out_ref, q_pl, kv_all):
    count = out_ref.shape[0]
    kv_all[0:count, :] = prior_kv[...]
    kv_all[count : 2 * count, :] = own_kv[...]
    q_pl[...] = matmul(select_rows(code_ref[...], 1, count), raw_ref[...]).astype(jnp.bfloat16)
    attend_core(me_ref[0], anc_ref, q_pl, kv_all, out_ref, kv_all.shape[1] // (2 * HEAD_SIZE))


def attend_padded(me, ancestors, codes, raw, own_kv, prior_kv):
    count, width = own_kv.shape[0], raw.shape[1]
    return pl.pallas_call(
        attend_padded_kernel,
        out_shape=jax.ShapeDtypeStruct((count, width), jnp.bfloat16),
        in_specs=[SM, SM] + [VM] * 4,
        out_specs=VM,
        scratch_shapes=[
            pltpu.VMEM((count, width), jnp.bfloat16),
            pltpu.VMEM((2 * count, own_kv.shape[1]), jnp.bfloat16),
        ],
        compiler_params=params(),
        name="attend_padded",
    )(me, ancestors, codes, raw, own_kv, prior_kv)


def positions(dest_shard, shards):
    onehot = (dest_shard[:, None] == jnp.arange(shards, dtype=jnp.int32)[None, :]).astype(jnp.int32)
    before = jnp.cumsum(onehot, axis=0) - onehot
    return jnp.sum(before * onehot, axis=1)


def exchange(source, index, total):
    buffer = jnp.zeros((total,) + source.shape[1:], source.dtype).at[index].set(source, mode="drop")
    return lax.all_to_all(buffer, "seq", split_axis=0, concat_axis=0, tiled=True)


def from_behind(block):
    n = lax.axis_size("seq")
    return lax.ppermute(block, "seq", [(i, i + 1) for i in range(n - 1)])


def rotate(block, r):
    n = lax.axis_size("seq")
    return lax.ppermute(block, "seq", [(i, (i + r) % n) for i in range(n)])


def padded_plan(me, queries, keys, values, dest_shard, dest_slot, ancestors):
    count = queries.shape[0]
    shards = lax.axis_size("seq")
    capacity = 2 * count // shards
    total = shards * capacity
    index = dest_shard * capacity + positions(dest_shard, shards)
    kv = exchange(jnp.concatenate([keys, values], axis=1), index, total)
    raw = exchange(queries, index, total)
    code = exchange(dest_slot + 1, index, total)
    slots = jnp.where(code > 0, code - 1, count)
    own_kv = jnp.zeros((count, kv.shape[1]), kv.dtype).at[slots].set(kv, mode="drop")
    prior_kv = from_behind(own_kv)
    return attend_padded(me, ancestors, code.reshape(1, total), raw, own_kv, prior_kv)


def after(block, *done):
    return lax.optimization_barrier((block, *done))[0]


def relay_plan(me, queries, keys, values, dest_shard, dest_slot, ancestors):
    count = queries.shape[0]
    shards = lax.axis_size("seq")
    unit = count // shards
    kv_blocks, index = pack_kv(me, dest_shard, dest_slot, keys, values, queries, shards, unit)
    got_kv = [kv_blocks[0]] + [rotate(kv_blocks[r], r) for r in range(1, shards)]
    q_blocks = pack_q(after(index, got_kv[1]), queries, shards, unit)
    own_kv, codes, crowd, q_blocks = relay(me, got_kv, q_blocks, unit)
    prior_kv = from_behind(own_kv)
    got_q = [q_blocks[0]] + [rotate(q_blocks[r], r) for r in range(1, shards)]
    result = attend(me, ancestors, codes, got_q, own_kv, prior_kv, unit)
    args = (queries, keys, values, dest_shard, dest_slot, ancestors)
    return lax.cond(crowd[0, 0] > 0, lambda: padded_plan(me, *args), lambda: result)


def local(queries, keys, values, dest_shard, dest_slot, ancestors):
    shards = lax.axis_size("seq")
    me = lax.axis_index("seq").astype(jnp.int32).reshape(1)
    plan = relay_plan if queries.shape[0] == 8 * PIECE * shards and shards == 8 else padded_plan
    return plan(me, queries, keys, values, dest_shard, dest_slot, ancestors)


def solution(mesh):
    rows = P(("groups", "seq"))
    heads = P(("groups", "seq"), "head")
    return jax.shard_map(
        local,
        mesh=mesh,
        in_specs=(heads, heads, heads, rows, rows, P(("groups", "seq"), None)),
        out_specs=heads,
        check_vma=False,
    )
```

time: 109 us -> 90.9 us (0.83)
  the two profiles are of different devices: /device:TPU:8 before, /device:TPU:28 now
where the time goes in v5:
time: 90.9 us; the launch traced here: 90.8 us
  waiting for transfers between devices  39.5 us (43%)
  starting transfers between devices  31.4 us (35%)
  Pallas kernels  17.9 us (20%)
  between operations  1.04 us (1%)
    ppermute x14, waiting for transfers between devices, rotate(): return lax.ppermute(block, 'seq', [(i, (i + r) % n) for i in range(n)])  39.5 us
    ppermute x14, starting transfers between devices, rotate(): return lax.ppermute(block, 'seq', [(i, (i + r) % n) for i in range(n)])  27.3 us
    pallas_call x1, Pallas kernels, attend(): pl.pallas_call(functools.partial(attend_kernel, shards, unit, groups), ou...  12.1 us
    ppermute x1, starting transfers between devices, from_behind(): return lax.ppermute(block, 'seq', [(i, i + 1) for i in range(n - 1)])  4.19 us
    pallas_call x1, Pallas kernels, pack_kv(): pl.pallas_call(functools.partial(pack_kv_kernel, shards, unit), out_shape...  2.66 us
    pallas_call x1, Pallas kernels, pack_q(): pl.pallas_call(functools.partial(pack_q_kernel, unit), out_shape=[jax.Sha...  1.92 us
  transfers between devices with their start and end apart: 15, of which 4 were waited for; matrix products, arithmetic and copies ran while one was open for 1% of the time, Pallas kernels for 2%

profile of v5, /device:TPU:28, one launch (start us, length us, event | category | flops | bytes accessed | tf_op | source)
XLA Modules:
  0.0 90.8 jit_solution(8151225981030620475)
XLA Ops:
  0.0 0.0 copy-start.1
  0.0 2.7 %pack_kv.1 = (bf16[96,512]{1,0:T(8,128)(2,1)S(1)}, bf16[96,512]{1,0:T(8,128)(2,1)S(1)}, bf16[96,512]{1,0:T(8,128)(2,1)S(1)}, bf16[96,512]{1,0:T(8,128)(2,1)S(1)}...) custom-call(s32[1]{0:T(128)} %bitcast.12.me_ref, ...), custom_call_target="tpu_custom_call" | custom-call | tf_op jit(solution)/shard_map/pack_kv/pallas_call | solution.py:102
  2.7 1.5 %collective-permute-start.1 = (bf16[96,512]{1,0:T(8,128)(2,1)S(1)}, bf16[96,512]{1,0:T(8,128)(2,1)S(1)}, u32[]{:S(2)}, u32[]{:S(2)}) collective-permute-start(bf16[96,512]{1,0:T(8,128)(2,1)S(1)} %get-tuple-element.60), channel_id=1, source_target_pairs={{0,2},{2,4},{4,6},{6,8},{8,10},{10,12},{12,14},{14,0},{1,3},{3,5},... | collective-permute-start | bytes 294920 | tf_op jit(solution)/shard_map/ppermute | solution.py:360
  4.2 0.2 collective-permute-start.2
  4.4 2.6 %collective-permute-start.3 = (bf16[96,512]{1,0:T(8,128)(2,1)S(1)}, bf16[96,512]{1,0:T(8,128)(2,1)S(1)}, u32[]{:S(2)}, u32[]{:S(2)}) collective-permute-start(bf16[96,512]{1,0:T(8,128)(2,1)S(1)} %get-tuple-element.62), channel_id=1, source_target_pairs={{0,6},{2,8},{4,10},{6,12},{8,14},{10,0},{12,2},{14,4},{1,7},{3,9},... | collective-permute-start | bytes 294920 | tf_op jit(solution)/shard_map/ppermute | solution.py:360
  7.0 0.3 collective-permute-start.4
  7.3 2.6 %collective-permute-start.5 = (bf16[96,512]{1,0:T(8,128)(2,1)S(1)}, bf16[96,512]{1,0:T(8,128)(2,1)S(1)}, u32[]{:S(2)}, u32[]{:S(2)}) collective-permute-start(bf16[96,512]{1,0:T(8,128)(2,1)S(1)} %get-tuple-element.64), channel_id=1, source_target_pairs={{0,10},{2,12},{4,14},{6,0},{8,2},{10,4},{12,6},{14,8},{1,11},{3,13... | collective-permute-start | bytes 294920 | tf_op jit(solution)/shard_map/ppermute | solution.py:360
  9.9 0.0 collective-permute-done.1.refs_1_
  10.0 0.5 collective-permute-start.6
  10.4 0.0 collective-permute-done.2.refs_2_
  10.4 9.7 %collective-permute-start.7 = (bf16[96,512]{1,0:T(8,128)(2,1)S(1)}, bf16[96,512]{1,0:T(8,128)(2,1)S(1)}, u32[]{:S(2)}, u32[]{:S(2)}) collective-permute-start(bf16[96,512]{1,0:T(8,128)(2,1)S(1)} %get-tuple-element.66), channel_id=1, source_target_pairs={{0,14},{2,0},{4,2},{6,4},{8,6},{10,8},{12,10},{14,12},{1,15},{3,1}... | collective-permute-start | bytes 294920 | tf_op jit(solution)/shard_map/ppermute | solution.py:360
  20.1 0.0 copy-done.1
  20.1 1.9 %pack_q.1 = (bf16[80,1280]{1,0:T(8,128)(2,1)S(1)}, bf16[80,1280]{1,0:T(8,128)(2,1)S(1)}, bf16[80,1280]{1,0:T(8,128)(2,1)S(1)}, bf16[80,1280]{1,0:T(8,128)(2,1)S(...) custom-call(s32[1,512]{1,0:T(1,128)S(1)} %get-tuple-element.68.index, ...), custom_call_target="tpu_custom_call" | custom-call | tf_op jit(solution)/shard_map/pack_q/pallas_call | solution.py:121
  22.0 0.0 copy-start.7
  22.0 0.0 collective-permute-done.3.refs_3_
  22.0 0.0 collective-permute-done.4.refs_4_
  22.1 0.0 collective-permute-done.5.refs_5_
  22.1 0.0 collective-permute-done.6.refs_6_
  22.1 0.2 collective-permute-done.7.refs_7_
  22.3 1.3 %relay.1 = (bf16[512,512]{1,0:T(8,128)(2,1)S(1)}, s32[1,512]{1,0:T(1,128)S(1)}, s32[8,128]{1,0:T(8,128)S(1)}, bf16[80,1280]{1,0:T(8,128)(2,1)S(1)}, bf16[80,1280...) custom-call(s32[1]{0:T(128)} %bitcast.12.me_ref, ...), custom_call_target="tpu_custom_call", output_to_operand_aliasing={{3}: (9, {}), {4}: (10, {}), {5}: (11, {}), {6}: (12, {}), ... | custom-call | tf_op jit(solution)/shard_map/relay/pallas_call | solution.py:201
  23.6 4.2 %collective-permute-start.15 = (bf16[512,512]{1,0:T(8,128)(2,1)S(1)}, bf16[512,512]{1,0:T(8,128)(2,1)S(1)}, u32[]{:S(2)}, u32[]{:S(2)}) collective-permute-start(bf16[512,512]{1,0:T(8,128)(2,1)S(1)} %get-tuple-element.87.refs_8_), channel_id=1, source_target_pairs={{0,2},{2,4},{4,6},{6,8},{8,10},{10,12},{12,14},{1,3},{3,5},{5,7},{... | collective-permute-start | bytes 1572872 | tf_op jit(solution)/shard_map/ppermute | solution.py:355
  27.8 0.1 collective-permute-start.8
  27.9 1.4 %collective-permute-start.9 = (bf16[80,1280]{1,0:T(8,128)(2,1)S(1)}, bf16[80,1280]{1,0:T(8,128)(2,1)S(1)}, u32[]{:S(2)}, u32[]{:S(2)}) collective-permute-start(bf16[80,1280]{1,0:T(8,128)(2,1)S(1)} %get-tuple-element.81), channel_id=1, source_target_pairs={{0,4},{2,6},{4,8},{6,10},{8,12},{10,14},{12,0},{14,2},{1,5},{3,7},... | collective-permute-start | bytes 614408 | tf_op jit(solution)/shard_map/ppermute | solution.py:360
  29.3 4.0 %collective-permute-start.10 = (bf16[80,1280]{1,0:T(8,128)(2,1)S(1)}, bf16[80,1280]{1,0:T(8,128)(2,1)S(1)}, u32[]{:S(2)}, u32[]{:S(2)}) collective-permute-start(bf16[80,1280]{1,0:T(8,128)(2,1)S(1)} %get-tuple-element.82), channel_id=1, source_target_pairs={{0,6},{2,8},{4,10},{6,12},{8,14},{10,0},{12,2},{14,4},{1,7},{3,9},... | collective-permute-start | bytes 614408 | tf_op jit(solution)/shard_map/ppermute | solution.py:360
  33.3 0.0 collective-permute-start.11
  33.3 13.8 %collective-permute-done.8.refs_1_ = bf16[80,1280]{1,0:T(8,128)(2,1)S(1)} collective-permute-done((bf16[80,1280]{1,0:T(8,128)(2,1)S(1)}, bf16[80,1280]{1,0:T(8,128)(2,1)S(1)}, u32[]{:S(2)}, u32[]{:S(2)}) %collective-permute-start.8) | collective-permute-done | bytes 204832 | tf_op jit(solution)/shard_map/ppermute | solution.py:360
  47.1 4.4 %collective-permute-start.12 = (bf16[80,1280]{1,0:T(8,128)(2,1)S(1)}, bf16[80,1280]{1,0:T(8,128)(2,1)S(1)}, u32[]{:S(2)}, u32[]{:S(2)}) collective-permute-start(bf16[80,1280]{1,0:T(8,128)(2,1)S(1)} %get-tuple-element.84), channel_id=1, source_target_pairs={{0,10},{2,12},{4,14},{6,0},{8,2},{10,4},{12,6},{14,8},{1,11},{3,13... | collective-permute-start | bytes 614408 | tf_op jit(solution)/shard_map/ppermute | solution.py:360
  51.4 0.0 collective-permute-done.9.refs_2_
  51.4 0.0 collective-permute-start.13
  51.5 20.8 %collective-permute-done.10.refs_3_ = bf16[80,1280]{1,0:T(8,128)(2,1)S(1)} collective-permute-done((bf16[80,1280]{1,0:T(8,128)(2,1)S(1)}, bf16[80,1280]{1,0:T(8,128)(2,1)S(1)}, u32[]{:S(2)}, u32[]{:S(2)}) %collective-permute-start.10) | collective-permute-done | bytes 204832 | tf_op jit(solution)/shard_map/ppermute | solution.py:360
  72.3 0.0 collective-permute-start.14
  72.3 0.5 slice.9
  73.4 0.0 collective-permute-done.11.refs_4_
  73.4 0.0 collective-permute-done.12.refs_5_
  73.5 0.0 collective-permute-done.13.refs_6_
  73.5 4.7 %collective-permute-done.14.refs_7_ = bf16[80,1280]{1,0:T(8,128)(2,1)S(1)} collective-permute-done((bf16[80,1280]{1,0:T(8,128)(2,1)S(1)}, bf16[80,1280]{1,0:T(8,128)(2,1)S(1)}, u32[]{:S(2)}, u32[]{:S(2)}) %collective-permute-start.14) | collective-permute-done | bytes 204832 | tf_op jit(solution)/shard_map/ppermute | solution.py:360
  78.1 0.0 collective-permute-done.15.refs_9_
  78.1 0.0 copy-done.7
  78.1 0.0 copy-start.3
  78.1 0.0 copy-start.4
  78.2 0.0 copy-start.6
  78.2 0.0 copy-start.8
  78.2 12.1 %attend.1 = bf16[512,1280]{1,0:T(8,128)(2,1)} custom-call(s32[1]{0:T(128)} %bitcast.12.me_ref, s32[4,4]{1,0:T(4,128)S(1)} %copy-done.7, s32[1,512]{1,0:T(1,128)S(1)} %get-tuple-element.78.code_ref, bf16[80,1280]{1,0:T(8,128)(2,1)S(1)} %get-tuple-element.79.refs_0_, bf16[80,1280]{1,0:T(8,128)(2,1)S(1)} %collective-permute-done.8.refs_1_, ...), custom_call_target="tpu_custom_call" | custom-call | tf_op jit(solution)/shard_map/attend/pallas_call | solution.py:300
  90.3 0.0 copy-done.3
  90.3 0.0 copy-done.4
  90.3 0.0 copy-done.6
  90.3 0.0 copy-done.8
  90.3 0.3 conditional.1
Async XLA Ops:
  0.0 20.1 %copy-start.1 = (bf16[512,1280]{1,0:T(8,128)(2,1)S(1)}, bf16[512,1280]{1,0:T(8,128)(2,1)}, u32[]{:S(2)}) copy-start(bf16[512,1280]{1,0:T(8,128)(2,1)} %q_ref.3) | copy-start | bytes 3932164
  2.7 7.3 %collective-permute-start.1 = (bf16[96,512]{1,0:T(8,128)(2,1)S(1)}, bf16[96,512]{1,0:T(8,128)(2,1)S(1)}, u32[]{:S(2)}, u32[]{:S(2)}) collective-permute-start(bf16[96,512]{1,0:T(8,128)(2,1)S(1)} %get-tuple-element.60), channel_id=1, source_target_pairs={{0,2},{2,4},{4,6},{6,8},{8,10},{10,12},{12,14},{14,0},{1,3},{3,5},... | collective-permute-start | bytes 294920 | tf_op jit(solution)/shard_map/ppermute | solution.py:360
  4.2 6.2 %collective-permute-start.2 = (bf16[96,512]{1,0:T(8,128)(2,1)S(1)}, bf16[96,512]{1,0:T(8,128)(2,1)S(1)}, u32[]{:S(2)}, u32[]{:S(2)}) collective-permute-start(bf16[96,512]{1,0:T(8,128)(2,1)S(1)} %get-tuple-element.61), channel_id=1, source_target_pairs={{0,4},{2,6},{4,8},{6,10},{8,12},{10,14},{12,0},{14,2},{1,5},{3,7},... | collective-permute-start | bytes 294920 | tf_op jit(solution)/shard_map/ppermute | solution.py:360
  4.4 17.6 %collective-permute-start.3 = (bf16[96,512]{1,0:T(8,128)(2,1)S(1)}, bf16[96,512]{1,0:T(8,128)(2,1)S(1)}, u32[]{:S(2)}, u32[]{:S(2)}) collective-permute-start(bf16[96,512]{1,0:T(8,128)(2,1)S(1)} %get-tuple-element.62), channel_id=1, source_target_pairs={{0,6},{2,8},{4,10},{6,12},{8,14},{10,0},{12,2},{14,4},{1,7},{3,9},... | collective-permute-start | bytes 294920 | tf_op jit(solution)/shard_map/ppermute | solution.py:360
  7.0 15.1 %collective-permute-start.4 = (bf16[96,512]{1,0:T(8,128)(2,1)S(1)}, bf16[96,512]{1,0:T(8,128)(2,1)S(1)}, u32[]{:S(2)}, u32[]{:S(2)}) collective-permute-start(bf16[96,512]{1,0:T(8,128)(2,1)S(1)} %get-tuple-element.63), channel_id=1, source_target_pairs={{0,8},{2,10},{4,12},{6,14},{8,0},{10,2},{12,4},{14,6},{1,9},{3,11}... | collective-permute-start | bytes 294920 | tf_op jit(solution)/shard_map/ppermute | solution.py:360
  7.3 14.7 %collective-permute-start.5 = (bf16[96,512]{1,0:T(8,128)(2,1)S(1)}, bf16[96,512]{1,0:T(8,128)(2,1)S(1)}, u32[]{:S(2)}, u32[]{:S(2)}) collective-permute-start(bf16[96,512]{1,0:T(8,128)(2,1)S(1)} %get-tuple-element.64), channel_id=1, source_target_pairs={{0,10},{2,12},{4,14},{6,0},{8,2},{10,4},{12,6},{14,8},{1,11},{3,13... | collective-permute-start | bytes 294920 | tf_op jit(solution)/shard_map/ppermute | solution.py:360
  10.0 12.1 %collective-permute-start.6 = (bf16[96,512]{1,0:T(8,128)(2,1)S(1)}, bf16[96,512]{1,0:T(8,128)(2,1)S(1)}, u32[]{:S(2)}, u32[]{:S(2)}) collective-permute-start(bf16[96,512]{1,0:T(8,128)(2,1)S(1)} %get-tuple-element.65), channel_id=1, source_target_pairs={{0,12},{2,14},{4,0},{6,2},{8,4},{10,6},{12,8},{14,10},{1,13},{3,15... | collective-permute-start | bytes 294920 | tf_op jit(solution)/shard_map/ppermute | solution.py:360
  10.4 11.9 %collective-permute-start.7 = (bf16[96,512]{1,0:T(8,128)(2,1)S(1)}, bf16[96,512]{1,0:T(8,128)(2,1)S(1)}, u32[]{:S(2)}, u32[]{:S(2)}) collective-permute-start(bf16[96,512]{1,0:T(8,128)(2,1)S(1)} %get-tuple-element.66), channel_id=1, source_target_pairs={{0,14},{2,0},{4,2},{6,4},{8,6},{10,8},{12,10},{14,12},{1,15},{3,1}... | collective-permute-start | bytes 294920 | tf_op jit(solution)/shard_map/ppermute | solution.py:360
  22.0 56.1 %copy-start.7 = (s32[4,4]{1,0:T(4,128)S(1)}, s32[4,4]{1,0:T(4,128)}, u32[]{:S(2)}) copy-start(s32[4,4]{1,0:T(4,128)} %anc_ref.1) | copy-start | bytes 196
  23.6 54.5 %collective-permute-start.15 = (bf16[512,512]{1,0:T(8,128)(2,1)S(1)}, bf16[512,512]{1,0:T(8,128)(2,1)S(1)}, u32[]{:S(2)}, u32[]{:S(2)}) collective-permute-start(bf16[512,512]{1,0:T(8,128)(2,1)S(1)} %get-tuple-element.87.refs_8_), channel_id=1, source_target_pairs={{0,2},{2,4},{4,6},{6,8},{8,10},{10,12},{12,14},{1,3},{3,5},{5,7},{... | collective-permute-start | bytes 1572872 | tf_op jit(solution)/shard_map/ppermute | solution.py:355
  27.8 19.3 %collective-permute-start.8 = (bf16[80,1280]{1,0:T(8,128)(2,1)S(1)}, bf16[80,1280]{1,0:T(8,128)(2,1)S(1)}, u32[]{:S(2)}, u32[]{:S(2)}) collective-permute-start(bf16[80,1280]{1,0:T(8,128)(2,1)S(1)} %get-tuple-element.80), channel_id=1, source_target_pairs={{0,2},{2,4},{4,6},{6,8},{8,10},{10,12},{12,14},{14,0},{1,3},{3,5},... | collective-permute-start | bytes 614408 | tf_op jit(solution)/shard_map/ppermute | solution.py:360
  27.9 23.6 %collective-permute-start.9 = (bf16[80,1280]{1,0:T(8,128)(2,1)S(1)}, bf16[80,1280]{1,0:T(8,128)(2,1)S(1)}, u32[]{:S(2)}, u32[]{:S(2)}) collective-permute-start(bf16[80,1280]{1,0:T(8,128)(2,1)S(1)} %get-tuple-element.81), channel_id=1, source_target_pairs={{0,4},{2,6},{4,8},{6,10},{8,12},{10,14},{12,0},{14,2},{1,5},{3,7},... | collective-permute-start | bytes 614408 | tf_op jit(solution)/shard_map/ppermute | solution.py:360
  29.3 43.0 %collective-permute-start.10 = (bf16[80,1280]{1,0:T(8,128)(2,1)S(1)}, bf16[80,1280]{1,0:T(8,128)(2,1)S(1)}, u32[]{:S(2)}, u32[]{:S(2)}) collective-permute-start(bf16[80,1280]{1,0:T(8,128)(2,1)S(1)} %get-tuple-element.82), channel_id=1, source_target_pairs={{0,6},{2,8},{4,10},{6,12},{8,14},{10,0},{12,2},{14,4},{1,7},{3,9},... | collective-permute-start | bytes 614408 | tf_op jit(solution)/shard_map/ppermute | solution.py:360
  33.3 40.2 %collective-permute-start.11 = (bf16[80,1280]{1,0:T(8,128)(2,1)S(1)}, bf16[80,1280]{1,0:T(8,128)(2,1)S(1)}, u32[]{:S(2)}, u32[]{:S(2)}) collective-permute-start(bf16[80,1280]{1,0:T(8,128)(2,1)S(1)} %get-tuple-element.83), channel_id=1, source_target_pairs={{0,8},{2,10},{4,12},{6,14},{8,0},{10,2},{12,4},{14,6},{1,9},{3,11}... | collective-permute-start | bytes 614408 | tf_op jit(solution)/shard_map/ppermute | solution.py:360
  47.1 26.4 %collective-permute-start.12 = (bf16[80,1280]{1,0:T(8,128)(2,1)S(1)}, bf16[80,1280]{1,0:T(8,128)(2,1)S(1)}, u32[]{:S(2)}, u32[]{:S(2)}) collective-permute-start(bf16[80,1280]{1,0:T(8,128)(2,1)S(1)} %get-tuple-element.84), channel_id=1, source_target_pairs={{0,10},{2,12},{4,14},{6,0},{8,2},{10,4},{12,6},{14,8},{1,11},{3,13... | collective-permute-start | bytes 614408 | tf_op jit(solution)/shard_map/ppermute | solution.py:360
  51.4 22.0 %collective-permute-start.13 = (bf16[80,1280]{1,0:T(8,128)(2,1)S(1)}, bf16[80,1280]{1,0:T(8,128)(2,1)S(1)}, u32[]{:S(2)}, u32[]{:S(2)}) collective-permute-start(bf16[80,1280]{1,0:T(8,128)(2,1)S(1)} %get-tuple-element.85), channel_id=1, source_target_pairs={{0,12},{2,14},{4,0},{6,2},{8,4},{10,6},{12,8},{14,10},{1,13},{3,15... | collective-permute-start | bytes 614408 | tf_op jit(solution)/shard_map/ppermute | solution.py:360
  72.3 5.9 %collective-permute-start.14 = (bf16[80,1280]{1,0:T(8,128)(2,1)S(1)}, bf16[80,1280]{1,0:T(8,128)(2,1)S(1)}, u32[]{:S(2)}, u32[]{:S(2)}) collective-permute-start(bf16[80,1280]{1,0:T(8,128)(2,1)S(1)} %get-tuple-element.86), channel_id=1, source_target_pairs={{0,14},{2,0},{4,2},{6,4},{8,6},{10,8},{12,10},{14,12},{1,15},{3,1}... | collective-permute-start | bytes 614408 | tf_op jit(solution)/shard_map/ppermute | solution.py:360
  78.1 12.1 %copy-start.3 = (bf16[512,256]{1,0:T(8,128)(2,1)S(1)}, bf16[512,256]{1,0:T(8,128)(2,1)}, u32[]{:S(2)}) copy-start(bf16[512,256]{1,0:T(8,128)(2,1)} %k_ref.1) | copy-start | bytes 786436
  78.1 12.1 %copy-start.4 = (bf16[512,256]{1,0:T(8,128)(2,1)S(1)}, bf16[512,256]{1,0:T(8,128)(2,1)}, u32[]{:S(2)}) copy-start(bf16[512,256]{1,0:T(8,128)(2,1)} %v_ref.1) | copy-start | bytes 786436
  78.2 12.1 %copy-start.6 = (s32[512]{0:T(512)S(1)}, s32[512]{0:T(512)}, u32[]{:S(2)}) copy-start(s32[512]{0:T(512)} %dest_ref.1) | copy-start | bytes 6148
  78.2 12.1 %copy-start.8 = (s32[512]{0:T(512)S(1)}, s32[512]{0:T(512)}, u32[]{:S(2)}) copy-start(s32[512]{0:T(512)} %slot_ref.1) | copy-start | bytes 6148

commit v6 on v5

--- a/solution.py
+++ b/solution.py
@@ -59,6 +59,7 @@
     base = position < unit
     index = jnp.where(base, ((dest - me_ref[0]) & (shards - 1)) * unit + position, -1)
     index_ref[...] = index
+    v_index = jnp.where(base, (((dest ^ 1) - me_ref[0]) & (shards - 1)) * unit + position, -1)
     over_index = jnp.where(base, -1, position - unit)
     totals = matmul_nt(jnp.ones((PIECE, count), jnp.bfloat16), onehot)
     flags = jnp.where(iota((PIECE, shards), 0) == 2, (totals > unit + 0.5).astype(jnp.float32), 0.0)
@@ -72,8 +73,10 @@
 
     picked = select_rows(index, 0, count)
     k_rows = matmul(picked, k_ref[...]).astype(jnp.bfloat16)
+    sent = matmul_nt(codes, picked)
+    picked = select_rows(v_index, 0, count)
     v_rows = matmul(picked, v_ref[...]).astype(jnp.bfloat16)
-    sent = matmul_nt(codes, picked)
+    v_sent = matmul_nt(codes, picked)
     picked = select_rows(over_index, 0, unit)
     over_k = matmul(picked, k_ref[...])
     over_v = matmul(picked, v_ref[...])
@@ -86,7 +89,7 @@
         blocks[r][0:unit, 0:kv] = k_rows[rows]
         blocks[r][0:unit, kv : 2 * kv] = v_rows[rows]
         piece = slice(r * PIECE, (r + 1) * PIECE)
-        meta = jnp.concatenate([sent[:, rows], flags, over_sent, empty], axis=1)
+        meta = jnp.concatenate([sent[:, rows], flags + v_sent[:, rows], over_sent, empty], axis=1)
         tail = [jnp.concatenate([over_k[piece], over_v[piece]], axis=1)]
         for start, stop in strips(over_q.shape[1], 2 * kv):
             tail.append(over_q[piece, start:stop])
@@ -143,10 +146,11 @@
 
 def relay_kernel(shards, unit, me_ref, *refs):
     got = refs[:shards]
-    placed_ref, codes_ref, crowd_ref = refs[2 * shards : 2 * shards + 3]
-    blocks = refs[2 * shards + 3 : 3 * shards + 3]
-    tails, sems = refs[3 * shards + 3 :]
-    count, kv_width = placed_ref.shape
+    k_out, v_out, codes_ref, crowd_ref = refs[2 * shards : 2 * shards + 4]
+    blocks = refs[2 * shards + 4 : 3 * shards + 4]
+    tails, sems = refs[3 * shards + 4 :]
+    count, half = k_out.shape
+    kv_width = 2 * half
     width = tails.shape[2]
     cuts = strips(width, kv_width)
     meta_at = cuts[-1][1] - cuts[-1][0]
@@ -180,8 +184,11 @@
 
     code = jnp.concatenate([decode(meta[0:1, 0:unit], meta[1:2, 0:unit]) for meta in metas], axis=1)
     codes_ref[...] = code
-    rows = jnp.concatenate([ref[0:unit, :] for ref in got], axis=0)
-    placed_ref[...] = matmul(select_rows(code, 1, count), rows).astype(jnp.bfloat16)
+    rows = jnp.concatenate([ref[0:unit, 0:half] for ref in got], axis=0)
+    k_out[...] = matmul(select_rows(code, 1, count), rows).astype(jnp.bfloat16)
+    code = [decode(meta[0:1, unit : 2 * unit], meta[1:2, unit : 2 * unit]) for meta in metas]
+    rows = jnp.concatenate([ref[0:unit, half:] for ref in got], axis=0)
+    v_out[...] = matmul(select_rows(jnp.concatenate(code, axis=1), 1, count), rows).astype(jnp.bfloat16)
     by_dest = jnp.zeros((1, unit), jnp.float32)
     most = jnp.zeros((1, 1), jnp.float32)
     for meta in metas:
@@ -201,23 +208,24 @@
     outs = pl.pallas_call(
         functools.partial(relay_kernel, shards, unit),
         out_shape=[
-            jax.ShapeDtypeStruct((count, got[0].shape[1]), jnp.bfloat16),
+            jax.ShapeDtypeStruct((count, got[0].shape[1] // 2), jnp.bfloat16),
+            jax.ShapeDtypeStruct((count, got[0].shape[1] // 2), jnp.bfloat16),
             jax.ShapeDtypeStruct((1, count), jnp.int32),
             jax.ShapeDtypeStruct((8, 128), jnp.int32),
         ]
         + [jax.ShapeDtypeStruct(shape, jnp.bfloat16)] * shards,
         in_specs=[SM] + [VM] * shards + [HB] * shards,
-        out_specs=[VM] * 3 + [HB] * shards,
+        out_specs=[VM] * 4 + [HB] * shards,
         scratch_shapes=[
             pltpu.VMEM((shards, 2 * PIECE, shape[1]), jnp.bfloat16),
             pltpu.SemaphoreType.DMA((shards,)),
         ],
-        input_output_aliases={1 + shards + r: 3 + r for r in range(shards)},
+        input_output_aliases={1 + shards + r: 4 + r for r in range(shards)},
         compiler_params=params(10),
         cost_estimate=light(),
         name="relay",
     )(me, *got, *q_blocks)
-    return outs[0], outs[1], outs[2], outs[3:]
+    return *outs[:4], outs[4:]
 
 
 def attend_core(shard, anc_ref, q_pl, kv_all, out_ref, groups):
@@ -260,10 +268,11 @@
 
 
 def attend_kernel(shards, unit, groups, me_ref, anc_ref, code_ref, *refs):
-    got, own_kv, prior_kv = refs[:shards], *refs[shards : shards + 2]
-    out_ref, raw, tails, q_pl, kv_all, sems = refs[shards + 2 :]
+    got, (own_k, own_v, prior_k, beside_v, prior_v) = refs[:shards], refs[shards : shards + 5]
+    out_ref, raw, tails, q_pl, kv_all, sems = refs[shards + 5 :]
     count, width = out_ref.shape
-    kv_width = own_kv.shape[1]
+    half = own_k.shape[1]
+    kv_width = 2 * half
     copies = []
 
     def fetch(source, target):
@@ -273,8 +282,19 @@
     for r, ref in enumerate(got):
         fetch(ref.at[pl.ds(unit, 2 * PIECE), :], tails.at[r])
         fetch(ref.at[pl.ds(0, unit), :], raw.at[pl.ds(r * unit, unit), :])
-    fetch(prior_kv, kv_all.at[pl.ds(0, count), :])
-    fetch(own_kv, kv_all.at[pl.ds(count, count), :])
+    fetch(prior_k, kv_all.at[pl.ds(0, count), pl.ds(0, half)])
+    fetch(own_k, kv_all.at[pl.ds(count, count), pl.ds(0, half)])
+    fetch(own_v, kv_all.at[pl.ds(count, count), pl.ds(half, half)])
+    odd = me_ref[0] & 1
+
+    @pl.when(odd == 1)
+    def _():
+        kv_all[0:count, half:] = beside_v[...]
+
+    @pl.when(odd == 0)
+    def _():
+        kv_all[0:count, half:] = prior_v[...]
+
     for c in copies:
         c.wait()
     ends = [tails[r].astype(jnp.float32) for r in range(shards)]
@@ -293,26 +313,26 @@
     attend_core(me_ref[0], anc_ref, q_pl, kv_all, out_ref, groups)
 
 
-def attend(me, ancestors, codes, got, own_kv, prior_kv, unit):
+def attend(me, ancestors, codes, got, own_k, own_v, prior_k, beside_v, prior_v, unit):
     shards = len(got)
     count, width = shards * unit, got[0].shape[1]
-    groups = own_kv.shape[1] // (2 * HEAD_SIZE)
+    groups = own_k.shape[1] // HEAD_SIZE
     return pl.pallas_call(
         functools.partial(attend_kernel, shards, unit, groups),
         out_shape=jax.ShapeDtypeStruct((count, width), jnp.bfloat16),
-        in_specs=[SM, SM, VM] + [HB] * (shards + 2),
+        in_specs=[SM, SM, VM] + [HB] * (shards + 3) + [VM, VM],
         out_specs=VM,
         scratch_shapes=[
             pltpu.VMEM((count + shards * PIECE, width), jnp.bfloat16),
             pltpu.VMEM((shards, 2 * PIECE, width), jnp.bfloat16),
             pltpu.VMEM((count, width), jnp.bfloat16),
-            pltpu.VMEM((2 * count, own_kv.shape[1]), jnp.bfloat16),
-            pltpu.SemaphoreType.DMA((2 * shards + 2,)),
+            pltpu.VMEM((2 * count, 2 * own_k.shape[1]), jnp.bfloat16),
+            pltpu.SemaphoreType.DMA((2 * shards + 3,)),
         ],
         compiler_params=params(28),
         cost_estimate=light(),
         name="attend",
-    )(me, ancestors, codes, *got, own_kv, prior_kv)
+    )(me, ancestors, codes, *got, own_k, own_v, prior_k, beside_v, prior_v)
 
 
 def attend_padded_kernel(me_ref, anc_ref, code_ref, raw_ref, own_kv, prior_kv, out_ref, q_pl, kv_all):
@@ -386,10 +406,12 @@
     kv_blocks, index = pack_kv(me, dest_shard, dest_slot, keys, values, queries, shards, unit)
     got_kv = [kv_blocks[0]] + [rotate(kv_blocks[r], r) for r in range(1, shards)]
     q_blocks = pack_q(after(index, got_kv[1]), queries, shards, unit)
-    own_kv, codes, crowd, q_blocks = relay(me, got_kv, q_blocks, unit)
-    prior_kv = from_behind(own_kv)
+    own_k, beside_v, codes, crowd, q_blocks = relay(me, got_kv, q_blocks, unit)
+    prior_k = from_behind(own_k)
+    prior_v = lax.ppermute(beside_v, "seq", [(i, i + 2) for i in range(0, shards - 2, 2)])
+    own_v = lax.ppermute(beside_v, "seq", [(i, i ^ 1) for i in range(shards)])
     got_q = [q_blocks[0]] + [rotate(q_blocks[r], r) for r in range(1, shards)]
-    result = attend(me, ancestors, codes, got_q, own_kv, prior_kv, unit)
+    result = attend(me, ancestors, codes, got_q, own_k, own_v, prior_k, beside_v, prior_v, unit)
     args = (queries, keys, values, dest_shard, dest_slot, ancestors)
     return lax.cond(crowd[0, 0] > 0, lambda: padded_plan(me, *args), lambda: result)
 

time: 90.9 us -> 85.7 us (0.943)
  the two profiles are of different devices: /device:TPU:28 before, /device:TPU:16 now
where the time goes in v6:
time: 85.7 us; the launch traced here: 84.6 us
  starting transfers between devices  50.2 us (59%)
  Pallas kernels  18.3 us (21%)
  waiting for transfers between devices  14.4 us (17%)
  between operations  1.03 us (1%)
    ppermute x14, starting transfers between devices, rotate(): return lax.ppermute(block, 'seq', [(i, (i + r) % n) for i in range(n)])  25.9 us
    ppermute x1, starting transfers between devices, from_behind(): return lax.ppermute(block, 'seq', [(i, i + 1) for i in range(n - 1)])  17.9 us
    pallas_call x1, Pallas kernels, attend(): pl.pallas_call(functools.partial(attend_kernel, shards, unit, groups), ou...  12.3 us
    ppermute x14, waiting for transfers between devices, rotate(): return lax.ppermute(block, 'seq', [(i, (i + r) % n) for i in range(n)])  9.73 us
    ppermute x1, starting transfers between devices, relay_plan(): lax.ppermute(beside_v, 'seq', [(i, i + 2) for i in range(0, shards - 2, 2)])  5.37 us
    ppermute x1, waiting for transfers between devices, relay_plan(): lax.ppermute(beside_v, 'seq', [(i, i + 2) for i in range(0, shards - 2, 2)])  2.9 us
    pallas_call x1, Pallas kernels, pack_kv(): pl.pallas_call(functools.partial(pack_kv_kernel, shards, unit), out_shape...  2.8 us
    pallas_call x1, Pallas kernels, pack_q(): pl.pallas_call(functools.partial(pack_q_kernel, unit), out_shape=[jax.Sha...  1.92 us
  transfers between devices with their start and end apart: 17, of which 6 were waited for; matrix products, arithmetic and copies ran while one was open for 1% of the time, Pallas kernels for 2%

profile of v6, /device:TPU:16, one launch (start us, length us, event | category | flops | bytes accessed | tf_op | source)
XLA Modules:
  0.0 84.6 jit_solution(934674290959044582)
XLA Ops:
  0.0 2.8 %pack_kv.1 = (bf16[96,512]{1,0:T(8,128)(2,1)S(1)}, bf16[96,512]{1,0:T(8,128)(2,1)S(1)}, bf16[96,512]{1,0:T(8,128)(2,1)S(1)}, bf16[96,512]{1,0:T(8,128)(2,1)S(1)}...) custom-call(s32[1]{0:T(128)} %bitcast.12.me_ref, ...), custom_call_target="tpu_custom_call" | custom-call | tf_op jit(solution)/shard_map/pack_kv/pallas_call | solution.py:105
  2.8 1.5 %collective-permute-start.1 = (bf16[96,512]{1,0:T(8,128)(2,1)S(1)}, bf16[96,512]{1,0:T(8,128)(2,1)S(1)}, u32[]{:S(2)}, u32[]{:S(2)}) collective-permute-start(bf16[96,512]{1,0:T(8,128)(2,1)S(1)} %get-tuple-element.61), channel_id=1, source_target_pairs={{0,2},{2,4},{4,6},{6,8},{8,10},{10,12},{12,14},{14,0},{1,3},{3,5},... | collective-permute-start | bytes 294920 | tf_op jit(solution)/shard_map/ppermute | solution.py:380
  4.4 1.6 %collective-permute-start.2 = (bf16[96,512]{1,0:T(8,128)(2,1)S(1)}, bf16[96,512]{1,0:T(8,128)(2,1)S(1)}, u32[]{:S(2)}, u32[]{:S(2)}) collective-permute-start(bf16[96,512]{1,0:T(8,128)(2,1)S(1)} %get-tuple-element.62), channel_id=1, source_target_pairs={{0,4},{2,6},{4,8},{6,10},{8,12},{10,14},{12,0},{14,2},{1,5},{3,7},... | collective-permute-start | bytes 294920 | tf_op jit(solution)/shard_map/ppermute | solution.py:380
  5.9 1.2 %collective-permute-start.3 = (bf16[96,512]{1,0:T(8,128)(2,1)S(1)}, bf16[96,512]{1,0:T(8,128)(2,1)S(1)}, u32[]{:S(2)}, u32[]{:S(2)}) collective-permute-start(bf16[96,512]{1,0:T(8,128)(2,1)S(1)} %get-tuple-element.63), channel_id=1, source_target_pairs={{0,6},{2,8},{4,10},{6,12},{8,14},{10,0},{12,2},{14,4},{1,7},{3,9},... | collective-permute-start | bytes 294920 | tf_op jit(solution)/shard_map/ppermute | solution.py:380
  7.1 1.7 %collective-permute-start.4 = (bf16[96,512]{1,0:T(8,128)(2,1)S(1)}, bf16[96,512]{1,0:T(8,128)(2,1)S(1)}, u32[]{:S(2)}, u32[]{:S(2)}) collective-permute-start(bf16[96,512]{1,0:T(8,128)(2,1)S(1)} %get-tuple-element.64), channel_id=1, source_target_pairs={{0,8},{2,10},{4,12},{6,14},{8,0},{10,2},{12,4},{14,6},{1,9},{3,11}... | collective-permute-start | bytes 294920 | tf_op jit(solution)/shard_map/ppermute | solution.py:380
  8.8 1.3 %collective-permute-start.5 = (bf16[96,512]{1,0:T(8,128)(2,1)S(1)}, bf16[96,512]{1,0:T(8,128)(2,1)S(1)}, u32[]{:S(2)}, u32[]{:S(2)}) collective-permute-start(bf16[96,512]{1,0:T(8,128)(2,1)S(1)} %get-tuple-element.65), channel_id=1, source_target_pairs={{0,10},{2,12},{4,14},{6,0},{8,2},{10,4},{12,6},{14,8},{1,11},{3,13... | collective-permute-start | bytes 294920 | tf_op jit(solution)/shard_map/ppermute | solution.py:380
  10.1 0.0 collective-permute-done.1.refs_1_
  10.1 1.3 %collective-permute-start.6 = (bf16[96,512]{1,0:T(8,128)(2,1)S(1)}, bf16[96,512]{1,0:T(8,128)(2,1)S(1)}, u32[]{:S(2)}, u32[]{:S(2)}) collective-permute-start(bf16[96,512]{1,0:T(8,128)(2,1)S(1)} %get-tuple-element.66), channel_id=1, source_target_pairs={{0,12},{2,14},{4,0},{6,2},{8,4},{10,6},{12,8},{14,10},{1,13},{3,15... | collective-permute-start | bytes 294920 | tf_op jit(solution)/shard_map/ppermute | solution.py:380
  11.4 0.0 collective-permute-done.2.refs_2_
  11.5 7.9 %collective-permute-start.7 = (bf16[96,512]{1,0:T(8,128)(2,1)S(1)}, bf16[96,512]{1,0:T(8,128)(2,1)S(1)}, u32[]{:S(2)}, u32[]{:S(2)}) collective-permute-start(bf16[96,512]{1,0:T(8,128)(2,1)S(1)} %get-tuple-element.67), channel_id=1, source_target_pairs={{0,14},{2,0},{4,2},{6,4},{8,6},{10,8},{12,10},{14,12},{1,15},{3,1}... | collective-permute-start | bytes 294920 | tf_op jit(solution)/shard_map/ppermute | solution.py:380
  19.3 0.0 copy-done.1
  19.4 1.9 %pack_q.1 = (bf16[80,1280]{1,0:T(8,128)(2,1)S(1)}, bf16[80,1280]{1,0:T(8,128)(2,1)S(1)}, bf16[80,1280]{1,0:T(8,128)(2,1)S(1)}, bf16[80,1280]{1,0:T(8,128)(2,1)S(...) custom-call(s32[1,512]{1,0:T(1,128)S(1)} %get-tuple-element.69.index, ...), custom_call_target="tpu_custom_call" | custom-call | tf_op jit(solution)/shard_map/pack_q/pallas_call | solution.py:124
  21.3 0.0 copy-start.7
  21.3 0.0 collective-permute-done.3.refs_3_
  21.3 0.0 collective-permute-done.4.refs_4_
  21.3 0.0 collective-permute-done.5.refs_5_
  21.3 0.0 collective-permute-done.6.refs_6_
  21.3 1.6 %collective-permute-done.7.refs_7_ = bf16[96,512]{1,0:T(8,128)(2,1)S(1)} collective-permute-done((bf16[96,512]{1,0:T(8,128)(2,1)S(1)}, bf16[96,512]{1,0:T(8,128)(2,1)S(1)}, u32[]{:S(2)}, u32[]{:S(2)}) %collective-permute-start.7) | collective-permute-done | bytes 98336 | tf_op jit(solution)/shard_map/ppermute | solution.py:380
  23.0 1.3 %relay.1 = (bf16[512,256]{1,0:T(8,128)(2,1)S(1)}, bf16[512,256]{1,0:T(8,128)(2,1)S(1)}, s32[1,512]{1,0:T(1,128)S(1)}, s32[8,128]{1,0:T(8,128)S(1)}, bf16[80,1280...) custom-call(s32[1]{0:T(128)} %bitcast.12.me_ref, ...), custom_call_target="tpu_custom_call", output_to_operand_aliasing={{4}: (9, {}), {5}: (10, {}), {6}: (11, {}), {7}: (12, {}), ... | custom-call | tf_op jit(solution)/shard_map/relay/pallas_call | solution.py:208
  24.2 3.0 %collective-permute-start.8 = (bf16[80,1280]{1,0:T(8,128)(2,1)S(1)}, bf16[80,1280]{1,0:T(8,128)(2,1)S(1)}, u32[]{:S(2)}, u32[]{:S(2)}) collective-permute-start(bf16[80,1280]{1,0:T(8,128)(2,1)S(1)} %get-tuple-element.81), channel_id=1, source_target_pairs={{0,2},{2,4},{4,6},{6,8},{8,10},{10,12},{12,14},{14,0},{1,3},{3,5},... | collective-permute-start | bytes 614408 | tf_op jit(solution)/shard_map/ppermute | solution.py:380
  27.2 0.4 collective-permute-start.9
  27.7 0.9 %collective-permute-start.10 = (bf16[80,1280]{1,0:T(8,128)(2,1)S(1)}, bf16[80,1280]{1,0:T(8,128)(2,1)S(1)}, u32[]{:S(2)}, u32[]{:S(2)}) collective-permute-start(bf16[80,1280]{1,0:T(8,128)(2,1)S(1)} %get-tuple-element.83), channel_id=1, source_target_pairs={{0,6},{2,8},{4,10},{6,12},{8,14},{10,0},{12,2},{14,4},{1,7},{3,9},... | collective-permute-start | bytes 614408 | tf_op jit(solution)/shard_map/ppermute | solution.py:380
  28.5 1.7 %collective-permute-start.11 = (bf16[80,1280]{1,0:T(8,128)(2,1)S(1)}, bf16[80,1280]{1,0:T(8,128)(2,1)S(1)}, u32[]{:S(2)}, u32[]{:S(2)}) collective-permute-start(bf16[80,1280]{1,0:T(8,128)(2,1)S(1)} %get-tuple-element.84), channel_id=1, source_target_pairs={{0,8},{2,10},{4,12},{6,14},{8,0},{10,2},{12,4},{14,6},{1,9},{3,11}... | collective-permute-start | bytes 614408 | tf_op jit(solution)/shard_map/ppermute | solution.py:380
  30.2 2.9 %collective-permute-start.12 = (bf16[80,1280]{1,0:T(8,128)(2,1)S(1)}, bf16[80,1280]{1,0:T(8,128)(2,1)S(1)}, u32[]{:S(2)}, u32[]{:S(2)}) collective-permute-start(bf16[80,1280]{1,0:T(8,128)(2,1)S(1)} %get-tuple-element.85), channel_id=1, source_target_pairs={{0,10},{2,12},{4,14},{6,0},{8,2},{10,4},{12,6},{14,8},{1,11},{3,13... | collective-permute-start | bytes 614408 | tf_op jit(solution)/shard_map/ppermute | solution.py:380
  33.1 0.0 collective-permute-done.8.refs_1_
  33.1 1.1 %collective-permute-start.15 = (bf16[512,256]{1,0:T(8,128)(2,1)S(1)}, bf16[512,256]{1,0:T(8,128)(2,1)S(1)}, u32[]{:S(2)}, u32[]{:S(2)}) collective-permute-start(bf16[512,256]{1,0:T(8,128)(2,1)S(1)} %get-tuple-element.89.refs_11_), channel_id=1, source_target_pairs={{0,2},{2,0},{4,6},{6,4},{8,10},{10,8},{12,14},{14,12},{1,3},{3,1},... | collective-permute-start | bytes 786440 | tf_op jit(solution)/shard_map/ppermute | solution.py:412
  34.2 1.1 %collective-permute-done.9.refs_2_ = bf16[80,1280]{1,0:T(8,128)(2,1)S(1)} collective-permute-done((bf16[80,1280]{1,0:T(8,128)(2,1)S(1)}, bf16[80,1280]{1,0:T(8,128)(2,1)S(1)}, u32[]{:S(2)}, u32[]{:S(2)}) %collective-permute-start.9) | collective-permute-done | bytes 204832 | tf_op jit(solution)/shard_map/ppermute | solution.py:380
  35.2 17.9 %collective-permute-start.16 = (bf16[512,256]{1,0:T(8,128)(2,1)S(1)}, bf16[512,256]{1,0:T(8,128)(2,1)S(1)}, u32[]{:S(2)}, u32[]{:S(2)}) collective-permute-start(bf16[512,256]{1,0:T(8,128)(2,1)S(1)} %get-tuple-element.88.refs_8_), channel_id=1, source_target_pairs={{0,2},{2,4},{4,6},{6,8},{8,10},{10,12},{12,14},{1,3},{3,5},{5,7},{... | collective-permute-start | bytes 786440 | tf_op jit(solution)/shard_map/ppermute | solution.py:375
  53.1 0.0 collective-permute-done.10.refs_3_
  53.1 5.4 %collective-permute-start.17 = (bf16[512,256]{1,0:T(8,128)(2,1)S(1)}, bf16[512,256]{1,0:T(8,128)(2,1)S(1)}, u32[]{:S(2)}, u32[]{:S(2)}) collective-permute-start(bf16[512,256]{1,0:T(8,128)(2,1)S(1)} %get-tuple-element.89.refs_11_), channel_id=1, source_target_pairs={{0,4},{4,8},{8,12},{1,5},{5,9},{9,13},{16,20},{20,24},{24,28},{17,... | collective-permute-start | bytes 786440 | tf_op jit(solution)/shard_map/ppermute | solution.py:411
  58.5 0.0 collective-permute-done.11.refs_4_
  58.5 0.1 collective-permute-start.13
  58.6 0.0 collective-permute-done.12.refs_5_
  58.6 0.4 collective-permute-start.14
  59.0 0.5 slice.9
  60.2 6.1 %collective-permute-done.13.refs_6_ = bf16[80,1280]{1,0:T(8,128)(2,1)S(1)} collective-permute-done((bf16[80,1280]{1,0:T(8,128)(2,1)S(1)}, bf16[80,1280]{1,0:T(8,128)(2,1)S(1)}, u32[]{:S(2)}, u32[]{:S(2)}) %collective-permute-start.13) | collective-permute-done | bytes 204832 | tf_op jit(solution)/shard_map/ppermute | solution.py:380
  66.3 0.9 %collective-permute-done.14.refs_7_ = bf16[80,1280]{1,0:T(8,128)(2,1)S(1)} collective-permute-done((bf16[80,1280]{1,0:T(8,128)(2,1)S(1)}, bf16[80,1280]{1,0:T(8,128)(2,1)S(1)}, u32[]{:S(2)}, u32[]{:S(2)}) %collective-permute-start.14) | collective-permute-done | bytes 204832 | tf_op jit(solution)/shard_map/ppermute | solution.py:380
  67.2 0.0 collective-permute-done.15.refs_9_
  67.2 1.7 %collective-permute-done.16.refs_10_ = bf16[512,256]{1,0:T(8,128)(2,1)S(1)} collective-permute-done((bf16[512,256]{1,0:T(8,128)(2,1)S(1)}, bf16[512,256]{1,0:T(8,128)(2,1)S(1)}, u32[]{:S(2)}, u32[]{:S(2)}) %collective-permute-start.16) | collective-permute-done | bytes 262176 | tf_op jit(solution)/shard_map/ppermute | solution.py:375
  68.9 2.9 %collective-permute-done.17.refs_12_ = bf16[512,256]{1,0:T(8,128)(2,1)S(1)} collective-permute-done((bf16[512,256]{1,0:T(8,128)(2,1)S(1)}, bf16[512,256]{1,0:T(8,128)(2,1)S(1)}, u32[]{:S(2)}, u32[]{:S(2)}) %collective-permute-start.17) | collective-permute-done | bytes 262176 | tf_op jit(solution)/shard_map/ppermute | solution.py:411
  71.8 0.0 copy-done.7
  71.8 0.0 copy-start.8
  71.8 12.3 %attend.1 = bf16[512,1280]{1,0:T(8,128)(2,1)} custom-call(s32[1]{0:T(128)} %bitcast.12.me_ref, s32[4,4]{1,0:T(4,128)S(1)} %copy-done.7, s32[1,512]{1,0:T(1,128)S(1)} %get-tuple-element.79.code_ref, bf16[80,1280]{1,0:T(8,128)(2,1)S(1)} %get-tuple-element.80.refs_0_, bf16[80,1280]{1,0:T(8,128)(2,1)S(1)} %collective-permute-done.8.refs_1_, ...), custom_call_target="tpu_custom_call" | custom-call | tf_op jit(solution)/shard_map/attend/pallas_call | solution.py:320
  84.1 0.0 copy-done.3
  84.1 0.0 copy-done.4
  84.2 0.0 copy-done.6
  84.2 0.0 copy-done.8
  84.2 0.3 conditional.1
  (4 shorter events, 0.0 us)
Async XLA Ops:
  0.0 19.3 %copy-start.1 = (bf16[512,1280]{1,0:T(8,128)(2,1)S(1)}, bf16[512,1280]{1,0:T(8,128)(2,1)}, u32[]{:S(2)}) copy-start(bf16[512,1280]{1,0:T(8,128)(2,1)} %q_ref.3) | copy-start | bytes 3932164
  2.8 7.3 %collective-permute-start.1 = (bf16[96,512]{1,0:T(8,128)(2,1)S(1)}, bf16[96,512]{1,0:T(8,128)(2,1)S(1)}, u32[]{:S(2)}, u32[]{:S(2)}) collective-permute-start(bf16[96,512]{1,0:T(8,128)(2,1)S(1)} %get-tuple-element.61), channel_id=1, source_target_pairs={{0,2},{2,4},{4,6},{6,8},{8,10},{10,12},{12,14},{14,0},{1,3},{3,5},... | collective-permute-start | bytes 294920 | tf_op jit(solution)/shard_map/ppermute | solution.py:380
  4.4 7.1 %collective-permute-start.2 = (bf16[96,512]{1,0:T(8,128)(2,1)S(1)}, bf16[96,512]{1,0:T(8,128)(2,1)S(1)}, u32[]{:S(2)}, u32[]{:S(2)}) collective-permute-start(bf16[96,512]{1,0:T(8,128)(2,1)S(1)} %get-tuple-element.62), channel_id=1, source_target_pairs={{0,4},{2,6},{4,8},{6,10},{8,12},{10,14},{12,0},{14,2},{1,5},{3,7},... | collective-permute-start | bytes 294920 | tf_op jit(solution)/shard_map/ppermute | solution.py:380
  5.9 15.4 %collective-permute-start.3 = (bf16[96,512]{1,0:T(8,128)(2,1)S(1)}, bf16[96,512]{1,0:T(8,128)(2,1)S(1)}, u32[]{:S(2)}, u32[]{:S(2)}) collective-permute-start(bf16[96,512]{1,0:T(8,128)(2,1)S(1)} %get-tuple-element.63), channel_id=1, source_target_pairs={{0,6},{2,8},{4,10},{6,12},{8,14},{10,0},{12,2},{14,4},{1,7},{3,9},... | collective-permute-start | bytes 294920 | tf_op jit(solution)/shard_map/ppermute | solution.py:380
  7.1 14.2 %collective-permute-start.4 = (bf16[96,512]{1,0:T(8,128)(2,1)S(1)}, bf16[96,512]{1,0:T(8,128)(2,1)S(1)}, u32[]{:S(2)}, u32[]{:S(2)}) collective-permute-start(bf16[96,512]{1,0:T(8,128)(2,1)S(1)} %get-tuple-element.64), channel_id=1, source_target_pairs={{0,8},{2,10},{4,12},{6,14},{8,0},{10,2},{12,4},{14,6},{1,9},{3,11}... | collective-permute-start | bytes 294920 | tf_op jit(solution)/shard_map/ppermute | solution.py:380
  8.8 12.5 %collective-permute-start.5 = (bf16[96,512]{1,0:T(8,128)(2,1)S(1)}, bf16[96,512]{1,0:T(8,128)(2,1)S(1)}, u32[]{:S(2)}, u32[]{:S(2)}) collective-permute-start(bf16[96,512]{1,0:T(8,128)(2,1)S(1)} %get-tuple-element.65), channel_id=1, source_target_pairs={{0,10},{2,12},{4,14},{6,0},{8,2},{10,4},{12,6},{14,8},{1,11},{3,13... | collective-permute-start | bytes 294920 | tf_op jit(solution)/shard_map/ppermute | solution.py:380
  10.1 11.2 %collective-permute-start.6 = (bf16[96,512]{1,0:T(8,128)(2,1)S(1)}, bf16[96,512]{1,0:T(8,128)(2,1)S(1)}, u32[]{:S(2)}, u32[]{:S(2)}) collective-permute-start(bf16[96,512]{1,0:T(8,128)(2,1)S(1)} %get-tuple-element.66), channel_id=1, source_target_pairs={{0,12},{2,14},{4,0},{6,2},{8,4},{10,6},{12,8},{14,10},{1,13},{3,15... | collective-permute-start | bytes 294920 | tf_op jit(solution)/shard_map/ppermute | solution.py:380
  11.5 11.5 %collective-permute-start.7 = (bf16[96,512]{1,0:T(8,128)(2,1)S(1)}, bf16[96,512]{1,0:T(8,128)(2,1)S(1)}, u32[]{:S(2)}, u32[]{:S(2)}) collective-permute-start(bf16[96,512]{1,0:T(8,128)(2,1)S(1)} %get-tuple-element.67), channel_id=1, source_target_pairs={{0,14},{2,0},{4,2},{6,4},{8,6},{10,8},{12,10},{14,12},{1,15},{3,1}... | collective-permute-start | bytes 294920 | tf_op jit(solution)/shard_map/ppermute | solution.py:380
  21.3 50.5 %copy-start.7 = (s32[4,4]{1,0:T(4,128)S(1)}, s32[4,4]{1,0:T(4,128)}, u32[]{:S(2)}) copy-start(s32[4,4]{1,0:T(4,128)} %anc_ref.1) | copy-start | bytes 196
  24.2 8.9 %collective-permute-start.8 = (bf16[80,1280]{1,0:T(8,128)(2,1)S(1)}, bf16[80,1280]{1,0:T(8,128)(2,1)S(1)}, u32[]{:S(2)}, u32[]{:S(2)}) collective-permute-start(bf16[80,1280]{1,0:T(8,128)(2,1)S(1)} %get-tuple-element.81), channel_id=1, source_target_pairs={{0,2},{2,4},{4,6},{6,8},{8,10},{10,12},{12,14},{14,0},{1,3},{3,5},... | collective-permute-start | bytes 614408 | tf_op jit(solution)/shard_map/ppermute | solution.py:380
  27.2 8.0 %collective-permute-start.9 = (bf16[80,1280]{1,0:T(8,128)(2,1)S(1)}, bf16[80,1280]{1,0:T(8,128)(2,1)S(1)}, u32[]{:S(2)}, u32[]{:S(2)}) collective-permute-start(bf16[80,1280]{1,0:T(8,128)(2,1)S(1)} %get-tuple-element.82), channel_id=1, source_target_pairs={{0,4},{2,6},{4,8},{6,10},{8,12},{10,14},{12,0},{14,2},{1,5},{3,7},... | collective-permute-start | bytes 614408 | tf_op jit(solution)/shard_map/ppermute | solution.py:380
  27.7 25.5 %collective-permute-start.10 = (bf16[80,1280]{1,0:T(8,128)(2,1)S(1)}, bf16[80,1280]{1,0:T(8,128)(2,1)S(1)}, u32[]{:S(2)}, u32[]{:S(2)}) collective-permute-start(bf16[80,1280]{1,0:T(8,128)(2,1)S(1)} %get-tuple-element.83), channel_id=1, source_target_pairs={{0,6},{2,8},{4,10},{6,12},{8,14},{10,0},{12,2},{14,4},{1,7},{3,9},... | collective-permute-start | bytes 614408 | tf_op jit(solution)/shard_map/ppermute | solution.py:380
  28.5 30.0 %collective-permute-start.11 = (bf16[80,1280]{1,0:T(8,128)(2,1)S(1)}, bf16[80,1280]{1,0:T(8,128)(2,1)S(1)}, u32[]{:S(2)}, u32[]{:S(2)}) collective-permute-start(bf16[80,1280]{1,0:T(8,128)(2,1)S(1)} %get-tuple-element.84), channel_id=1, source_target_pairs={{0,8},{2,10},{4,12},{6,14},{8,0},{10,2},{12,4},{14,6},{1,9},{3,11}... | collective-permute-start | bytes 614408 | tf_op jit(solution)/shard_map/ppermute | solution.py:380
  30.2 28.4 %collective-permute-start.12 = (bf16[80,1280]{1,0:T(8,128)(2,1)S(1)}, bf16[80,1280]{1,0:T(8,128)(2,1)S(1)}, u32[]{:S(2)}, u32[]{:S(2)}) collective-permute-start(bf16[80,1280]{1,0:T(8,128)(2,1)S(1)} %get-tuple-element.85), channel_id=1, source_target_pairs={{0,10},{2,12},{4,14},{6,0},{8,2},{10,4},{12,6},{14,8},{1,11},{3,13... | collective-permute-start | bytes 614408 | tf_op jit(solution)/shard_map/ppermute | solution.py:380
  33.1 34.1 %collective-permute-start.15 = (bf16[512,256]{1,0:T(8,128)(2,1)S(1)}, bf16[512,256]{1,0:T(8,128)(2,1)S(1)}, u32[]{:S(2)}, u32[]{:S(2)}) collective-permute-start(bf16[512,256]{1,0:T(8,128)(2,1)S(1)} %get-tuple-element.89.refs_11_), channel_id=1, source_target_pairs={{0,2},{2,0},{4,6},{6,4},{8,10},{10,8},{12,14},{14,12},{1,3},{3,1},... | collective-permute-start | bytes 786440 | tf_op jit(solution)/shard_map/ppermute | solution.py:412
  35.2 33.7 %collective-permute-start.16 = (bf16[512,256]{1,0:T(8,128)(2,1)S(1)}, bf16[512,256]{1,0:T(8,128)(2,1)S(1)}, u32[]{:S(2)}, u32[]{:S(2)}) collective-permute-start(bf16[512,256]{1,0:T(8,128)(2,1)S(1)} %get-tuple-element.88.refs_8_), channel_id=1, source_target_pairs={{0,2},{2,4},{4,6},{6,8},{8,10},{10,12},{12,14},{1,3},{3,5},{5,7},{... | collective-permute-start | bytes 786440 | tf_op jit(solution)/shard_map/ppermute | solution.py:375
  53.1 18.7 %collective-permute-start.17 = (bf16[512,256]{1,0:T(8,128)(2,1)S(1)}, bf16[512,256]{1,0:T(8,128)(2,1)S(1)}, u32[]{:S(2)}, u32[]{:S(2)}) collective-permute-start(bf16[512,256]{1,0:T(8,128)(2,1)S(1)} %get-tuple-element.89.refs_11_), channel_id=1, source_target_pairs={{0,4},{4,8},{8,12},{1,5},{5,9},{9,13},{16,20},{20,24},{24,28},{17,... | collective-permute-start | bytes 786440 | tf_op jit(solution)/shard_map/ppermute | solution.py:411
  58.5 7.8 %collective-permute-start.13 = (bf16[80,1280]{1,0:T(8,128)(2,1)S(1)}, bf16[80,1280]{1,0:T(8,128)(2,1)S(1)}, u32[]{:S(2)}, u32[]{:S(2)}) collective-permute-start(bf16[80,1280]{1,0:T(8,128)(2,1)S(1)} %get-tuple-element.86), channel_id=1, source_target_pairs={{0,12},{2,14},{4,0},{6,2},{8,4},{10,6},{12,8},{14,10},{1,13},{3,15... | collective-permute-start | bytes 614408 | tf_op jit(solution)/shard_map/ppermute | solution.py:380
  58.6 8.6 %collective-permute-start.14 = (bf16[80,1280]{1,0:T(8,128)(2,1)S(1)}, bf16[80,1280]{1,0:T(8,128)(2,1)S(1)}, u32[]{:S(2)}, u32[]{:S(2)}) collective-permute-start(bf16[80,1280]{1,0:T(8,128)(2,1)S(1)} %get-tuple-element.87), channel_id=1, source_target_pairs={{0,14},{2,0},{4,2},{6,4},{8,6},{10,8},{12,10},{14,12},{1,15},{3,1}... | collective-permute-start | bytes 614408 | tf_op jit(solution)/shard_map/ppermute | solution.py:380
  71.8 12.3 %copy-start.3 = (bf16[512,256]{1,0:T(8,128)(2,1)S(1)}, bf16[512,256]{1,0:T(8,128)(2,1)}, u32[]{:S(2)}) copy-start(bf16[512,256]{1,0:T(8,128)(2,1)} %k_ref.1) | copy-start | bytes 786436
  71.8 12.3 %copy-start.4 = (bf16[512,256]{1,0:T(8,128)(2,1)S(1)}, bf16[512,256]{1,0:T(8,128)(2,1)}, u32[]{:S(2)}) copy-start(bf16[512,256]{1,0:T(8,128)(2,1)} %v_ref.1) | copy-start | bytes 786436
  71.8 12.3 %copy-start.6 = (s32[512]{0:T(512)S(1)}, s32[512]{0:T(512)}, u32[]{:S(2)}) copy-start(s32[512]{0:T(512)} %dest_ref.1) | copy-start | bytes 6148
  71.8 12.3 %copy-start.8 = (s32[512]{0:T(512)S(1)}, s32[512]{0:T(512)}, u32[]{:S(2)}) copy-start(s32[512]{0:T(512)} %slot_ref.1) | copy-start | bytes 6148

commit v7 on v6

--- a/solution.py
+++ b/solution.py
@@ -261,8 +261,7 @@
             peak = jnp.max(scores, axis=1, keepdims=True)
             expo = jnp.exp2(scores - peak)
             total = jnp.sum(expo, axis=1, keepdims=True)
-            weights = (expo * (1.0 / total)).astype(jnp.bfloat16)
-            output = matmul(weights, v).astype(jnp.bfloat16)
+            output = (matmul(expo.astype(jnp.bfloat16), v) * (1.0 / total)).astype(jnp.bfloat16)
             for h, c in enumerate(columns):
                 out_ref[b * size : (b + 1) * size, c : c + HEAD_SIZE] = output[h * size : (h + 1) * size]
 
@@ -407,10 +406,11 @@
     got_kv = [kv_blocks[0]] + [rotate(kv_blocks[r], r) for r in range(1, shards)]
     q_blocks = pack_q(after(index, got_kv[1]), queries, shards, unit)
     own_k, beside_v, codes, crowd, q_blocks = relay(me, got_kv, q_blocks, unit)
-    prior_k = from_behind(own_k)
-    prior_v = lax.ppermute(beside_v, "seq", [(i, i + 2) for i in range(0, shards - 2, 2)])
-    own_v = lax.ppermute(beside_v, "seq", [(i, i ^ 1) for i in range(shards)])
     got_q = [q_blocks[0]] + [rotate(q_blocks[r], r) for r in range(1, shards)]
+    prior_k = from_behind(after(own_k, got_q[1]))
+    to_v = after(beside_v, got_q[2])
+    prior_v = lax.ppermute(to_v, "seq", [(i, i + 2) for i in range(0, shards - 2, 2)])
+    own_v = lax.ppermute(after(beside_v, got_q[3]), "seq", [(i, i ^ 1) for i in range(shards)])
     result = attend(me, ancestors, codes, got_q, own_k, own_v, prior_k, beside_v, prior_v, unit)
     args = (queries, keys, values, dest_shard, dest_slot, ancestors)
     return lax.cond(crowd[0, 0] > 0, lambda: padded_plan(me, *args), lambda: result)

time: 85.7 us -> 81.2 us (0.947)
  waiting for transfers between devices: 14.4 us -> 11.3 us
  Pallas kernels: 18.3 us -> 17.1 us
    ppermute x1, starting transfers between devices: 17.9 us -> 1.91 us  [from_behind(): return lax.ppermute(block, 'seq', [(i, i + 1) for i in range(n - 1)])]
    ppermute x2, starting transfers between devices: 6.43 us -> 16.5 us  [the longest x1 14.6 us: relay_plan(): lax.ppermute(after(beside_v, got_q[3]), 'seq', [(i, i ^ 1) for i in range...]
    ppermute x14, starting transfers between devices: 25.9 us -> 32.1 us  [rotate(): return lax.ppermute(block, 'seq', [(i, (i + r) % n) for i in range(n)])]
    ppermute x2, waiting for transfers between devices: 2.91 us -> 0.01 us  [the longest x1 0.01 us: relay_plan(): lax.ppermute(after(beside_v, got_q[3]), 'seq', [(i, i ^ 1) for i in range...]
    pallas_call x1, Pallas kernels: 12.3 us -> 11.1 us  [attend(): pl.pallas_call(functools.partial(attend_kernel, shards, unit, groups), ou...]
  transfers between devices with their start and end apart: 17 -> 17, of which waited for: 6 -> 5; matrix products, arithmetic and copies ran while one was open for 1% -> 1% of each run, Pallas kernels for 2% -> 2%
where the time goes in v7:
time: 81.2 us; the launch traced here: 80.7 us
  starting transfers between devices  50.4 us (62%)
  Pallas kernels  17.1 us (21%)
  waiting for transfers between devices  11.3 us (14%)
  between operations  1.04 us (1%)
    ppermute x14, starting transfers between devices, rotate(): return lax.ppermute(block, 'seq', [(i, (i + r) % n) for i in range(n)])  32.1 us
    ppermute x1, starting transfers between devices, relay_plan(): lax.ppermute(after(beside_v, got_q[3]), 'seq', [(i, i ^ 1) for i in range...  14.6 us
    pallas_call x1, Pallas kernels, attend(): pl.pallas_call(functools.partial(attend_kernel, shards, unit, groups), ou...  11.1 us
    ppermute x14, waiting for transfers between devices, rotate(): return lax.ppermute(block, 'seq', [(i, (i + r) % n) for i in range(n)])  9.93 us
    pallas_call x1, Pallas kernels, pack_kv(): pl.pallas_call(functools.partial(pack_kv_kernel, shards, unit), out_shape...  2.8 us
    ppermute x1, starting transfers between devices, relay_plan(): lax.ppermute(to_v, 'seq', [(i, i + 2) for i in range(0, shards - 2, 2)])  1.92 us
    pallas_call x1, Pallas kernels, pack_q(): pl.pallas_call(functools.partial(pack_q_kernel, unit), out_shape=[jax.Sha...  1.92 us
    ppermute x1, starting transfers between devices, from_behind(): return lax.ppermute(block, 'seq', [(i, i + 1) for i in range(n - 1)])  1.91 us
  transfers between devices with their start and end apart: 17, of which 5 were waited for; matrix products, arithmetic and copies ran while one was open for 1% of the time, Pallas kernels for 2%

profile of v7, /device:TPU:16, one launch (start us, length us, event | category | flops | bytes accessed | tf_op | source)
XLA Modules:
  0.0 80.7 jit_solution(1002009956285708158)
XLA Ops:
  0.0 2.8 %pack_kv.1 = (bf16[96,512]{1,0:T(8,128)(2,1)S(1)}, bf16[96,512]{1,0:T(8,128)(2,1)S(1)}, bf16[96,512]{1,0:T(8,128)(2,1)S(1)}, bf16[96,512]{1,0:T(8,128)(2,1)S(1)}...) custom-call(s32[1]{0:T(128)} %bitcast.12.me_ref, ...), custom_call_target="tpu_custom_call" | custom-call | tf_op jit(solution)/shard_map/pack_kv/pallas_call | solution.py:105
  2.8 1.5 %collective-permute-start.1 = (bf16[96,512]{1,0:T(8,128)(2,1)S(1)}, bf16[96,512]{1,0:T(8,128)(2,1)S(1)}, u32[]{:S(2)}, u32[]{:S(2)}) collective-permute-start(bf16[96,512]{1,0:T(8,128)(2,1)S(1)} %get-tuple-element.64), channel_id=1, source_target_pairs={{0,2},{2,4},{4,6},{6,8},{8,10},{10,12},{12,14},{14,0},{1,3},{3,5},... | collective-permute-start | bytes 294920 | tf_op jit(solution)/shard_map/ppermute | solution.py:379
  4.4 1.6 %collective-permute-start.2 = (bf16[96,512]{1,0:T(8,128)(2,1)S(1)}, bf16[96,512]{1,0:T(8,128)(2,1)S(1)}, u32[]{:S(2)}, u32[]{:S(2)}) collective-permute-start(bf16[96,512]{1,0:T(8,128)(2,1)S(1)} %get-tuple-element.65), channel_id=1, source_target_pairs={{0,4},{2,6},{4,8},{6,10},{8,12},{10,14},{12,0},{14,2},{1,5},{3,7},... | collective-permute-start | bytes 294920 | tf_op jit(solution)/shard_map/ppermute | solution.py:379
  5.9 1.2 %collective-permute-start.3 = (bf16[96,512]{1,0:T(8,128)(2,1)S(1)}, bf16[96,512]{1,0:T(8,128)(2,1)S(1)}, u32[]{:S(2)}, u32[]{:S(2)}) collective-permute-start(bf16[96,512]{1,0:T(8,128)(2,1)S(1)} %get-tuple-element.66), channel_id=1, source_target_pairs={{0,6},{2,8},{4,10},{6,12},{8,14},{10,0},{12,2},{14,4},{1,7},{3,9},... | collective-permute-start | bytes 294920 | tf_op jit(solution)/shard_map/ppermute | solution.py:379
  7.1 1.7 %collective-permute-start.4 = (bf16[96,512]{1,0:T(8,128)(2,1)S(1)}, bf16[96,512]{1,0:T(8,128)(2,1)S(1)}, u32[]{:S(2)}, u32[]{:S(2)}) collective-permute-start(bf16[96,512]{1,0:T(8,128)(2,1)S(1)} %get-tuple-element.67), channel_id=1, source_target_pairs={{0,8},{2,10},{4,12},{6,14},{8,0},{10,2},{12,4},{14,6},{1,9},{3,11}... | collective-permute-start | bytes 294920 | tf_op jit(solution)/shard_map/ppermute | solution.py:379
  8.8 1.3 %collective-permute-start.5 = (bf16[96,512]{1,0:T(8,128)(2,1)S(1)}, bf16[96,512]{1,0:T(8,128)(2,1)S(1)}, u32[]{:S(2)}, u32[]{:S(2)}) collective-permute-start(bf16[96,512]{1,0:T(8,128)(2,1)S(1)} %get-tuple-element.68), channel_id=1, source_target_pairs={{0,10},{2,12},{4,14},{6,0},{8,2},{10,4},{12,6},{14,8},{1,11},{3,13... | collective-permute-start | bytes 294920 | tf_op jit(solution)/shard_map/ppermute | solution.py:379
  10.1 0.0 collective-permute-done.1.refs_1_
  10.1 1.3 %collective-permute-start.6 = (bf16[96,512]{1,0:T(8,128)(2,1)S(1)}, bf16[96,512]{1,0:T(8,128)(2,1)S(1)}, u32[]{:S(2)}, u32[]{:S(2)}) collective-permute-start(bf16[96,512]{1,0:T(8,128)(2,1)S(1)} %get-tuple-element.69), channel_id=1, source_target_pairs={{0,12},{2,14},{4,0},{6,2},{8,4},{10,6},{12,8},{14,10},{1,13},{3,15... | collective-permute-start | bytes 294920 | tf_op jit(solution)/shard_map/ppermute | solution.py:379
  11.4 0.0 collective-permute-done.2.refs_2_
  11.5 7.9 %collective-permute-start.7 = (bf16[96,512]{1,0:T(8,128)(2,1)S(1)}, bf16[96,512]{1,0:T(8,128)(2,1)S(1)}, u32[]{:S(2)}, u32[]{:S(2)}) collective-permute-start(bf16[96,512]{1,0:T(8,128)(2,1)S(1)} %get-tuple-element.70), channel_id=1, source_target_pairs={{0,14},{2,0},{4,2},{6,4},{8,6},{10,8},{12,10},{14,12},{1,15},{3,1}... | collective-permute-start | bytes 294920 | tf_op jit(solution)/shard_map/ppermute | solution.py:379
  19.3 0.0 copy-done.1
  19.4 1.9 %pack_q.1 = (bf16[80,1280]{1,0:T(8,128)(2,1)S(1)}, bf16[80,1280]{1,0:T(8,128)(2,1)S(1)}, bf16[80,1280]{1,0:T(8,128)(2,1)S(1)}, bf16[80,1280]{1,0:T(8,128)(2,1)S(...) custom-call(s32[1,512]{1,0:T(1,128)S(1)} %get-tuple-element.72.index, ...), custom_call_target="tpu_custom_call" | custom-call | tf_op jit(solution)/shard_map/pack_q/pallas_call | solution.py:124
  21.3 0.0 copy-start.7
  21.3 0.0 collective-permute-done.3.refs_3_
  21.3 0.0 collective-permute-done.4.refs_4_
  21.3 0.0 collective-permute-done.5.refs_5_
  21.3 0.0 collective-permute-done.6.refs_6_
  21.3 1.6 %collective-permute-done.7.refs_7_ = bf16[96,512]{1,0:T(8,128)(2,1)S(1)} collective-permute-done((bf16[96,512]{1,0:T(8,128)(2,1)S(1)}, bf16[96,512]{1,0:T(8,128)(2,1)S(1)}, u32[]{:S(2)}, u32[]{:S(2)}) %collective-permute-start.7) | collective-permute-done | bytes 98336 | tf_op jit(solution)/shard_map/ppermute | solution.py:379
  23.0 1.3 %relay.1 = (bf16[512,256]{1,0:T(8,128)(2,1)S(1)}, bf16[512,256]{1,0:T(8,128)(2,1)S(1)}, s32[1,512]{1,0:T(1,128)S(1)}, s32[8,128]{1,0:T(8,128)S(1)}, bf16[80,1280...) custom-call(s32[1]{0:T(128)} %bitcast.12.me_ref, ...), custom_call_target="tpu_custom_call", output_to_operand_aliasing={{4}: (9, {}), {5}: (10, {}), {6}: (11, {}), {7}: (12, {}), ... | custom-call | tf_op jit(solution)/shard_map/relay/pallas_call | solution.py:208
  24.2 2.8 %collective-permute-start.10 = (bf16[80,1280]{1,0:T(8,128)(2,1)S(1)}, bf16[80,1280]{1,0:T(8,128)(2,1)S(1)}, u32[]{:S(2)}, u32[]{:S(2)}) collective-permute-start(bf16[80,1280]{1,0:T(8,128)(2,1)S(1)} %get-tuple-element.86), channel_id=1, source_target_pairs={{0,6},{2,8},{4,10},{6,12},{8,14},{10,0},{12,2},{14,4},{1,7},{3,9},... | collective-permute-start | bytes 614408 | tf_op jit(solution)/shard_map/ppermute | solution.py:379
  27.1 0.2 collective-permute-start.8
  27.3 0.4 collective-permute-start.9
  27.7 2.4 %collective-permute-start.11 = (bf16[80,1280]{1,0:T(8,128)(2,1)S(1)}, bf16[80,1280]{1,0:T(8,128)(2,1)S(1)}, u32[]{:S(2)}, u32[]{:S(2)}) collective-permute-start(bf16[80,1280]{1,0:T(8,128)(2,1)S(1)} %get-tuple-element.87), channel_id=1, source_target_pairs={{0,8},{2,10},{4,12},{6,14},{8,0},{10,2},{12,4},{14,6},{1,9},{3,11}... | collective-permute-start | bytes 614408 | tf_op jit(solution)/shard_map/ppermute | solution.py:379
  30.1 3.8 %collective-permute-start.12 = (bf16[80,1280]{1,0:T(8,128)(2,1)S(1)}, bf16[80,1280]{1,0:T(8,128)(2,1)S(1)}, u32[]{:S(2)}, u32[]{:S(2)}) collective-permute-start(bf16[80,1280]{1,0:T(8,128)(2,1)S(1)} %get-tuple-element.88), channel_id=1, source_target_pairs={{0,10},{2,12},{4,14},{6,0},{8,2},{10,4},{12,6},{14,8},{1,11},{3,13... | collective-permute-start | bytes 614408 | tf_op jit(solution)/shard_map/ppermute | solution.py:379
  34.0 0.1 collective-permute-done.10.refs_3_
  34.1 14.6 %collective-permute-start.15 = (bf16[512,256]{1,0:T(8,128)(2,1)S(1)}, bf16[512,256]{1,0:T(8,128)(2,1)S(1)}, u32[]{:S(2)}, u32[]{:S(2)}) collective-permute-start(bf16[512,256]{1,0:T(8,128)(2,1)S(1)} %get-tuple-element.95.refs_11_), channel_id=1, source_target_pairs={{0,2},{2,0},{4,6},{6,4},{8,10},{10,8},{12,14},{14,12},{1,3},{3,1},... | collective-permute-start | bytes 786440 | tf_op jit(solution)/shard_map/ppermute | solution.py:413
  48.7 0.4 collective-permute-done.8.refs_1_
  49.1 1.9 %collective-permute-start.16 = (bf16[512,256]{1,0:T(8,128)(2,1)S(1)}, bf16[512,256]{1,0:T(8,128)(2,1)S(1)}, u32[]{:S(2)}, u32[]{:S(2)}) collective-permute-start(bf16[512,256]{1,0:T(8,128)(2,1)S(1)} %get-tuple-element.94.refs_8_), channel_id=1, source_target_pairs={{0,2},{2,4},{4,6},{6,8},{8,10},{10,12},{12,14},{1,3},{3,5},{5,7},{... | collective-permute-start | bytes 786440 | tf_op jit(solution)/shard_map/ppermute | solution.py:374
  51.0 0.0 collective-permute-done.9.refs_2_
  51.0 1.9 %collective-permute-start.17 = (bf16[512,256]{1,0:T(8,128)(2,1)S(1)}, bf16[512,256]{1,0:T(8,128)(2,1)S(1)}, u32[]{:S(2)}, u32[]{:S(2)}) collective-permute-start(bf16[512,256]{1,0:T(8,128)(2,1)S(1)} %get-tuple-element.95.refs_11_), channel_id=1, source_target_pairs={{0,4},{4,8},{8,12},{1,5},{5,9},{9,13},{16,20},{20,24},{24,28},{17,... | collective-permute-start | bytes 786440 | tf_op jit(solution)/shard_map/ppermute | solution.py:412
  53.0 0.0 collective-permute-done.11.refs_4_
  53.0 2.1 %collective-permute-start.13 = (bf16[80,1280]{1,0:T(8,128)(2,1)S(1)}, bf16[80,1280]{1,0:T(8,128)(2,1)S(1)}, u32[]{:S(2)}, u32[]{:S(2)}) collective-permute-start(bf16[80,1280]{1,0:T(8,128)(2,1)S(1)} %get-tuple-element.89), channel_id=1, source_target_pairs={{0,12},{2,14},{4,0},{6,2},{8,4},{10,6},{12,8},{14,10},{1,13},{3,15... | collective-permute-start | bytes 614408 | tf_op jit(solution)/shard_map/ppermute | solution.py:379
  55.0 0.0 collective-permute-done.12.refs_5_
  55.0 3.7 %collective-permute-start.14 = (bf16[80,1280]{1,0:T(8,128)(2,1)S(1)}, bf16[80,1280]{1,0:T(8,128)(2,1)S(1)}, u32[]{:S(2)}, u32[]{:S(2)}) collective-permute-start(bf16[80,1280]{1,0:T(8,128)(2,1)S(1)} %get-tuple-element.90), channel_id=1, source_target_pairs={{0,14},{2,0},{4,2},{6,4},{8,6},{10,8},{12,10},{14,12},{1,15},{3,1}... | collective-permute-start | bytes 614408 | tf_op jit(solution)/shard_map/ppermute | solution.py:379
  58.8 0.5 slice.9
  59.9 0.0 collective-permute-done.13.refs_6_
  59.9 7.7 %collective-permute-done.14.refs_7_ = bf16[80,1280]{1,0:T(8,128)(2,1)S(1)} collective-permute-done((bf16[80,1280]{1,0:T(8,128)(2,1)S(1)}, bf16[80,1280]{1,0:T(8,128)(2,1)S(1)}, u32[]{:S(2)}, u32[]{:S(2)}) %collective-permute-start.14) | collective-permute-done | bytes 204832 | tf_op jit(solution)/shard_map/ppermute | solution.py:379
  67.7 0.0 collective-permute-done.15.refs_9_
  67.7 1.4 %collective-permute-done.16.refs_10_ = bf16[512,256]{1,0:T(8,128)(2,1)S(1)} collective-permute-done((bf16[512,256]{1,0:T(8,128)(2,1)S(1)}, bf16[512,256]{1,0:T(8,128)(2,1)S(1)}, u32[]{:S(2)}, u32[]{:S(2)}) %collective-permute-start.16) | collective-permute-done | bytes 262176 | tf_op jit(solution)/shard_map/ppermute | solution.py:374
  69.0 0.0 collective-permute-done.17.refs_12_
  69.0 0.0 copy-done.7
  69.0 0.0 copy-start.4
  69.0 0.0 copy-start.6
  69.1 0.0 copy-start.8
  69.1 11.1 %attend.1 = bf16[512,1280]{1,0:T(8,128)(2,1)} custom-call(s32[1]{0:T(128)} %bitcast.12.me_ref, s32[4,4]{1,0:T(4,128)S(1)} %copy-done.7, s32[1,512]{1,0:T(1,128)S(1)} %get-tuple-element.82.code_ref, bf16[80,1280]{1,0:T(8,128)(2,1)S(1)} %get-tuple-element.83.refs_0_, bf16[80,1280]{1,0:T(8,128)(2,1)S(1)} %collective-permute-done.8.refs_1_, ...), custom_call_target="tpu_custom_call" | custom-call | tf_op jit(solution)/shard_map/attend/pallas_call | solution.py:319
  80.2 0.0 copy-done.3
  80.2 0.0 copy-done.4
  80.3 0.3 conditional.1
  (4 shorter events, 0.0 us)
Async XLA Ops:
  0.0 19.3 %copy-start.1 = (bf16[512,1280]{1,0:T(8,128)(2,1)S(1)}, bf16[512,1280]{1,0:T(8,128)(2,1)}, u32[]{:S(2)}) copy-start(bf16[512,1280]{1,0:T(8,128)(2,1)} %q_ref.3) | copy-start | bytes 3932164
  2.8 7.3 %collective-permute-start.1 = (bf16[96,512]{1,0:T(8,128)(2,1)S(1)}, bf16[96,512]{1,0:T(8,128)(2,1)S(1)}, u32[]{:S(2)}, u32[]{:S(2)}) collective-permute-start(bf16[96,512]{1,0:T(8,128)(2,1)S(1)} %get-tuple-element.64), channel_id=1, source_target_pairs={{0,2},{2,4},{4,6},{6,8},{8,10},{10,12},{12,14},{14,0},{1,3},{3,5},... | collective-permute-start | bytes 294920 | tf_op jit(solution)/shard_map/ppermute | solution.py:379
  4.4 7.1 %collective-permute-start.2 = (bf16[96,512]{1,0:T(8,128)(2,1)S(1)}, bf16[96,512]{1,0:T(8,128)(2,1)S(1)}, u32[]{:S(2)}, u32[]{:S(2)}) collective-permute-start(bf16[96,512]{1,0:T(8,128)(2,1)S(1)} %get-tuple-element.65), channel_id=1, source_target_pairs={{0,4},{2,6},{4,8},{6,10},{8,12},{10,14},{12,0},{14,2},{1,5},{3,7},... | collective-permute-start | bytes 294920 | tf_op jit(solution)/shard_map/ppermute | solution.py:379
  5.9 15.4 %collective-permute-start.3 = (bf16[96,512]{1,0:T(8,128)(2,1)S(1)}, bf16[96,512]{1,0:T(8,128)(2,1)S(1)}, u32[]{:S(2)}, u32[]{:S(2)}) collective-permute-start(bf16[96,512]{1,0:T(8,128)(2,1)S(1)} %get-tuple-element.66), channel_id=1, source_target_pairs={{0,6},{2,8},{4,10},{6,12},{8,14},{10,0},{12,2},{14,4},{1,7},{3,9},... | collective-permute-start | bytes 294920 | tf_op jit(solution)/shard_map/ppermute | solution.py:379
  7.1 14.2 %collective-permute-start.4 = (bf16[96,512]{1,0:T(8,128)(2,1)S(1)}, bf16[96,512]{1,0:T(8,128)(2,1)S(1)}, u32[]{:S(2)}, u32[]{:S(2)}) collective-permute-start(bf16[96,512]{1,0:T(8,128)(2,1)S(1)} %get-tuple-element.67), channel_id=1, source_target_pairs={{0,8},{2,10},{4,12},{6,14},{8,0},{10,2},{12,4},{14,6},{1,9},{3,11}... | collective-permute-start | bytes 294920 | tf_op jit(solution)/shard_map/ppermute | solution.py:379
  8.8 12.5 %collective-permute-start.5 = (bf16[96,512]{1,0:T(8,128)(2,1)S(1)}, bf16[96,512]{1,0:T(8,128)(2,1)S(1)}, u32[]{:S(2)}, u32[]{:S(2)}) collective-permute-start(bf16[96,512]{1,0:T(8,128)(2,1)S(1)} %get-tuple-element.68), channel_id=1, source_target_pairs={{0,10},{2,12},{4,14},{6,0},{8,2},{10,4},{12,6},{14,8},{1,11},{3,13... | collective-permute-start | bytes 294920 | tf_op jit(solution)/shard_map/ppermute | solution.py:379
  10.1 11.2 %collective-permute-start.6 = (bf16[96,512]{1,0:T(8,128)(2,1)S(1)}, bf16[96,512]{1,0:T(8,128)(2,1)S(1)}, u32[]{:S(2)}, u32[]{:S(2)}) collective-permute-start(bf16[96,512]{1,0:T(8,128)(2,1)S(1)} %get-tuple-element.69), channel_id=1, source_target_pairs={{0,12},{2,14},{4,0},{6,2},{8,4},{10,6},{12,8},{14,10},{1,13},{3,15... | collective-permute-start | bytes 294920 | tf_op jit(solution)/shard_map/ppermute | solution.py:379
  11.5 11.5 %collective-permute-start.7 = (bf16[96,512]{1,0:T(8,128)(2,1)S(1)}, bf16[96,512]{1,0:T(8,128)(2,1)S(1)}, u32[]{:S(2)}, u32[]{:S(2)}) collective-permute-start(bf16[96,512]{1,0:T(8,128)(2,1)S(1)} %get-tuple-element.70), channel_id=1, source_target_pairs={{0,14},{2,0},{4,2},{6,4},{8,6},{10,8},{12,10},{14,12},{1,15},{3,1}... | collective-permute-start | bytes 294920 | tf_op jit(solution)/shard_map/ppermute | solution.py:379
  21.3 47.7 %copy-start.7 = (s32[4,4]{1,0:T(4,128)S(1)}, s32[4,4]{1,0:T(4,128)}, u32[]{:S(2)}) copy-start(s32[4,4]{1,0:T(4,128)} %anc_ref.1) | copy-start | bytes 196
  24.2 9.9 %collective-permute-start.10 = (bf16[80,1280]{1,0:T(8,128)(2,1)S(1)}, bf16[80,1280]{1,0:T(8,128)(2,1)S(1)}, u32[]{:S(2)}, u32[]{:S(2)}) collective-permute-start(bf16[80,1280]{1,0:T(8,128)(2,1)S(1)} %get-tuple-element.86), channel_id=1, source_target_pairs={{0,6},{2,8},{4,10},{6,12},{8,14},{10,0},{12,2},{14,4},{1,7},{3,9},... | collective-permute-start | bytes 614408 | tf_op jit(solution)/shard_map/ppermute | solution.py:379
  27.1 22.0 %collective-permute-start.8 = (bf16[80,1280]{1,0:T(8,128)(2,1)S(1)}, bf16[80,1280]{1,0:T(8,128)(2,1)S(1)}, u32[]{:S(2)}, u32[]{:S(2)}) collective-permute-start(bf16[80,1280]{1,0:T(8,128)(2,1)S(1)} %get-tuple-element.84), channel_id=1, source_target_pairs={{0,2},{2,4},{4,6},{6,8},{8,10},{10,12},{12,14},{14,0},{1,3},{3,5},... | collective-permute-start | bytes 614408 | tf_op jit(solution)/shard_map/ppermute | solution.py:379
  27.3 23.7 %collective-permute-start.9 = (bf16[80,1280]{1,0:T(8,128)(2,1)S(1)}, bf16[80,1280]{1,0:T(8,128)(2,1)S(1)}, u32[]{:S(2)}, u32[]{:S(2)}) collective-permute-start(bf16[80,1280]{1,0:T(8,128)(2,1)S(1)} %get-tuple-element.85), channel_id=1, source_target_pairs={{0,4},{2,6},{4,8},{6,10},{8,12},{10,14},{12,0},{14,2},{1,5},{3,7},... | collective-permute-start | bytes 614408 | tf_op jit(solution)/shard_map/ppermute | solution.py:379
  27.7 25.2 %collective-permute-start.11 = (bf16[80,1280]{1,0:T(8,128)(2,1)S(1)}, bf16[80,1280]{1,0:T(8,128)(2,1)S(1)}, u32[]{:S(2)}, u32[]{:S(2)}) collective-permute-start(bf16[80,1280]{1,0:T(8,128)(2,1)S(1)} %get-tuple-element.87), channel_id=1, source_target_pairs={{0,8},{2,10},{4,12},{6,14},{8,0},{10,2},{12,4},{14,6},{1,9},{3,11}... | collective-permute-start | bytes 614408 | tf_op jit(solution)/shard_map/ppermute | solution.py:379
  30.1 24.9 %collective-permute-start.12 = (bf16[80,1280]{1,0:T(8,128)(2,1)S(1)}, bf16[80,1280]{1,0:T(8,128)(2,1)S(1)}, u32[]{:S(2)}, u32[]{:S(2)}) collective-permute-start(bf16[80,1280]{1,0:T(8,128)(2,1)S(1)} %get-tuple-element.88), channel_id=1, source_target_pairs={{0,10},{2,12},{4,14},{6,0},{8,2},{10,4},{12,6},{14,8},{1,11},{3,13... | collective-permute-start | bytes 614408 | tf_op jit(solution)/shard_map/ppermute | solution.py:379
  34.1 33.6 %collective-permute-start.15 = (bf16[512,256]{1,0:T(8,128)(2,1)S(1)}, bf16[512,256]{1,0:T(8,128)(2,1)S(1)}, u32[]{:S(2)}, u32[]{:S(2)}) collective-permute-start(bf16[512,256]{1,0:T(8,128)(2,1)S(1)} %get-tuple-element.95.refs_11_), channel_id=1, source_target_pairs={{0,2},{2,0},{4,6},{6,4},{8,10},{10,8},{12,14},{14,12},{1,3},{3,1},... | collective-permute-start | bytes 786440 | tf_op jit(solution)/shard_map/ppermute | solution.py:413
  49.1 19.9 %collective-permute-start.16 = (bf16[512,256]{1,0:T(8,128)(2,1)S(1)}, bf16[512,256]{1,0:T(8,128)(2,1)S(1)}, u32[]{:S(2)}, u32[]{:S(2)}) collective-permute-start(bf16[512,256]{1,0:T(8,128)(2,1)S(1)} %get-tuple-element.94.refs_8_), channel_id=1, source_target_pairs={{0,2},{2,4},{4,6},{6,8},{8,10},{10,12},{12,14},{1,3},{3,5},{5,7},{... | collective-permute-start | bytes 786440 | tf_op jit(solution)/shard_map/ppermute | solution.py:374
  51.0 18.0 %collective-permute-start.17 = (bf16[512,256]{1,0:T(8,128)(2,1)S(1)}, bf16[512,256]{1,0:T(8,128)(2,1)S(1)}, u32[]{:S(2)}, u32[]{:S(2)}) collective-permute-start(bf16[512,256]{1,0:T(8,128)(2,1)S(1)} %get-tuple-element.95.refs_11_), channel_id=1, source_target_pairs={{0,4},{4,8},{8,12},{1,5},{5,9},{9,13},{16,20},{20,24},{24,28},{17,... | collective-permute-start | bytes 786440 | tf_op jit(solution)/shard_map/ppermute | solution.py:412
  53.0 7.0 %collective-permute-start.13 = (bf16[80,1280]{1,0:T(8,128)(2,1)S(1)}, bf16[80,1280]{1,0:T(8,128)(2,1)S(1)}, u32[]{:S(2)}, u32[]{:S(2)}) collective-permute-start(bf16[80,1280]{1,0:T(8,128)(2,1)S(1)} %get-tuple-element.89), channel_id=1, source_target_pairs={{0,12},{2,14},{4,0},{6,2},{8,4},{10,6},{12,8},{14,10},{1,13},{3,15... | collective-permute-start | bytes 614408 | tf_op jit(solution)/shard_map/ppermute | solution.py:379
  55.0 12.6 %collective-permute-start.14 = (bf16[80,1280]{1,0:T(8,128)(2,1)S(1)}, bf16[80,1280]{1,0:T(8,128)(2,1)S(1)}, u32[]{:S(2)}, u32[]{:S(2)}) collective-permute-start(bf16[80,1280]{1,0:T(8,128)(2,1)S(1)} %get-tuple-element.90), channel_id=1, source_target_pairs={{0,14},{2,0},{4,2},{6,4},{8,6},{10,8},{12,10},{14,12},{1,15},{3,1}... | collective-permute-start | bytes 614408 | tf_op jit(solution)/shard_map/ppermute | solution.py:379
  69.0 11.2 %copy-start.3 = (bf16[512,256]{1,0:T(8,128)(2,1)S(1)}, bf16[512,256]{1,0:T(8,128)(2,1)}, u32[]{:S(2)}) copy-start(bf16[512,256]{1,0:T(8,128)(2,1)} %k_ref.1) | copy-start | bytes 786436
  69.0 11.2 %copy-start.4 = (bf16[512,256]{1,0:T(8,128)(2,1)S(1)}, bf16[512,256]{1,0:T(8,128)(2,1)}, u32[]{:S(2)}) copy-start(bf16[512,256]{1,0:T(8,128)(2,1)} %v_ref.1) | copy-start | bytes 786436
  69.0 11.2 %copy-start.6 = (s32[512]{0:T(512)S(1)}, s32[512]{0:T(512)}, u32[]{:S(2)}) copy-start(s32[512]{0:T(512)} %dest_ref.1) | copy-start | bytes 6148
  69.1 11.2 %copy-start.8 = (s32[512]{0:T(512)S(1)}, s32[512]{0:T(512)}, u32[]{:S(2)}) copy-start(s32[512]{0:T(512)} %slot_ref.1) | copy-start | bytes 6148

commit v8 on v7

--- a/solution.py
+++ b/solution.py
@@ -236,34 +236,44 @@
     window = (block_count + 1) * size
     scale = math.log2(math.e) / math.sqrt(HEAD_SIZE)
     lane = iota((size, window), 1)
-    for b in range(block_count):
-        first = (shard - 1) * block_count + b
-        key_block = lane // size + first
+    causal = (lane >= block_count * size) & (lane - block_count * size <= iota((size, window), 0))
+
+    def columns(g):
+        return [(g * ratio + h) * HEAD_SIZE for h in range(ratio)]
+
+    def scores_of(b, g):
+        q = jnp.concatenate([q_pl[b * size : (b + 1) * size, c : c + HEAD_SIZE] for c in columns(g)], axis=0)
+        return matmul_nt(q, kv_all[b * size : b * size + window, g * HEAD_SIZE : (g + 1) * HEAD_SIZE])
+
+    def bias_of(b):
+        key_block = lane // size + (shard - 1) * block_count + b
         seen = lane < 0
         for a in range(anc_ref.shape[1]):
             seen = seen | (key_block == anc_ref[b, a])
-        own = lane >= block_count * size
-        causal = lane - block_count * size <= iota((size, window), 0)
-        seen = (seen & (lane < block_count * size)) | (own & causal)
-        bias = jnp.where(seen, 0.0, NEG)
-        for g in range(groups):
-            columns = [(g * ratio + h) * HEAD_SIZE for h in range(ratio)]
-            q = jnp.concatenate(
-                [q_pl[b * size : (b + 1) * size, c : c + HEAD_SIZE] for c in columns], axis=0
-            )
-            k = kv_all[b * size : b * size + window, g * HEAD_SIZE : (g + 1) * HEAD_SIZE]
-            v = kv_all[
-                b * size : b * size + window,
-                (groups + g) * HEAD_SIZE : (groups + g + 1) * HEAD_SIZE,
-            ]
-            scores = (matmul_nt(q, k) * scale).reshape(ratio, size, window) + bias[None]
-            scores = scores.reshape(ratio * size, window)
-            peak = jnp.max(scores, axis=1, keepdims=True)
-            expo = jnp.exp2(scores - peak)
-            total = jnp.sum(expo, axis=1, keepdims=True)
-            output = (matmul(expo.astype(jnp.bfloat16), v) * (1.0 / total)).astype(jnp.bfloat16)
-            for h, c in enumerate(columns):
-                out_ref[b * size : (b + 1) * size, c : c + HEAD_SIZE] = output[h * size : (h + 1) * size]
+        return jnp.where((seen & (lane < block_count * size)) | causal, 0.0, NEG)
+
+    def softmax(scores, bias):
+        scores = (scores * scale).reshape(ratio, size, window) + bias[None]
+        scores = scores.reshape(ratio * size, window)
+        expo = jnp.exp2(scores - jnp.max(scores, axis=1, keepdims=True))
+        return expo.astype(jnp.bfloat16), 1.0 / jnp.sum(expo, axis=1, keepdims=True)
+
+    def finish(b, g, expo, inverse):
+        column = (groups + g) * HEAD_SIZE
+        v = kv_all[b * size : b * size + window, column : column + HEAD_SIZE]
+        output = (matmul(expo, v) * inverse).astype(jnp.bfloat16)
+        for h, c in enumerate(columns(g)):
+            out_ref[b * size : (b + 1) * size, c : c + HEAD_SIZE] = output[h * size : (h + 1) * size]
+
+    tiles = [(b, g) for b in range(block_count) for g in range(groups)]
+    scores, held = scores_of(*tiles[0]), None
+    for i, tile in enumerate(tiles):
+        upcoming = scores_of(*tiles[i + 1]) if i + 1 < len(tiles) else None
+        if held is not None:
+            finish(*held)
+        held = (*tile, *softmax(scores, bias_of(tile[0])))
+        scores = upcoming
+    finish(*held)
 
 
 def attend_kernel(shards, unit, groups, me_ref, anc_ref, code_ref, *refs):
@@ -408,9 +418,9 @@
     own_k, beside_v, codes, crowd, q_blocks = relay(me, got_kv, q_blocks, unit)
     got_q = [q_blocks[0]] + [rotate(q_blocks[r], r) for r in range(1, shards)]
     prior_k = from_behind(after(own_k, got_q[1]))
-    to_v = after(beside_v, got_q[2])
+    to_v = after(beside_v, got_q[7])
     prior_v = lax.ppermute(to_v, "seq", [(i, i + 2) for i in range(0, shards - 2, 2)])
-    own_v = lax.ppermute(after(beside_v, got_q[3]), "seq", [(i, i ^ 1) for i in range(shards)])
+    own_v = lax.ppermute(after(beside_v, got_q[4]), "seq", [(i, i ^ 1) for i in range(shards)])
     result = attend(me, ancestors, codes, got_q, own_k, own_v, prior_k, beside_v, prior_v, unit)
     args = (queries, keys, values, dest_shard, dest_slot, ancestors)
     return lax.cond(crowd[0, 0] > 0, lambda: padded_plan(me, *args), lambda: result)

time: 81.2 us -> 79.2 us (0.975)
  starting transfers between devices: 50.4 us -> 46 us
  waiting for transfers between devices: 11.3 us -> 14.3 us
  Pallas kernels: 17.1 us -> 15.9 us
    ppermute x14, starting transfers between devices: 32.1 us -> 27.5 us  [rotate(): return lax.ppermute(block, 'seq', [(i, (i + r) % n) for i in range(n)])]
    ppermute x1, waiting for transfers between devices: 1.35 us -> 2.86 us  [from_behind(): return lax.ppermute(block, 'seq', [(i, i + 1) for i in range(n - 1)])]
    ppermute x14, waiting for transfers between devices: 9.93 us -> 11.4 us  [rotate(): return lax.ppermute(block, 'seq', [(i, (i + r) % n) for i in range(n)])]
    pallas_call x1, Pallas kernels: 11.1 us -> 9.91 us  [attend(): pl.pallas_call(functools.partial(attend_kernel, shards, unit, groups), ou...]
where the time goes in v8:
time: 79.2 us; the launch traced here: 78 us
  starting transfers between devices  46 us (58%)
  Pallas kernels  15.9 us (20%)
  waiting for transfers between devices  14.3 us (18%)
  between operations  1.02 us (1%)
    ppermute x14, starting transfers between devices, rotate(): return lax.ppermute(block, 'seq', [(i, (i + r) % n) for i in range(n)])  27.5 us
    ppermute x1, starting transfers between devices, relay_plan(): lax.ppermute(after(beside_v, got_q[4]), 'seq', [(i, i ^ 1) for i in range...  14.7 us
    ppermute x14, waiting for transfers between devices, rotate(): return lax.ppermute(block, 'seq', [(i, (i + r) % n) for i in range(n)])  11.4 us
    pallas_call x1, Pallas kernels, attend(): pl.pallas_call(functools.partial(attend_kernel, shards, unit, groups), ou...  9.91 us
    ppermute x1, waiting for transfers between devices, from_behind(): return lax.ppermute(block, 'seq', [(i, i + 1) for i in range(n - 1)])  2.86 us
    pallas_call x1, Pallas kernels, pack_kv(): pl.pallas_call(functools.partial(pack_kv_kernel, shards, unit), out_shape...  2.8 us
    ppermute x1, starting transfers between devices, relay_plan(): lax.ppermute(to_v, 'seq', [(i, i + 2) for i in range(0, shards - 2, 2)])  1.92 us
    pallas_call x1, Pallas kernels, pack_q(): pl.pallas_call(functools.partial(pack_q_kernel, unit), out_shape=[jax.Sha...  1.92 us
  transfers between devices with their start and end apart: 17, of which 5 were waited for; matrix products, arithmetic and copies ran while one was open for 1% of the time, Pallas kernels for 2%

profile of v8, /device:TPU:16, one launch (start us, length us, event | category | flops | bytes accessed | tf_op | source)
XLA Modules:
  0.0 78.0 jit_solution(15595873400237328017)
XLA Ops:
  0.0 2.8 %pack_kv.1 = (bf16[96,512]{1,0:T(8,128)(2,1)S(1)}, bf16[96,512]{1,0:T(8,128)(2,1)S(1)}, bf16[96,512]{1,0:T(8,128)(2,1)S(1)}, bf16[96,512]{1,0:T(8,128)(2,1)S(1)}...) custom-call(s32[1]{0:T(128)} %bitcast.12.me_ref, ...), custom_call_target="tpu_custom_call" | custom-call | tf_op jit(solution)/shard_map/pack_kv/pallas_call | solution.py:105
  2.8 1.5 %collective-permute-start.1 = (bf16[96,512]{1,0:T(8,128)(2,1)S(1)}, bf16[96,512]{1,0:T(8,128)(2,1)S(1)}, u32[]{:S(2)}, u32[]{:S(2)}) collective-permute-start(bf16[96,512]{1,0:T(8,128)(2,1)S(1)} %get-tuple-element.64), channel_id=1, source_target_pairs={{0,2},{2,4},{4,6},{6,8},{8,10},{10,12},{12,14},{14,0},{1,3},{3,5},... | collective-permute-start | bytes 294920 | tf_op jit(solution)/shard_map/ppermute | solution.py:389
  4.4 1.6 %collective-permute-start.2 = (bf16[96,512]{1,0:T(8,128)(2,1)S(1)}, bf16[96,512]{1,0:T(8,128)(2,1)S(1)}, u32[]{:S(2)}, u32[]{:S(2)}) collective-permute-start(bf16[96,512]{1,0:T(8,128)(2,1)S(1)} %get-tuple-element.65), channel_id=1, source_target_pairs={{0,4},{2,6},{4,8},{6,10},{8,12},{10,14},{12,0},{14,2},{1,5},{3,7},... | collective-permute-start | bytes 294920 | tf_op jit(solution)/shard_map/ppermute | solution.py:389
  5.9 1.2 %collective-permute-start.3 = (bf16[96,512]{1,0:T(8,128)(2,1)S(1)}, bf16[96,512]{1,0:T(8,128)(2,1)S(1)}, u32[]{:S(2)}, u32[]{:S(2)}) collective-permute-start(bf16[96,512]{1,0:T(8,128)(2,1)S(1)} %get-tuple-element.66), channel_id=1, source_target_pairs={{0,6},{2,8},{4,10},{6,12},{8,14},{10,0},{12,2},{14,4},{1,7},{3,9},... | collective-permute-start | bytes 294920 | tf_op jit(solution)/shard_map/ppermute | solution.py:389
  7.1 1.7 %collective-permute-start.4 = (bf16[96,512]{1,0:T(8,128)(2,1)S(1)}, bf16[96,512]{1,0:T(8,128)(2,1)S(1)}, u32[]{:S(2)}, u32[]{:S(2)}) collective-permute-start(bf16[96,512]{1,0:T(8,128)(2,1)S(1)} %get-tuple-element.67), channel_id=1, source_target_pairs={{0,8},{2,10},{4,12},{6,14},{8,0},{10,2},{12,4},{14,6},{1,9},{3,11}... | collective-permute-start | bytes 294920 | tf_op jit(solution)/shard_map/ppermute | solution.py:389
  8.8 1.3 %collective-permute-start.5 = (bf16[96,512]{1,0:T(8,128)(2,1)S(1)}, bf16[96,512]{1,0:T(8,128)(2,1)S(1)}, u32[]{:S(2)}, u32[]{:S(2)}) collective-permute-start(bf16[96,512]{1,0:T(8,128)(2,1)S(1)} %get-tuple-element.68), channel_id=1, source_target_pairs={{0,10},{2,12},{4,14},{6,0},{8,2},{10,4},{12,6},{14,8},{1,11},{3,13... | collective-permute-start | bytes 294920 | tf_op jit(solution)/shard_map/ppermute | solution.py:389
  10.1 0.0 collective-permute-done.1.refs_1_
  10.1 1.3 %collective-permute-start.6 = (bf16[96,512]{1,0:T(8,128)(2,1)S(1)}, bf16[96,512]{1,0:T(8,128)(2,1)S(1)}, u32[]{:S(2)}, u32[]{:S(2)}) collective-permute-start(bf16[96,512]{1,0:T(8,128)(2,1)S(1)} %get-tuple-element.69), channel_id=1, source_target_pairs={{0,12},{2,14},{4,0},{6,2},{8,4},{10,6},{12,8},{14,10},{1,13},{3,15... | collective-permute-start | bytes 294920 | tf_op jit(solution)/shard_map/ppermute | solution.py:389
  11.4 0.0 collective-permute-done.2.refs_2_
  11.5 7.9 %collective-permute-start.7 = (bf16[96,512]{1,0:T(8,128)(2,1)S(1)}, bf16[96,512]{1,0:T(8,128)(2,1)S(1)}, u32[]{:S(2)}, u32[]{:S(2)}) collective-permute-start(bf16[96,512]{1,0:T(8,128)(2,1)S(1)} %get-tuple-element.70), channel_id=1, source_target_pairs={{0,14},{2,0},{4,2},{6,4},{8,6},{10,8},{12,10},{14,12},{1,15},{3,1}... | collective-permute-start | bytes 294920 | tf_op jit(solution)/shard_map/ppermute | solution.py:389
  19.3 0.0 copy-done.1
  19.4 1.9 %pack_q.1 = (bf16[80,1280]{1,0:T(8,128)(2,1)S(1)}, bf16[80,1280]{1,0:T(8,128)(2,1)S(1)}, bf16[80,1280]{1,0:T(8,128)(2,1)S(1)}, bf16[80,1280]{1,0:T(8,128)(2,1)S(...) custom-call(s32[1,512]{1,0:T(1,128)S(1)} %get-tuple-element.72.index, ...), custom_call_target="tpu_custom_call" | custom-call | tf_op jit(solution)/shard_map/pack_q/pallas_call | solution.py:124
  21.3 0.0 copy-start.7
  21.3 0.0 collective-permute-done.3.refs_3_
  21.3 0.0 collective-permute-done.4.refs_4_
  21.3 0.0 collective-permute-done.5.refs_5_
  21.3 0.0 collective-permute-done.6.refs_6_
  21.3 1.6 %collective-permute-done.7.refs_7_ = bf16[96,512]{1,0:T(8,128)(2,1)S(1)} collective-permute-done((bf16[96,512]{1,0:T(8,128)(2,1)S(1)}, bf16[96,512]{1,0:T(8,128)(2,1)S(1)}, u32[]{:S(2)}, u32[]{:S(2)}) %collective-permute-start.7) | collective-permute-done | bytes 98336 | tf_op jit(solution)/shard_map/ppermute | solution.py:389
  23.0 1.3 %relay.1 = (bf16[512,256]{1,0:T(8,128)(2,1)S(1)}, bf16[512,256]{1,0:T(8,128)(2,1)S(1)}, s32[1,512]{1,0:T(1,128)S(1)}, s32[8,128]{1,0:T(8,128)S(1)}, bf16[80,1280...) custom-call(s32[1]{0:T(128)} %bitcast.12.me_ref, ...), custom_call_target="tpu_custom_call", output_to_operand_aliasing={{4}: (9, {}), {5}: (10, {}), {6}: (11, {}), {7}: (12, {}), ... | custom-call | tf_op jit(solution)/shard_map/relay/pallas_call | solution.py:208
  24.2 0.1 collective-permute-start.11
  24.3 3.0 %collective-permute-start.8 = (bf16[80,1280]{1,0:T(8,128)(2,1)S(1)}, bf16[80,1280]{1,0:T(8,128)(2,1)S(1)}, u32[]{:S(2)}, u32[]{:S(2)}) collective-permute-start(bf16[80,1280]{1,0:T(8,128)(2,1)S(1)} %get-tuple-element.84), channel_id=1, source_target_pairs={{0,2},{2,4},{4,6},{6,8},{8,10},{10,12},{12,14},{14,0},{1,3},{3,5},... | collective-permute-start | bytes 614408 | tf_op jit(solution)/shard_map/ppermute | solution.py:389
  27.3 1.3 %collective-permute-start.14 = (bf16[80,1280]{1,0:T(8,128)(2,1)S(1)}, bf16[80,1280]{1,0:T(8,128)(2,1)S(1)}, u32[]{:S(2)}, u32[]{:S(2)}) collective-permute-start(bf16[80,1280]{1,0:T(8,128)(2,1)S(1)} %get-tuple-element.90), channel_id=1, source_target_pairs={{0,14},{2,0},{4,2},{6,4},{8,6},{10,8},{12,10},{14,12},{1,15},{3,1}... | collective-permute-start | bytes 614408 | tf_op jit(solution)/shard_map/ppermute | solution.py:389
  28.6 0.7 collective-permute-start.9
  29.3 3.8 %collective-permute-start.10 = (bf16[80,1280]{1,0:T(8,128)(2,1)S(1)}, bf16[80,1280]{1,0:T(8,128)(2,1)S(1)}, u32[]{:S(2)}, u32[]{:S(2)}) collective-permute-start(bf16[80,1280]{1,0:T(8,128)(2,1)S(1)} %get-tuple-element.86), channel_id=1, source_target_pairs={{0,6},{2,8},{4,10},{6,12},{8,14},{10,0},{12,2},{14,4},{1,7},{3,9},... | collective-permute-start | bytes 614408 | tf_op jit(solution)/shard_map/ppermute | solution.py:389
  33.1 1.8 %collective-permute-done.11.refs_4_ = bf16[80,1280]{1,0:T(8,128)(2,1)S(1)} collective-permute-done((bf16[80,1280]{1,0:T(8,128)(2,1)S(1)}, bf16[80,1280]{1,0:T(8,128)(2,1)S(1)}, u32[]{:S(2)}, u32[]{:S(2)}) %collective-permute-start.11) | collective-permute-done | bytes 204832 | tf_op jit(solution)/shard_map/ppermute | solution.py:389
  34.9 14.7 %collective-permute-start.15 = (bf16[512,256]{1,0:T(8,128)(2,1)S(1)}, bf16[512,256]{1,0:T(8,128)(2,1)S(1)}, u32[]{:S(2)}, u32[]{:S(2)}) collective-permute-start(bf16[512,256]{1,0:T(8,128)(2,1)S(1)} %get-tuple-element.95.refs_11_), channel_id=1, source_target_pairs={{0,2},{2,0},{4,6},{6,4},{8,10},{10,8},{12,14},{14,12},{1,3},{3,1},... | collective-permute-start | bytes 786440 | tf_op jit(solution)/shard_map/ppermute | solution.py:423
  49.6 0.0 collective-permute-done.8.refs_1_
  49.6 1.9 %collective-permute-start.16 = (bf16[512,256]{1,0:T(8,128)(2,1)S(1)}, bf16[512,256]{1,0:T(8,128)(2,1)S(1)}, u32[]{:S(2)}, u32[]{:S(2)}) collective-permute-start(bf16[512,256]{1,0:T(8,128)(2,1)S(1)} %get-tuple-element.94.refs_8_), channel_id=1, source_target_pairs={{0,2},{2,4},{4,6},{6,8},{8,10},{10,12},{12,14},{1,3},{3,5},{5,7},{... | collective-permute-start | bytes 786440 | tf_op jit(solution)/shard_map/ppermute | solution.py:384
  51.5 0.0 collective-permute-done.14.refs_7_
  51.5 1.9 %collective-permute-start.17 = (bf16[512,256]{1,0:T(8,128)(2,1)S(1)}, bf16[512,256]{1,0:T(8,128)(2,1)S(1)}, u32[]{:S(2)}, u32[]{:S(2)}) collective-permute-start(bf16[512,256]{1,0:T(8,128)(2,1)S(1)} %get-tuple-element.95.refs_11_), channel_id=1, source_target_pairs={{0,4},{4,8},{8,12},{1,5},{5,9},{9,13},{16,20},{20,24},{24,28},{17,... | collective-permute-start | bytes 786440 | tf_op jit(solution)/shard_map/ppermute | solution.py:422
  53.4 0.0 collective-permute-done.9.refs_2_
  53.5 1.7 %collective-permute-start.12 = (bf16[80,1280]{1,0:T(8,128)(2,1)S(1)}, bf16[80,1280]{1,0:T(8,128)(2,1)S(1)}, u32[]{:S(2)}, u32[]{:S(2)}) collective-permute-start(bf16[80,1280]{1,0:T(8,128)(2,1)S(1)} %get-tuple-element.88), channel_id=1, source_target_pairs={{0,10},{2,12},{4,14},{6,0},{8,2},{10,4},{12,6},{14,8},{1,11},{3,13... | collective-permute-start | bytes 614408 | tf_op jit(solution)/shard_map/ppermute | solution.py:389
  55.1 0.0 collective-permute-done.10.refs_3_
  55.1 0.5 collective-permute-start.13
  55.6 0.5 slice.9
  56.8 4.0 %collective-permute-done.12.refs_5_ = bf16[80,1280]{1,0:T(8,128)(2,1)S(1)} collective-permute-done((bf16[80,1280]{1,0:T(8,128)(2,1)S(1)}, bf16[80,1280]{1,0:T(8,128)(2,1)S(1)}, u32[]{:S(2)}, u32[]{:S(2)}) %collective-permute-start.12) | collective-permute-done | bytes 204832 | tf_op jit(solution)/shard_map/ppermute | solution.py:389
  60.7 4.0 %collective-permute-done.13.refs_6_ = bf16[80,1280]{1,0:T(8,128)(2,1)S(1)} collective-permute-done((bf16[80,1280]{1,0:T(8,128)(2,1)S(1)}, bf16[80,1280]{1,0:T(8,128)(2,1)S(1)}, u32[]{:S(2)}, u32[]{:S(2)}) %collective-permute-start.13) | collective-permute-done | bytes 204832 | tf_op jit(solution)/shard_map/ppermute | solution.py:389
  64.8 0.0 collective-permute-done.15.refs_9_
  64.8 2.9 %collective-permute-done.16.refs_10_ = bf16[512,256]{1,0:T(8,128)(2,1)S(1)} collective-permute-done((bf16[512,256]{1,0:T(8,128)(2,1)S(1)}, bf16[512,256]{1,0:T(8,128)(2,1)S(1)}, u32[]{:S(2)}, u32[]{:S(2)}) %collective-permute-start.16) | collective-permute-done | bytes 262176 | tf_op jit(solution)/shard_map/ppermute | solution.py:384
  67.6 0.0 collective-permute-done.17.refs_12_
  67.6 0.0 copy-done.7
  67.6 0.0 copy-start.4
  67.6 0.0 copy-start.6
  67.7 0.0 copy-start.8
  67.7 9.9 %attend.1 = bf16[512,1280]{1,0:T(8,128)(2,1)} custom-call(s32[1]{0:T(128)} %bitcast.12.me_ref, s32[4,4]{1,0:T(4,128)S(1)} %copy-done.7, s32[1,512]{1,0:T(1,128)S(1)} %get-tuple-element.82.code_ref, bf16[80,1280]{1,0:T(8,128)(2,1)S(1)} %get-tuple-element.83.refs_0_, bf16[80,1280]{1,0:T(8,128)(2,1)S(1)} %collective-permute-done.8.refs_1_, ...), custom_call_target="tpu_custom_call" | custom-call | tf_op jit(solution)/shard_map/attend/pallas_call | solution.py:329
  77.6 0.0 copy-done.3
  77.6 0.0 copy-done.4
  77.6 0.2 conditional.1
  (4 shorter events, 0.0 us)
Async XLA Ops:
  0.0 19.3 %copy-start.1 = (bf16[512,1280]{1,0:T(8,128)(2,1)S(1)}, bf16[512,1280]{1,0:T(8,128)(2,1)}, u32[]{:S(2)}) copy-start(bf16[512,1280]{1,0:T(8,128)(2,1)} %q_ref.3) | copy-start | bytes 3932164
  2.8 7.3 %collective-permute-start.1 = (bf16[96,512]{1,0:T(8,128)(2,1)S(1)}, bf16[96,512]{1,0:T(8,128)(2,1)S(1)}, u32[]{:S(2)}, u32[]{:S(2)}) collective-permute-start(bf16[96,512]{1,0:T(8,128)(2,1)S(1)} %get-tuple-element.64), channel_id=1, source_target_pairs={{0,2},{2,4},{4,6},{6,8},{8,10},{10,12},{12,14},{14,0},{1,3},{3,5},... | collective-permute-start | bytes 294920 | tf_op jit(solution)/shard_map/ppermute | solution.py:389
  4.4 7.1 %collective-permute-start.2 = (bf16[96,512]{1,0:T(8,128)(2,1)S(1)}, bf16[96,512]{1,0:T(8,128)(2,1)S(1)}, u32[]{:S(2)}, u32[]{:S(2)}) collective-permute-start(bf16[96,512]{1,0:T(8,128)(2,1)S(1)} %get-tuple-element.65), channel_id=1, source_target_pairs={{0,4},{2,6},{4,8},{6,10},{8,12},{10,14},{12,0},{14,2},{1,5},{3,7},... | collective-permute-start | bytes 294920 | tf_op jit(solution)/shard_map/ppermute | solution.py:389
  5.9 15.4 %collective-permute-start.3 = (bf16[96,512]{1,0:T(8,128)(2,1)S(1)}, bf16[96,512]{1,0:T(8,128)(2,1)S(1)}, u32[]{:S(2)}, u32[]{:S(2)}) collective-permute-start(bf16[96,512]{1,0:T(8,128)(2,1)S(1)} %get-tuple-element.66), channel_id=1, source_target_pairs={{0,6},{2,8},{4,10},{6,12},{8,14},{10,0},{12,2},{14,4},{1,7},{3,9},... | collective-permute-start | bytes 294920 | tf_op jit(solution)/shard_map/ppermute | solution.py:389
  7.1 14.2 %collective-permute-start.4 = (bf16[96,512]{1,0:T(8,128)(2,1)S(1)}, bf16[96,512]{1,0:T(8,128)(2,1)S(1)}, u32[]{:S(2)}, u32[]{:S(2)}) collective-permute-start(bf16[96,512]{1,0:T(8,128)(2,1)S(1)} %get-tuple-element.67), channel_id=1, source_target_pairs={{0,8},{2,10},{4,12},{6,14},{8,0},{10,2},{12,4},{14,6},{1,9},{3,11}... | collective-permute-start | bytes 294920 | tf_op jit(solution)/shard_map/ppermute | solution.py:389
  8.8 12.5 %collective-permute-start.5 = (bf16[96,512]{1,0:T(8,128)(2,1)S(1)}, bf16[96,512]{1,0:T(8,128)(2,1)S(1)}, u32[]{:S(2)}, u32[]{:S(2)}) collective-permute-start(bf16[96,512]{1,0:T(8,128)(2,1)S(1)} %get-tuple-element.68), channel_id=1, source_target_pairs={{0,10},{2,12},{4,14},{6,0},{8,2},{10,4},{12,6},{14,8},{1,11},{3,13... | collective-permute-start | bytes 294920 | tf_op jit(solution)/shard_map/ppermute | solution.py:389
  10.1 11.2 %collective-permute-start.6 = (bf16[96,512]{1,0:T(8,128)(2,1)S(1)}, bf16[96,512]{1,0:T(8,128)(2,1)S(1)}, u32[]{:S(2)}, u32[]{:S(2)}) collective-permute-start(bf16[96,512]{1,0:T(8,128)(2,1)S(1)} %get-tuple-element.69), channel_id=1, source_target_pairs={{0,12},{2,14},{4,0},{6,2},{8,4},{10,6},{12,8},{14,10},{1,13},{3,15... | collective-permute-start | bytes 294920 | tf_op jit(solution)/shard_map/ppermute | solution.py:389
  11.5 11.5 %collective-permute-start.7 = (bf16[96,512]{1,0:T(8,128)(2,1)S(1)}, bf16[96,512]{1,0:T(8,128)(2,1)S(1)}, u32[]{:S(2)}, u32[]{:S(2)}) collective-permute-start(bf16[96,512]{1,0:T(8,128)(2,1)S(1)} %get-tuple-element.70), channel_id=1, source_target_pairs={{0,14},{2,0},{4,2},{6,4},{8,6},{10,8},{12,10},{14,12},{1,15},{3,1}... | collective-permute-start | bytes 294920 | tf_op jit(solution)/shard_map/ppermute | solution.py:389
  21.3 46.3 %copy-start.7 = (s32[4,4]{1,0:T(4,128)S(1)}, s32[4,4]{1,0:T(4,128)}, u32[]{:S(2)}) copy-start(s32[4,4]{1,0:T(4,128)} %anc_ref.1) | copy-start | bytes 196
  24.2 10.6 %collective-permute-start.11 = (bf16[80,1280]{1,0:T(8,128)(2,1)S(1)}, bf16[80,1280]{1,0:T(8,128)(2,1)S(1)}, u32[]{:S(2)}, u32[]{:S(2)}) collective-permute-start(bf16[80,1280]{1,0:T(8,128)(2,1)S(1)} %get-tuple-element.87), channel_id=1, source_target_pairs={{0,8},{2,10},{4,12},{6,14},{8,0},{10,2},{12,4},{14,6},{1,9},{3,11}... | collective-permute-start | bytes 614408 | tf_op jit(solution)/shard_map/ppermute | solution.py:389
  24.3 25.3 %collective-permute-start.8 = (bf16[80,1280]{1,0:T(8,128)(2,1)S(1)}, bf16[80,1280]{1,0:T(8,128)(2,1)S(1)}, u32[]{:S(2)}, u32[]{:S(2)}) collective-permute-start(bf16[80,1280]{1,0:T(8,128)(2,1)S(1)} %get-tuple-element.84), channel_id=1, source_target_pairs={{0,2},{2,4},{4,6},{6,8},{8,10},{10,12},{12,14},{14,0},{1,3},{3,5},... | collective-permute-start | bytes 614408 | tf_op jit(solution)/shard_map/ppermute | solution.py:389
  27.3 24.2 %collective-permute-start.14 = (bf16[80,1280]{1,0:T(8,128)(2,1)S(1)}, bf16[80,1280]{1,0:T(8,128)(2,1)S(1)}, u32[]{:S(2)}, u32[]{:S(2)}) collective-permute-start(bf16[80,1280]{1,0:T(8,128)(2,1)S(1)} %get-tuple-element.90), channel_id=1, source_target_pairs={{0,14},{2,0},{4,2},{6,4},{8,6},{10,8},{12,10},{14,12},{1,15},{3,1}... | collective-permute-start | bytes 614408 | tf_op jit(solution)/shard_map/ppermute | solution.py:389
  28.6 24.9 %collective-permute-start.9 = (bf16[80,1280]{1,0:T(8,128)(2,1)S(1)}, bf16[80,1280]{1,0:T(8,128)(2,1)S(1)}, u32[]{:S(2)}, u32[]{:S(2)}) collective-permute-start(bf16[80,1280]{1,0:T(8,128)(2,1)S(1)} %get-tuple-element.85), channel_id=1, source_target_pairs={{0,4},{2,6},{4,8},{6,10},{8,12},{10,14},{12,0},{14,2},{1,5},{3,7},... | collective-permute-start | bytes 614408 | tf_op jit(solution)/shard_map/ppermute | solution.py:389
  29.3 25.9 %collective-permute-start.10 = (bf16[80,1280]{1,0:T(8,128)(2,1)S(1)}, bf16[80,1280]{1,0:T(8,128)(2,1)S(1)}, u32[]{:S(2)}, u32[]{:S(2)}) collective-permute-start(bf16[80,1280]{1,0:T(8,128)(2,1)S(1)} %get-tuple-element.86), channel_id=1, source_target_pairs={{0,6},{2,8},{4,10},{6,12},{8,14},{10,0},{12,2},{14,4},{1,7},{3,9},... | collective-permute-start | bytes 614408 | tf_op jit(solution)/shard_map/ppermute | solution.py:389
  34.9 29.9 %collective-permute-start.15 = (bf16[512,256]{1,0:T(8,128)(2,1)S(1)}, bf16[512,256]{1,0:T(8,128)(2,1)S(1)}, u32[]{:S(2)}, u32[]{:S(2)}) collective-permute-start(bf16[512,256]{1,0:T(8,128)(2,1)S(1)} %get-tuple-element.95.refs_11_), channel_id=1, source_target_pairs={{0,2},{2,0},{4,6},{6,4},{8,10},{10,8},{12,14},{14,12},{1,3},{3,1},... | collective-permute-start | bytes 786440 | tf_op jit(solution)/shard_map/ppermute | solution.py:423
  49.6 18.0 %collective-permute-start.16 = (bf16[512,256]{1,0:T(8,128)(2,1)S(1)}, bf16[512,256]{1,0:T(8,128)(2,1)S(1)}, u32[]{:S(2)}, u32[]{:S(2)}) collective-permute-start(bf16[512,256]{1,0:T(8,128)(2,1)S(1)} %get-tuple-element.94.refs_8_), channel_id=1, source_target_pairs={{0,2},{2,4},{4,6},{6,8},{8,10},{10,12},{12,14},{1,3},{3,5},{5,7},{... | collective-permute-start | bytes 786440 | tf_op jit(solution)/shard_map/ppermute | solution.py:384
  51.5 16.1 %collective-permute-start.17 = (bf16[512,256]{1,0:T(8,128)(2,1)S(1)}, bf16[512,256]{1,0:T(8,128)(2,1)S(1)}, u32[]{:S(2)}, u32[]{:S(2)}) collective-permute-start(bf16[512,256]{1,0:T(8,128)(2,1)S(1)} %get-tuple-element.95.refs_11_), channel_id=1, source_target_pairs={{0,4},{4,8},{8,12},{1,5},{5,9},{9,13},{16,20},{20,24},{24,28},{17,... | collective-permute-start | bytes 786440 | tf_op jit(solution)/shard_map/ppermute | solution.py:422
  53.5 7.3 %collective-permute-start.12 = (bf16[80,1280]{1,0:T(8,128)(2,1)S(1)}, bf16[80,1280]{1,0:T(8,128)(2,1)S(1)}, u32[]{:S(2)}, u32[]{:S(2)}) collective-permute-start(bf16[80,1280]{1,0:T(8,128)(2,1)S(1)} %get-tuple-element.88), channel_id=1, source_target_pairs={{0,10},{2,12},{4,14},{6,0},{8,2},{10,4},{12,6},{14,8},{1,11},{3,13... | collective-permute-start | bytes 614408 | tf_op jit(solution)/shard_map/ppermute | solution.py:389
  55.1 9.6 %collective-permute-start.13 = (bf16[80,1280]{1,0:T(8,128)(2,1)S(1)}, bf16[80,1280]{1,0:T(8,128)(2,1)S(1)}, u32[]{:S(2)}, u32[]{:S(2)}) collective-permute-start(bf16[80,1280]{1,0:T(8,128)(2,1)S(1)} %get-tuple-element.89), channel_id=1, source_target_pairs={{0,12},{2,14},{4,0},{6,2},{8,4},{10,6},{12,8},{14,10},{1,13},{3,15... | collective-permute-start | bytes 614408 | tf_op jit(solution)/shard_map/ppermute | solution.py:389
  67.6 10.0 %copy-start.3 = (bf16[512,256]{1,0:T(8,128)(2,1)S(1)}, bf16[512,256]{1,0:T(8,128)(2,1)}, u32[]{:S(2)}) copy-start(bf16[512,256]{1,0:T(8,128)(2,1)} %k_ref.1) | copy-start | bytes 786436
  67.6 10.0 %copy-start.4 = (bf16[512,256]{1,0:T(8,128)(2,1)S(1)}, bf16[512,256]{1,0:T(8,128)(2,1)}, u32[]{:S(2)}) copy-start(bf16[512,256]{1,0:T(8,128)(2,1)} %v_ref.1) | copy-start | bytes 786436
  67.6 10.0 %copy-start.6 = (s32[512]{0:T(512)S(1)}, s32[512]{0:T(512)}, u32[]{:S(2)}) copy-start(s32[512]{0:T(512)} %dest_ref.1) | copy-start | bytes 6148
  67.7 10.0 %copy-start.8 = (s32[512]{0:T(512)S(1)}, s32[512]{0:T(512)}, u32[]{:S(2)}) copy-start(s32[512]{0:T(512)} %slot_ref.1) | copy-start | bytes 6148

commit v9 on v8

--- a/solution.py
+++ b/solution.py
@@ -278,7 +278,7 @@
 
 def attend_kernel(shards, unit, groups, me_ref, anc_ref, code_ref, *refs):
     got, (own_k, own_v, prior_k, beside_v, prior_v) = refs[:shards], refs[shards : shards + 5]
-    out_ref, raw, tails, q_pl, kv_all, sems = refs[shards + 5 :]
+    out_ref, raw, q_pl, kv_all, sems = refs[shards + 5 :]
     count, width = out_ref.shape
     half = own_k.shape[1]
     kv_width = 2 * half
@@ -288,9 +288,6 @@
         copies.append(pltpu.make_async_copy(source, target, sems.at[len(copies)]))
         copies[-1].start()
 
-    for r, ref in enumerate(got):
-        fetch(ref.at[pl.ds(unit, 2 * PIECE), :], tails.at[r])
-        fetch(ref.at[pl.ds(0, unit), :], raw.at[pl.ds(r * unit, unit), :])
     fetch(prior_k, kv_all.at[pl.ds(0, count), pl.ds(0, half)])
     fetch(own_k, kv_all.at[pl.ds(count, count), pl.ds(0, half)])
     fetch(own_v, kv_all.at[pl.ds(count, count), pl.ds(half, half)])
@@ -304,9 +301,11 @@
     def _():
         kv_all[0:count, half:] = prior_v[...]
 
+    for r, ref in enumerate(got):
+        raw[r * unit : (r + 1) * unit, :] = ref[0:unit, :]
     for c in copies:
         c.wait()
-    ends = [tails[r].astype(jnp.float32) for r in range(shards)]
+    ends = [ref[unit:, :].astype(jnp.float32) for ref in got]
     metas = [end[PIECE:, 2 * kv_width :] for end in ends]
     own = [meta[:, 0:unit] for meta in metas]
     behind = [meta[:, unit : 2 * unit] for meta in metas]
@@ -329,14 +328,13 @@
     return pl.pallas_call(
         functools.partial(attend_kernel, shards, unit, groups),
         out_shape=jax.ShapeDtypeStruct((count, width), jnp.bfloat16),
-        in_specs=[SM, SM, VM] + [HB] * (shards + 3) + [VM, VM],
+        in_specs=[SM, SM, VM] + [VM] * shards + [HB] * 3 + [VM, VM],
         out_specs=VM,
         scratch_shapes=[
             pltpu.VMEM((count + shards * PIECE, width), jnp.bfloat16),
-            pltpu.VMEM((shards, 2 * PIECE, width), jnp.bfloat16),
             pltpu.VMEM((count, width), jnp.bfloat16),
             pltpu.VMEM((2 * count, 2 * own_k.shape[1]), jnp.bfloat16),
-            pltpu.SemaphoreType.DMA((2 * shards + 3,)),
+            pltpu.SemaphoreType.DMA((3,)),
         ],
         compiler_params=params(28),
         cost_estimate=light(),

time: 79.2 us -> 77 us (0.972)
  Pallas kernels: 15.9 us -> 13.7 us
    pallas_call x1, Pallas kernels: 9.91 us -> 7.72 us  [attend(): pl.pallas_call(functools.partial(attend_kernel, shards, unit, groups), ou...]
  transfers between devices with their start and end apart: 17 -> 17, of which waited for: 5 -> 5; matrix products, arithmetic and copies ran while one was open for 1% -> 1% of each run, Pallas kernels for 2% -> 3%
where the time goes in v9:
time: 77 us; the launch traced here: 75.9 us
  starting transfers between devices  46 us (60%)
  waiting for transfers between devices  14.3 us (19%)
  Pallas kernels  13.7 us (18%)
  between operations  1.02 us (1%)
    ppermute x14, starting transfers between devices, rotate(): return lax.ppermute(block, 'seq', [(i, (i + r) % n) for i in range(n)])  27.5 us
    ppermute x1, starting transfers between devices, relay_plan(): lax.ppermute(after(beside_v, got_q[4]), 'seq', [(i, i ^ 1) for i in range...  14.7 us
    ppermute x14, waiting for transfers between devices, rotate(): return lax.ppermute(block, 'seq', [(i, (i + r) % n) for i in range(n)])  11.4 us
    pallas_call x1, Pallas kernels, attend(): pl.pallas_call(functools.partial(attend_kernel, shards, unit, groups), ou...  7.72 us
    ppermute x1, waiting for transfers between devices, from_behind(): return lax.ppermute(block, 'seq', [(i, i + 1) for i in range(n - 1)])  2.86 us
    pallas_call x1, Pallas kernels, pack_kv(): pl.pallas_call(functools.partial(pack_kv_kernel, shards, unit), out_shape...  2.8 us
    ppermute x1, starting transfers between devices, relay_plan(): lax.ppermute(to_v, 'seq', [(i, i + 2) for i in range(0, shards - 2, 2)])  1.92 us
    pallas_call x1, Pallas kernels, pack_q(): pl.pallas_call(functools.partial(pack_q_kernel, unit), out_shape=[jax.Sha...  1.92 us
  transfers between devices with their start and end apart: 17, of which 5 were waited for; matrix products, arithmetic and copies ran while one was open for 1% of the time, Pallas kernels for 3%

profile of v9, /device:TPU:16, one launch (start us, length us, event | category | flops | bytes accessed | tf_op | source)
XLA Modules:
  0.0 75.9 jit_solution(13836797842551330456)
XLA Ops:
  0.0 2.8 %pack_kv.1 = (bf16[96,512]{1,0:T(8,128)(2,1)S(1)}, bf16[96,512]{1,0:T(8,128)(2,1)S(1)}, bf16[96,512]{1,0:T(8,128)(2,1)S(1)}, bf16[96,512]{1,0:T(8,128)(2,1)S(1)}...) custom-call(s32[1]{0:T(128)} %bitcast.12.me_ref, ...), custom_call_target="tpu_custom_call" | custom-call | tf_op jit(solution)/shard_map/pack_kv/pallas_call | solution.py:105
  2.8 1.5 %collective-permute-start.1 = (bf16[96,512]{1,0:T(8,128)(2,1)S(1)}, bf16[96,512]{1,0:T(8,128)(2,1)S(1)}, u32[]{:S(2)}, u32[]{:S(2)}) collective-permute-start(bf16[96,512]{1,0:T(8,128)(2,1)S(1)} %get-tuple-element.64), channel_id=1, source_target_pairs={{0,2},{2,4},{4,6},{6,8},{8,10},{10,12},{12,14},{14,0},{1,3},{3,5},... | collective-permute-start | bytes 294920 | tf_op jit(solution)/shard_map/ppermute | solution.py:387
  4.4 1.6 %collective-permute-start.2 = (bf16[96,512]{1,0:T(8,128)(2,1)S(1)}, bf16[96,512]{1,0:T(8,128)(2,1)S(1)}, u32[]{:S(2)}, u32[]{:S(2)}) collective-permute-start(bf16[96,512]{1,0:T(8,128)(2,1)S(1)} %get-tuple-element.65), channel_id=1, source_target_pairs={{0,4},{2,6},{4,8},{6,10},{8,12},{10,14},{12,0},{14,2},{1,5},{3,7},... | collective-permute-start | bytes 294920 | tf_op jit(solution)/shard_map/ppermute | solution.py:387
  5.9 1.2 %collective-permute-start.3 = (bf16[96,512]{1,0:T(8,128)(2,1)S(1)}, bf16[96,512]{1,0:T(8,128)(2,1)S(1)}, u32[]{:S(2)}, u32[]{:S(2)}) collective-permute-start(bf16[96,512]{1,0:T(8,128)(2,1)S(1)} %get-tuple-element.66), channel_id=1, source_target_pairs={{0,6},{2,8},{4,10},{6,12},{8,14},{10,0},{12,2},{14,4},{1,7},{3,9},... | collective-permute-start | bytes 294920 | tf_op jit(solution)/shard_map/ppermute | solution.py:387
  7.1 1.7 %collective-permute-start.4 = (bf16[96,512]{1,0:T(8,128)(2,1)S(1)}, bf16[96,512]{1,0:T(8,128)(2,1)S(1)}, u32[]{:S(2)}, u32[]{:S(2)}) collective-permute-start(bf16[96,512]{1,0:T(8,128)(2,1)S(1)} %get-tuple-element.67), channel_id=1, source_target_pairs={{0,8},{2,10},{4,12},{6,14},{8,0},{10,2},{12,4},{14,6},{1,9},{3,11}... | collective-permute-start | bytes 294920 | tf_op jit(solution)/shard_map/ppermute | solution.py:387
  8.8 1.3 %collective-permute-start.5 = (bf16[96,512]{1,0:T(8,128)(2,1)S(1)}, bf16[96,512]{1,0:T(8,128)(2,1)S(1)}, u32[]{:S(2)}, u32[]{:S(2)}) collective-permute-start(bf16[96,512]{1,0:T(8,128)(2,1)S(1)} %get-tuple-element.68), channel_id=1, source_target_pairs={{0,10},{2,12},{4,14},{6,0},{8,2},{10,4},{12,6},{14,8},{1,11},{3,13... | collective-permute-start | bytes 294920 | tf_op jit(solution)/shard_map/ppermute | solution.py:387
  10.1 0.0 collective-permute-done.1.refs_1_
  10.1 1.3 %collective-permute-start.6 = (bf16[96,512]{1,0:T(8,128)(2,1)S(1)}, bf16[96,512]{1,0:T(8,128)(2,1)S(1)}, u32[]{:S(2)}, u32[]{:S(2)}) collective-permute-start(bf16[96,512]{1,0:T(8,128)(2,1)S(1)} %get-tuple-element.69), channel_id=1, source_target_pairs={{0,12},{2,14},{4,0},{6,2},{8,4},{10,6},{12,8},{14,10},{1,13},{3,15... | collective-permute-start | bytes 294920 | tf_op jit(solution)/shard_map/ppermute | solution.py:387
  11.4 0.0 collective-permute-done.2.refs_2_
  11.5 7.9 %collective-permute-start.7 = (bf16[96,512]{1,0:T(8,128)(2,1)S(1)}, bf16[96,512]{1,0:T(8,128)(2,1)S(1)}, u32[]{:S(2)}, u32[]{:S(2)}) collective-permute-start(bf16[96,512]{1,0:T(8,128)(2,1)S(1)} %get-tuple-element.70), channel_id=1, source_target_pairs={{0,14},{2,0},{4,2},{6,4},{8,6},{10,8},{12,10},{14,12},{1,15},{3,1}... | collective-permute-start | bytes 294920 | tf_op jit(solution)/shard_map/ppermute | solution.py:387
  19.3 0.0 copy-done.1
  19.4 1.9 %pack_q.1 = (bf16[80,1280]{1,0:T(8,128)(2,1)S(1)}, bf16[80,1280]{1,0:T(8,128)(2,1)S(1)}, bf16[80,1280]{1,0:T(8,128)(2,1)S(1)}, bf16[80,1280]{1,0:T(8,128)(2,1)S(...) custom-call(s32[1,512]{1,0:T(1,128)S(1)} %get-tuple-element.72.index, ...), custom_call_target="tpu_custom_call" | custom-call | tf_op jit(solution)/shard_map/pack_q/pallas_call | solution.py:124
  21.3 0.0 copy-start.7
  21.3 0.0 collective-permute-done.3.refs_3_
  21.3 0.0 collective-permute-done.4.refs_4_
  21.3 0.0 collective-permute-done.5.refs_5_
  21.3 0.0 collective-permute-done.6.refs_6_
  21.3 1.6 %collective-permute-done.7.refs_7_ = bf16[96,512]{1,0:T(8,128)(2,1)S(1)} collective-permute-done((bf16[96,512]{1,0:T(8,128)(2,1)S(1)}, bf16[96,512]{1,0:T(8,128)(2,1)S(1)}, u32[]{:S(2)}, u32[]{:S(2)}) %collective-permute-start.7) | collective-permute-done | bytes 98336 | tf_op jit(solution)/shard_map/ppermute | solution.py:387
  23.0 1.3 %relay.1 = (bf16[512,256]{1,0:T(8,128)(2,1)S(1)}, bf16[512,256]{1,0:T(8,128)(2,1)S(1)}, s32[1,512]{1,0:T(1,128)S(1)}, s32[8,128]{1,0:T(8,128)S(1)}, bf16[80,1280...) custom-call(s32[1]{0:T(128)} %bitcast.12.me_ref, ...), custom_call_target="tpu_custom_call", output_to_operand_aliasing={{4}: (9, {}), {5}: (10, {}), {6}: (11, {}), {7}: (12, {}), ... | custom-call | tf_op jit(solution)/shard_map/relay/pallas_call | solution.py:208
  24.2 0.1 collective-permute-start.11
  24.3 3.0 %collective-permute-start.8 = (bf16[80,1280]{1,0:T(8,128)(2,1)S(1)}, bf16[80,1280]{1,0:T(8,128)(2,1)S(1)}, u32[]{:S(2)}, u32[]{:S(2)}) collective-permute-start(bf16[80,1280]{1,0:T(8,128)(2,1)S(1)} %get-tuple-element.84), channel_id=1, source_target_pairs={{0,2},{2,4},{4,6},{6,8},{8,10},{10,12},{12,14},{14,0},{1,3},{3,5},... | collective-permute-start | bytes 614408 | tf_op jit(solution)/shard_map/ppermute | solution.py:387
  27.3 1.3 %collective-permute-start.14 = (bf16[80,1280]{1,0:T(8,128)(2,1)S(1)}, bf16[80,1280]{1,0:T(8,128)(2,1)S(1)}, u32[]{:S(2)}, u32[]{:S(2)}) collective-permute-start(bf16[80,1280]{1,0:T(8,128)(2,1)S(1)} %get-tuple-element.90), channel_id=1, source_target_pairs={{0,14},{2,0},{4,2},{6,4},{8,6},{10,8},{12,10},{14,12},{1,15},{3,1}... | collective-permute-start | bytes 614408 | tf_op jit(solution)/shard_map/ppermute | solution.py:387
  28.6 0.7 collective-permute-start.9
  29.3 3.8 %collective-permute-start.10 = (bf16[80,1280]{1,0:T(8,128)(2,1)S(1)}, bf16[80,1280]{1,0:T(8,128)(2,1)S(1)}, u32[]{:S(2)}, u32[]{:S(2)}) collective-permute-start(bf16[80,1280]{1,0:T(8,128)(2,1)S(1)} %get-tuple-element.86), channel_id=1, source_target_pairs={{0,6},{2,8},{4,10},{6,12},{8,14},{10,0},{12,2},{14,4},{1,7},{3,9},... | collective-permute-start | bytes 614408 | tf_op jit(solution)/shard_map/ppermute | solution.py:387
  33.1 1.8 %collective-permute-done.11.refs_4_ = bf16[80,1280]{1,0:T(8,128)(2,1)S(1)} collective-permute-done((bf16[80,1280]{1,0:T(8,128)(2,1)S(1)}, bf16[80,1280]{1,0:T(8,128)(2,1)S(1)}, u32[]{:S(2)}, u32[]{:S(2)}) %collective-permute-start.11) | collective-permute-done | bytes 204832 | tf_op jit(solution)/shard_map/ppermute | solution.py:387
  34.9 14.7 %collective-permute-start.15 = (bf16[512,256]{1,0:T(8,128)(2,1)S(1)}, bf16[512,256]{1,0:T(8,128)(2,1)S(1)}, u32[]{:S(2)}, u32[]{:S(2)}) collective-permute-start(bf16[512,256]{1,0:T(8,128)(2,1)S(1)} %get-tuple-element.95.refs_11_), channel_id=1, source_target_pairs={{0,2},{2,0},{4,6},{6,4},{8,10},{10,8},{12,14},{14,12},{1,3},{3,1},... | collective-permute-start | bytes 786440 | tf_op jit(solution)/shard_map/ppermute | solution.py:421
  49.6 0.0 collective-permute-done.8.refs_1_
  49.6 1.9 %collective-permute-start.16 = (bf16[512,256]{1,0:T(8,128)(2,1)S(1)}, bf16[512,256]{1,0:T(8,128)(2,1)S(1)}, u32[]{:S(2)}, u32[]{:S(2)}) collective-permute-start(bf16[512,256]{1,0:T(8,128)(2,1)S(1)} %get-tuple-element.94.refs_8_), channel_id=1, source_target_pairs={{0,2},{2,4},{4,6},{6,8},{8,10},{10,12},{12,14},{1,3},{3,5},{5,7},{... | collective-permute-start | bytes 786440 | tf_op jit(solution)/shard_map/ppermute | solution.py:382
  51.5 0.0 collective-permute-done.14.refs_7_
  51.5 1.9 %collective-permute-start.17 = (bf16[512,256]{1,0:T(8,128)(2,1)S(1)}, bf16[512,256]{1,0:T(8,128)(2,1)S(1)}, u32[]{:S(2)}, u32[]{:S(2)}) collective-permute-start(bf16[512,256]{1,0:T(8,128)(2,1)S(1)} %get-tuple-element.95.refs_11_), channel_id=1, source_target_pairs={{0,4},{4,8},{8,12},{1,5},{5,9},{9,13},{16,20},{20,24},{24,28},{17,... | collective-permute-start | bytes 786440 | tf_op jit(solution)/shard_map/ppermute | solution.py:420
  53.4 0.0 collective-permute-done.9.refs_2_
  53.5 1.7 %collective-permute-start.12 = (bf16[80,1280]{1,0:T(8,128)(2,1)S(1)}, bf16[80,1280]{1,0:T(8,128)(2,1)S(1)}, u32[]{:S(2)}, u32[]{:S(2)}) collective-permute-start(bf16[80,1280]{1,0:T(8,128)(2,1)S(1)} %get-tuple-element.88), channel_id=1, source_target_pairs={{0,10},{2,12},{4,14},{6,0},{8,2},{10,4},{12,6},{14,8},{1,11},{3,13... | collective-permute-start | bytes 614408 | tf_op jit(solution)/shard_map/ppermute | solution.py:387
  55.1 0.0 collective-permute-done.10.refs_3_
  55.1 0.5 collective-permute-start.13
  55.6 0.5 slice.9
  56.8 4.0 %collective-permute-done.12.refs_5_ = bf16[80,1280]{1,0:T(8,128)(2,1)S(1)} collective-permute-done((bf16[80,1280]{1,0:T(8,128)(2,1)S(1)}, bf16[80,1280]{1,0:T(8,128)(2,1)S(1)}, u32[]{:S(2)}, u32[]{:S(2)}) %collective-permute-start.12) | collective-permute-done | bytes 204832 | tf_op jit(solution)/shard_map/ppermute | solution.py:387
  60.7 4.0 %collective-permute-done.13.refs_6_ = bf16[80,1280]{1,0:T(8,128)(2,1)S(1)} collective-permute-done((bf16[80,1280]{1,0:T(8,128)(2,1)S(1)}, bf16[80,1280]{1,0:T(8,128)(2,1)S(1)}, u32[]{:S(2)}, u32[]{:S(2)}) %collective-permute-start.13) | collective-permute-done | bytes 204832 | tf_op jit(solution)/shard_map/ppermute | solution.py:387
  64.8 0.0 collective-permute-done.15.refs_9_
  64.8 2.9 %collective-permute-done.16.refs_10_ = bf16[512,256]{1,0:T(8,128)(2,1)S(1)} collective-permute-done((bf16[512,256]{1,0:T(8,128)(2,1)S(1)}, bf16[512,256]{1,0:T(8,128)(2,1)S(1)}, u32[]{:S(2)}, u32[]{:S(2)}) %collective-permute-start.16) | collective-permute-done | bytes 262176 | tf_op jit(solution)/shard_map/ppermute | solution.py:382
  67.6 0.0 collective-permute-done.17.refs_12_
  67.6 0.0 copy-done.7
  67.6 0.0 copy-start.4
  67.6 0.0 copy-start.6
  67.7 0.0 copy-start.8
  67.7 7.7 %attend.1 = bf16[512,1280]{1,0:T(8,128)(2,1)} custom-call(s32[1]{0:T(128)} %bitcast.12.me_ref, s32[4,4]{1,0:T(4,128)S(1)} %copy-done.7, s32[1,512]{1,0:T(1,128)S(1)} %get-tuple-element.82.code_ref, bf16[80,1280]{1,0:T(8,128)(2,1)S(1)} %get-tuple-element.83.refs_0_, bf16[80,1280]{1,0:T(8,128)(2,1)S(1)} %collective-permute-done.8.refs_1_, ...), custom_call_target="tpu_custom_call" | custom-call | tf_op jit(solution)/shard_map/attend/pallas_call | solution.py:328
  75.4 0.0 copy-done.3
  75.4 0.0 copy-done.4
  75.4 0.2 conditional.1
  (4 shorter events, 0.0 us)
Async XLA Ops:
  0.0 19.3 %copy-start.1 = (bf16[512,1280]{1,0:T(8,128)(2,1)S(1)}, bf16[512,1280]{1,0:T(8,128)(2,1)}, u32[]{:S(2)}) copy-start(bf16[512,1280]{1,0:T(8,128)(2,1)} %q_ref.3) | copy-start | bytes 3932164
  2.8 7.3 %collective-permute-start.1 = (bf16[96,512]{1,0:T(8,128)(2,1)S(1)}, bf16[96,512]{1,0:T(8,128)(2,1)S(1)}, u32[]{:S(2)}, u32[]{:S(2)}) collective-permute-start(bf16[96,512]{1,0:T(8,128)(2,1)S(1)} %get-tuple-element.64), channel_id=1, source_target_pairs={{0,2},{2,4},{4,6},{6,8},{8,10},{10,12},{12,14},{14,0},{1,3},{3,5},... | collective-permute-start | bytes 294920 | tf_op jit(solution)/shard_map/ppermute | solution.py:387
  4.4 7.1 %collective-permute-start.2 = (bf16[96,512]{1,0:T(8,128)(2,1)S(1)}, bf16[96,512]{1,0:T(8,128)(2,1)S(1)}, u32[]{:S(2)}, u32[]{:S(2)}) collective-permute-start(bf16[96,512]{1,0:T(8,128)(2,1)S(1)} %get-tuple-element.65), channel_id=1, source_target_pairs={{0,4},{2,6},{4,8},{6,10},{8,12},{10,14},{12,0},{14,2},{1,5},{3,7},... | collective-permute-start | bytes 294920 | tf_op jit(solution)/shard_map/ppermute | solution.py:387
  5.9 15.4 %collective-permute-start.3 = (bf16[96,512]{1,0:T(8,128)(2,1)S(1)}, bf16[96,512]{1,0:T(8,128)(2,1)S(1)}, u32[]{:S(2)}, u32[]{:S(2)}) collective-permute-start(bf16[96,512]{1,0:T(8,128)(2,1)S(1)} %get-tuple-element.66), channel_id=1, source_target_pairs={{0,6},{2,8},{4,10},{6,12},{8,14},{10,0},{12,2},{14,4},{1,7},{3,9},... | collective-permute-start | bytes 294920 | tf_op jit(solution)/shard_map/ppermute | solution.py:387
  7.1 14.2 %collective-permute-start.4 = (bf16[96,512]{1,0:T(8,128)(2,1)S(1)}, bf16[96,512]{1,0:T(8,128)(2,1)S(1)}, u32[]{:S(2)}, u32[]{:S(2)}) collective-permute-start(bf16[96,512]{1,0:T(8,128)(2,1)S(1)} %get-tuple-element.67), channel_id=1, source_target_pairs={{0,8},{2,10},{4,12},{6,14},{8,0},{10,2},{12,4},{14,6},{1,9},{3,11}... | collective-permute-start | bytes 294920 | tf_op jit(solution)/shard_map/ppermute | solution.py:387
  8.8 12.5 %collective-permute-start.5 = (bf16[96,512]{1,0:T(8,128)(2,1)S(1)}, bf16[96,512]{1,0:T(8,128)(2,1)S(1)}, u32[]{:S(2)}, u32[]{:S(2)}) collective-permute-start(bf16[96,512]{1,0:T(8,128)(2,1)S(1)} %get-tuple-element.68), channel_id=1, source_target_pairs={{0,10},{2,12},{4,14},{6,0},{8,2},{10,4},{12,6},{14,8},{1,11},{3,13... | collective-permute-start | bytes 294920 | tf_op jit(solution)/shard_map/ppermute | solution.py:387
  10.1 11.2 %collective-permute-start.6 = (bf16[96,512]{1,0:T(8,128)(2,1)S(1)}, bf16[96,512]{1,0:T(8,128)(2,1)S(1)}, u32[]{:S(2)}, u32[]{:S(2)}) collective-permute-start(bf16[96,512]{1,0:T(8,128)(2,1)S(1)} %get-tuple-element.69), channel_id=1, source_target_pairs={{0,12},{2,14},{4,0},{6,2},{8,4},{10,6},{12,8},{14,10},{1,13},{3,15... | collective-permute-start | bytes 294920 | tf_op jit(solution)/shard_map/ppermute | solution.py:387
  11.5 11.5 %collective-permute-start.7 = (bf16[96,512]{1,0:T(8,128)(2,1)S(1)}, bf16[96,512]{1,0:T(8,128)(2,1)S(1)}, u32[]{:S(2)}, u32[]{:S(2)}) collective-permute-start(bf16[96,512]{1,0:T(8,128)(2,1)S(1)} %get-tuple-element.70), channel_id=1, source_target_pairs={{0,14},{2,0},{4,2},{6,4},{8,6},{10,8},{12,10},{14,12},{1,15},{3,1}... | collective-permute-start | bytes 294920 | tf_op jit(solution)/shard_map/ppermute | solution.py:387
  21.3 46.3 %copy-start.7 = (s32[4,4]{1,0:T(4,128)S(1)}, s32[4,4]{1,0:T(4,128)}, u32[]{:S(2)}) copy-start(s32[4,4]{1,0:T(4,128)} %anc_ref.1) | copy-start | bytes 196
  24.2 10.6 %collective-permute-start.11 = (bf16[80,1280]{1,0:T(8,128)(2,1)S(1)}, bf16[80,1280]{1,0:T(8,128)(2,1)S(1)}, u32[]{:S(2)}, u32[]{:S(2)}) collective-permute-start(bf16[80,1280]{1,0:T(8,128)(2,1)S(1)} %get-tuple-element.87), channel_id=1, source_target_pairs={{0,8},{2,10},{4,12},{6,14},{8,0},{10,2},{12,4},{14,6},{1,9},{3,11}... | collective-permute-start | bytes 614408 | tf_op jit(solution)/shard_map/ppermute | solution.py:387
  24.3 25.3 %collective-permute-start.8 = (bf16[80,1280]{1,0:T(8,128)(2,1)S(1)}, bf16[80,1280]{1,0:T(8,128)(2,1)S(1)}, u32[]{:S(2)}, u32[]{:S(2)}) collective-permute-start(bf16[80,1280]{1,0:T(8,128)(2,1)S(1)} %get-tuple-element.84), channel_id=1, source_target_pairs={{0,2},{2,4},{4,6},{6,8},{8,10},{10,12},{12,14},{14,0},{1,3},{3,5},... | collective-permute-start | bytes 614408 | tf_op jit(solution)/shard_map/ppermute | solution.py:387
  27.3 24.2 %collective-permute-start.14 = (bf16[80,1280]{1,0:T(8,128)(2,1)S(1)}, bf16[80,1280]{1,0:T(8,128)(2,1)S(1)}, u32[]{:S(2)}, u32[]{:S(2)}) collective-permute-start(bf16[80,1280]{1,0:T(8,128)(2,1)S(1)} %get-tuple-element.90), channel_id=1, source_target_pairs={{0,14},{2,0},{4,2},{6,4},{8,6},{10,8},{12,10},{14,12},{1,15},{3,1}... | collective-permute-start | bytes 614408 | tf_op jit(solution)/shard_map/ppermute | solution.py:387
  28.6 24.9 %collective-permute-start.9 = (bf16[80,1280]{1,0:T(8,128)(2,1)S(1)}, bf16[80,1280]{1,0:T(8,128)(2,1)S(1)}, u32[]{:S(2)}, u32[]{:S(2)}) collective-permute-start(bf16[80,1280]{1,0:T(8,128)(2,1)S(1)} %get-tuple-element.85), channel_id=1, source_target_pairs={{0,4},{2,6},{4,8},{6,10},{8,12},{10,14},{12,0},{14,2},{1,5},{3,7},... | collective-permute-start | bytes 614408 | tf_op jit(solution)/shard_map/ppermute | solution.py:387
  29.3 25.9 %collective-permute-start.10 = (bf16[80,1280]{1,0:T(8,128)(2,1)S(1)}, bf16[80,1280]{1,0:T(8,128)(2,1)S(1)}, u32[]{:S(2)}, u32[]{:S(2)}) collective-permute-start(bf16[80,1280]{1,0:T(8,128)(2,1)S(1)} %get-tuple-element.86), channel_id=1, source_target_pairs={{0,6},{2,8},{4,10},{6,12},{8,14},{10,0},{12,2},{14,4},{1,7},{3,9},... | collective-permute-start | bytes 614408 | tf_op jit(solution)/shard_map/ppermute | solution.py:387
  34.9 29.9 %collective-permute-start.15 = (bf16[512,256]{1,0:T(8,128)(2,1)S(1)}, bf16[512,256]{1,0:T(8,128)(2,1)S(1)}, u32[]{:S(2)}, u32[]{:S(2)}) collective-permute-start(bf16[512,256]{1,0:T(8,128)(2,1)S(1)} %get-tuple-element.95.refs_11_), channel_id=1, source_target_pairs={{0,2},{2,0},{4,6},{6,4},{8,10},{10,8},{12,14},{14,12},{1,3},{3,1},... | collective-permute-start | bytes 786440 | tf_op jit(solution)/shard_map/ppermute | solution.py:421
  49.6 18.0 %collective-permute-start.16 = (bf16[512,256]{1,0:T(8,128)(2,1)S(1)}, bf16[512,256]{1,0:T(8,128)(2,1)S(1)}, u32[]{:S(2)}, u32[]{:S(2)}) collective-permute-start(bf16[512,256]{1,0:T(8,128)(2,1)S(1)} %get-tuple-element.94.refs_8_), channel_id=1, source_target_pairs={{0,2},{2,4},{4,6},{6,8},{8,10},{10,12},{12,14},{1,3},{3,5},{5,7},{... | collective-permute-start | bytes 786440 | tf_op jit(solution)/shard_map/ppermute | solution.py:382
  51.5 16.1 %collective-permute-start.17 = (bf16[512,256]{1,0:T(8,128)(2,1)S(1)}, bf16[512,256]{1,0:T(8,128)(2,1)S(1)}, u32[]{:S(2)}, u32[]{:S(2)}) collective-permute-start(bf16[512,256]{1,0:T(8,128)(2,1)S(1)} %get-tuple-element.95.refs_11_), channel_id=1, source_target_pairs={{0,4},{4,8},{8,12},{1,5},{5,9},{9,13},{16,20},{20,24},{24,28},{17,... | collective-permute-start | bytes 786440 | tf_op jit(solution)/shard_map/ppermute | solution.py:420
  53.5 7.3 %collective-permute-start.12 = (bf16[80,1280]{1,0:T(8,128)(2,1)S(1)}, bf16[80,1280]{1,0:T(8,128)(2,1)S(1)}, u32[]{:S(2)}, u32[]{:S(2)}) collective-permute-start(bf16[80,1280]{1,0:T(8,128)(2,1)S(1)} %get-tuple-element.88), channel_id=1, source_target_pairs={{0,10},{2,12},{4,14},{6,0},{8,2},{10,4},{12,6},{14,8},{1,11},{3,13... | collective-permute-start | bytes 614408 | tf_op jit(solution)/shard_map/ppermute | solution.py:387
  55.1 9.6 %collective-permute-start.13 = (bf16[80,1280]{1,0:T(8,128)(2,1)S(1)}, bf16[80,1280]{1,0:T(8,128)(2,1)S(1)}, u32[]{:S(2)}, u32[]{:S(2)}) collective-permute-start(bf16[80,1280]{1,0:T(8,128)(2,1)S(1)} %get-tuple-element.89), channel_id=1, source_target_pairs={{0,12},{2,14},{4,0},{6,2},{8,4},{10,6},{12,8},{14,10},{1,13},{3,15... | collective-permute-start | bytes 614408 | tf_op jit(solution)/shard_map/ppermute | solution.py:387
  67.6 7.8 %copy-start.3 = (bf16[512,256]{1,0:T(8,128)(2,1)S(1)}, bf16[512,256]{1,0:T(8,128)(2,1)}, u32[]{:S(2)}) copy-start(bf16[512,256]{1,0:T(8,128)(2,1)} %k_ref.1) | copy-start | bytes 786436
  67.6 7.8 %copy-start.4 = (bf16[512,256]{1,0:T(8,128)(2,1)S(1)}, bf16[512,256]{1,0:T(8,128)(2,1)}, u32[]{:S(2)}) copy-start(bf16[512,256]{1,0:T(8,128)(2,1)} %v_ref.1) | copy-start | bytes 786436
  67.6 7.8 %copy-start.6 = (s32[512]{0:T(512)S(1)}, s32[512]{0:T(512)}, u32[]{:S(2)}) copy-start(s32[512]{0:T(512)} %dest_ref.1) | copy-start | bytes 6148
  67.7 7.8 %copy-start.8 = (s32[512]{0:T(512)S(1)}, s32[512]{0:T(512)}, u32[]{:S(2)}) copy-start(s32[512]{0:T(512)} %slot_ref.1) | copy-start | bytes 6148

commit v10 on v9

--- a/solution.py
+++ b/solution.py
@@ -146,11 +146,9 @@
 
 def relay_kernel(shards, unit, me_ref, *refs):
     got = refs[:shards]
-    k_out, v_out, codes_ref, crowd_ref = refs[2 * shards : 2 * shards + 4]
-    blocks = refs[2 * shards + 4 : 3 * shards + 4]
-    tails, sems = refs[3 * shards + 4 :]
-    count, half = k_out.shape
-    kv_width = 2 * half
+    blocks = refs[2 * shards : 3 * shards]
+    tails, sems = refs[3 * shards :]
+    kv_width = got[0].shape[1]
     width = tails.shape[2]
     cuts = strips(width, kv_width)
     meta_at = cuts[-1][1] - cuts[-1][0]
@@ -182,6 +180,15 @@
         copies.append(pltpu.make_async_copy(tails.at[r], blocks[r].at[pl.ds(unit, 2 * PIECE), :], sems.at[r]))
         copies[-1].start()
 
+    for c in copies:
+        c.wait()
+
+
+def place_kernel(shards, unit, *refs):
+    got, (k_out, v_out, codes_ref, crowd_ref) = refs[:shards], refs[shards:]
+    count, half = k_out.shape
+    meta_at = got[0].shape[1] - 4 * unit
+    metas = [ref[got[0].shape[0] - PIECE :, meta_at:].astype(jnp.float32) for ref in got]
     code = jnp.concatenate([decode(meta[0:1, 0:unit], meta[1:2, 0:unit]) for meta in metas], axis=1)
     codes_ref[...] = code
     rows = jnp.concatenate([ref[0:unit, 0:half] for ref in got], axis=0)
@@ -197,38 +204,43 @@
         most = jnp.maximum(most, jnp.sum(flags, axis=1, keepdims=True))
     most = jnp.maximum(most, jnp.max(by_dest, axis=1, keepdims=True))
     crowd_ref[...] = jnp.broadcast_to((most > 1.5).astype(jnp.int32), crowd_ref.shape)
-    for c in copies:
-        c.wait()
+
+
+def place(got, unit):
+    shards = len(got)
+    count, half = shards * unit, got[0].shape[1] // 2
+    shapes = [((count, half), jnp.bfloat16)] * 2 + [((1, count), jnp.int32), ((8, 128), jnp.int32)]
+    return pl.pallas_call(
+        functools.partial(place_kernel, shards, unit),
+        out_shape=[jax.ShapeDtypeStruct(*shape) for shape in shapes],
+        in_specs=[VM] * shards,
+        out_specs=[VM] * 4,
+        compiler_params=params(10),
+        cost_estimate=light(),
+        name="place",
+    )(*got)
 
 
 def relay(me, got, q_blocks, unit):
     shards = len(got)
-    count = shards * unit
     shape = q_blocks[0].shape
-    outs = pl.pallas_call(
+    return pl.pallas_call(
         functools.partial(relay_kernel, shards, unit),
-        out_shape=[
-            jax.ShapeDtypeStruct((count, got[0].shape[1] // 2), jnp.bfloat16),
-            jax.ShapeDtypeStruct((count, got[0].shape[1] // 2), jnp.bfloat16),
-            jax.ShapeDtypeStruct((1, count), jnp.int32),
-            jax.ShapeDtypeStruct((8, 128), jnp.int32),
-        ]
-        + [jax.ShapeDtypeStruct(shape, jnp.bfloat16)] * shards,
+        out_shape=[jax.ShapeDtypeStruct(shape, jnp.bfloat16)] * shards,
         in_specs=[SM] + [VM] * shards + [HB] * shards,
-        out_specs=[VM] * 4 + [HB] * shards,
+        out_specs=[HB] * shards,
         scratch_shapes=[
             pltpu.VMEM((shards, 2 * PIECE, shape[1]), jnp.bfloat16),
             pltpu.SemaphoreType.DMA((shards,)),
         ],
-        input_output_aliases={1 + shards + r: 4 + r for r in range(shards)},
+        input_output_aliases={1 + shards + r: r for r in range(shards)},
         compiler_params=params(10),
         cost_estimate=light(),
         name="relay",
     )(me, *got, *q_blocks)
-    return *outs[:4], outs[4:]
-
-
-def attend_core(shard, anc_ref, q_pl, kv_all, out_ref, groups):
+
+
+def attend_core(shard, anc_ref, q_pl, kv_all, out_ref, groups, flush=None):
     count, width = out_ref.shape
     block_count = anc_ref.shape[0]
     size = count // block_count
@@ -264,6 +276,8 @@
         output = (matmul(expo, v) * inverse).astype(jnp.bfloat16)
         for h, c in enumerate(columns(g)):
             out_ref[b * size : (b + 1) * size, c : c + HEAD_SIZE] = output[h * size : (h + 1) * size]
+        if flush is not None and g == groups - 1:
+            flush(b)
 
     tiles = [(b, g) for b in range(block_count) for g in range(groups)]
     scores, held = scores_of(*tiles[0]), None
@@ -278,7 +292,7 @@
 
 def attend_kernel(shards, unit, groups, me_ref, anc_ref, code_ref, *refs):
     got, (own_k, own_v, prior_k, beside_v, prior_v) = refs[:shards], refs[shards : shards + 5]
-    out_ref, raw, q_pl, kv_all, sems = refs[shards + 5 :]
+    out_hbm, raw, q_pl, kv_all, out_ref, sems, out_sems = refs[shards + 5 :]
     count, width = out_ref.shape
     half = own_k.shape[1]
     kv_width = 2 * half
@@ -318,7 +332,16 @@
         rows = jnp.concatenate([end[PIECE:, start : start + kv_width] for end in ends], axis=0)
         rows = matmul(select_rows(code, 1, count), rows.astype(jnp.bfloat16))
         kv_all[j * count : (j + 1) * count, :] += rows.astype(jnp.bfloat16)
-    attend_core(me_ref[0], anc_ref, q_pl, kv_all, out_ref, groups)
+    written = []
+
+    def flush(b):
+        rows = pl.ds(b * (count // anc_ref.shape[0]), count // anc_ref.shape[0])
+        written.append(pltpu.make_async_copy(out_ref.at[rows, :], out_hbm.at[rows, :], out_sems.at[b]))
+        written[-1].start()
+
+    attend_core(me_ref[0], anc_ref, q_pl, kv_all, out_ref, groups, flush)
+    for c in written:
+        c.wait()
 
 
 def attend(me, ancestors, codes, got, own_k, own_v, prior_k, beside_v, prior_v, unit):
@@ -329,12 +352,14 @@
         functools.partial(attend_kernel, shards, unit, groups),
         out_shape=jax.ShapeDtypeStruct((count, width), jnp.bfloat16),
         in_specs=[SM, SM, VM] + [VM] * shards + [HB] * 3 + [VM, VM],
-        out_specs=VM,
+        out_specs=HB,
         scratch_shapes=[
             pltpu.VMEM((count + shards * PIECE, width), jnp.bfloat16),
             pltpu.VMEM((count, width), jnp.bfloat16),
             pltpu.VMEM((2 * count, 2 * own_k.shape[1]), jnp.bfloat16),
+            pltpu.VMEM((count, width), jnp.bfloat16),
             pltpu.SemaphoreType.DMA((3,)),
+            pltpu.SemaphoreType.DMA((ancestors.shape[0],)),
         ],
         compiler_params=params(28),
         cost_estimate=light(),
@@ -413,8 +438,9 @@
     kv_blocks, index = pack_kv(me, dest_shard, dest_slot, keys, values, queries, shards, unit)
     got_kv = [kv_blocks[0]] + [rotate(kv_blocks[r], r) for r in range(1, shards)]
     q_blocks = pack_q(after(index, got_kv[1]), queries, shards, unit)
-    own_k, beside_v, codes, crowd, q_blocks = relay(me, got_kv, q_blocks, unit)
+    q_blocks = relay(me, got_kv, q_blocks, unit)
     got_q = [q_blocks[0]] + [rotate(q_blocks[r], r) for r in range(1, shards)]
+    own_k, beside_v, codes, crowd = place([after(got_kv[0], got_q[4]), *got_kv[1:]], unit)
     prior_k = from_behind(after(own_k, got_q[1]))
     to_v = after(beside_v, got_q[7])
     prior_v = lax.ppermute(to_v, "seq", [(i, i + 2) for i in range(0, shards - 2, 2)])

time: 77 us -> 76.7 us (level)
  the two profiles are of different devices: /device:TPU:16 before, /device:TPU:30 now
where the time goes in v10:
time: 76.7 us; the launch traced here: 76.5 us
  starting transfers between devices  33.4 us (44%)
  waiting for transfers between devices  27.9 us (36%)
  Pallas kernels  13.4 us (17%)
  between operations  1.01 us (1%)
    ppermute x14, waiting for transfers between devices, rotate(): return lax.ppermute(block, 'seq', [(i, (i + r) % n) for i in range(n)])  27.9 us
    ppermute x14, starting transfers between devices, rotate(): return lax.ppermute(block, 'seq', [(i, (i + r) % n) for i in range(n)])  27.1 us
    pallas_call x1, Pallas kernels, attend(): pl.pallas_call(functools.partial(attend_kernel, shards, unit, groups), ou...  7.43 us
    ppermute x1, starting transfers between devices, relay_plan(): lax.ppermute(after(beside_v, got_q[4]), 'seq', [(i, i ^ 1) for i in range...  4.34 us
    pallas_call x1, Pallas kernels, pack_kv(): pl.pallas_call(functools.partial(pack_kv_kernel, shards, unit), out_shape...  2.8 us
    pallas_call x1, Pallas kernels, pack_q(): pl.pallas_call(functools.partial(pack_q_kernel, unit), out_shape=[jax.Sha...  1.92 us
  transfers between devices with their start and end apart: 17, of which 4 were waited for; matrix products, arithmetic and copies ran while one was open for 1% of the time, Pallas kernels for 3%

profile of v10, /device:TPU:30, one launch (start us, length us, event | category | flops | bytes accessed | tf_op | source)
XLA Modules:
  0.0 76.5 jit_solution(4456883758533113912)
XLA Ops:
  0.0 2.8 %pack_kv.1 = (bf16[96,512]{1,0:T(8,128)(2,1)S(1)}, bf16[96,512]{1,0:T(8,128)(2,1)S(1)}, bf16[96,512]{1,0:T(8,128)(2,1)S(1)}, bf16[96,512]{1,0:T(8,128)(2,1)S(1)}...) custom-call(s32[1]{0:T(128)} %bitcast.12.me_ref, ...), custom_call_target="tpu_custom_call" | custom-call | tf_op jit(solution)/shard_map/pack_kv/pallas_call | solution.py:105
  2.8 0.2 collective-permute-start.1
  3.1 1.6 %collective-permute-start.2 = (bf16[96,512]{1,0:T(8,128)(2,1)S(1)}, bf16[96,512]{1,0:T(8,128)(2,1)S(1)}, u32[]{:S(2)}, u32[]{:S(2)}) collective-permute-start(bf16[96,512]{1,0:T(8,128)(2,1)S(1)} %get-tuple-element.66), channel_id=1, source_target_pairs={{0,4},{2,6},{4,8},{6,10},{8,12},{10,14},{12,0},{14,2},{1,5},{3,7},... | collective-permute-start | bytes 294920 | tf_op jit(solution)/shard_map/ppermute | solution.py:412
  4.6 1.6 %collective-permute-start.3 = (bf16[96,512]{1,0:T(8,128)(2,1)S(1)}, bf16[96,512]{1,0:T(8,128)(2,1)S(1)}, u32[]{:S(2)}, u32[]{:S(2)}) collective-permute-start(bf16[96,512]{1,0:T(8,128)(2,1)S(1)} %get-tuple-element.67), channel_id=1, source_target_pairs={{0,6},{2,8},{4,10},{6,12},{8,14},{10,0},{12,2},{14,4},{1,7},{3,9},... | collective-permute-start | bytes 294920 | tf_op jit(solution)/shard_map/ppermute | solution.py:412
  6.2 1.2 %collective-permute-start.4 = (bf16[96,512]{1,0:T(8,128)(2,1)S(1)}, bf16[96,512]{1,0:T(8,128)(2,1)S(1)}, u32[]{:S(2)}, u32[]{:S(2)}) collective-permute-start(bf16[96,512]{1,0:T(8,128)(2,1)S(1)} %get-tuple-element.68), channel_id=1, source_target_pairs={{0,8},{2,10},{4,12},{6,14},{8,0},{10,2},{12,4},{14,6},{1,9},{3,11}... | collective-permute-start | bytes 294920 | tf_op jit(solution)/shard_map/ppermute | solution.py:412
  7.5 1.8 %collective-permute-start.5 = (bf16[96,512]{1,0:T(8,128)(2,1)S(1)}, bf16[96,512]{1,0:T(8,128)(2,1)S(1)}, u32[]{:S(2)}, u32[]{:S(2)}) collective-permute-start(bf16[96,512]{1,0:T(8,128)(2,1)S(1)} %get-tuple-element.69), channel_id=1, source_target_pairs={{0,10},{2,12},{4,14},{6,0},{8,2},{10,4},{12,6},{14,8},{1,11},{3,13... | collective-permute-start | bytes 294920 | tf_op jit(solution)/shard_map/ppermute | solution.py:412
  9.3 0.0 collective-permute-done.1.refs_1_
  9.3 1.4 %collective-permute-start.6 = (bf16[96,512]{1,0:T(8,128)(2,1)S(1)}, bf16[96,512]{1,0:T(8,128)(2,1)S(1)}, u32[]{:S(2)}, u32[]{:S(2)}) collective-permute-start(bf16[96,512]{1,0:T(8,128)(2,1)S(1)} %get-tuple-element.70), channel_id=1, source_target_pairs={{0,12},{2,14},{4,0},{6,2},{8,4},{10,6},{12,8},{14,10},{1,13},{3,15... | collective-permute-start | bytes 294920 | tf_op jit(solution)/shard_map/ppermute | solution.py:412
  10.6 0.0 collective-permute-done.2.refs_2_
  10.6 0.5 collective-permute-start.7
  11.1 0.0 copy-done.1
  11.1 1.9 %pack_q.1 = (bf16[80,1280]{1,0:T(8,128)(2,1)S(1)}, bf16[80,1280]{1,0:T(8,128)(2,1)S(1)}, bf16[80,1280]{1,0:T(8,128)(2,1)S(1)}, bf16[80,1280]{1,0:T(8,128)(2,1)S(...) custom-call(s32[1,512]{1,0:T(1,128)S(1)} %get-tuple-element.73.index, ...), custom_call_target="tpu_custom_call" | custom-call | tf_op jit(solution)/shard_map/pack_q/pallas_call | solution.py:124
  13.0 0.0 collective-permute-done.3.refs_3_
  13.0 9.1 %collective-permute-done.4.refs_4_ = bf16[96,512]{1,0:T(8,128)(2,1)S(1)} collective-permute-done((bf16[96,512]{1,0:T(8,128)(2,1)S(1)}, bf16[96,512]{1,0:T(8,128)(2,1)S(1)}, u32[]{:S(2)}, u32[]{:S(2)}) %collective-permute-start.4) | collective-permute-done | bytes 98336 | tf_op jit(solution)/shard_map/ppermute | solution.py:412
  22.1 1.2 %collective-permute-done.5.refs_5_ = bf16[96,512]{1,0:T(8,128)(2,1)S(1)} collective-permute-done((bf16[96,512]{1,0:T(8,128)(2,1)S(1)}, bf16[96,512]{1,0:T(8,128)(2,1)S(1)}, u32[]{:S(2)}, u32[]{:S(2)}) %collective-permute-start.5) | collective-permute-done | bytes 98336 | tf_op jit(solution)/shard_map/ppermute | solution.py:412
  23.2 0.0 collective-permute-done.6.refs_6_
  23.2 0.0 collective-permute-done.7.refs_7_
  23.3 0.8 %relay.1 = (bf16[80,1280]{1,0:T(8,128)(2,1)S(1)}, bf16[80,1280]{1,0:T(8,128)(2,1)S(1)}, bf16[80,1280]{1,0:T(8,128)(2,1)S(1)}, bf16[80,1280]{1,0:T(8,128)(2,1)S(1...) custom-call(s32[1]{0:T(128)} %bitcast.12.me_ref, ...), custom_call_target="tpu_custom_call", output_to_operand_aliasing={{0}: (9, {}), {1}: (10, {}), {2}: (11, {}), {3}: (12, {}), ... | custom-call | tf_op jit(solution)/shard_map/relay/pallas_call | solution.py:227
  24.1 1.7 %collective-permute-start.8 = (bf16[80,1280]{1,0:T(8,128)(2,1)S(1)}, bf16[80,1280]{1,0:T(8,128)(2,1)S(1)}, u32[]{:S(2)}, u32[]{:S(2)}) collective-permute-start(bf16[80,1280]{1,0:T(8,128)(2,1)S(1)} %get-tuple-element.82), channel_id=1, source_target_pairs={{0,8},{2,10},{4,12},{6,14},{8,0},{10,2},{12,4},{14,6},{1,9},{3,11}... | collective-permute-start | bytes 614408 | tf_op jit(solution)/shard_map/ppermute | solution.py:412
  25.7 0.9 %collective-permute-start.9 = (bf16[80,1280]{1,0:T(8,128)(2,1)S(1)}, bf16[80,1280]{1,0:T(8,128)(2,1)S(1)}, u32[]{:S(2)}, u32[]{:S(2)}) collective-permute-start(bf16[80,1280]{1,0:T(8,128)(2,1)S(1)} %get-tuple-element.87), channel_id=1, source_target_pairs={{0,2},{2,4},{4,6},{6,8},{8,10},{10,12},{12,14},{14,0},{1,3},{3,5},... | collective-permute-start | bytes 614408 | tf_op jit(solution)/shard_map/ppermute | solution.py:412
  26.6 1.1 %collective-permute-start.14 = (bf16[80,1280]{1,0:T(8,128)(2,1)S(1)}, bf16[80,1280]{1,0:T(8,128)(2,1)S(1)}, u32[]{:S(2)}, u32[]{:S(2)}) collective-permute-start(bf16[80,1280]{1,0:T(8,128)(2,1)S(1)} %get-tuple-element.92), channel_id=1, source_target_pairs={{0,14},{2,0},{4,2},{6,4},{8,6},{10,8},{12,10},{14,12},{1,15},{3,1}... | collective-permute-start | bytes 614408 | tf_op jit(solution)/shard_map/ppermute | solution.py:412
  27.7 2.3 %collective-permute-start.10 = (bf16[80,1280]{1,0:T(8,128)(2,1)S(1)}, bf16[80,1280]{1,0:T(8,128)(2,1)S(1)}, u32[]{:S(2)}, u32[]{:S(2)}) collective-permute-start(bf16[80,1280]{1,0:T(8,128)(2,1)S(1)} %get-tuple-element.88), channel_id=1, source_target_pairs={{0,4},{2,6},{4,8},{6,10},{8,12},{10,14},{12,0},{14,2},{1,5},{3,7},... | collective-permute-start | bytes 614408 | tf_op jit(solution)/shard_map/ppermute | solution.py:412
  30.1 0.0 collective-permute-start.11
  30.1 6.3 %collective-permute-done.8.refs_4_ = bf16[80,1280]{1,0:T(8,128)(2,1)S(1)} collective-permute-done((bf16[80,1280]{1,0:T(8,128)(2,1)S(1)}, bf16[80,1280]{1,0:T(8,128)(2,1)S(1)}, u32[]{:S(2)}, u32[]{:S(2)}) %collective-permute-start.8) | collective-permute-done | bytes 204832 | tf_op jit(solution)/shard_map/ppermute | solution.py:412
  36.4 0.5 place.1
  36.9 4.3 %collective-permute-start.15 = (bf16[512,256]{1,0:T(8,128)(2,1)S(1)}, bf16[512,256]{1,0:T(8,128)(2,1)S(1)}, u32[]{:S(2)}, u32[]{:S(2)}) collective-permute-start(bf16[512,256]{1,0:T(8,128)(2,1)S(1)} %get-tuple-element.97.refs_11_), channel_id=1, source_target_pairs={{0,2},{2,0},{4,6},{6,4},{8,10},{10,8},{12,14},{14,12},{1,3},{3,1},... | collective-permute-start | bytes 786440 | tf_op jit(solution)/shard_map/ppermute | solution.py:447
  41.2 0.0 collective-permute-done.9.refs_1_
  41.3 1.3 %collective-permute-start.16 = (bf16[512,256]{1,0:T(8,128)(2,1)S(1)}, bf16[512,256]{1,0:T(8,128)(2,1)S(1)}, u32[]{:S(2)}, u32[]{:S(2)}) collective-permute-start(bf16[512,256]{1,0:T(8,128)(2,1)S(1)} %get-tuple-element.96.refs_8_), channel_id=1, source_target_pairs={{0,2},{2,4},{4,6},{6,8},{8,10},{10,12},{12,14},{1,3},{3,5},{5,7},{... | collective-permute-start | bytes 786440 | tf_op jit(solution)/shard_map/ppermute | solution.py:407
  42.5 0.0 collective-permute-done.14.refs_7_
  42.6 0.7 collective-permute-start.17
  43.2 0.0 collective-permute-done.10.refs_2_
  43.2 10.8 %collective-permute-start.12 = (bf16[80,1280]{1,0:T(8,128)(2,1)S(1)}, bf16[80,1280]{1,0:T(8,128)(2,1)S(1)}, u32[]{:S(2)}, u32[]{:S(2)}) collective-permute-start(bf16[80,1280]{1,0:T(8,128)(2,1)S(1)} %get-tuple-element.90), channel_id=1, source_target_pairs={{0,10},{2,12},{4,14},{6,0},{8,2},{10,4},{12,6},{14,8},{1,11},{3,13... | collective-permute-start | bytes 614408 | tf_op jit(solution)/shard_map/ppermute | solution.py:412
  54.0 0.0 collective-permute-done.11.refs_3_
  54.0 2.0 %collective-permute-start.13 = (bf16[80,1280]{1,0:T(8,128)(2,1)S(1)}, bf16[80,1280]{1,0:T(8,128)(2,1)S(1)}, u32[]{:S(2)}, u32[]{:S(2)}) collective-permute-start(bf16[80,1280]{1,0:T(8,128)(2,1)S(1)} %get-tuple-element.91), channel_id=1, source_target_pairs={{0,12},{2,14},{4,0},{6,2},{8,4},{10,6},{12,8},{14,10},{1,13},{3,15... | collective-permute-start | bytes 614408 | tf_op jit(solution)/shard_map/ppermute | solution.py:412
  56.0 0.5 slice.9
  57.2 11.3 %collective-permute-done.12.refs_5_ = bf16[80,1280]{1,0:T(8,128)(2,1)S(1)} collective-permute-done((bf16[80,1280]{1,0:T(8,128)(2,1)S(1)}, bf16[80,1280]{1,0:T(8,128)(2,1)S(1)}, u32[]{:S(2)}, u32[]{:S(2)}) %collective-permute-start.12) | collective-permute-done | bytes 204832 | tf_op jit(solution)/shard_map/ppermute | solution.py:412
  68.5 0.0 collective-permute-done.13.refs_6_
  68.5 0.0 collective-permute-done.15.refs_9_
  68.5 0.0 collective-permute-done.16.refs_10_
  68.5 0.0 collective-permute-done.17.refs_12_
  68.5 0.0 copy-done.7
  68.5 0.0 copy-start.3
  68.6 0.0 copy-start.4
  68.6 0.0 copy-start.6
  68.6 0.0 copy-start.8
  68.6 7.4 %attend.1 = bf16[512,1280]{1,0:T(8,128)(2,1)} custom-call(s32[1]{0:T(128)} %bitcast.12.me_ref, s32[4,4]{1,0:T(4,128)S(1)} %copy-done.7, s32[1,512]{1,0:T(1,128)S(1)} %get-tuple-element.85.code_ref, bf16[80,1280]{1,0:T(8,128)(2,1)S(1)} %get-tuple-element.86.refs_0_, bf16[80,1280]{1,0:T(8,128)(2,1)S(1)} %collective-permute-done.9.refs_1_, ...), custom_call_target="tpu_custom_call" | custom-call | tf_op jit(solution)/shard_map/attend/pallas_call | solution.py:351
  76.0 0.0 copy-done.3
  76.1 0.2 conditional.1
  (5 shorter events, 0.0 us)
Async XLA Ops:
  0.0 11.1 %copy-start.1 = (bf16[512,1280]{1,0:T(8,128)(2,1)S(1)}, bf16[512,1280]{1,0:T(8,128)(2,1)}, u32[]{:S(2)}) copy-start(bf16[512,1280]{1,0:T(8,128)(2,1)} %q_ref.3) | copy-start | bytes 3932164
  2.8 6.4 %collective-permute-start.1 = (bf16[96,512]{1,0:T(8,128)(2,1)S(1)}, bf16[96,512]{1,0:T(8,128)(2,1)S(1)}, u32[]{:S(2)}, u32[]{:S(2)}) collective-permute-start(bf16[96,512]{1,0:T(8,128)(2,1)S(1)} %get-tuple-element.65), channel_id=1, source_target_pairs={{0,2},{2,4},{4,6},{6,8},{8,10},{10,12},{12,14},{14,0},{1,3},{3,5},... | collective-permute-start | bytes 294920 | tf_op jit(solution)/shard_map/ppermute | solution.py:412
  3.1 7.5 %collective-permute-start.2 = (bf16[96,512]{1,0:T(8,128)(2,1)S(1)}, bf16[96,512]{1,0:T(8,128)(2,1)S(1)}, u32[]{:S(2)}, u32[]{:S(2)}) collective-permute-start(bf16[96,512]{1,0:T(8,128)(2,1)S(1)} %get-tuple-element.66), channel_id=1, source_target_pairs={{0,4},{2,6},{4,8},{6,10},{8,12},{10,14},{12,0},{14,2},{1,5},{3,7},... | collective-permute-start | bytes 294920 | tf_op jit(solution)/shard_map/ppermute | solution.py:412
  4.6 8.4 %collective-permute-start.3 = (bf16[96,512]{1,0:T(8,128)(2,1)S(1)}, bf16[96,512]{1,0:T(8,128)(2,1)S(1)}, u32[]{:S(2)}, u32[]{:S(2)}) collective-permute-start(bf16[96,512]{1,0:T(8,128)(2,1)S(1)} %get-tuple-element.67), channel_id=1, source_target_pairs={{0,6},{2,8},{4,10},{6,12},{8,14},{10,0},{12,2},{14,4},{1,7},{3,9},... | collective-permute-start | bytes 294920 | tf_op jit(solution)/shard_map/ppermute | solution.py:412
  6.2 15.8 %collective-permute-start.4 = (bf16[96,512]{1,0:T(8,128)(2,1)S(1)}, bf16[96,512]{1,0:T(8,128)(2,1)S(1)}, u32[]{:S(2)}, u32[]{:S(2)}) collective-permute-start(bf16[96,512]{1,0:T(8,128)(2,1)S(1)} %get-tuple-element.68), channel_id=1, source_target_pairs={{0,8},{2,10},{4,12},{6,14},{8,0},{10,2},{12,4},{14,6},{1,9},{3,11}... | collective-permute-start | bytes 294920 | tf_op jit(solution)/shard_map/ppermute | solution.py:412
  7.5 15.8 %collective-permute-start.5 = (bf16[96,512]{1,0:T(8,128)(2,1)S(1)}, bf16[96,512]{1,0:T(8,128)(2,1)S(1)}, u32[]{:S(2)}, u32[]{:S(2)}) collective-permute-start(bf16[96,512]{1,0:T(8,128)(2,1)S(1)} %get-tuple-element.69), channel_id=1, source_target_pairs={{0,10},{2,12},{4,14},{6,0},{8,2},{10,4},{12,6},{14,8},{1,11},{3,13... | collective-permute-start | bytes 294920 | tf_op jit(solution)/shard_map/ppermute | solution.py:412
  9.3 14.0 %collective-permute-start.6 = (bf16[96,512]{1,0:T(8,128)(2,1)S(1)}, bf16[96,512]{1,0:T(8,128)(2,1)S(1)}, u32[]{:S(2)}, u32[]{:S(2)}) collective-permute-start(bf16[96,512]{1,0:T(8,128)(2,1)S(1)} %get-tuple-element.70), channel_id=1, source_target_pairs={{0,12},{2,14},{4,0},{6,2},{8,4},{10,6},{12,8},{14,10},{1,13},{3,15... | collective-permute-start | bytes 294920 | tf_op jit(solution)/shard_map/ppermute | solution.py:412
  10.6 12.6 %collective-permute-start.7 = (bf16[96,512]{1,0:T(8,128)(2,1)S(1)}, bf16[96,512]{1,0:T(8,128)(2,1)S(1)}, u32[]{:S(2)}, u32[]{:S(2)}) collective-permute-start(bf16[96,512]{1,0:T(8,128)(2,1)S(1)} %get-tuple-element.71), channel_id=1, source_target_pairs={{0,14},{2,0},{4,2},{6,4},{8,6},{10,8},{12,10},{14,12},{1,15},{3,1}... | collective-permute-start | bytes 294920 | tf_op jit(solution)/shard_map/ppermute | solution.py:412
  23.2 45.3 %copy-start.7 = (s32[4,4]{1,0:T(4,128)S(1)}, s32[4,4]{1,0:T(4,128)}, u32[]{:S(2)}) copy-start(s32[4,4]{1,0:T(4,128)} %anc_ref.1) | copy-start | bytes 196
  24.1 12.4 %collective-permute-start.8 = (bf16[80,1280]{1,0:T(8,128)(2,1)S(1)}, bf16[80,1280]{1,0:T(8,128)(2,1)S(1)}, u32[]{:S(2)}, u32[]{:S(2)}) collective-permute-start(bf16[80,1280]{1,0:T(8,128)(2,1)S(1)} %get-tuple-element.82), channel_id=1, source_target_pairs={{0,8},{2,10},{4,12},{6,14},{8,0},{10,2},{12,4},{14,6},{1,9},{3,11}... | collective-permute-start | bytes 614408 | tf_op jit(solution)/shard_map/ppermute | solution.py:412
  25.7 15.5 %collective-permute-start.9 = (bf16[80,1280]{1,0:T(8,128)(2,1)S(1)}, bf16[80,1280]{1,0:T(8,128)(2,1)S(1)}, u32[]{:S(2)}, u32[]{:S(2)}) collective-permute-start(bf16[80,1280]{1,0:T(8,128)(2,1)S(1)} %get-tuple-element.87), channel_id=1, source_target_pairs={{0,2},{2,4},{4,6},{6,8},{8,10},{10,12},{12,14},{14,0},{1,3},{3,5},... | collective-permute-start | bytes 614408 | tf_op jit(solution)/shard_map/ppermute | solution.py:412
  26.6 15.9 %collective-permute-start.14 = (bf16[80,1280]{1,0:T(8,128)(2,1)S(1)}, bf16[80,1280]{1,0:T(8,128)(2,1)S(1)}, u32[]{:S(2)}, u32[]{:S(2)}) collective-permute-start(bf16[80,1280]{1,0:T(8,128)(2,1)S(1)} %get-tuple-element.92), channel_id=1, source_target_pairs={{0,14},{2,0},{4,2},{6,4},{8,6},{10,8},{12,10},{14,12},{1,15},{3,1}... | collective-permute-start | bytes 614408 | tf_op jit(solution)/shard_map/ppermute | solution.py:412
  27.7 15.5 %collective-permute-start.10 = (bf16[80,1280]{1,0:T(8,128)(2,1)S(1)}, bf16[80,1280]{1,0:T(8,128)(2,1)S(1)}, u32[]{:S(2)}, u32[]{:S(2)}) collective-permute-start(bf16[80,1280]{1,0:T(8,128)(2,1)S(1)} %get-tuple-element.88), channel_id=1, source_target_pairs={{0,4},{2,6},{4,8},{6,10},{8,12},{10,14},{12,0},{14,2},{1,5},{3,7},... | collective-permute-start | bytes 614408 | tf_op jit(solution)/shard_map/ppermute | solution.py:412
  30.1 23.9 %collective-permute-start.11 = (bf16[80,1280]{1,0:T(8,128)(2,1)S(1)}, bf16[80,1280]{1,0:T(8,128)(2,1)S(1)}, u32[]{:S(2)}, u32[]{:S(2)}) collective-permute-start(bf16[80,1280]{1,0:T(8,128)(2,1)S(1)} %get-tuple-element.89), channel_id=1, source_target_pairs={{0,6},{2,8},{4,10},{6,12},{8,14},{10,0},{12,2},{14,4},{1,7},{3,9},... | collective-permute-start | bytes 614408 | tf_op jit(solution)/shard_map/ppermute | solution.py:412
  36.9 31.6 %collective-permute-start.15 = (bf16[512,256]{1,0:T(8,128)(2,1)S(1)}, bf16[512,256]{1,0:T(8,128)(2,1)S(1)}, u32[]{:S(2)}, u32[]{:S(2)}) collective-permute-start(bf16[512,256]{1,0:T(8,128)(2,1)S(1)} %get-tuple-element.97.refs_11_), channel_id=1, source_target_pairs={{0,2},{2,0},{4,6},{6,4},{8,10},{10,8},{12,14},{14,12},{1,3},{3,1},... | collective-permute-start | bytes 786440 | tf_op jit(solution)/shard_map/ppermute | solution.py:447
  41.3 27.3 %collective-permute-start.16 = (bf16[512,256]{1,0:T(8,128)(2,1)S(1)}, bf16[512,256]{1,0:T(8,128)(2,1)S(1)}, u32[]{:S(2)}, u32[]{:S(2)}) collective-permute-start(bf16[512,256]{1,0:T(8,128)(2,1)S(1)} %get-tuple-element.96.refs_8_), channel_id=1, source_target_pairs={{0,2},{2,4},{4,6},{6,8},{8,10},{10,12},{12,14},{1,3},{3,5},{5,7},{... | collective-permute-start | bytes 786440 | tf_op jit(solution)/shard_map/ppermute | solution.py:407
  42.6 26.0 %collective-permute-start.17 = (bf16[512,256]{1,0:T(8,128)(2,1)S(1)}, bf16[512,256]{1,0:T(8,128)(2,1)S(1)}, u32[]{:S(2)}, u32[]{:S(2)}) collective-permute-start(bf16[512,256]{1,0:T(8,128)(2,1)S(1)} %get-tuple-element.97.refs_11_), channel_id=1, source_target_pairs={{0,4},{4,8},{8,12},{1,5},{5,9},{9,13},{16,20},{20,24},{24,28},{17,... | collective-permute-start | bytes 786440 | tf_op jit(solution)/shard_map/ppermute | solution.py:446
  43.2 25.3 %collective-permute-start.12 = (bf16[80,1280]{1,0:T(8,128)(2,1)S(1)}, bf16[80,1280]{1,0:T(8,128)(2,1)S(1)}, u32[]{:S(2)}, u32[]{:S(2)}) collective-permute-start(bf16[80,1280]{1,0:T(8,128)(2,1)S(1)} %get-tuple-element.90), channel_id=1, source_target_pairs={{0,10},{2,12},{4,14},{6,0},{8,2},{10,4},{12,6},{14,8},{1,11},{3,13... | collective-permute-start | bytes 614408 | tf_op jit(solution)/shard_map/ppermute | solution.py:412
  54.0 14.5 %collective-permute-start.13 = (bf16[80,1280]{1,0:T(8,128)(2,1)S(1)}, bf16[80,1280]{1,0:T(8,128)(2,1)S(1)}, u32[]{:S(2)}, u32[]{:S(2)}) collective-permute-start(bf16[80,1280]{1,0:T(8,128)(2,1)S(1)} %get-tuple-element.91), channel_id=1, source_target_pairs={{0,12},{2,14},{4,0},{6,2},{8,4},{10,6},{12,8},{14,10},{1,13},{3,15... | collective-permute-start | bytes 614408 | tf_op jit(solution)/shard_map/ppermute | solution.py:412
  68.5 7.5 %copy-start.3 = (bf16[512,256]{1,0:T(8,128)(2,1)S(1)}, bf16[512,256]{1,0:T(8,128)(2,1)}, u32[]{:S(2)}) copy-start(bf16[512,256]{1,0:T(8,128)(2,1)} %k_ref.1) | copy-start | bytes 786436
  68.6 7.5 %copy-start.4 = (bf16[512,256]{1,0:T(8,128)(2,1)S(1)}, bf16[512,256]{1,0:T(8,128)(2,1)}, u32[]{:S(2)}) copy-start(bf16[512,256]{1,0:T(8,128)(2,1)} %v_ref.1) | copy-start | bytes 786436
  68.6 7.5 %copy-start.6 = (s32[512]{0:T(512)S(1)}, s32[512]{0:T(512)}, u32[]{:S(2)}) copy-start(s32[512]{0:T(512)} %dest_ref.1) | copy-start | bytes 6148
  68.6 7.5 %copy-start.8 = (s32[512]{0:T(512)S(1)}, s32[512]{0:T(512)}, u32[]{:S(2)}) copy-start(s32[512]{0:T(512)} %slot_ref.1) | copy-start | bytes 6148
